TPU v7x, 32 devices: a whole 2x2x4 slice. The times are simulated.
32 devices in a mesh: dp: 4 (over y, x), ctx: 4 (over z), tp: 2 (over core).
Axes of the slice: x: 2, y: 2, z: 4, core: 2. Of those that a mesh axis runs over, the one named last changes fastest.
Arguments:
- hidden: bfloat16 [4, 2048, 1024], P('dp', 'ctx'), may hold values from -6 to 6
- lengths: int32 [4], P('dp'), may hold values from 512 to 2048, as said below
- cotangent: bfloat16 [4, 2048, 1024], P('dp', 'ctx'), may hold values from -6 to 6
- norm_gain: float32 [1024], replicated, may hold values from 0.5 to 1.5
- proj_main: bfloat16 [1024, 2, 2048], P('dp', None, 'tp'), may hold values from -0.1875 to 0.1875
- proj_state: bfloat16 [1024, 256], P('dp'), may hold values from -0.1875 to 0.1875
- proj_delta: bfloat16 [1024, 32], P('dp', 'tp'), may hold values from -0.1875 to 0.1875
- conv_main: float32 [4, 2048], P(None, 'tp'), may hold values from -3 to 3
- conv_state: float32 [4, 256], replicated, may hold values from -3 to 3
- bias_main: float32 [2048], P('tp'), may hold values from -3 to 3
- bias_state: float32 [256], replicated, may hold values from -3 to 3
- delta_bias: float32 [32], P('tp'), may hold values from -5 to -3
- log_rate: float32 [32], P('tp'), may hold values from -5.5 to 0
- skip_gain: float32 [32], P('tp'), may hold values from 0.5 to 2
- gate_gain: float32 [2048], P('tp'), may hold values from 0.25 to 1.75
- proj_out: bfloat16 [1024, 2048], P('dp', 'tp'), may hold values from -0.125 to 0.125
Outputs:
- mixed: bfloat16 [4, 2048, 1024], P('dp', 'ctx')
- grad_hidden: float32 [4, 2048, 1024], P('dp', 'ctx')
- grad_norm_gain: float32 [1024], P(('dp', 'ctx'))
- grad_proj_main: float32 [1024, 2, 2048], P(('dp', 'ctx'), None, 'tp')
- grad_proj_state: float32 [1024, 256], P(('dp', 'ctx'))
- grad_proj_delta: float32 [1024, 32], P(('dp', 'ctx'), 'tp')
- grad_conv_main: float32 [4, 2048], P(None, 'tp')
- grad_conv_state: float32 [4, 256], replicated
- grad_bias_main: float32 [2048], P('tp')
- grad_bias_state: float32 [256], replicated
- grad_delta_bias: float32 [32], P('tp')
- grad_log_rate: float32 [32], P('tp')
- grad_skip_gain: float32 [32], P('tp')
- grad_gate_gain: float32 [2048], P('tp')
- grad_proj_out: float32 [1024, 2048], P(('dp', 'ctx'), 'tp')
Inputs may be any that keep to these rules, and one draw needn't show every extreme that they name: `lengths`: each sequence's valid tokens come first, the rest is padding.
All inputs are finite; a program needn't handle non-finite values.
Results may differ from a plain program's by a relative error of at most 0.00165.
The roundings to bfloat16 on the way count: a program that leaves them out, or rounds other values in their place, can miss the bound.
Values may be sent and summed in bfloat16 or wider, within the bound.
No kernel may reach another device: no remote copies, remote signals or barrier semaphores. Data moves between devices by JAX's collectives and lax.ppermute only.
A program may use at most 192 MiB of HBM per device.

v0:
```python
import jax
import jax.numpy as jnp
from jax import lax
from jax.sharding import PartitionSpec as P

BLOCK = 256


EPSILON = 1e-05
HIGHEST = lax.Precision.HIGHEST
ROWS_CONTRACT = (((0,), (0,)), ((), ()))
COLS_CONTRACT = (((1,), (1,)), ((), ()))


def passed_along(value, axis, steps):
    count = lax.axis_size(axis)
    first, last = (max(0, -steps), min(count, count - steps))
    return lax.ppermute(value, axis, [(source, source + steps) for source in range(first, last)])


def carried_in(value, axis, join, neutral, backward):
    count, mine = (lax.axis_size(axis), lax.axis_index(axis))
    pieces = jax.tree.map(lambda part: lax.all_gather(part, axis), value)
    if backward:
        pieces = jax.tree.map(lambda part: part[::-1], pieces)
        mine = count - 1 - mine
    so_far = jax.tree.map(
        lambda part, zero: jnp.full_like(part, 0) + jnp.asarray(zero, part.dtype), value, neutral
    )

    def hop(position, so_far):
        longer = join(so_far, jax.tree.map(lambda part: part[position], pieces))
        return jax.tree.map(lambda new, old: jnp.where(position < mine, new, old), longer, so_far)

    return lax.fori_loop(0, count - 1, hop, so_far)


def causal_mix(extended, conv_taps, conv_bias, steps):
    total = conv_bias + conv_taps[0] * extended[:, 0:steps]
    for tap in range(1, conv_taps.shape[0]):
        total = total + conv_taps[tap] * extended[:, tap : tap + steps]
    return total


def silu_slope(value):
    sigmoid = jax.nn.sigmoid(value)
    return sigmoid * (1.0 + value * (1.0 - sigmoid))


def local_scan(signal, inject, readout, delta, rate):
    batch, steps, heads, width = signal.shape
    states = inject.shape[-1]
    count = steps // BLOCK
    signal_blocks = signal.reshape(batch, count, BLOCK, heads, width)
    inject_blocks = inject.reshape(batch, count, BLOCK, states)
    readout_blocks = readout.reshape(batch, count, BLOCK, states)
    delta_blocks = delta.reshape(batch, count, BLOCK, heads)
    levels = jnp.cumsum(delta_blocks * rate, axis=2)
    lower = lax.broadcasted_iota(jnp.int32, (BLOCK, BLOCK), 0) >= lax.broadcasted_iota(
        jnp.int32, (BLOCK, BLOCK), 1
    )
    lower = lower[None, None, :, :, None]
    decay = jnp.where(
        lower,
        jnp.exp(jnp.where(lower, levels[:, :, :, None, :] - levels[:, :, None, :, :], 0.0)),
        0.0,
    )
    affinity = jnp.einsum("bcqn,bckn->bcqk", readout_blocks, inject_blocks, precision=HIGHEST)
    within = jnp.einsum(
        "bcqkh,bckhp->bcqhp",
        decay * affinity[..., None],
        signal_blocks * delta_blocks[..., None],
        precision=HIGHEST,
    )
    final_level = levels[:, :, -1]
    weights = jnp.exp(final_level[:, :, None, :] - levels) * delta_blocks
    fresh = jnp.einsum(
        "bckh,bckhp,bckn->bchpn", weights, signal_blocks, inject_blocks, precision=HIGHEST
    )
    carry = jnp.zeros((batch, heads, width, states), jnp.float32)
    entering = []
    for block in range(count):
        entering.append(carry)
        carry = jnp.exp(final_level[:, block])[:, :, None, None] * carry + fresh[:, block]
    entered = jnp.stack(entering, axis=1)
    across = (
        jnp.einsum("bcqn,bchpn->bcqhp", readout_blocks, entered, precision=HIGHEST)
        * jnp.exp(levels)[..., None]
    )
    before = jnp.cumsum(final_level, axis=1) - final_level
    growth = jnp.exp(levels + before[:, :, None, :]).reshape(batch, steps, heads)
    return ((within + across).reshape(batch, steps, heads, width), carry, growth)


def join_forward(earlier, later):
    return (earlier[0] * later[0], later[0][:, :, None, None] * earlier[1] + later[1])


def join_backward(earlier, later):
    return (later[0] * earlier[0], later[1] + later[0][:, :, None, None] * earlier[1])


def per_device(
    hidden,
    lengths,
    cotangent,
    norm_gain,
    proj_main,
    proj_state,
    proj_delta,
    conv_main,
    conv_state,
    bias_main,
    bias_state,
    delta_bias,
    log_rate,
    skip_gain,
    gate_gain,
    proj_out,
):
    batch, steps, model = hidden.shape
    heads = delta_bias.shape[0]
    inner = bias_main.shape[0]
    width = inner // heads
    states = bias_state.shape[0] // 2
    taps = conv_main.shape[0]
    rows = batch * steps
    full_main, full_state, full_delta, full_out = (
        lax.all_gather(proj_main, "dp", axis=0, tiled=True),
        lax.all_gather(proj_state, "dp", axis=0, tiled=True),
        lax.all_gather(proj_delta, "dp", axis=0, tiled=True),
        lax.all_gather(proj_out, "dp", axis=0, tiled=True),
    )
    main_matrix = full_main.reshape(model, 2 * inner)
    residual = hidden.astype(jnp.float32).reshape(rows, model)
    inverse = lax.rsqrt(jnp.mean(residual * residual, axis=1, keepdims=True) + EPSILON)
    scaled = residual * inverse
    normed = (scaled * norm_gain).astype(jnp.bfloat16)
    main_pre = jnp.dot(normed, main_matrix, preferred_element_type=jnp.float32)
    state_pre = jnp.dot(normed, full_state, preferred_element_type=jnp.float32)
    delta_raw = (
        jnp.dot(normed, full_delta, preferred_element_type=jnp.float32) + delta_bias
    ).reshape(batch, steps, heads)
    gate = main_pre[:, :inner]
    conv_in = jnp.concatenate([main_pre[:, inner:], state_pre], axis=1).reshape(
        batch, steps, inner + 2 * states
    )
    rim = passed_along(conv_in[:, steps - taps + 1 :], "ctx", 1)
    extended = jnp.concatenate([rim, conv_in], axis=1)
    conv_taps = jnp.concatenate([conv_main, conv_state], axis=1)
    conv_bias = jnp.concatenate([bias_main, bias_state])
    conv_out = causal_mix(extended, conv_taps, conv_bias, steps)
    activated = jax.nn.silu(conv_out)
    signal = activated[:, :, :inner].reshape(batch, steps, heads, width)
    inject = activated[:, :, inner : inner + states]
    readout = activated[:, :, inner + states :]
    position = lax.axis_index("ctx") * steps + lax.broadcasted_iota(jnp.int32, (batch, steps), 1)
    valid = (position < lengths[:, None]).astype(jnp.float32)
    delta = jax.nn.softplus(delta_raw) * valid[:, :, None]
    rate = -jnp.exp(log_rate)
    (partial_out, local_end, growth), pull_scan = jax.vjp(
        local_scan, signal, inject, readout, delta, rate
    )
    decay_total = growth[:, -1]
    carried_decay, carried_state = carried_in(
        (decay_total, local_end),
        "ctx",
        join_forward,
        (jnp.ones_like(decay_total), jnp.zeros_like(local_end)),
        False,
    )
    entry = jnp.einsum("bqn,bhpn->bqhp", readout, carried_state, precision=HIGHEST)
    output = partial_out + growth[..., None] * entry + skip_gain[:, None] * signal
    gate_act = jax.nn.silu(gate)
    output_rows = output.reshape(rows, inner)
    product = output_rows * gate_act
    square = lax.psum(jnp.sum(product * product, axis=1), "tp")
    total_inner = inner * lax.axis_size("tp")
    gate_inverse = lax.rsqrt(square / total_inner + EPSILON)[:, None]
    unit = product * gate_inverse
    gated = (unit * gate_gain).astype(jnp.bfloat16)
    branch_part = lax.dot_general(
        gated, full_out, COLS_CONTRACT, preferred_element_type=jnp.float32
    )
    branch = lax.psum(branch_part, "tp")
    valid_rows = valid.reshape(rows, 1)
    mixed = (residual + valid_rows * branch).astype(jnp.bfloat16).reshape(batch, steps, model)
    upstream = cotangent.astype(jnp.float32).reshape(rows, model)
    branch_grad = (valid_rows * upstream).astype(jnp.bfloat16)
    out_weight_grad = lax.dot_general(
        branch_grad, gated, ROWS_CONTRACT, preferred_element_type=jnp.float32
    )
    gated_grad = jnp.dot(branch_grad, full_out, preferred_element_type=jnp.float32)
    gate_gain_grad = jnp.sum(gated_grad * unit, axis=0)
    unit_grad = gated_grad * gate_gain
    inner_dot = lax.psum(jnp.sum(unit_grad * unit, axis=1), "tp")
    product_grad = gate_inverse * (unit_grad - unit * (inner_dot / total_inner)[:, None])
    output_grad = (product_grad * gate_act).reshape(batch, steps, heads, width)
    gate_grad = product_grad * output_rows * silu_slope(gate)
    skip_grad = jnp.sum(output_grad * signal, axis=(0, 1, 3))
    source = jnp.einsum("bqh,bqhp,bqn->bhpn", growth, output_grad, readout, precision=HIGHEST)
    later_decay, later_state = carried_in(
        (decay_total, source),
        "ctx",
        join_backward,
        (jnp.ones_like(decay_total), jnp.zeros_like(source)),
        True,
    )
    growth_grad = jnp.sum(output_grad * entry, axis=3)
    growth_grad = growth_grad.at[:, -1].add(jnp.sum(later_state * carried_state, axis=(2, 3)))
    readout_extra = jnp.einsum(
        "bqhp,bhpn->bqn", output_grad * growth[..., None], carried_state, precision=HIGHEST
    )
    signal_grad, inject_grad, readout_grad, delta_grad, rate_grad = pull_scan(
        (output_grad, later_state, growth_grad)
    )
    signal_grad = signal_grad + output_grad * skip_gain[:, None]
    readout_grad = readout_grad + readout_extra
    state_grad = lax.psum(jnp.concatenate([inject_grad, readout_grad], axis=2), "tp")
    raw_grad = delta_grad * valid[:, :, None] * jax.nn.sigmoid(delta_raw)
    delta_bias_grad = jnp.sum(raw_grad, axis=(0, 1))
    act_grad = jnp.concatenate([signal_grad.reshape(batch, steps, inner), state_grad], axis=2)
    conv_grad = act_grad * silu_slope(conv_out)
    ahead = passed_along(conv_grad[:, : taps - 1], "ctx", -1)
    following = jnp.concatenate([conv_grad, ahead], axis=1)
    pre_grad = conv_taps[0] * following[:, taps - 1 : taps - 1 + steps]
    for tap in range(1, taps):
        pre_grad = pre_grad + conv_taps[tap] * following[:, taps - 1 - tap : taps - 1 - tap + steps]
    taps_grad = jnp.stack(
        [jnp.sum(conv_grad * extended[:, tap : tap + steps], axis=(0, 1)) for tap in range(taps)]
    )
    conv_bias_grad = jnp.sum(conv_grad, axis=(0, 1))
    main_grad = jnp.concatenate(
        [gate_grad, pre_grad[:, :, :inner].reshape(rows, inner)], axis=1
    ).astype(jnp.bfloat16)
    state_pre_grad = pre_grad[:, :, inner:].reshape(rows, 2 * states).astype(jnp.bfloat16)
    delta_raw_grad = raw_grad.reshape(rows, heads).astype(jnp.bfloat16)
    main_weight_grad = lax.dot_general(
        normed, main_grad, ROWS_CONTRACT, preferred_element_type=jnp.float32
    ).reshape(model, 2, inner)
    state_weight_grad = lax.dot_general(
        normed, state_pre_grad, ROWS_CONTRACT, preferred_element_type=jnp.float32
    )
    delta_weight_grad = lax.dot_general(
        normed, delta_raw_grad, ROWS_CONTRACT, preferred_element_type=jnp.float32
    )
    feature_part = lax.dot_general(
        main_grad, main_matrix, COLS_CONTRACT, preferred_element_type=jnp.float32
    )
    feature_part = feature_part + lax.dot_general(
        delta_raw_grad, full_delta, COLS_CONTRACT, preferred_element_type=jnp.float32
    )
    feature_grad = lax.psum(feature_part, "tp")
    feature_grad = feature_grad + lax.dot_general(
        state_pre_grad, full_state, COLS_CONTRACT, preferred_element_type=jnp.float32
    )
    norm_gain_grad = jnp.sum(feature_grad * scaled, axis=0)
    scaled_grad = feature_grad * norm_gain
    input_grad = upstream + inverse * (
        scaled_grad - scaled * jnp.mean(scaled_grad * scaled, axis=1, keepdims=True)
    )
    grad_hidden = input_grad.reshape(batch, steps, model)
    gain_sum, main_sum, state_sum, delta_sum, out_sum = (
        lax.psum_scatter(norm_gain_grad, ("dp", "ctx"), scatter_dimension=0, tiled=True),
        lax.psum_scatter(main_weight_grad, ("dp", "ctx"), scatter_dimension=0, tiled=True),
        lax.psum_scatter(state_weight_grad, ("dp", "ctx"), scatter_dimension=0, tiled=True),
        lax.psum_scatter(delta_weight_grad, ("dp", "ctx"), scatter_dimension=0, tiled=True),
        lax.psum_scatter(out_weight_grad, ("dp", "ctx"), scatter_dimension=0, tiled=True),
    )
    small = lax.psum(
        (
            taps_grad[:, :inner],
            taps_grad[:, inner:],
            conv_bias_grad[:inner],
            conv_bias_grad[inner:],
            delta_bias_grad,
            rate_grad * rate,
            skip_grad,
            gate_gain_grad,
        ),
        ("dp", "ctx"),
    )
    return (
        mixed,
        grad_hidden,
        gain_sum,
        main_sum,
        state_sum,
        delta_sum,
        small[0],
        small[1],
        small[2],
        small[3],
        small[4],
        small[5],
        small[6],
        small[7],
        out_sum,
    )


def solution(mesh):
    in_specs = (
        P("dp", "ctx", None),
        P("dp"),
        P("dp", "ctx", None),
        P(),
        P("dp", None, "tp"),
        P("dp", None),
        P("dp", "tp"),
        P(None, "tp"),
        P(),
        P("tp"),
        P(),
        P("tp"),
        P("tp"),
        P("tp"),
        P("tp"),
        P("dp", "tp"),
    )
    out_specs = (
        P("dp", "ctx", None),
        P("dp", "ctx", None),
        P(("dp", "ctx")),
        P(("dp", "ctx"), None, "tp"),
        P(("dp", "ctx"), None),
        P(("dp", "ctx"), "tp"),
        P(None, "tp"),
        P(),
        P("tp"),
        P(),
        P("tp"),
        P("tp"),
        P("tp"),
        P("tp"),
        P(("dp", "ctx"), "tp"),
    )
    return jax.shard_map(
        per_device, mesh=mesh, in_specs=in_specs, out_specs=out_specs, check_vma=False
    )
```

profile of v0, /device:TPU:0, one launch (start us, length us, event | category | flops | bytes accessed | tf_op | source)
XLA Modules:
  0.0 830.9 jit_solution(10208562655331342029)
XLA Ops:
  8.7 9.8 %all_gather.28 = bf16[1024,16]{0,1:T(8,128)(2,1)S(1)} all-gather(bf16[256,16]{0,1:T(8,128)(2,1)} %param.28), channel_id=1, replica_groups=mesh['dp'=4,'ctx'=4,'tp'=2] {'dp'}, dimensions={0}, use_global_device_ids=true | all-gather | bytes 40960 | tf_op jit(solution)/shard_map/all_gather | solution.py:131
  23.3 14.6 %all_gather.27 = bf16[1024,256]{1,0:T(8,128)(2,1)S(1)} all-gather(bf16[256,256]{1,0:T(8,128)(2,1)S(1)} %copy-done.52), channel_id=1, replica_groups=mesh['dp'=4,'ctx'=4,'tp'=2] {'dp'}, dimensions={0}, use_global_device_ids=true | all-gather | bytes 655360 | tf_op jit(solution)/shard_map/all_gather | solution.py:130
  40.9 28.6 %all-gather.6.cloned.1.call-done = bf16[1024,2,1024]{2,1,0:T(2,128)(2,1)} async-done(((bf16[256,2,1024]{2,1,0:T(2,128)(2,1)}), bf16[1024,2,1024]{2,1,0:T(2,128)(2,1)}) %all-gather.6.cloned.1.call-update) | async-done | bytes 4194320 | tf_op jit(solution)/shard_map/all_gather | solution.py:129
  69.6 3.6 copy.300
  81.0 3.4 collective-permute-start
  106.8 11.9 %all_gather.29 = f32[4,1,16]{2,1,0:T(1,128)} all-gather(f32[1,1,16]{2,1,0:T(1,128)} %copy.236), channel_id=1, replica_groups=mesh['dp'=4,'ctx'=4,'tp'=2] {'ctx'}, dimensions={0}, use_global_device_ids=true | all-gather | bytes 320 | tf_op jit(solution)/shard_map/all_gather | solution.py:23
  130.6 5.0 reshape.826
  139.9 9.3 %bitcast_add_fusion.2 = f32[1,2,256,16,64]{2,4,3,1,0:T(8,128)S(1)} fusion(f32[2,256,16,64]{1,3,2,0:T(8,128)S(1)} %fusion.82, f32[2,256,256]{2,1,0:T(8,128)S(1)} %fusion.154, f32[2,256,16]{1,2,0:T(8,128)S(1)} %bitcast.410, pred[256,256]{1,0:T(8,128)(4,1)S(1)} %copy-done.59, f32[2,256,16,64]{1,0,3,2:T(2,128)S(1)} %broadcast_multiply_fusion, ...), kind=kOutput, calls=%fused_computation.78 | convolution fusion | flops 1620049920 | bytes 6946816 | tf_op jit(solution)/shard_map/jvp(bcqkh,bckhp->bcqhp)/dot_general | solution.py:69
  149.2 3.1 copy.233
  152.3 3.9 reshape.785
  156.2 4.5 copy.258
  160.8 7.1 while.29
  170.8 4.5 multiply_add_fusion
  175.3 2.9 copy.238
  178.2 4.7 multiply_reduce_fusion.9
  182.9 3.1 psum.91
  187.4 5.9 multiply_reduce_fusion.5
  193.3 3.1 psum.93
  197.1 6.6 fusion.50
  203.7 2.9 copy.240
  206.6 3.5 reshape_reshape.11
  210.1 3.6 reshape_reshape.12
  213.8 4.2 fusion.53
  218.0 15.5 %fusion.9 = (f32[2,256,16]{1,2,0:T(8,128)S(1)}, f32[2,256,16]{1,2,0:T(8,128)}, f32[2,256,256]{2,1,0:T(8,128)S(1)}) fusion(f32[2,256,256]{2,1,0:T(8,128)} %copy-done.42, f32[2,256,16]{1,2,0:T(8,128)} %bitcast.409, pred[256,256]{1,0:T(8,128)(4,1)} %iota_compare_fusion, f32[2,256,16,64]{1,0,3,2:T(2,128)} %copy-done.36, f32[2,16,64,256]{3,0,2,1:T(2,128)} %bitcast.379), kind=kOutput, calls=%fused_computation.17 | convolution fusion | flops 1633533952 | bytes 5406720 | tf_op jit(solution)/shard_map/transpose(jvp(bcqkh,bckhp->bcqhp))/dot_general | solution.py:69
  238.8 3.5 fusion.71
  248.6 8.6 %fusion.6 = f32[2,16,64,256]{3,2,1,0:T(8,128)} fusion(f32[2,256,256]{2,1,0:T(8,128)S(1)} %copy-done.43, f32[2,256,16]{1,2,0:T(8,128)S(1)} %bitcast.411, pred[256,256]{1,0:T(8,128)(4,1)S(1)} %copy-done.60, f32[2,16,64,256]{3,0,2,1:T(2,128)S(1)} %bitcast.380), kind=kOutput, calls=%fused_computation.14 | convolution fusion | flops 1619001344 | bytes 4816896 | tf_op jit(solution)/shard_map/transpose(jvp(bcqkh,bckhp->bcqhp))/dot_general | solution.py:69
  257.1 4.1 all-gather.12.cloned.1.call-done
  261.3 3.3 rev.6
  264.5 5.9 while.30
  290.2 5.8 reduce-window.16
  301.4 4.5 fusion.51
  305.9 4.9 copy.287
  310.7 5.0 reshape.825
  315.7 5.2 add_bitcast_fusion
  323.0 3.4 fusion.74
  332.2 12.7 %all-reduce.12.cloned.1.call-done = f32[1,512,256]{2,1,0:T(8,128)} async-done(((f32[1,512,256]{2,1,0:T(8,128)}), f32[1,512,256]{2,1,0:T(8,128)}) %all-reduce.12.cloned.1.call-update) | async-done | bytes 524304 | tf_op jit(solution)/shard_map/psum | solution.py:219
  344.9 4.4 fusion.145
  356.5 5.7 fusion.31
  363.4 5.4 convolution_add_fusion.1
  372.9 7.6 fusion.77
  383.3 4.6 fusion.104
  390.0 43.0 %reduce-scatter.13.cloned.1.call-done = f32[64,16]{1,0:T(8,128)} async-done(((f32[1024,16]{1,0:T(8,128)}), f32[64,16]{1,0:T(8,128)}) %reduce-scatter.13.cloned.1.call-update) | async-done | bytes 4112
  434.6 26.1 %all-reduce.14.cloned.1.call-done = (f32[512,1024]{1,0:T(8,128)}, f32[512,1024]{1,0:T(8,128)}) async-done(((f32[512,1024]{1,0:T(8,128)}, f32[512,1024]{1,0:T(8,128)}), (f32[512,1024]{1,0:T(8,128)}, f32[512,1024]{1,0:T(8,128)})) %all-reduce.14.cloned.1.call-update) | async-done | bytes 4194320 | tf_op jit(solution)/shard_map/psum | solution.py:185
  463.4 83.0 %all-reduce.7 = (f32[1024]{0:T(1024)S(1)}, f32[4,1024]{1,0:T(4,128)}, f32[4,256]{1,0:T(4,128)}, f32[1024]{0:T(1024)}, f32[256]{0:T(256)}, /*index=5*/f32[16]{0:T(128)}, f32[16]{0:T(128)}, f32[16]{0:T(128)}, f32[1024]{0:T(1024)}) all-reduce(f32[1024]{0:T(1024)S(1)} %get-tuple-element.356, ...), channel_id=3, replica_groups=mesh['dp'=4,'ctx'=4,'tp'=2] {'dp','ctx'}, use_global_device_ids=true, to_apply=%region_31.32.clone | all-reduce | flops 8496 | bytes 67968
  547.0 4.3 fusion.49
  551.3 97.3 %reduce-scatter.7.cloned.1.call-done = f32[64,2,1024]{2,0,1:T(8,128)} async-done(((f32[1024,2,1024]{2,0,1:T(8,128)}), f32[64,2,1024]{2,0,1:T(8,128)}) %reduce-scatter.7.cloned.1.call-update) | async-done | bytes 524304 | tf_op jit(solution)/shard_map/reduce_scatter | solution.py:265
  650.8 77.5 %reduce-scatter.9.cloned.1.call-done = f32[64,256]{1,0:T(8,128)} async-done(((f32[1024,256]{1,0:T(8,128)}), f32[64,256]{1,0:T(8,128)}) %reduce-scatter.9.cloned.1.call-update) | async-done | bytes 65552 | tf_op jit(solution)/shard_map/reduce_scatter | solution.py:266
  728.3 95.5 %reduce-scatter.11.cloned.1.call-done = f32[64,1024]{1,0:T(8,128)} async-done(((f32[1024,1024]{1,0:T(8,128)}), f32[64,1024]{1,0:T(8,128)}) %reduce-scatter.11.cloned.1.call-update) | async-done | bytes 262160 | tf_op jit(solution)/shard_map/reduce_scatter | solution.py:268
  (345 shorter events, 139.7 us)
Async XLA Ops:
  7.2 13.0 %copy-start.16 = (bf16[1,512,1024]{2,1,0:T(8,128)(2,1)S(1)}, bf16[1,512,1024]{2,1,0:T(8,128)(2,1)}, u32[]{:S(2)}) copy-start(bf16[1,512,1024]{2,1,0:T(8,128)(2,1)} %param.22) | copy-start | bytes 3145732
  7.2 13.0 %copy-start.72 = (f32[1024]{0:T(1024)S(1)}, f32[1024]{0:T(1024)}, u32[]{:S(2)}) copy-start(f32[1024]{0:T(1024)} %param.25) | copy-start | bytes 12292
  7.2 13.0 %copy-start.89 = (f32[16]{0:T(128)S(1)}, f32[16]{0:T(128)}, u32[]{:S(2)}) copy-start(f32[16]{0:T(128)} %param.33) | copy-start | bytes 196
  7.2 14.1 %copy-start.90 = (f32[16]{0:T(128)S(1)}, f32[16]{0:T(128)}, u32[]{:S(2)}) copy-start(f32[16]{0:T(128)} %param.34) | copy-start | bytes 196
  7.2 16.1 %copy-start.52 = (bf16[256,256]{1,0:T(8,128)(2,1)S(1)}, bf16[256,256]{1,0:T(8,128)(2,1)}, u32[]{:S(2)}) copy-start(bf16[256,256]{1,0:T(8,128)(2,1)} %param.27) | copy-start | bytes 393220
  7.2 62.3 %all-gather.6.cloned.1.call-start = ((), (), s32[]{:S(2)}) async-start(), calls=%async_computation.4 | async-start | bytes 5242880 | tf_op jit(solution)/shard_map/all_gather | solution.py:129
  8.0 29.9 %copy-start.76 = (f32[4,1024]{1,0:T(4,128)S(1)}, f32[4,1024]{1,0:T(4,128)}, u32[]{:S(2)}) copy-start(f32[4,1024]{1,0:T(4,128)} %param.29) | copy-start | bytes 49156
  8.0 152.8 %all-gather.8.cloned.1.call-start = ((), (), s32[]{:S(2)}) async-start(), calls=%async_computation.5 | async-start | bytes 2621440 | tf_op jit(solution)/shard_map/all_gather | solution.py:23
  8.0 29.9 %copy-start.82 = (f32[4,256]{1,0:T(4,128)S(1)}, f32[4,256]{1,0:T(4,128)}, u32[]{:S(2)}) copy-start(f32[4,256]{1,0:T(4,128)} %param.30) | copy-start | bytes 12292
  20.2 53.0 %copy-start.66 = (f32[512]{0:T(512)}, f32[512]{0:T(512)S(1)}, u32[]{:S(2)}) copy-start(f32[512]{0:T(512)S(1)} %add_rsqrt_fusion.1) | copy-start | bytes 6148
  21.3 79.5 %copy-start.44 = (f32[512,16]{0,1:T(8,128)}, f32[512,16]{0,1:T(8,128)S(1)}, u32[]{:S(2)}) copy-start(f32[512,16]{0,1:T(8,128)S(1)} %get-tuple-element.436) | copy-start | bytes 98308
  39.1 34.1 %copy-start.63 = (f32[2,16]{1,0:T(2,128)}, f32[2,16]{1,0:T(2,128)S(1)}, u32[]{:S(2)}) copy-start(f32[2,16]{1,0:T(2,128)S(1)} %slice_reduce_fusion.2) | copy-start | bytes 388
  39.1 46.7 %copy-start.55 = (f32[1280]{0:T(1024)}, f32[1280]{0:T(1024)S(1)}, u32[]{:S(2)}) copy-start(f32[1280]{0:T(1024)S(1)} %get-tuple-element.368) | copy-start | bytes 15364
  39.2 46.7 %copy-start.57 = (f32[1280]{0:T(1024)}, f32[1280]{0:T(1024)S(1)}, u32[]{:S(2)}) copy-start(f32[1280]{0:T(1024)S(1)} %get-tuple-element.369) | copy-start | bytes 15364
  39.2 58.7 %copy-start.77 = (f32[16]{0:T(128)}, f32[16]{0:T(128)S(1)}, u32[]{:S(2)}) copy-start(f32[16]{0:T(128)S(1)} %get-tuple-element.434) | copy-start | bytes 196
  39.2 58.7 %copy-start.79 = (f32[16]{0:T(128)}, f32[16]{0:T(128)S(1)}, u32[]{:S(2)}) copy-start(f32[16]{0:T(128)S(1)} %get-tuple-element.435) | copy-start | bytes 196
  40.9 44.9 %copy-start.30 = (f32[512,256]{1,0:T(8,128)}, f32[512,256]{1,0:T(8,128)S(1)}, u32[]{:S(2)}) copy-start(f32[512,256]{1,0:T(8,128)S(1)} %fusion.109) | copy-start | bytes 1572868
  81.0 7.7 copy-start.2
  81.0 4.9 collective-permute-start
  100.0 87.4 %all-gather.10.cloned.1.call-start = ((), (), s32[]{:S(2)}) async-start(), calls=%async_computation.6 | async-start | bytes 2621440 | tf_op jit(solution)/shard_map/all_gather | solution.py:132
  100.7 160.5 %all-gather.12.cloned.1.call-start = ((), (), s32[]{:S(2)}) async-start(), calls=%async_computation.11 | async-start | bytes 2621440 | tf_op jit(solution)/shard_map/all_gather | solution.py:23
  103.5 16.5 %copy-start.48 = (f32[1,2,256,16]{2,1,3,0:T(2,128)}, f32[1,2,256,16]{2,1,3,0:T(2,128)S(1)}, u32[]{:S(2)}) copy-start(f32[1,2,256,16]{2,1,3,0:T(2,128)S(1)} %copy.234) | copy-start | bytes 98308
  137.3 11.9 %copy-start.36 = (f32[2,256,16,64]{1,0,3,2:T(2,128)}, f32[2,256,16,64]{1,0,3,2:T(2,128)S(1)}, u32[]{:S(2)}) copy-start(f32[2,256,16,64]{1,0,3,2:T(2,128)S(1)} %broadcast_multiply_fusion) | copy-start | bytes 6291460
  139.2 10.0 %copy-start.20 = (f32[2,256,16,64]{1,3,2,0:T(8,128)}, f32[2,256,16,64]{1,3,2,0:T(8,128)S(1)}, u32[]{:S(2)}) copy-start(f32[2,256,16,64]{1,3,2,0:T(8,128)S(1)} %fusion.82) | copy-start | bytes 6291460
  139.8 9.4 %copy-start.42 = (f32[2,256,256]{2,1,0:T(8,128)}, f32[2,256,256]{2,1,0:T(8,128)S(1)}, u32[]{:S(2)}) copy-start(f32[2,256,256]{2,1,0:T(8,128)S(1)} %fusion.154) | copy-start | bytes 1572868
  218.0 126.9 %all-reduce.12.cloned.1.call-start = ((), (), s32[]{:S(2)}) async-start(), calls=%async_computation.7 | async-start | bytes 1048576 | tf_op jit(solution)/shard_map/psum | solution.py:219
  218.0 16.2 %copy-start = (f32[512,1024]{0,1:T(8,128)S(1)}, f32[512,1024]{0,1:T(8,128)}, u32[]{:S(2)}) copy-start(f32[512,1024]{0,1:T(8,128)} %copy.240) | copy-start | bytes 6291460
  218.0 16.2 %copy-start.12 = (f32[512,16,64]{0,2,1:T(8,128)S(1)}, f32[512,16,64]{0,2,1:T(8,128)}, u32[]{:S(2)}) copy-start(f32[512,16,64]{0,2,1:T(8,128)} %copy-done.11) | copy-start | bytes 6291460
  233.6 8.7 %copy-start.38 = (f32[2,256,256]{2,1,0:T(8,128)}, f32[2,256,256]{2,1,0:T(8,128)S(1)}, u32[]{:S(2)}) copy-start(f32[2,256,256]{2,1,0:T(8,128)S(1)} %get-tuple-element.350) | copy-start | bytes 1572868
  234.8 7.5 copy-start.49
  277.1 20.1 %copy-start.39 = (f32[2,256,256]{2,1,0:T(8,128)S(1)}, f32[2,256,256]{2,1,0:T(8,128)}, u32[]{:S(2)}) copy-start(f32[2,256,256]{2,1,0:T(8,128)} %copy-done.38) | copy-start | bytes 1572868
  279.7 21.7 %copy-start.10 = (f32[2,256,16,64]{1,3,2,0:T(8,128)S(1)}, f32[2,256,16,64]{1,3,2,0:T(8,128)}, u32[]{:S(2)}) copy-start(f32[2,256,16,64]{1,3,2,0:T(8,128)} %copy-done.9) | copy-start | bytes 6291460
  322.9 7.5 copy-start.51
  326.4 18.5 %copy-start.3 = (f32[1,512,1280]{2,1,0:T(8,128)S(1)}, f32[1,512,1280]{2,1,0:T(8,128)}, u32[]{:S(2)}) copy-start(f32[1,512,1280]{2,1,0:T(8,128)} %copy-done.2) | copy-start | bytes 7864324
  326.4 18.5 %copy-start.31 = (f32[512,256]{1,0:T(8,128)S(1)}, f32[512,256]{1,0:T(8,128)}, u32[]{:S(2)}) copy-start(f32[512,256]{1,0:T(8,128)} %copy-done.30) | copy-start | bytes 1572868
  327.2 17.6 %copy-start.54 = (f32[1,3,1280]{2,1,0:T(4,128)S(1)}, f32[1,3,1280]{2,1,0:T(4,128)}, u32[]{:S(2)}) copy-start(f32[1,3,1280]{2,1,0:T(4,128)} %copy-done.53) | copy-start | bytes 46084
  327.3 105.8 %reduce-scatter.13.cloned.1.call-start = ((), (), s32[]{:S(2)}) async-start(), calls=%async_computation.12 | async-start | bytes 557056
  344.9 7.2 copy-start.17
  344.9 7.2 copy-start.67
  344.9 7.2 copy-start.73
  349.3 7.2 copy-start.56
  350.8 5.7 collective-permute-start.1
  353.7 9.8 %copy-start.34 = (bf16[512,1024]{1,0:T(8,128)(2,1)S(1)}, bf16[512,1024]{1,0:T(8,128)(2,1)}, u32[]{:S(2)}) copy-start(bf16[512,1024]{1,0:T(8,128)(2,1)} %get-tuple-element.414) | copy-start | bytes 3145732
  353.7 107.0 %all-reduce.14.cloned.1.call-start = ((), (), s32[]{:S(2)}) async-start(), calls=%async_computation.13 | async-start | bytes 8388608 | tf_op jit(solution)/shard_map/psum | solution.py:185
  353.7 9.7 %copy-start.33 = (bf16[128,8,2,1024]{3,1,2,0:T(8,128)(2,1)S(1)}, bf16[128,8,2,1024]{3,1,2,0:T(8,128)(2,1)}, u32[]{:S(2)}) copy-start(bf16[128,8,2,1024]{3,1,2,0:T(8,128)(2,1)} %copy-done.32) | copy-start | bytes 12582916
  368.8 279.7 %reduce-scatter.7.cloned.1.call-start = ((), (), s32[]{:S(2)}) async-start(), calls=%async_computation.8 | async-start | bytes 8912896 | tf_op jit(solution)/shard_map/reduce_scatter | solution.py:265
  380.5 347.8 %reduce-scatter.9.cloned.1.call-start = ((), (), s32[]{:S(2)}) async-start(), calls=%async_computation.9 | async-start | bytes 1114112 | tf_op jit(solution)/shard_map/reduce_scatter | solution.py:266
  383.2 440.6 %reduce-scatter.11.cloned.1.call-start = ((), (), s32[]{:S(2)}) async-start(), calls=%async_computation.10 | async-start | bytes 4456448 | tf_op jit(solution)/shard_map/reduce_scatter | solution.py:268
  (57 other events, 157.4 us)
Sparse Core Ops, SparseCore 0:
  9.9 59.6 all-gather.5
  100.1 46.8 all-gather.7
  148.8 34.1 all-gather.9
  218.1 43.1 all-gather.11
  327.4 17.4 all-reduce.11
  353.8 79.1 reduce-scatter.12
  435.6 25.1 all-reduce.13
  463.1 185.4 reduce-scatter.6
  651.5 76.7 reduce-scatter.8
  731.0 92.7 reduce-scatter.10
where the time goes:
time: 842 us; the launch traced here: 831 us
  waiting for transfers between devices  391 us (46%)
  blocking collectives  126 us (15%)
  local copies, waits for them, and re-layouts  106 us (13%)
  matrix products  102 us (12%)
  other arithmetic  84.3 us (10%)
  between operations  17 us (2%)
    reduce_scatter x1, waiting for transfers between devices, per_device(): lax.psum_scatter(main_weight_grad, ('dp', 'ctx'), scatter_dimension=0, ti...  97.3 us
    reduce_scatter x1, waiting for transfers between devices, per_device(): lax.psum_scatter(out_weight_grad, ('dp', 'ctx'), scatter_dimension=0, til...  95.5 us
    unnamed x1, blocking collectives  83 us
    reduce_scatter x1, waiting for transfers between devices, per_device(): lax.psum_scatter(state_weight_grad, ('dp', 'ctx'), scatter_dimension=0, t...  77.5 us
    unnamed x11, waiting for transfers between devices  44.5 us
    dot_general x3, matrix products, local_scan(): jnp.einsum('bcqkh,bckhp->bcqhp', decay * affinity[..., None], signal_bloc...  33.4 us
    all_gather x1, waiting for transfers between devices, per_device(): lax.all_gather(proj_main, 'dp', axis=0, tiled=True)  28.6 us
    psum x1, waiting for transfers between devices, per_device(): branch = lax.psum(branch_part, 'tp')  26.1 us
  transfers between devices with their start and end apart: 12, of which 10 were waited for; matrix products, arithmetic and copies ran while one was open for 20% of the time, Pallas kernels for 0%

commit v1 on v0

v1 whole, which is shorter than its diff:
```python
import functools

import jax
import jax.numpy as jnp
from jax import lax
from jax.experimental import pallas as pl
from jax.experimental.pallas import tpu as pltpu
from jax.sharding import PartitionSpec as P

BLOCK = 256
EPSILON = 1e-05
HIGH = lax.Precision.HIGH
HIGHEST = lax.Precision.HIGHEST
F32 = jnp.float32
BF16 = jnp.bfloat16
NN = (((1,), (0,)), ((), ()))
NT = (((1,), (1,)), ((), ()))
TN = (((0,), (0,)), ((), ()))
HEAD0 = 64
LO, CORE, BASE, LENGTH, HASPREV, HASNEXT, SLOT0 = range(7)


def mm(a, b, dims=NN, precision=None):
    return lax.dot_general(a, b, dims, precision=precision, preferred_element_type=F32)


def grid_call(body, grid, in_specs, out_specs, out_shape, scratch=(), name=None):
    return pl.pallas_call(
        body,
        grid_spec=pltpu.PrefetchScalarGridSpec(
            num_scalar_prefetch=1,
            grid=grid,
            in_specs=in_specs,
            out_specs=out_specs,
            scratch_shapes=list(scratch),
        ),
        out_shape=out_shape,
        compiler_params=pltpu.CompilerParams(dimension_semantics=("arbitrary",) * len(grid)),
        name=name,
    )


def rows_spec(width, rows=BLOCK, lane=0):
    return pl.BlockSpec((rows, width), lambda b, s: (b, lane))


def whole(shape):
    return pl.BlockSpec(shape, lambda b, s: (0,) * len(shape))


def shaped(shape, dtype=F32):
    return jax.ShapeDtypeStruct(shape, dtype)


def slope(v, sig):
    return sig * (1.0 + v * (1.0 - sig))


def lanes_of(s_ref, slot, width):
    return pl.ds(pl.multiple_of(s_ref[SLOT0 + slot] * width, width), width)


def column_mask(width=128):
    lane = lax.broadcasted_iota(jnp.int32, (1, width), 1)
    return lane


def normalize(x, gain):
    value = x.astype(F32)
    inverse = lax.rsqrt(jnp.mean(value * value, axis=1, keepdims=True) + EPSILON)
    scaled = value * inverse
    return scaled, (scaled * gain).astype(BF16)


def pick(s_ref, b, quarter, own, near, far):
    lo, core = s_ref[LO], s_ref[CORE]
    place = b // quarter
    mine = (place // 2) == lo
    from_near = (place % 2) == core
    return jnp.where(mine, own, jnp.where(from_near, near, far))


def valid_rows(s_ref, b):
    position = s_ref[BASE] + b * BLOCK + lax.broadcasted_iota(jnp.int32, (BLOCK, 1), 0)
    return (position < s_ref[LENGTH]).astype(F32)


def lower_tri():
    row = lax.broadcasted_iota(jnp.int32, (BLOCK, BLOCK), 0)
    col = lax.broadcasted_iota(jnp.int32, (BLOCK, BLOCK), 1)
    return row, col


def front_body(parts, inner, states, quarter, s_ref, own, near, far, halo, gain, taps, bias, dbias, rate,
               expand, *rest):
    ws = rest[:parts]
    (normed_ref, scaled_ref, u_ref, uh_ref, co_ref, draw_ref, delta_ref, lev_ref, hloc_ref, pre_ref) = rest[
        parts : parts + 10
    ]
    hsc, usc, state, pre = rest[parts + 10 :]
    b = pl.program_id(0)
    wide = inner + 2 * states
    shard = ws[0].shape[0]
    scaled, normed = normalize(pick(s_ref, b, quarter, own[...], near[...], far[...]), gain[...])
    scaled_ref[...] = scaled
    normed_ref[...] = normed

    @pl.when(b == 0)
    def _():
        hsc[...] = normalize(halo[...], gain[...])[1]
        edge = jnp.zeros((16, wide), F32)
        for j in range(parts):
            edge += mm(hsc[:, lanes_of(s_ref, j, shard)], ws[j][:, :wide])
        edge = jnp.where(s_ref[HASPREV] > 0, edge[8:], 0.0)
        usc[0:8] = edge
        uh_ref[...] = edge
        state[...] = jnp.zeros_like(state)
        pre[...] = jnp.zeros_like(pre)

    @pl.when(b > 0)
    def _():
        usc[0:8] = usc[BLOCK : BLOCK + 8]

    u = jnp.zeros((BLOCK, wide + 128), F32)
    for j in range(parts):
        u += mm(normed_ref[:, lanes_of(s_ref, j, shard)], ws[j][...])
    usc[8 : 8 + BLOCK] = u[:, :wide]
    u_ref[...] = u[:, :wide]
    conv = bias[...] + taps[0:1] * usc[5 : 5 + BLOCK]
    for k in range(1, 4):
        conv = conv + taps[k : k + 1] * usc[5 + k : 5 + k + BLOCK]
    co_ref[...] = conv
    raw = u[:, wide:] + dbias[...]
    draw_ref[...] = raw
    lane = column_mask()
    heads = inner // 64
    use = (lane >= HEAD0) & (lane < HEAD0 + heads)
    delta = jnp.where(use, jnp.maximum(raw, 0.0) + jnp.log1p(jnp.exp(-jnp.abs(raw))), 0.0)
    delta = delta * valid_rows(s_ref, b)
    delta_ref[...] = delta
    row, col = lower_tri()
    lower = (row >= col).astype(F32)
    level = mm(lower, delta * rate[...], precision=HIGHEST)
    lev_ref[...] = level
    level_x = mm(level, expand[...], precision=HIGHEST)
    delta_x = mm(delta, expand[...], precision=HIGHEST)
    act = conv * jax.nn.sigmoid(conv)
    last = level_x[BLOCK - 1 : BLOCK]
    weighted = jnp.exp(last - level_x) * delta_x * act[:, :inner]
    inject_t = act[:, inner : inner + states].T
    fresh = mm(inject_t, weighted, precision=HIGH)
    before = state[...]

    hloc_ref[b] = before
    pre_ref[b] = pre[...]
    after = jnp.exp(last) * before + fresh
    state[...] = after
    pre[...] = pre[...] + last

    @pl.when(b == pl.num_programs(0) - 1)
    def _():
        hloc_ref[b + 1] = after
        pre_ref[b + 1] = pre[...]


def within_body(inner, states, s_ref, co, delta, lev, expand, yw_ref):
    conv = co[...]
    act = conv * jax.nn.sigmoid(conv)
    inject = act[:, inner : inner + states]
    readout = act[:, inner + states :]
    affinity = mm(readout, inject, NT, HIGH)
    level = lev[...]
    level_t = level.T
    xs = mm(delta[...], expand[...], precision=HIGHEST) * act[:, :inner]
    row, col = lower_tri()
    keep = row >= col
    half = lax.broadcasted_iota(jnp.int32, (1, 128), 1) < 64
    for pair in range(inner // 128):
        x = xs[:, pair * 128 : pair * 128 + 128]
        total = jnp.zeros((BLOCK, 128), F32)
        for side in range(2):
            h = HEAD0 + pair * 2 + side
            diff = level[:, h : h + 1] - level_t[h : h + 1, :]
            mix = jnp.exp(jnp.where(keep, diff, -1e30)) * affinity
            total += mm(mix, jnp.where(half if side == 0 else ~half, x, 0.0), precision=HIGH)
        yw_ref[:, pair * 128 : pair * 128 + 128] = total


def gates_body(parts, quarter, s_ref, normed, own, near, far, *rest):
    ws = rest[:parts]
    gate_ref, gg_ref, bg_ref = rest[parts:]
    b = pl.program_id(0)
    shard = ws[0].shape[0]
    inner = gate_ref.shape[1]
    up = pick(s_ref, b, quarter, own[...], near[...], far[...])
    bg_ref[...] = (up.astype(F32) * valid_rows(s_ref, b)).astype(BF16)
    gate = jnp.zeros(gate_ref.shape, F32)
    gg = jnp.zeros(gg_ref.shape, F32)
    for j in range(parts):
        at = lanes_of(s_ref, j, shard)
        gate += mm(normed[:, at], ws[j][:, :inner])
        gg += mm(bg_ref[:, at], ws[j][:, inner:])
    gate_ref[...] = gate
    gg_ref[...] = gg


def entering(hloc, pre, hin):
    return hloc + jnp.exp(pre[0:1]) * hin


def output_body(inner, states, s_ref, co, lev, yw, gate, gg, hloc, pre, hin, expand, skip, ggain, y_ref, sum_ref):
    conv = co[...]
    act = conv * jax.nn.sigmoid(conv)
    readout = act[:, inner + states :]
    level_x = mm(lev[...], expand[...], precision=HIGHEST)
    held = entering(hloc[0], pre[0], hin[...])
    y = yw[...] + jnp.exp(level_x) * mm(readout, held, precision=HIGH)
    y_ref[...] = y
    out = y + skip[...] * act[:, :inner]
    g = gate[...]
    product = out * (g * jax.nn.sigmoid(g))
    ones = jnp.ones((8, inner), F32)
    sum_ref[0:8] = mm(ones, product * product, NT, HIGHEST)
    sum_ref[8:16] = mm(ones, gg[...] * ggain[...] * product, NT, HIGHEST)


def turn_body(inner, states, total, s_ref, co, lev, y, gate, gg, sums, expand, skip, ggain,
              gated_ref, ggrad_ref, og_ref, gloc_ref, cols_ref, chain):
    step = pl.program_id(0)
    conv = co[...]
    act = conv * jax.nn.sigmoid(conv)
    x = act[:, :inner]
    readout_t = act[:, inner + states :].T
    level_x = mm(lev[...], expand[...], precision=HIGHEST)
    both = sums[...].T
    ginv = lax.rsqrt(both[:, 0:1] / total + EPSILON)
    dot = ginv * both[:, 8:9] / total
    g = gate[...]
    sig = jax.nn.sigmoid(g)
    ga = g * sig
    out = y[...] + skip[...] * x
    unit = out * ga * ginv
    gated_ref[...] = (unit * ggain[...]).astype(BF16)
    grad = gg[...]
    pg = ginv * (grad * ggain[...] - unit * dot)
    og = pg * ga
    og_ref[...] = og
    ggrad_ref[...] = (pg * out * slope(g, sig)).astype(BF16)

    @pl.when(step == 0)
    def _():
        chain[...] = jnp.zeros_like(chain)
        cols_ref[...] = jnp.zeros_like(cols_ref)

    cols_ref[0:1] += jnp.sum(grad * unit, axis=0, keepdims=True)
    cols_ref[1:2] += jnp.sum(og * x, axis=0, keepdims=True)
    b = pl.num_programs(0) - 1 - step
    held = chain[...]
    gloc_ref[b + 1] = held
    last = level_x[BLOCK - 1 : BLOCK]
    held = jnp.exp(last) * held + mm(readout_t, jnp.exp(level_x) * og, precision=HIGH)
    chain[...] = held

    @pl.when(b == 0)
    def _():
        gloc_ref[0] = held


def back_body(inner, states, s_ref, co, delta, lev, og, hloc, pre, hin, expand, z_ref, dbc_ref):
    conv = co[...]
    act = conv * jax.nn.sigmoid(conv)
    inject = act[:, inner : inner + states]
    readout = act[:, inner + states :]
    affinity = mm(inject, readout, NT, HIGH)
    level = lev[...]
    level_t = level.T
    level_x = mm(level, expand[...], precision=HIGHEST)
    xs = mm(delta[...], expand[...], precision=HIGHEST) * act[:, :inner]
    row, col = lower_tri()
    keep = col >= row
    half = lax.broadcasted_iota(jnp.int32, (1, 128), 1) < 64
    grad = jnp.zeros((BLOCK, BLOCK), F32)
    for pair in range(inner // 128):
        at = slice(pair * 128, pair * 128 + 128)
        x = xs[:, at]
        g = og[:, at]
        total = jnp.zeros((BLOCK, 128), F32)
        for side in range(2):
            h = HEAD0 + pair * 2 + side
            mine = half if side == 0 else ~half
            diff = level_t[h : h + 1, :] - level[:, h : h + 1]
            fade = jnp.exp(jnp.where(keep, diff, -1e30))
            total += mm(fade * affinity, jnp.where(mine, g, 0.0), precision=HIGH)
            grad += fade * mm(jnp.where(mine, x, 0.0), g, NT, HIGH)
        z_ref[:, at] = total
    held = entering(hloc[0], pre[0], hin[...])
    dbc_ref[:, :states] = mm(grad, readout, precision=HIGH)
    dbc_ref[:, states:] = mm(grad.T, inject, precision=HIGH) + mm(
        jnp.exp(level_x) * og[...], held, NT, HIGH
    )


def join_body(inner, states, s_ref, co, delta, lev, draw, og, y, z, dbc, hloc, pre, total, gloc, gin, hin,
              expand, rate, skip, cg_ref, dbco_ref, rg_ref, cols_ref):
    step = pl.program_id(0)
    conv = co[...]
    sig = jax.nn.sigmoid(conv)
    act = conv * sig
    x = act[:, :inner]
    inject = act[:, inner : inner + states]
    level_x = mm(lev[...], expand[...], precision=HIGHEST)
    dlt = delta[...]
    delta_x = mm(dlt, expand[...], precision=HIGHEST)
    last = level_x[BLOCK - 1 : BLOCK]
    later = gloc[0] + jnp.exp(total[0, 0:1] - pre[0, 0:1]) * gin[...]
    fade = jnp.exp(last - level_x)
    zed = z[...] + fade * mm(inject, later, precision=HIGH)
    dbco_ref[:, :states] = dbc[:, :states] + mm(fade * delta_x * x, later, NT, HIGH)
    dbco_ref[:, states:] = dbc[:, states:]
    g = og[...]
    dx = delta_x * zed + skip[...] * g
    cg_ref[...] = dx * slope(conv[:, :inner], sig[:, :inner])
    direct = mm(x * zed, expand[...], NT, HIGHEST)
    read = mm(g * y[...], expand[...], NT, HIGHEST)
    held = entering(hloc[0], pre[0], hin[...])
    ends = jnp.sum(later * held, axis=0, keepdims=True)
    ends = mm(jnp.broadcast_to(ends, (8, inner)), expand[...], NT, HIGHEST)[0:1]
    row, col = lower_tri()
    upper = (col >= row).astype(F32)
    q = mm(upper, read - dlt * direct, precision=HIGHEST) + ends
    b = pl.num_programs(0) - 1 - step
    lane = column_mask()
    use = (lane >= HEAD0) & (lane < HEAD0 + inner // 64)
    rg = (direct + rate[...] * q) * valid_rows(s_ref, b) * jax.nn.sigmoid(draw[...])
    rg = jnp.where(use, rg, 0.0)
    rg_ref[...] = rg

    @pl.when(step == 0)
    def _():
        cols_ref[...] = jnp.zeros_like(cols_ref)

    cols_ref[0:1] += jnp.sum(rg, axis=0, keepdims=True)
    cols_ref[1:2] += jnp.sum(jnp.where(use, dlt * q, 0.0), axis=0, keepdims=True)


def conv_body(mix, s_ref, cg, after, ahead, u, prior, uh, taps, *rest):
    if mix:
        rg, out_ref, cols_ref, csc, usc = rest
    else:
        out_ref, cols_ref, csc, usc = rest
    b = pl.program_id(0)
    count = pl.num_programs(0)
    grad = cg[...]
    csc[0:BLOCK] = grad
    csc[BLOCK : BLOCK + 8] = jnp.where(
        b == count - 1, jnp.where(s_ref[HASNEXT] > 0, ahead[...], 0.0), after[...]
    )
    usc[0:8] = jnp.where(b == 0, uh[...], prior[...])
    usc[8 : 8 + BLOCK] = u[...]
    pre = taps[0:1] * csc[3 : 3 + BLOCK]
    for k in range(1, 4):
        pre = pre + taps[k : k + 1] * csc[3 - k : 3 - k + BLOCK]

    @pl.when(b == 0)
    def _():
        cols_ref[...] = jnp.zeros_like(cols_ref)

    for k in range(4):
        cols_ref[k : k + 1] += jnp.sum(grad * usc[5 + k : 5 + k + BLOCK], axis=0, keepdims=True)
    cols_ref[4:5] += jnp.sum(grad, axis=0, keepdims=True)
    if mix:
        turned = pltpu.roll(pre, 64, 1)
        pre = jnp.where(s_ref[CORE] > 0, turned, pre)
        lane = lax.broadcasted_iota(jnp.int32, (BLOCK, 128), 1)
        pre = jnp.where(lane < HEAD0, pre, rg[...])
    out_ref[...] = pre.astype(BF16)


def weight_body(parts, s_ref, left, right, *outs):
    j = pl.program_id(0)
    value = mm(left[...], right[...], TN)
    for k in range(parts):

        @pl.when(j == k)
        def _():
            outs[k][...] = value


def feature_body(parts, s_ref, ggrad, mg, xg, scaled, *rest):
    ws1 = rest[:parts]
    ws2 = rest[parts : 2 * parts]
    out_ref, cols_ref = rest[2 * parts :]
    b = pl.program_id(0)
    inner = ggrad.shape[1]
    shard = ws1[0].shape[0]
    for j in range(parts):
        at = lanes_of(s_ref, j, shard)
        out_ref[:, at] = (
            mm(ggrad[...], ws2[j][:, :inner], NT)
            + mm(mg[...], ws1[j][:, :inner], NT)
            + mm(xg[...], ws1[j][:, -128:], NT)
        )

    @pl.when(b == 0)
    def _():
        cols_ref[...] = jnp.zeros_like(cols_ref)

    cols_ref[0:1] += jnp.sum(out_ref[...] * scaled[...], axis=0, keepdims=True)


def branch_body(parts, s_ref, gated, *rest):
    ws2 = rest[:parts]
    out_ref = rest[parts]
    inner = gated.shape[1]
    shard = ws2[0].shape[0]
    for j in range(parts):
        out_ref[:, lanes_of(s_ref, j, shard)] = mm(gated[...], ws2[j][:, inner:], NT)


def per_device(
    hidden, lengths, cotangent, norm_gain, proj_main, proj_state, proj_delta, conv_main, conv_state,
    bias_main, bias_state, delta_bias, log_rate, skip_gain, gate_gain, proj_out,
):
    _, steps, model = hidden.shape
    hidden, cotangent = hidden[0], cotangent[0]
    dps, ctxs, tps = lax.axis_size("dp"), lax.axis_size("ctx"), lax.axis_size("tp")
    dp, z, core = lax.axis_index("dp"), lax.axis_index("ctx"), lax.axis_index("tp")
    lo, hi = z % 2, z // 2
    pairs = ctxs // 2
    tokens = 2 * steps
    count = tokens // BLOCK
    quarter = count // 4
    inner = bias_main.shape[0] // 2
    heads = delta_bias.shape[0] // 2
    states = bias_state.shape[0] // 2
    wide = inner + 2 * states

    def swap(value):
        return lax.ppermute(value, "tp", [(0, 1), (1, 0)])

    def across(value, j):
        return lax.ppermute(value, "ctx", [(i, i ^ j) for i in range(ctxs)])

    def along(value, step):
        return lax.ppermute(
            value, "ctx", [(i, i + step) for i in range(ctxs) if 0 <= i + step < ctxs]
        )

    def spread(value, j):
        return lax.ppermute(value, "dp", [(i, i ^ j) for i in range(dps)])

    def mine(value, axis, size):
        return lax.dynamic_slice_in_dim(value, lo * size, size, axis)

    def piece(value, at, size):
        return lax.dynamic_slice_in_dim(value, at * size, size, 0)

    apart = proj_main.shape[0] % 128 == 0
    parts = dps if apart else 1
    shard = proj_main.shape[0] * (dps // parts)

    def gathered(value):
        if not apart:
            return [lax.all_gather(value, "dp", axis=0, tiled=True)]
        return [value] + [spread(value, j) for j in range(1, dps)]

    scalars = jnp.stack(
        [lo, core, hi * tokens, lengths[0], (hi > 0).astype(jnp.int32), (hi < pairs - 1).astype(jnp.int32)]
        + [dp ^ j if apart else 0 * dp for j in range(parts)]
    ).astype(jnp.int32)

    main_part = mine(proj_main, 2, inner)
    state_own = lax.dynamic_slice_in_dim(proj_state, lo * states + core * (states // 2), states // 2, 1)
    delta_own = mine(proj_delta, 1, heads)
    first = jnp.concatenate(
        [main_part[:, 1], proj_state, state_own, delta_own, jnp.zeros((proj_main.shape[0], 64 - heads), BF16)], axis=1
    )
    second = jnp.concatenate([main_part[:, 0], mine(proj_out, 1, inner)], axis=1)

    edge = along(hidden[steps - 16 :], 1)
    ws1 = gathered(first)
    halfway = steps // 2
    near = across(jnp.concatenate([piece(hidden, core, halfway), edge]), 1)
    halo = jnp.where(lo == 0, edge, near[halfway:])
    near = near[:halfway]
    far = swap(near)
    cot_near = across(piece(cotangent, core, halfway), 1)
    cot_far = swap(cot_near)
    ws2 = gathered(second)

    taps_x = jnp.concatenate([mine(conv_main, 1, inner), conv_state], axis=1)
    bias_x = jnp.concatenate([mine(bias_main, 0, inner), bias_state])[None]
    rate_own = -jnp.exp(mine(log_rate, 0, heads))

    def in_heads(value):
        return jnp.pad(value, (HEAD0, 128 - HEAD0 - heads))[None]

    rate_row = in_heads(rate_own)
    dbias_row = in_heads(mine(delta_bias, 0, heads))
    skip_row = jnp.repeat(mine(skip_gain, 0, heads), inner // heads)[None]
    ggain_row = mine(gate_gain, 0, inner)[None]
    gain_row = norm_gain[None]
    expand = (
        lax.broadcasted_iota(jnp.int32, (128, inner), 0) - HEAD0
        == lax.broadcasted_iota(jnp.int32, (128, inner), 1) // (inner // heads)
    ).astype(F32)

    own_spec = pl.BlockSpec(
        (BLOCK, model), lambda b, s: (jnp.clip(b - s[LO] * 2 * quarter, 0, 2 * quarter - 1), 0)
    )
    part_spec = pl.BlockSpec((BLOCK, model), lambda b, s: (b % quarter, 0))
    state_block = pl.BlockSpec((1, states, inner), lambda b, s: (b, 0, 0))
    pre_block = pl.BlockSpec((1, 8, inner), lambda b, s: (b, 0, 0))

    normed, scaled, u, uh, conv, draw, delta, level, hloc, pre = grid_call(
        functools.partial(front_body, parts, inner, states, quarter),
        (count,),
        [own_spec, part_spec, part_spec, whole((16, model)), whole((1, model)), whole((4, wide)),
         whole((1, wide)), whole((1, 128)), whole((1, 128)), whole((128, inner))]
        + [whole((shard, wide + 128))] * parts,
        [rows_spec(model), rows_spec(model), rows_spec(wide), whole((8, wide)), rows_spec(wide),
         rows_spec(128), rows_spec(128), rows_spec(128), whole((count + 1, states, inner)),
         whole((count + 1, 8, inner))],
        [shaped((tokens, model), BF16), shaped((tokens, model)), shaped((tokens, wide)), shaped((8, wide)),
         shaped((tokens, wide)), shaped((tokens, 128)), shaped((tokens, 128)), shaped((tokens, 128)),
         shaped((count + 1, states, inner)), shaped((count + 1, 8, inner))],
        [pltpu.VMEM((16, model), BF16), pltpu.VMEM((8 + BLOCK, wide), F32), pltpu.VMEM((states, inner), F32),
         pltpu.VMEM((8, inner), F32)],
        name="front",
    )(scalars, hidden, near, far, halo, gain_row, taps_x, bias_x, dbias_row, rate_row, expand, *ws1)

    own_end = hloc[count]
    growth = jnp.exp(pre[count][0:1])
    carried = jnp.zeros_like(own_end)
    sending = own_end
    for hop in range(pairs - 1):
        carried = along(sending, 2)
        if hop < pairs - 2:
            sending = own_end + growth * carried

    (inside,) = grid_call(
        functools.partial(within_body, inner, states),
        (count,),
        [rows_spec(wide), rows_spec(128), rows_spec(128), whole((128, inner))],
        [rows_spec(inner)],
        [shaped((tokens, inner))],
        name="within",
    )(scalars, conv, delta, level, expand)

    gate, gated_grad, branch_grad = grid_call(
        functools.partial(gates_body, parts, quarter),
        (count,),
        [rows_spec(model), own_spec, part_spec, part_spec] + [whole((shard, 2 * inner))] * parts,
        [rows_spec(inner), rows_spec(inner), rows_spec(model)],
        [shaped((tokens, inner)), shaped((tokens, inner)), shaped((tokens, model), BF16)],
        name="gates",
    )(scalars, normed, cotangent, cot_near, cot_far, *ws2)

    y, sums = grid_call(
        functools.partial(output_body, inner, states),
        (count,),
        [rows_spec(wide), rows_spec(128), rows_spec(inner), rows_spec(inner), rows_spec(inner), state_block,
         pre_block, whole((states, inner)), whole((128, inner)), whole((1, inner)), whole((1, inner))],
        [rows_spec(inner), pl.BlockSpec((16, BLOCK), lambda b, s: (0, b))],
        [shaped((tokens, inner)), shaped((16, tokens))],
        name="output",
    )(scalars, conv, level, inside, gate, gated_grad, hloc, pre, carried, expand, skip_row, ggain_row)

    sums = sums + swap(sums)
    sums = sums + across(sums, 1)

    def back(width, rows=BLOCK):
        return pl.BlockSpec((rows, width), lambda b, s: (count - 1 - b, 0))

    gated, gate_grad, out_grad, gloc, turn_cols = grid_call(
        functools.partial(turn_body, inner, states, 2 * tps * inner),
        (count,),
        [back(wide), back(128), back(inner), back(inner), back(inner),
         pl.BlockSpec((16, BLOCK), lambda b, s: (0, count - 1 - b)), whole((128, inner)), whole((1, inner)),
         whole((1, inner))],
        [back(inner), back(inner), back(inner), whole((count + 1, states, inner)), whole((8, inner))],
        [shaped((tokens, inner), BF16), shaped((tokens, inner), BF16), shaped((tokens, inner)),
         shaped((count + 1, states, inner)), shaped((8, inner))],
        [pltpu.VMEM((states, inner), F32)],
        name="turn",
    )(scalars, conv, level, y, gate, gated_grad, sums, expand, skip_row, ggain_row)

    own_start = gloc[0]
    returned = jnp.zeros_like(own_start)
    sending = own_start
    for hop in range(pairs - 1):
        returned = along(sending, -2)
        if hop < pairs - 2:
            sending = own_start + growth * returned

    zed, dbc = grid_call(
        functools.partial(back_body, inner, states),
        (count,),
        [rows_spec(wide), rows_spec(128), rows_spec(128), rows_spec(inner), state_block, pre_block,
         whole((states, inner)), whole((128, inner))],
        [rows_spec(inner), rows_spec(2 * states)],
        [shaped((tokens, inner)), shaped((tokens, 2 * states))],
        name="back",
    )(scalars, conv, delta, level, out_grad, hloc, pre, carried, expand)

    later_state = pl.BlockSpec((1, states, inner), lambda b, s: (count - b, 0, 0))
    later_pre = pl.BlockSpec((1, 8, inner), lambda b, s: (count - b, 0, 0))
    conv_grad, dbc, raw_grad, head_cols = grid_call(
        functools.partial(join_body, inner, states),
        (count,),
        [back(wide), back(128), back(128), back(128), back(inner), back(inner), back(inner), back(2 * states),
         later_state, later_pre, pl.BlockSpec((1, 8, inner), lambda b, s: (count, 0, 0)), later_state,
         whole((states, inner)), whole((states, inner)), whole((128, inner)), whole((1, 128)),
         whole((1, inner))],
        [back(inner), back(2 * states), back(128), whole((8, 128))],
        [shaped((tokens, inner)), shaped((tokens, 2 * states)), shaped((tokens, 128)), shaped((8, 128))],
        name="join",
    )(scalars, conv, delta, level, draw, out_grad, y, zed, dbc, hloc, pre, pre, gloc, returned, carried, expand,
      rate_row, skip_row)

    dbc = piece(dbc, core, tokens // 2) + swap(piece(dbc, 1 - core, tokens // 2))
    dbc = mine(dbc, 1, states) + across(lax.dynamic_slice_in_dim(dbc, (1 - lo) * states, states, 1), 1)
    other = swap(dbc)
    dbc = jnp.where(core == 0, jnp.concatenate([dbc, other]), jnp.concatenate([other, dbc]))
    conv_x = lax.dynamic_slice_in_dim(conv, inner + lo * states, states, 1)
    state_cg = dbc * slope(conv_x, jax.nn.sigmoid(conv_x))

    def conv_call(grad, lanes, width, name, mixed_in=None):
        ahead = along(grad[:8], -2)
        per = BLOCK // 8
        extra = [] if mixed_in is None else [mixed_in]
        return grid_call(
            functools.partial(conv_body, mixed_in is not None),
            (count,),
            [rows_spec(width),
             pl.BlockSpec((8, width), lambda b, s: (jnp.minimum((b + 1) * per, count * per - 1), 0)),
             whole((8, width)),
             pl.BlockSpec((BLOCK, width), lambda b, s: (b, lanes(s))),
             pl.BlockSpec((8, width), lambda b, s: (jnp.maximum(b * per - 1, 0), lanes(s))),
             pl.BlockSpec((8, width), lambda b, s: (0, lanes(s))),
             pl.BlockSpec((4, width), lambda b, s: (0, lanes(s)))] + [rows_spec(128)] * len(extra),
            [rows_spec(width), whole((8, width))],
            [shaped((tokens, width), BF16), shaped((8, width))],
            [pltpu.VMEM((BLOCK + 8, width), F32), pltpu.VMEM((BLOCK + 8, width), F32)],
            name=name,
        )(scalars, grad, grad, ahead, u, u, uh, taps_x, *extra)

    signal_pre, signal_cols = conv_call(conv_grad, lambda s: 0, inner, "conv_signal")
    extra_pre, state_cols = conv_call(
        state_cg, lambda s: inner // states + s[LO], states, "conv_state", raw_grad
    )

    def weight_grad(left, right, name):
        width = right.shape[1]
        return grid_call(
            functools.partial(weight_body, parts),
            (parts,),
            [pl.BlockSpec((tokens, shard), lambda j, s: (0, s[SLOT0 + j])), whole((tokens, width))],
            [whole((shard, width))] * parts,
            [shaped((shard, width))] * parts,
            name=name,
        )(scalars, left, right)

    def over_tokens(pieces):
        total = pieces[0]
        if not apart:
            total = lax.psum_scatter(total, "dp", scatter_dimension=0, tiled=True)
        for j in range(1, parts):
            total = total + spread(pieces[j], j)
        size = total.shape[0] // ctxs
        own = piece(total, z, size)
        width = total.shape[1]
        opposite = jnp.zeros((size, width), F32)
        for j in range(1, ctxs):
            got = across(piece(total, z ^ j, size), j)
            if j % 2 == 0:
                own = own + got
            else:
                opposite = opposite + got
        return jnp.where(lo == 0, own, opposite), jnp.where(lo == 0, opposite, own)

    gate_sum = over_tokens(weight_grad(normed, gate_grad, "grad_gate"))
    out_sum = over_tokens(weight_grad(branch_grad, gated, "grad_out"))
    signal_sum = over_tokens(weight_grad(normed, signal_pre, "grad_signal"))
    extra_sum = over_tokens(weight_grad(normed, extra_pre, "grad_extra"))

    (branch,) = grid_call(
        functools.partial(branch_body, parts),
        (count,),
        [rows_spec(inner)] + [whole((shard, 2 * inner))] * parts,
        [rows_spec(model)],
        [shaped((tokens, model))],
        name="branch",
    )(scalars, gated, *ws2)

    feature, feature_cols = grid_call(
        functools.partial(feature_body, parts),
        (count,),
        [rows_spec(inner), rows_spec(inner), rows_spec(128), rows_spec(model)]
        + [whole((shard, wide + 128))] * parts + [whole((shard, 2 * inner))] * parts,
        [rows_spec(model), whole((8, model))],
        [shaped((tokens, model)), shaped((8, model))],
        name="feature",
    )(scalars, gate_grad, signal_pre, extra_pre, scaled, *ws1, *ws2)

    def over_channels(value):
        value = value.reshape(2, 2, halfway, model)
        keep = lax.dynamic_index_in_dim(value, core, 1, False)
        give = lax.dynamic_index_in_dim(value, 1 - core, 1, False)
        value = keep + swap(give)
        return lax.dynamic_index_in_dim(value, lo, 0, False) + across(
            lax.dynamic_index_in_dim(value, 1 - lo, 0, False), 1
        )

    def both_halves(value):
        other = swap(value)
        return jnp.where(core == 0, jnp.concatenate([value, other]), jnp.concatenate([other, value]))

    residual = piece(hidden, core, halfway).astype(F32)
    place = z * steps + core * halfway + lax.broadcasted_iota(jnp.int32, (halfway, 1), 0)
    valid = (place < lengths[0]).astype(F32)
    mixed = both_halves((residual + valid * over_channels(branch)).astype(BF16))

    feature_grad = over_channels(feature)
    inverse = lax.rsqrt(jnp.mean(residual * residual, axis=1, keepdims=True) + EPSILON)
    scaled_own = residual * inverse
    scaled_grad = feature_grad * norm_gain
    upstream = piece(cotangent, core, halfway).astype(F32)
    grad_hidden = both_halves(
        upstream + inverse * (scaled_grad - scaled_own * jnp.mean(scaled_grad * scaled_own, axis=1, keepdims=True))
    )

    def halves(value, axis=-1):
        blank = jnp.zeros_like(value)
        return jnp.where(
            lo == 0, jnp.concatenate([value, blank], axis), jnp.concatenate([blank, value], axis)
        )

    skip_sum = turn_cols[1].reshape(heads, inner // heads).sum(axis=1)
    head_rows = head_cols[0:2, HEAD0 : HEAD0 + heads]
    small = lax.psum(
        (
            halves(signal_cols[:5]),
            halves(state_cols[:5]),
            halves(turn_cols[0:1]),
            halves(jnp.stack([head_rows[0], head_rows[1] * rate_own, skip_sum])),
        ),
        ("dp", "ctx"),
    )
    gain_sum = lax.psum(
        lax.psum_scatter(feature_cols[0], ("dp", "ctx"), scatter_dimension=0, tiled=True), "tp"
    )

    main_sum = jnp.stack(
        [jnp.concatenate(gate_sum, axis=1), jnp.concatenate(signal_sum, axis=1)], axis=1
    )
    delta_sum = jnp.concatenate([part[:, HEAD0 : HEAD0 + heads] for part in extra_sum], axis=1)
    state_here = jnp.stack([part[:, :HEAD0] for part in extra_sum])
    state_there = swap(state_here)
    in_order = jnp.where(
        core == 0, jnp.stack([state_here, state_there], 1), jnp.stack([state_there, state_here], 1)
    )
    state_sum = jnp.transpose(in_order, (2, 0, 1, 3)).reshape(-1, 2 * states)

    return (
        mixed[None],
        grad_hidden[None],
        gain_sum,
        main_sum,
        state_sum,
        delta_sum,
        small[0][:4],
        small[1][:4],
        small[0][4],
        small[1][4],
        small[3][0],
        small[3][1],
        small[3][2],
        small[2][0],
        jnp.concatenate(out_sum, axis=1),
    )


def solution(mesh):
    in_specs = (
        P("dp", "ctx", None), P("dp"), P("dp", "ctx", None), P(), P("dp", None, "tp"), P("dp", None),
        P("dp", "tp"), P(None, "tp"), P(), P("tp"), P(), P("tp"), P("tp"), P("tp"), P("tp"), P("dp", "tp"),
    )
    out_specs = (
        P("dp", "ctx", None), P("dp", "ctx", None), P(("dp", "ctx")), P(("dp", "ctx"), None, "tp"),
        P(("dp", "ctx"), None), P(("dp", "ctx"), "tp"), P(None, "tp"), P(), P("tp"), P(), P("tp"), P("tp"),
        P("tp"), P("tp"), P(("dp", "ctx"), "tp"),
    )
    return jax.shard_map(
        per_device, mesh=mesh, in_specs=in_specs, out_specs=out_specs, check_vma=False
    )
```

time: 842 us -> 439 us (0.52); the launches traced: 831 us -> 437 us
  waiting for transfers between devices: 391 us -> 49.5 us
  Pallas kernels: 0 us -> 141 us
  matrix products: 102 us -> 0 us
  local copies, waits for them, and re-layouts: 106 us -> 36 us
  starting transfers between devices: 5.08 us -> 71.1 us
  other arithmetic: 84.3 us -> 34.1 us
  blocking collectives: 126 us -> 102 us
  between operations: 17 us -> 2.98 us
    reduce_scatter x3 -> x0, waiting for transfers between devices: 270 us -> none  [the longest x1 97.3 us: per_device(): lax.psum_scatter(main_weight_grad, ('dp', 'ctx'), scatter_dimension=0, ti...]
    pallas_call x0 -> x15, Pallas kernels: none -> 141 us  [the longest x4 23.1 us: weight_grad(): grid_call(functools.partial(weight_body, parts), (parts,), [pl.BlockSpec(...]
    dot_general x26 -> x0, matrix products: 100 us -> none  [the longest x3 33.4 us: local_scan(): jnp.einsum('bcqkh,bckhp->bcqhp', decay * affinity[..., None], signal_bloc...]
    ppermute x2 -> x51, starting transfers between devices: 4.67 us -> 71.1 us  [the longest x18 34 us: across(): return lax.ppermute(value, 'ctx', [(i, i ^ j) for i in range(ctxs)])]
    ppermute x2 -> x51, waiting for transfers between devices: 4.17 us -> 49.5 us  [the longest x18 29.6 us: across(): return lax.ppermute(value, 'ctx', [(i, i ^ j) for i in range(ctxs)])]
    unnamed x11 -> x0, waiting for transfers between devices: 44.5 us -> none
    psum x2 -> x0, waiting for transfers between devices: 38.8 us -> none  [the longest x1 26.1 us: per_device(): branch = lax.psum(branch_part, 'tp')]
    all_gather x3 -> x0, blocking collectives: 36.3 us -> none  [the longest x1 14.6 us: per_device(): lax.all_gather(proj_state, 'dp', axis=0, tiled=True)]
  transfers between devices with their start and end apart: 12 -> 51, of which waited for: 10 -> 12; matrix products, arithmetic and copies ran while one was open for 20% -> 12% of each run, Pallas kernels for 0% -> 24%
where the time goes in v1:
time: 439 us; the launch traced here: 437 us
  Pallas kernels  141 us (32%)
  blocking collectives  102 us (23%)
  starting transfers between devices  71.1 us (16%)
  waiting for transfers between devices  49.5 us (11%)
  local copies, waits for them, and re-layouts  36 us (8%)
  other arithmetic  34.1 us (8%)
    unnamed x1, blocking collectives  99.3 us
    ppermute x18, starting transfers between devices, across(): return lax.ppermute(value, 'ctx', [(i, i ^ j) for i in range(ctxs)])  34 us
    ppermute x18, waiting for transfers between devices, across(): return lax.ppermute(value, 'ctx', [(i, i ^ j) for i in range(ctxs)])  29.6 us
    pallas_call x4, Pallas kernels, weight_grad(): grid_call(functools.partial(weight_body, parts), (parts,), [pl.BlockSpec(...  23.1 us
    ppermute x18, starting transfers between devices, spread(): return lax.ppermute(value, 'dp', [(i, i ^ j) for i in range(dps)])  23.1 us
    pallas_call x1, Pallas kernels, per_device(): grid_call(functools.partial(front_body, parts, inner, states, quarter), (...  18 us
    pallas_call x1, Pallas kernels, per_device(): grid_call(functools.partial(join_body, inner, states), (count,), [back(wi...  16.8 us
    ppermute x18, waiting for transfers between devices, spread(): return lax.ppermute(value, 'dp', [(i, i ^ j) for i in range(dps)])  16.7 us
  transfers between devices with their start and end apart: 51, of which 12 were waited for; matrix products, arithmetic and copies ran while one was open for 12% of the time, Pallas kernels for 24%

profile of v1, /device:TPU:0, one launch (start us, length us, event | category | flops | bytes accessed | tf_op | source)
XLA Modules:
  0.0 437.0 jit_solution(2202974533873171187)
XLA Ops:
  0.7 2.6 constant_dynamic-slice_fusion.18
  3.8 3.0 collective-permute-start.3
  9.7 4.5 %collective-permute-start = (bf16[16,1024]{1,0:T(8,128)(2,1)}, bf16[16,1024]{1,0:T(8,128)(2,1)}, u32[]{:S(2)}, u32[]{:S(2)}) collective-permute-start(bf16[16,1024]{1,0:T(8,128)(2,1)} %slice_bitcast_fusion.4), channel_id=1, source_target_pairs={{0,2},{2,4},{4,6},{1,3},{3,5},{5,7},{8,10},{10,12},{12,14},{9,11},... | collective-permute-start | bytes 98312 | tf_op jit(solution)/shard_map/ppermute | solution.py:445
  24.1 15.7 %collective-permute-done.1 = bf16[272,1024]{1,0:T(8,128)(2,1)S(1)} collective-permute-done((bf16[272,1024]{1,0:T(8,128)(2,1)S(1)}, bf16[272,1024]{1,0:T(8,128)(2,1)S(1)}, u32[]{:S(2)}, u32[]{:S(2)}) %collective-permute-start.1) | collective-permute-done | bytes 557088 | tf_op jit(solution)/shard_map/ppermute | solution.py:442
  41.5 1.6 collective-permute-start.8
  47.2 18.0 %front.1 = (bf16[1024,1024]{1,0:T(8,128)(2,1)}, f32[1024,1024]{1,0:T(8,128)}, f32[1024,768]{1,0:T(8,128)}, f32[8,768]{1,0:T(8,128)}, f32[1024,768]{1,0:T(8,128)}...) custom-call(s32[10]{0:T(128)} %stack.88.s_ref, ...), custom_call_target="tpu_custom_call" | custom-call | tf_op jit(solution)/shard_map/front/pallas_call | solution.py:515
  66.2 4.1 collective-permute-start.11
  71.8 10.0 %within.1.yw = f32[1024,512]{1,0:T(8,128)} custom-call(s32[10]{0:T(128)} %stack.88.s_ref, f32[1024,768]{1,0:T(8,128)} %get-tuple-element.63.co, f32[1024,128]{1,0:T(8,128)} %get-tuple-element.65.delta, f32[1024,128]{1,0:T(8,128)} %get-tuple-element.64.lev, f32[128,512]{1,0:T(8,128)} %fusion.11.expand), custom_call_target="tpu_custom_call" | custom-call | tf_op jit(solution)/shard_map/within/pallas_call | solution.py:541
  83.0 8.4 %gates.1 = (f32[1024,512]{1,0:T(8,128)}, f32[1024,512]{1,0:T(8,128)}, bf16[1024,1024]{1,0:T(8,128)(2,1)}) custom-call(s32[10]{0:T(128)} %stack.88.s_ref, bf16[1024,1024]{1,0:T(8,128)(2,1)} %get-tuple-element.66.normed.left, bf16[512,1024]{1,0:T(8,128)(2,1)} %bitcast.107, bf16[256,1024]{1,0:T(8,128)(2,1)} %collective-permute-done.6.near, ...), custom_call_target="tpu_custom_call" | custom-call | tf_op jit(solution)/shard_map/gates/pallas_call | solution.py:550
  92.1 10.7 %output.1 = (f32[1024,512]{1,0:T(8,128)}, f32[16,1024]{1,0:T(8,128)}) custom-call(s32[10]{0:T(128)} %stack.88.s_ref, f32[1024,768]{1,0:T(8,128)} %get-tuple-element.63.co, f32[1024,128]{1,0:T(8,128)} %get-tuple-element.64.lev, f32[1024,512]{1,0:T(8,128)} %within.1.yw, f32[1024,512]{1,0:T(8,128)} %get-tuple-element.67.gate, ...), custom_call_target="tpu_custom_call" | custom-call | tf_op jit(solution)/shard_map/output/pallas_call | solution.py:559
  106.1 3.4 collective-permute-done.13
  110.2 10.2 %turn.1 = (bf16[1024,512]{1,0:T(8,128)(2,1)}, bf16[1024,512]{1,0:T(8,128)(2,1)}, f32[1024,512]{1,0:T(8,128)}, f32[5,128,512]{2,1,0:T(8,128)}, f32[8,512]{1,0:T(8,128)}) custom-call(s32[10]{0:T(128)} %stack.88.s_ref, f32[1024,768]{1,0:T(8,128)} %get-tuple-element.63.co, f32[1024,128]{1,0:T(8,128)} %get-tuple-element.64.lev, f32[1024,512]{1,0:T(8,128)} %get-tuple-element.71.y, ...), custom_call_target="tpu_custom_call" | custom-call | tf_op jit(solution)/shard_map/turn/pallas_call | solution.py:575
  122.9 16.7 %back.1 = (f32[1024,512]{1,0:T(8,128)}, f32[1024,256]{1,0:T(8,128)}) custom-call(s32[10]{0:T(128)} %stack.88.s_ref, f32[1024,768]{1,0:T(8,128)} %get-tuple-element.63.co, f32[1024,128]{1,0:T(8,128)} %get-tuple-element.65.delta, f32[1024,128]{1,0:T(8,128)} %get-tuple-element.64.lev, f32[1024,512]{1,0:T(8,128)} %get-tuple-element.76.og, ...), custom_call_target="tpu_custom_call" | custom-call | tf_op jit(solution)/shard_map/back/pallas_call | solution.py:596
  140.3 16.8 %join.1 = (f32[1024,512]{1,0:T(8,128)}, f32[1024,256]{1,0:T(8,128)}, f32[1024,128]{1,0:T(8,128)}, f32[8,128]{1,0:T(8,128)}) custom-call(s32[10]{0:T(128)} %stack.88.s_ref, f32[1024,768]{1,0:T(8,128)} %get-tuple-element.63.co, f32[1024,128]{1,0:T(8,128)} %get-tuple-element.65.delta, f32[1024,128]{1,0:T(8,128)} %get-tuple-element.64.lev, ...), custom_call_target="tpu_custom_call" | custom-call | tf_op jit(solution)/shard_map/join/pallas_call | solution.py:608
  164.1 6.0 %grad_out.1 = (f32[256,512]{1,0:T(8,128)}, f32[256,512]{1,0:T(8,128)}, f32[256,512]{1,0:T(8,128)}, f32[256,512]{1,0:T(8,128)}) custom-call(s32[10]{0:T(128)} %stack.88.s_ref, bf16[1024,1024]{1,0:T(8,128)(2,1)} %get-tuple-element.106.left, bf16[1024,512]{1,0:T(8,128)(2,1)} %get-tuple-element.73.gated.right), custom_call_target="tpu_custom_call" | custom-call | tf_op jit(solution)/shard_map/grad_out/pallas_call | solution.py:655
  170.1 2.5 collective-permute-start.47
  173.6 6.2 %branch.1 = f32[1024,1024]{1,0:T(8,128)} custom-call(s32[10]{0:T(128)} %stack.88.s_ref, bf16[1024,512]{1,0:T(8,128)(2,1)} %get-tuple-element.73.gated.right, bf16[256,1024]{1,0:T(8,128)(2,1)} %copy-done.5, bf16[256,1024]{1,0:T(8,128)(2,1)} %copy-done.7, bf16[256,1024]{1,0:T(8,128)(2,1)} %copy-done.8, bf16[256,1024]{1,0:T(8,128)(2,1)} %copy-done.9), custom_call_target="tpu_custom_call" | custom-call | tf_op jit(solution)/shard_map/branch/pallas_call | solution.py:687
  180.7 3.2 dynamic-slice_bitcast_fusion.1
  184.6 6.0 %grad_gate.1 = (f32[256,512]{1,0:T(8,128)}, f32[256,512]{1,0:T(8,128)}, f32[256,512]{1,0:T(8,128)}, f32[256,512]{1,0:T(8,128)}) custom-call(s32[10]{0:T(128)} %stack.88.s_ref, bf16[1024,1024]{1,0:T(8,128)(2,1)} %get-tuple-element.66.normed.left, bf16[1024,512]{1,0:T(8,128)(2,1)} %get-tuple-element.74.ggrad.right), custom_call_target="tpu_custom_call" | custom-call | tf_op jit(solution)/shard_map/grad_gate/pallas_call | solution.py:655
  194.5 1.6 collective-permute-start.22
  198.7 2.5 collective-permute-start.28
  201.1 6.9 %conv_signal.1 = (bf16[1024,512]{1,0:T(8,128)(2,1)}, f32[8,512]{1,0:T(8,128)}) custom-call(s32[10]{0:T(128)} %stack.88.s_ref, f32[1024,512]{1,0:T(8,128)} %get-tuple-element.80.cg.after, f32[1024,512]{1,0:T(8,128)} %get-tuple-element.80.cg.after, f32[8,512]{1,0:T(8,128)} %copy-done.25, f32[1024,768]{1,0:T(8,128)} %get-tuple-element.81.u.prior, ...), custom_call_target="tpu_custom_call" | custom-call | tf_op jit(solution)/shard_map/conv_signal/pallas_call | solution.py:632
  208.6 4.4 %conv_state.1 = (bf16[1024,128]{1,0:T(8,128)(2,1)}, f32[8,128]{1,0:T(8,128)}) custom-call(s32[10]{0:T(128)} %stack.88.s_ref, f32[1024,128]{1,0:T(8,128)} %copy-done.6, f32[1024,128]{1,0:T(8,128)} %copy-done.6, f32[8,128]{1,0:T(8,128)} %copy-done.31, f32[1024,768]{1,0:T(8,128)} %get-tuple-element.81.u.prior, f32[1024,768]{1,0:T(8,128)} %get-tuple-element.81.u.prior, ...), custom_call_target="tpu_custom_call" | custom-call | tf_op jit(solution)/shard_map/conv_state/pallas_call | solution.py:632
  213.0 9.3 %feature.1 = (f32[1024,1024]{1,0:T(8,128)}, f32[8,1024]{1,0:T(8,128)}) custom-call(s32[10]{0:T(128)} %stack.88.s_ref, bf16[1024,512]{1,0:T(8,128)(2,1)} %get-tuple-element.74.ggrad.right, bf16[1024,512]{1,0:T(8,128)(2,1)} %get-tuple-element.83.mg.right, bf16[1024,128]{1,0:T(8,128)(2,1)} %get-tuple-element.86.xg.right, ...), custom_call_target="tpu_custom_call" | custom-call | tf_op jit(solution)/shard_map/feature/pallas_call | solution.py:696
  222.2 1.8 dynamic-slice_bitcast_fusion
  224.8 1.6 add_add_fusion
  227.8 3.8 collective-permute-start.50
  232.3 6.1 %grad_signal.1 = (f32[256,512]{1,0:T(8,128)}, f32[256,512]{1,0:T(8,128)}, f32[256,512]{1,0:T(8,128)}, f32[256,512]{1,0:T(8,128)}) custom-call(s32[10]{0:T(128)} %stack.88.s_ref, bf16[1024,1024]{1,0:T(8,128)(2,1)} %get-tuple-element.66.normed.left, bf16[1024,512]{1,0:T(8,128)(2,1)} %get-tuple-element.83.mg.right), custom_call_target="tpu_custom_call" | custom-call | tf_op jit(solution)/shard_map/grad_signal/pallas_call | solution.py:655
  238.5 2.4 collective-permute-start.34
  241.4 2.3 collective-permute-done.48
  245.7 1.7 add_add_fusion.2
  247.5 6.9 %collective-permute-done.34 = f32[256,512]{1,0:T(8,128)S(1)} collective-permute-done((f32[256,512]{1,0:T(8,128)}, f32[256,512]{1,0:T(8,128)S(1)}, u32[]{:S(2)}, u32[]{:S(2)}) %collective-permute-start.34) | collective-permute-done | bytes 524320 | tf_op jit(solution)/shard_map/ppermute | solution.py:450
  255.6 9.6 %collective-permute-done.33 = f32[256,512]{1,0:T(8,128)S(1)} collective-permute-done((f32[256,512]{1,0:T(8,128)}, f32[256,512]{1,0:T(8,128)S(1)}, u32[]{:S(2)}, u32[]{:S(2)}) %collective-permute-start.33) | collective-permute-done | bytes 524320 | tf_op jit(solution)/shard_map/ppermute | solution.py:450
  265.2 4.2 collective-permute-start.31
  269.7 3.0 collective-permute-start.35
  273.8 8.2 %collective-permute-start.36 = (f32[64,512]{1,0:T(8,128)S(1)}, f32[64,512]{1,0:T(8,128)S(1)}, u32[]{:S(2)}, u32[]{:S(2)}) collective-permute-start(f32[64,512]{1,0:T(8,128)S(1)} %get-tuple-element.179), channel_id=1, source_target_pairs={{0,2},{2,0},{4,6},{6,4},{1,3},{3,1},{5,7},{7,5},{8,10},{10,8},{12,... | collective-permute-start | bytes 393224 | tf_op jit(solution)/shard_map/ppermute | solution.py:442
  282.0 2.3 collective-permute-done.29
  284.4 3.0 collective-permute-start.37
  287.4 4.7 %collective-permute-done.36 = f32[64,512]{1,0:T(8,128)S(1)} collective-permute-done((f32[64,512]{1,0:T(8,128)S(1)}, f32[64,512]{1,0:T(8,128)S(1)}, u32[]{:S(2)}, u32[]{:S(2)}) %collective-permute-start.36) | collective-permute-done | bytes 131104 | tf_op jit(solution)/shard_map/ppermute | solution.py:442
  293.3 2.1 bitcast_add_fusion
  301.6 4.9 %grad_extra.1 = (f32[256,128]{1,0:T(8,128)}, f32[256,128]{1,0:T(8,128)}, f32[256,128]{1,0:T(8,128)}, f32[256,128]{1,0:T(8,128)}) custom-call(s32[10]{0:T(128)} %stack.88.s_ref, bf16[1024,1024]{1,0:T(8,128)(2,1)} %get-tuple-element.66.normed.left, bf16[1024,128]{1,0:T(8,128)(2,1)} %get-tuple-element.86.xg.right), custom_call_target="tpu_custom_call" | custom-call | tf_op jit(solution)/shard_map/grad_extra/pallas_call | solution.py:655
  306.5 1.6 collective-permute-start.40
  313.5 99.3 %all-reduce.11 = (f32[1024]{0:T(1024)}, f32[5,1024]{1,0:T(8,128)}, f32[5,256]{1,0:T(8,128)}, f32[3,16]{1,0:T(4,128)}, f32[1024]{0:T(1024)}) all-reduce(f32[1024]{0:T(1024)S(1)} %bitcast.119, f32[5,1024]{1,0:T(8,128)} %pad_select_fusion, f32[5,256]{1,0:T(8,128)S(1)} %pad_select_fusion.1, ...), channel_id=2, replica_groups=mesh['dp'=4,'ctx'=4,'tp'=2] {'dp','ctx'}, use_global_device_ids=true, to_apply=%region_2.3.clone | all-reduce | flops 8496 | bytes 67968
  414.2 3.4 collective-permute-start.41
  417.6 1.6 fusion.2
  419.3 3.1 fusion.5
  426.0 3.1 psum.35
  433.7 3.3 maximum_select_fusion
  (264 shorter events, 75.6 us)
Async XLA Ops:
  3.8 37.6 %collective-permute-start.3 = (bf16[256,896]{1,0:T(8,128)(2,1)S(1)}, bf16[256,896]{1,0:T(8,128)(2,1)S(1)}, u32[]{:S(2)}, u32[]{:S(2)}) collective-permute-start(bf16[256,896]{1,0:T(8,128)(2,1)S(1)} %concatenate.108.rest_0_), channel_id=1, source_target_pairs={{0,8},{8,0},{16,24},{24,16},{1,9},{9,1},{17,25},{25,17},{2,10},{10... | collective-permute-start | bytes 1376264 | tf_op jit(solution)/shard_map/ppermute | solution.py:450
  6.8 36.2 %collective-permute-start.4 = (bf16[256,896]{1,0:T(8,128)(2,1)S(1)}, bf16[256,896]{1,0:T(8,128)(2,1)}, u32[]{:S(2)}, u32[]{:S(2)}) collective-permute-start(bf16[256,896]{1,0:T(8,128)(2,1)S(1)} %concatenate.108.rest_0_), channel_id=1, source_target_pairs={{0,16},{8,24},{16,0},{24,8},{1,17},{9,25},{17,1},{25,9},{2,18},{10... | collective-permute-start | bytes 1376264 | tf_op jit(solution)/shard_map/ppermute | solution.py:450
  8.3 36.2 %collective-permute-start.5 = (bf16[256,896]{1,0:T(8,128)(2,1)S(1)}, bf16[256,896]{1,0:T(8,128)(2,1)}, u32[]{:S(2)}, u32[]{:S(2)}) collective-permute-start(bf16[256,896]{1,0:T(8,128)(2,1)S(1)} %concatenate.108.rest_0_), channel_id=1, source_target_pairs={{0,24},{8,16},{16,8},{24,0},{1,25},{9,17},{17,9},{25,1},{2,26},{10... | collective-permute-start | bytes 1376264 | tf_op jit(solution)/shard_map/ppermute | solution.py:450
  9.7 9.2 %collective-permute-start = (bf16[16,1024]{1,0:T(8,128)(2,1)}, bf16[16,1024]{1,0:T(8,128)(2,1)}, u32[]{:S(2)}, u32[]{:S(2)}) collective-permute-start(bf16[16,1024]{1,0:T(8,128)(2,1)} %slice_bitcast_fusion.4), channel_id=1, source_target_pairs={{0,2},{2,4},{4,6},{1,3},{3,5},{5,7},{8,10},{10,12},{12,14},{9,11},... | collective-permute-start | bytes 98312 | tf_op jit(solution)/shard_map/ppermute | solution.py:445
  15.1 29.9 %collective-permute-start.6 = (bf16[256,1024]{1,0:T(8,128)(2,1)}, bf16[256,1024]{1,0:T(8,128)(2,1)}, u32[]{:S(2)}, u32[]{:S(2)}) collective-permute-start(bf16[256,1024]{1,0:T(8,128)(2,1)} %dynamic-slice_bitcast_fusion.4), channel_id=1, source_target_pairs={{0,2},{2,0},{4,6},{6,4},{1,3},{3,1},{5,7},{7,5},{8,10},{10,8},{12,... | collective-permute-start | bytes 1572872 | tf_op jit(solution)/shard_map/ppermute | solution.py:442
  19.7 20.1 %collective-permute-start.1 = (bf16[272,1024]{1,0:T(8,128)(2,1)S(1)}, bf16[272,1024]{1,0:T(8,128)(2,1)S(1)}, u32[]{:S(2)}, u32[]{:S(2)}) collective-permute-start(bf16[272,1024]{1,0:T(8,128)(2,1)S(1)} %pad_maximum_fusion), channel_id=1, source_target_pairs={{0,2},{2,0},{4,6},{6,4},{1,3},{3,1},{5,7},{7,5},{8,10},{10,8},{12,... | collective-permute-start | bytes 1671176 | tf_op jit(solution)/shard_map/ppermute | solution.py:442
  39.8 6.6 %collective-permute-start.2 = (bf16[256,1024]{1,0:T(8,128)(2,1)S(1)}, bf16[256,1024]{1,0:T(8,128)(2,1)S(1)}, u32[]{:S(2)}, u32[]{:S(2)}) collective-permute-start(bf16[256,1024]{1,0:T(8,128)(2,1)S(1)} %slice.115.near), channel_id=1, source_target_pairs={{0,1},{1,0},{2,3},{3,2},{4,5},{5,4},{6,7},{7,6},{8,9},{9,8},{10,11... | collective-permute-start | bytes 1572872 | tf_op jit(solution)/shard_map/ppermute | solution.py:439
  41.5 40.4 %collective-permute-start.8 = (bf16[256,1024]{1,0:T(8,128)(2,1)S(1)}, bf16[256,1024]{1,0:T(8,128)(2,1)S(1)}, u32[]{:S(2)}, u32[]{:S(2)}) collective-permute-start(bf16[256,1024]{1,0:T(8,128)(2,1)S(1)} %pad_maximum_fusion.1.rest_0_.rest_4_), channel_id=1, source_target_pairs={{0,8},{8,0},{16,24},{24,16},{1,9},{9,1},{17,25},{25,17},{2,10},{10... | collective-permute-start | bytes 1572872 | tf_op jit(solution)/shard_map/ppermute | solution.py:450
  43.0 38.9 %collective-permute-start.9 = (bf16[256,1024]{1,0:T(8,128)(2,1)S(1)}, bf16[256,1024]{1,0:T(8,128)(2,1)S(1)}, u32[]{:S(2)}, u32[]{:S(2)}) collective-permute-start(bf16[256,1024]{1,0:T(8,128)(2,1)S(1)} %pad_maximum_fusion.1.rest_0_.rest_4_), channel_id=1, source_target_pairs={{0,16},{8,24},{16,0},{24,8},{1,17},{9,25},{17,1},{25,9},{2,18},{10... | collective-permute-start | bytes 1572872 | tf_op jit(solution)/shard_map/ppermute | solution.py:450
  44.5 37.4 %collective-permute-start.10 = (bf16[256,1024]{1,0:T(8,128)(2,1)S(1)}, bf16[256,1024]{1,0:T(8,128)(2,1)S(1)}, u32[]{:S(2)}, u32[]{:S(2)}) collective-permute-start(bf16[256,1024]{1,0:T(8,128)(2,1)S(1)} %pad_maximum_fusion.1.rest_0_.rest_4_), channel_id=1, source_target_pairs={{0,24},{8,16},{16,8},{24,0},{1,25},{9,17},{17,9},{25,1},{2,26},{10... | collective-permute-start | bytes 1572872 | tf_op jit(solution)/shard_map/ppermute | solution.py:450
  45.0 36.9 %collective-permute-start.7 = (bf16[256,1024]{1,0:T(8,128)(2,1)}, bf16[256,1024]{1,0:T(8,128)(2,1)}, u32[]{:S(2)}, u32[]{:S(2)}) collective-permute-start(bf16[256,1024]{1,0:T(8,128)(2,1)} %collective-permute-done.6.near), channel_id=1, source_target_pairs={{0,1},{1,0},{2,3},{3,2},{4,5},{5,4},{6,7},{7,6},{8,9},{9,8},{10,11... | collective-permute-start | bytes 1572872 | tf_op jit(solution)/shard_map/ppermute | solution.py:439
  66.2 25.2 %collective-permute-start.11 = (f32[128,512]{1,0:T(8,128)S(1)}, f32[128,512]{1,0:T(8,128)S(1)}, u32[]{:S(2)}, u32[]{:S(2)}) collective-permute-start(f32[128,512]{1,0:T(8,128)S(1)} %slice_bitcast_fusion.1), channel_id=1, source_target_pairs={{0,4},{2,6},{1,5},{3,7},{8,12},{10,14},{9,13},{11,15},{16,20},{18,... | collective-permute-start | bytes 786440 | tf_op jit(solution)/shard_map/ppermute | solution.py:445
  105.2 4.3 collective-permute-start.13
  121.4 18.2 %collective-permute-start.17 = (f32[128,512]{1,0:T(8,128)S(1)}, f32[128,512]{1,0:T(8,128)S(1)}, u32[]{:S(2)}, u32[]{:S(2)}) collective-permute-start(f32[128,512]{1,0:T(8,128)S(1)} %slice_bitcast_fusion), channel_id=1, source_target_pairs={{4,0},{6,2},{5,1},{7,3},{12,8},{14,10},{13,9},{15,11},{20,16},{22,... | collective-permute-start | bytes 786440 | tf_op jit(solution)/shard_map/ppermute | solution.py:445
  161.4 19.3 %collective-permute-start.20 = (f32[512,128]{1,0:T(8,128)S(1)}, f32[512,128]{1,0:T(8,128)S(1)}, u32[]{:S(2)}, u32[]{:S(2)}) collective-permute-start(f32[512,128]{1,0:T(8,128)S(1)} %constant_dynamic-slice_fusion.13), channel_id=1, source_target_pairs={{0,2},{2,0},{4,6},{6,4},{1,3},{3,1},{5,7},{7,5},{8,10},{10,8},{12,... | collective-permute-start | bytes 786440 | tf_op jit(solution)/shard_map/ppermute | solution.py:442
  170.1 54.0 %collective-permute-start.47 = (f32[256,512]{1,0:T(8,128)}, f32[256,512]{1,0:T(8,128)}, u32[]{:S(2)}, u32[]{:S(2)}) collective-permute-start(f32[256,512]{1,0:T(8,128)} %get-tuple-element.110), channel_id=1, source_target_pairs={{0,24},{8,16},{16,8},{24,0},{1,25},{9,17},{17,9},{25,1},{2,26},{10... | collective-permute-start | bytes 1572872 | tf_op jit(solution)/shard_map/ppermute | solution.py:450
  172.6 52.2 %collective-permute-start.46 = (f32[256,512]{1,0:T(8,128)}, f32[256,512]{1,0:T(8,128)}, u32[]{:S(2)}, u32[]{:S(2)}) collective-permute-start(f32[256,512]{1,0:T(8,128)} %get-tuple-element.109), channel_id=1, source_target_pairs={{0,16},{8,24},{16,0},{24,8},{1,17},{9,25},{17,1},{25,9},{2,18},{10... | collective-permute-start | bytes 1572872 | tf_op jit(solution)/shard_map/ppermute | solution.py:450
  173.1 51.7 %collective-permute-start.45 = (f32[256,512]{1,0:T(8,128)}, f32[256,512]{1,0:T(8,128)}, u32[]{:S(2)}, u32[]{:S(2)}) collective-permute-start(f32[256,512]{1,0:T(8,128)} %get-tuple-element.108), channel_id=1, source_target_pairs={{0,8},{8,0},{16,24},{24,16},{1,9},{9,1},{17,25},{25,17},{2,10},{10... | collective-permute-start | bytes 1572872 | tf_op jit(solution)/shard_map/ppermute | solution.py:450
  180.7 12.6 %collective-permute-start.21 = (f32[512,128]{1,0:T(8,128)S(1)}, f32[512,128]{1,0:T(8,128)S(1)}, u32[]{:S(2)}, u32[]{:S(2)}) collective-permute-start(f32[512,128]{1,0:T(8,128)S(1)} %dynamic-slice_add_fusion.1), channel_id=1, source_target_pairs={{0,1},{1,0},{2,3},{3,2},{4,5},{5,4},{6,7},{7,6},{8,9},{9,8},{10,11... | collective-permute-start | bytes 786440 | tf_op jit(solution)/shard_map/ppermute | solution.py:439
  192.0 6.7 %collective-permute-start.18 = (f32[8,512]{1,0:T(8,128)S(1)}, f32[8,512]{1,0:T(8,128)S(1)}, u32[]{:S(2)}, u32[]{:S(2)}) collective-permute-start(f32[8,512]{1,0:T(8,128)S(1)} %slice.95), channel_id=1, source_target_pairs={{4,0},{6,2},{5,1},{7,3},{12,8},{14,10},{13,9},{15,11},{20,16},{22,... | collective-permute-start | bytes 49160 | tf_op jit(solution)/shard_map/ppermute | solution.py:445
  194.5 13.5 %collective-permute-start.22 = (f32[8,128]{1,0:T(8,128)S(1)}, f32[8,128]{1,0:T(8,128)S(1)}, u32[]{:S(2)}, u32[]{:S(2)}) collective-permute-start(f32[8,128]{1,0:T(8,128)S(1)} %slice.117), channel_id=1, source_target_pairs={{4,0},{6,2},{5,1},{7,3},{12,8},{14,10},{13,9},{15,11},{20,16},{22,... | collective-permute-start | bytes 12296 | tf_op jit(solution)/shard_map/ppermute | solution.py:445
  198.7 29.1 %collective-permute-start.28 = (f32[256,512]{1,0:T(8,128)}, f32[256,512]{1,0:T(8,128)}, u32[]{:S(2)}, u32[]{:S(2)}) collective-permute-start(f32[256,512]{1,0:T(8,128)} %get-tuple-element.93), channel_id=1, source_target_pairs={{0,24},{8,16},{16,8},{24,0},{1,25},{9,17},{17,9},{25,1},{2,26},{10... | collective-permute-start | bytes 1572872 | tf_op jit(solution)/shard_map/ppermute | solution.py:450
  208.0 23.5 %collective-permute-start.27 = (f32[256,512]{1,0:T(8,128)}, f32[256,512]{1,0:T(8,128)}, u32[]{:S(2)}, u32[]{:S(2)}) collective-permute-start(f32[256,512]{1,0:T(8,128)} %get-tuple-element.92), channel_id=1, source_target_pairs={{0,16},{8,24},{16,0},{24,8},{1,17},{9,25},{17,1},{25,9},{2,18},{10... | collective-permute-start | bytes 1572872 | tf_op jit(solution)/shard_map/ppermute | solution.py:450
  224.1 14.4 %collective-permute-start.26 = (f32[256,512]{1,0:T(8,128)}, f32[256,512]{1,0:T(8,128)}, u32[]{:S(2)}, u32[]{:S(2)}) collective-permute-start(f32[256,512]{1,0:T(8,128)} %get-tuple-element.91), channel_id=1, source_target_pairs={{0,8},{8,0},{16,24},{24,16},{1,9},{9,1},{17,25},{25,17},{2,10},{10... | collective-permute-start | bytes 1572872 | tf_op jit(solution)/shard_map/ppermute | solution.py:450
  224.8 68.5 %collective-permute-start.23 = (f32[2,256,1024]{2,1,0:T(8,128)S(1)}, f32[2,256,1024]{2,1,0:T(8,128)}, u32[]{:S(2)}, u32[]{:S(2)}) collective-permute-start(f32[2,256,1024]{2,1,0:T(8,128)S(1)} %dynamic-slice_bitcast_fusion), channel_id=1, source_target_pairs={{0,1},{1,0},{2,3},{3,2},{4,5},{5,4},{6,7},{7,6},{8,9},{9,8},{10,11... | collective-permute-start | bytes 6291464 | tf_op jit(solution)/shard_map/ppermute | solution.py:439
  226.5 12.0 %collective-permute-start.49 = (f32[64,512]{1,0:T(8,128)S(1)}, f32[64,512]{1,0:T(8,128)}, u32[]{:S(2)}, u32[]{:S(2)}) collective-permute-start(f32[64,512]{1,0:T(8,128)S(1)} %get-tuple-element.173), channel_id=1, source_target_pairs={{0,2},{2,0},{4,6},{6,4},{1,3},{3,1},{5,7},{7,5},{8,10},{10,8},{12,... | collective-permute-start | bytes 393224 | tf_op jit(solution)/shard_map/ppermute | solution.py:442
  227.8 13.1 %collective-permute-start.50 = (f32[64,512]{1,0:T(8,128)S(1)}, f32[64,512]{1,0:T(8,128)}, u32[]{:S(2)}, u32[]{:S(2)}) collective-permute-start(f32[64,512]{1,0:T(8,128)S(1)} %get-tuple-element.172), channel_id=1, source_target_pairs={{0,6},{2,4},{4,2},{6,0},{1,7},{3,5},{5,3},{7,1},{8,14},{10,12},{12... | collective-permute-start | bytes 393224 | tf_op jit(solution)/shard_map/ppermute | solution.py:442
  231.6 12.1 %collective-permute-start.48 = (f32[64,512]{1,0:T(8,128)S(1)}, f32[64,512]{1,0:T(8,128)}, u32[]{:S(2)}, u32[]{:S(2)}) collective-permute-start(f32[64,512]{1,0:T(8,128)S(1)} %get-tuple-element.171), channel_id=1, source_target_pairs={{0,4},{2,6},{4,0},{6,2},{1,5},{3,7},{5,1},{7,3},{8,12},{10,14},{12... | collective-permute-start | bytes 393224 | tf_op jit(solution)/shard_map/ppermute | solution.py:442
  238.5 58.6 %collective-permute-start.14 = (f32[2,256,1024]{2,1,0:T(8,128)}, f32[2,256,1024]{2,1,0:T(8,128)S(1)}, u32[]{:S(2)}, u32[]{:S(2)}) collective-permute-start(f32[2,256,1024]{2,1,0:T(8,128)} %dynamic-slice_bitcast_fusion.1), channel_id=1, source_target_pairs={{0,1},{1,0},{2,3},{3,2},{4,5},{5,4},{6,7},{7,6},{8,9},{9,8},{10,11... | collective-permute-start | bytes 6291464 | tf_op jit(solution)/shard_map/ppermute | solution.py:439
  238.5 15.9 %collective-permute-start.34 = (f32[256,512]{1,0:T(8,128)}, f32[256,512]{1,0:T(8,128)S(1)}, u32[]{:S(2)}, u32[]{:S(2)}) collective-permute-start(f32[256,512]{1,0:T(8,128)} %get-tuple-element.97), channel_id=1, source_target_pairs={{0,24},{8,16},{16,8},{24,0},{1,25},{9,17},{17,9},{25,1},{2,26},{10... | collective-permute-start | bytes 1572872 | tf_op jit(solution)/shard_map/ppermute | solution.py:450
  240.9 24.3 %collective-permute-start.33 = (f32[256,512]{1,0:T(8,128)}, f32[256,512]{1,0:T(8,128)S(1)}, u32[]{:S(2)}, u32[]{:S(2)}) collective-permute-start(f32[256,512]{1,0:T(8,128)} %get-tuple-element.96), channel_id=1, source_target_pairs={{0,16},{8,24},{16,0},{24,8},{1,17},{9,25},{17,1},{25,9},{2,18},{10... | collective-permute-start | bytes 1572872 | tf_op jit(solution)/shard_map/ppermute | solution.py:450
  243.7 25.7 %collective-permute-start.32 = (f32[256,512]{1,0:T(8,128)}, f32[256,512]{1,0:T(8,128)S(1)}, u32[]{:S(2)}, u32[]{:S(2)}) collective-permute-start(f32[256,512]{1,0:T(8,128)} %get-tuple-element.95), channel_id=1, source_target_pairs={{0,8},{8,0},{16,24},{24,16},{1,9},{9,1},{17,25},{25,17},{2,10},{10... | collective-permute-start | bytes 1572872 | tf_op jit(solution)/shard_map/ppermute | solution.py:450
  254.4 15.2 %collective-permute-start.30 = (f32[64,512]{1,0:T(8,128)S(1)}, f32[64,512]{1,0:T(8,128)S(1)}, u32[]{:S(2)}, u32[]{:S(2)}) collective-permute-start(f32[64,512]{1,0:T(8,128)S(1)} %get-tuple-element.176), channel_id=1, source_target_pairs={{0,2},{2,0},{4,6},{6,4},{1,3},{3,1},{5,7},{7,5},{8,10},{10,8},{12,... | collective-permute-start | bytes 393224 | tf_op jit(solution)/shard_map/ppermute | solution.py:442
  265.2 8.6 %collective-permute-start.31 = (f32[64,512]{1,0:T(8,128)S(1)}, f32[64,512]{1,0:T(8,128)S(1)}, u32[]{:S(2)}, u32[]{:S(2)}) collective-permute-start(f32[64,512]{1,0:T(8,128)S(1)} %get-tuple-element.175), channel_id=1, source_target_pairs={{0,6},{2,4},{4,2},{6,0},{1,7},{3,5},{5,3},{7,1},{8,14},{10,12},{12... | collective-permute-start | bytes 393224 | tf_op jit(solution)/shard_map/ppermute | solution.py:442
  269.4 15.0 %collective-permute-start.29 = (f32[64,512]{1,0:T(8,128)S(1)}, f32[64,512]{1,0:T(8,128)S(1)}, u32[]{:S(2)}, u32[]{:S(2)}) collective-permute-start(f32[64,512]{1,0:T(8,128)S(1)} %get-tuple-element.174), channel_id=1, source_target_pairs={{0,4},{2,6},{4,0},{6,2},{1,5},{3,7},{5,1},{7,3},{8,12},{10,14},{12... | collective-permute-start | bytes 393224 | tf_op jit(solution)/shard_map/ppermute | solution.py:442
  269.7 17.7 %collective-permute-start.35 = (f32[64,512]{1,0:T(8,128)S(1)}, f32[64,512]{1,0:T(8,128)S(1)}, u32[]{:S(2)}, u32[]{:S(2)}) collective-permute-start(f32[64,512]{1,0:T(8,128)S(1)} %get-tuple-element.177), channel_id=1, source_target_pairs={{0,4},{2,6},{4,0},{6,2},{1,5},{3,7},{5,1},{7,3},{8,12},{10,14},{12... | collective-permute-start | bytes 393224 | tf_op jit(solution)/shard_map/ppermute | solution.py:442
  273.8 18.3 %collective-permute-start.36 = (f32[64,512]{1,0:T(8,128)S(1)}, f32[64,512]{1,0:T(8,128)S(1)}, u32[]{:S(2)}, u32[]{:S(2)}) collective-permute-start(f32[64,512]{1,0:T(8,128)S(1)} %get-tuple-element.179), channel_id=1, source_target_pairs={{0,2},{2,0},{4,6},{6,4},{1,3},{3,1},{5,7},{7,5},{8,10},{10,8},{12,... | collective-permute-start | bytes 393224 | tf_op jit(solution)/shard_map/ppermute | solution.py:442
  284.4 7.7 %collective-permute-start.37 = (f32[64,512]{1,0:T(8,128)S(1)}, f32[64,512]{1,0:T(8,128)S(1)}, u32[]{:S(2)}, u32[]{:S(2)}) collective-permute-start(f32[64,512]{1,0:T(8,128)S(1)} %get-tuple-element.178), channel_id=1, source_target_pairs={{0,6},{2,4},{4,2},{6,0},{1,7},{3,5},{5,3},{7,1},{8,14},{10,12},{12... | collective-permute-start | bytes 393224 | tf_op jit(solution)/shard_map/ppermute | solution.py:442
  296.5 121.1 %collective-permute-start.24 = (f32[256,1024]{1,0:T(8,128)}, f32[256,1024]{1,0:T(8,128)}, u32[]{:S(2)}, u32[]{:S(2)}) collective-permute-start(f32[256,1024]{1,0:T(8,128)} %dynamic-slice_bitcast_fusion.2), channel_id=1, source_target_pairs={{0,2},{2,0},{4,6},{6,4},{1,3},{3,1},{5,7},{7,5},{8,10},{10,8},{12,... | collective-permute-start | bytes 3145736 | tf_op jit(solution)/shard_map/ppermute | solution.py:442
  300.1 119.2 %collective-permute-start.15 = (f32[256,1024]{1,0:T(8,128)}, f32[256,1024]{1,0:T(8,128)}, u32[]{:S(2)}, u32[]{:S(2)}) collective-permute-start(f32[256,1024]{1,0:T(8,128)} %dynamic-slice_bitcast_fusion.3), channel_id=1, source_target_pairs={{0,2},{2,0},{4,6},{6,4},{1,3},{3,1},{5,7},{7,5},{8,10},{10,8},{12,... | collective-permute-start | bytes 3145736 | tf_op jit(solution)/shard_map/ppermute | solution.py:442
  306.5 106.3 %collective-permute-start.40 = (f32[256,128]{1,0:T(8,128)}, f32[256,128]{1,0:T(8,128)S(1)}, u32[]{:S(2)}, u32[]{:S(2)}) collective-permute-start(f32[256,128]{1,0:T(8,128)} %get-tuple-element.101), channel_id=1, source_target_pairs={{0,24},{8,16},{16,8},{24,0},{1,25},{9,17},{17,9},{25,1},{2,26},{10... | collective-permute-start | bytes 393224 | tf_op jit(solution)/shard_map/ppermute | solution.py:450
  308.2 104.7 %collective-permute-start.39 = (f32[256,128]{1,0:T(8,128)}, f32[256,128]{1,0:T(8,128)}, u32[]{:S(2)}, u32[]{:S(2)}) collective-permute-start(f32[256,128]{1,0:T(8,128)} %get-tuple-element.100), channel_id=1, source_target_pairs={{0,16},{8,24},{16,0},{24,8},{1,17},{9,25},{17,1},{25,9},{2,18},{10... | collective-permute-start | bytes 393224 | tf_op jit(solution)/shard_map/ppermute | solution.py:450
  308.7 104.1 %collective-permute-start.38 = (f32[256,128]{1,0:T(8,128)}, f32[256,128]{1,0:T(8,128)}, u32[]{:S(2)}, u32[]{:S(2)}) collective-permute-start(f32[256,128]{1,0:T(8,128)} %get-tuple-element.99), channel_id=1, source_target_pairs={{0,8},{8,0},{16,24},{24,16},{1,9},{9,1},{17,25},{25,17},{2,10},{10... | collective-permute-start | bytes 393224 | tf_op jit(solution)/shard_map/ppermute | solution.py:450
  414.1 15.0 %collective-permute-start.42 = (f32[64,128]{1,0:T(8,128)S(1)}, f32[64,128]{1,0:T(8,128)S(1)}, u32[]{:S(2)}, u32[]{:S(2)}) collective-permute-start(f32[64,128]{1,0:T(8,128)S(1)} %get-tuple-element.186), channel_id=1, source_target_pairs={{0,2},{2,0},{4,6},{6,4},{1,3},{3,1},{5,7},{7,5},{8,10},{10,8},{12,... | collective-permute-start | bytes 98312 | tf_op jit(solution)/shard_map/ppermute | solution.py:442
  414.2 15.0 %collective-permute-start.43 = (f32[64,128]{1,0:T(8,128)S(1)}, f32[64,128]{1,0:T(8,128)S(1)}, u32[]{:S(2)}, u32[]{:S(2)}) collective-permute-start(f32[64,128]{1,0:T(8,128)S(1)} %get-tuple-element.185), channel_id=1, source_target_pairs={{0,6},{2,4},{4,2},{6,0},{1,7},{3,5},{5,3},{7,1},{8,14},{10,12},{12... | collective-permute-start | bytes 98312 | tf_op jit(solution)/shard_map/ppermute | solution.py:442
  414.2 14.9 %collective-permute-start.41 = (f32[64,128]{1,0:T(8,128)S(1)}, f32[64,128]{1,0:T(8,128)S(1)}, u32[]{:S(2)}, u32[]{:S(2)}) collective-permute-start(f32[64,128]{1,0:T(8,128)S(1)} %get-tuple-element.184), channel_id=1, source_target_pairs={{0,4},{2,6},{4,0},{6,2},{1,5},{3,7},{5,1},{7,3},{8,12},{10,14},{12... | collective-permute-start | bytes 98312 | tf_op jit(solution)/shard_map/ppermute | solution.py:442
  422.3 11.4 %collective-permute-start.25 = (f32[256,1024]{1,0:T(8,128)}, f32[256,1024]{1,0:T(8,128)S(1)}, u32[]{:S(2)}, u32[]{:S(2)}) collective-permute-start(f32[256,1024]{1,0:T(8,128)} %get-tuple-element.180), channel_id=1, source_target_pairs={{0,1},{1,0},{2,3},{3,2},{4,5},{5,4},{6,7},{7,6},{8,9},{9,8},{10,11... | collective-permute-start | bytes 3145736 | tf_op jit(solution)/shard_map/ppermute | solution.py:439
  429.3 2.9 collective-permute-start.16
  (48 other events, 644.1 us)

commit v2 on v1

v2 whole, which is shorter than its diff:
```python
import functools

import jax
import jax.numpy as jnp
from jax import lax
from jax.experimental import pallas as pl
from jax.experimental.pallas import tpu as pltpu
from jax.sharding import PartitionSpec as P

BLOCK = 256
SUB = 128
EPSILON = 1e-05
HIGH = lax.Precision.HIGH
HIGHEST = lax.Precision.HIGHEST
F32 = jnp.float32
BF16 = jnp.bfloat16
NN = (((1,), (0,)), ((), ()))
NT = (((1,), (1,)), ((), ()))
TN = (((0,), (0,)), ((), ()))
HEAD0 = 64
LO, CORE, BASE, LENGTH, HASPREV, HASNEXT, SLOT0 = range(7)


def mm(a, b, dims=NN, precision=None):
    return lax.dot_general(a, b, dims, precision=precision, preferred_element_type=F32)


def grid_call(body, grid, in_specs, out_specs, out_shape, scratch=(), name=None):
    return pl.pallas_call(
        body,
        grid_spec=pltpu.PrefetchScalarGridSpec(
            num_scalar_prefetch=1,
            grid=grid,
            in_specs=in_specs,
            out_specs=out_specs,
            scratch_shapes=list(scratch),
        ),
        out_shape=out_shape,
        compiler_params=pltpu.CompilerParams(dimension_semantics=("arbitrary",) * len(grid)
        ),
        name=name,
    )


def rows_spec(width, rows=BLOCK, lane=0):
    return pl.BlockSpec((rows, width), lambda b, s: (b, lane))


def whole(shape):
    return pl.BlockSpec(shape, lambda b, s: (0,) * len(shape))


def shaped(shape, dtype=F32):
    return jax.ShapeDtypeStruct(shape, dtype)


def slope(v, sig):
    return sig * (1.0 + v * (1.0 - sig))


def lanes_of(s_ref, slot, width):
    return pl.ds(pl.multiple_of(s_ref[SLOT0 + slot] * width, width), width)


def normalize(x, gain):
    value = x.astype(F32)
    inverse = lax.rsqrt(jnp.mean(value * value, axis=1, keepdims=True) + EPSILON)
    scaled = value * inverse
    return scaled, (scaled * gain).astype(BF16)


def pick(s_ref, b, quarter, own, near, far):
    lo, core = s_ref[LO], s_ref[CORE]
    place = b // quarter
    mine = (place // 2) == lo
    from_near = (place % 2) == core
    return jnp.where(mine, own, jnp.where(from_near, near, far))


def valid_rows(s_ref, b):
    position = s_ref[BASE] + b * BLOCK + lax.broadcasted_iota(jnp.int32, (BLOCK, 1), 0)
    return (position < s_ref[LENGTH]).astype(F32)


def expander(inner):
    lane = lax.broadcasted_iota(jnp.int32, (384, inner), 0) % 128 - HEAD0
    head = lax.broadcasted_iota(jnp.int32, (384, inner), 1) // 64
    return (lane == head).astype(F32).astype(BF16)


def collector(inner):
    head = lax.broadcasted_iota(jnp.int32, (3 * inner, 128), 0) % inner // 64
    lane = lax.broadcasted_iota(jnp.int32, (3 * inner, 128), 1) - HEAD0
    return (lane == head).astype(F32).astype(BF16)


def two(x):
    high = x.astype(BF16)
    return high, (x - high.astype(F32)).astype(BF16)


def three(x, axis=1):
    high = x.astype(BF16)
    rest = x - high.astype(F32)
    middle = rest.astype(BF16)
    return jnp.concatenate([high, middle, (rest - middle.astype(F32)).astype(BF16)], axis=axis)


def running(tri, x):
    width = x.shape[1]
    wide = mm(tri, three(x))
    return wide[:, :width] + wide[:, width : 2 * width] + wide[:, 2 * width :]


def triangle(forward):
    row = lax.broadcasted_iota(jnp.int32, (BLOCK, BLOCK), 0)
    col = lax.broadcasted_iota(jnp.int32, (BLOCK, BLOCK), 1)
    same = (row // SUB) == (col // SUB)
    keep = (row >= col) if forward else (col >= row)
    return (same & keep).astype(F32).astype(BF16)


def stacked_heads(x):
    half = lax.broadcasted_iota(jnp.int32, (1, 128), 1) < 64
    return two(jnp.concatenate([jnp.where(half, x, 0.0), jnp.where(half, 0.0, x)], axis=0))


def faded(keep, level, level_t, level_x, pair, forward):
    out = []
    for side in range(2):
        h = HEAD0 + 2 * pair + side
        at = pair * 128 + side * 64
        column, row = level_x[:, at : at + 1], level_t[h : h + 1, :]
        diff = column - row if forward else row - column
        out.append(jnp.exp(jnp.where(keep, diff, -1e30)))
    return jnp.concatenate(out, axis=1)


def mixed_heads(mix, high, low):
    mh, ml = two(mix)
    wide = mm(mh, jnp.concatenate([high, low], axis=1))
    return wide[:, :128] + wide[:, 128:] + mm(ml, high)


def head_lanes(inner):
    lane = lax.broadcasted_iota(jnp.int32, (1, 128), 1)
    return (lane >= HEAD0) & (lane < HEAD0 + inner // 64)


def front_body(parts, inner, states, quarter, s_ref, own, near, far, halo, gain, taps, bias, dbias, rate,
               *rest):
    ws = rest[:parts]
    (normed_ref, u_ref, uh_ref, co_ref, draw_ref, delta_ref, lev_ref, lx_ref, dx_ref, hloc_ref,
     pre_ref, end_ref) = rest[parts : parts + 12]
    hsc, usc, state, pre, esc = rest[parts + 12 :]
    b = pl.program_id(0)
    wide = inner + 2 * states
    shard = ws[0].shape[0]
    normed_ref[...] = normalize(pick(s_ref, b, quarter, own[...], near[...], far[...]), gain[...])[1]

    @pl.when(b == 0)
    def _():
        hsc[...] = normalize(halo[...], gain[...])[1]
        edge = jnp.zeros((16, wide), F32)
        for j in range(parts):
            edge += mm(hsc[:, lanes_of(s_ref, j, shard)], ws[j][:, :wide])
        edge = jnp.where(s_ref[HASPREV] > 0, edge[8:], 0.0)
        usc[0:8] = edge
        uh_ref[...] = edge
        state[...] = jnp.zeros_like(state)
        pre[...] = jnp.zeros_like(pre)
        esc[...] = expander(inner)

    @pl.when(b > 0)
    def _():
        usc[0:8] = usc[BLOCK : BLOCK + 8]

    u = jnp.zeros((BLOCK, wide + 128), F32)
    for j in range(parts):
        u += mm(normed_ref[:, lanes_of(s_ref, j, shard)], ws[j][...])
    usc[8 : 8 + BLOCK] = u[:, :wide]
    u_ref[...] = u[:, :wide]
    conv = bias[...] + taps[0:1] * usc[5 : 5 + BLOCK]
    for k in range(1, 4):
        conv = conv + taps[k : k + 1] * usc[5 + k : 5 + k + BLOCK]
    co_ref[...] = conv
    raw = u[:, wide:] + dbias[...]
    draw_ref[...] = raw
    delta = jnp.where(head_lanes(inner), jnp.maximum(raw, 0.0) + jnp.log1p(jnp.exp(-jnp.abs(raw))), 0.0)
    delta = delta * valid_rows(s_ref, b)
    delta_ref[...] = delta
    level = running(triangle(True), delta * rate[...])
    lev_ref[...] = level
    both = mm(jnp.concatenate([three(level), three(delta)], axis=0), esc[...])
    level_x, delta_x = both[:BLOCK], both[BLOCK:]
    lx_ref[...] = level_x
    dx_ref[...] = delta_x
    act = conv * jax.nn.sigmoid(conv)
    source = delta_x * act[:, :inner]
    inject_t = act[:, inner : inner + states].T
    for i in range(BLOCK // SUB):
        at = slice(i * SUB, (i + 1) * SUB)
        last = level_x[(i + 1) * SUB - 1 : (i + 1) * SUB]
        fresh = mm(inject_t[:, at], jnp.exp(last - level_x[at]) * source[at], precision=HIGH)
        before = state[...]
        n = b * (BLOCK // SUB) + i
        hloc_ref[n] = before
        pre_ref[n] = pre[...]
        state[...] = jnp.exp(last) * before + fresh
        pre[...] = pre[...] + last

    @pl.when(b == pl.num_programs(0) - 1)
    def _():
        hloc_ref[n + 1] = state[...]
        end_ref[...] = state[...]
        pre_ref[n + 1] = pre[...]


def within_body(inner, states, s_ref, co, lev, lx, dx, yw_ref):
    conv = co[...]
    act = conv * jax.nn.sigmoid(conv)
    xs = dx[...] * act[:, :inner]
    level = lev[...]
    keep = lax.broadcasted_iota(jnp.int32, (SUB, SUB), 0) >= lax.broadcasted_iota(jnp.int32, (SUB, SUB), 1)
    for i in range(BLOCK // SUB):
        at = slice(i * SUB, (i + 1) * SUB)
        affinity = mm(act[at, inner + states :], act[at, inner : inner + states], NT, HIGH)
        affinity = jnp.concatenate([affinity, affinity], axis=1)
        level_t = level[at].T
        level_x = lx[at]
        for pair in range(inner // 128):
            lanes = slice(pair * 128, pair * 128 + 128)
            mix = faded(keep, level, level_t, level_x, pair, True) * affinity
            yw_ref[at, lanes] = mixed_heads(mix, *stacked_heads(xs[at, lanes]))


def gates_body(parts, quarter, s_ref, normed, own, near, far, *rest):
    ws = rest[:parts]
    gate_ref, gg_ref, bg_ref = rest[parts:]
    b = pl.program_id(0)
    shard = ws[0].shape[0]
    inner = gate_ref.shape[1]
    up = pick(s_ref, b, quarter, own[...], near[...], far[...])
    bg_ref[...] = (up.astype(F32) * valid_rows(s_ref, b)).astype(BF16)
    gate = jnp.zeros(gate_ref.shape, F32)
    gg = jnp.zeros(gg_ref.shape, F32)
    for j in range(parts):
        at = lanes_of(s_ref, j, shard)
        gate += mm(normed[:, at], ws[j][:, :inner])
        gg += mm(bg_ref[:, at], ws[j][:, inner:])
    gate_ref[...] = gate
    gg_ref[...] = gg


def entering(hloc, pre, hin):
    return hloc + jnp.exp(pre[0:1]) * hin


def output_body(inner, states, s_ref, co, lx, yw, gate, gg, hloc, pre, hin, skip, ggain, y_ref, sum_ref):
    conv = co[...]
    act = conv * jax.nn.sigmoid(conv)
    for i in range(BLOCK // SUB):
        at = slice(i * SUB, (i + 1) * SUB)
        held = entering(hloc[i], pre[i], hin[...])
        y_ref[at] = yw[at] + jnp.exp(lx[at]) * mm(act[at, inner + states :], held, precision=HIGH)
    out = y_ref[...] + skip[...] * act[:, :inner]
    g = gate[...]
    product = out * (g * jax.nn.sigmoid(g))
    ones = jnp.ones((8, 3 * inner), BF16)
    sum_ref[0:8] = mm(ones, three(product * product), NT)
    sum_ref[8:16] = mm(ones, three(gg[...] * ggain[...] * product), NT)


def turn_body(inner, states, total, s_ref, co, lx, y, gate, gg, sums, more, skip, ggain,
              gated_ref, ggrad_ref, og_ref, gloc_ref, start_ref, cols_ref, chain):
    step = pl.program_id(0)
    conv = co[...]
    act = conv * jax.nn.sigmoid(conv)
    x = act[:, :inner]
    readout_t = act[:, inner + states :].T
    both = (sums[...] + more[...]).T
    ginv = lax.rsqrt(both[:, 0:1] / total + EPSILON)
    dot = ginv * both[:, 8:9] / total
    g = gate[...]
    sig = jax.nn.sigmoid(g)
    ga = g * sig
    out = y[...] + skip[...] * x
    unit = out * ga * ginv
    gated_ref[...] = (unit * ggain[...]).astype(BF16)
    grad = gg[...]
    pg = ginv * (grad * ggain[...] - unit * dot)
    og = pg * ga
    og_ref[...] = og
    ggrad_ref[...] = (pg * out * slope(g, sig)).astype(BF16)

    @pl.when(step == 0)
    def _():
        chain[...] = jnp.zeros_like(chain)
        cols_ref[...] = jnp.zeros_like(cols_ref)

    cols_ref[0:1] += jnp.sum(grad * unit, axis=0, keepdims=True)
    cols_ref[1:2] += jnp.sum(og * x, axis=0, keepdims=True)
    b = pl.num_programs(0) - 1 - step
    for i in reversed(range(BLOCK // SUB)):
        at = slice(i * SUB, (i + 1) * SUB)
        held = chain[...]
        n = b * (BLOCK // SUB) + i
        gloc_ref[n + 1] = held
        level_x = lx[at]
        chain[...] = jnp.exp(level_x[SUB - 1 : SUB]) * held + mm(
            readout_t[:, at], jnp.exp(level_x) * og[at], precision=HIGH
        )

    @pl.when(b == 0)
    def _():
        gloc_ref[0] = chain[...]
        start_ref[...] = chain[...]


def back_body(inner, states, s_ref, co, lev, lx, dx, og, hloc, pre, hin, z_ref, dbc_ref):
    conv = co[...]
    act = conv * jax.nn.sigmoid(conv)
    xs = dx[...] * act[:, :inner]
    level = lev[...]
    keep = lax.broadcasted_iota(jnp.int32, (SUB, SUB), 1) >= lax.broadcasted_iota(jnp.int32, (SUB, SUB), 0)
    for i in range(BLOCK // SUB):
        at = slice(i * SUB, (i + 1) * SUB)
        inject, readout = act[at, inner : inner + states], act[at, inner + states :]
        affinity = mm(inject, readout, NT, HIGH)
        affinity = jnp.concatenate([affinity, affinity], axis=1)
        level_t = level[at].T
        level_x = lx[at]
        grad = jnp.zeros((SUB, SUB), F32)
        for pair in range(inner // 128):
            lanes = slice(pair * 128, pair * 128 + 128)
            fade = faded(keep, level, level_t, level_x, pair, False)
            g = og[at, lanes]
            z_ref[at, lanes] = mixed_heads(fade * affinity, *stacked_heads(g))
            xh, xl = stacked_heads(xs[at, lanes])
            gh, gl = two(g)
            outer = mm(
                jnp.concatenate([xh, xl], axis=1), jnp.concatenate([gh, gh], axis=1), NT
            ) + mm(xh, gl, NT)
            grad += fade[:, :SUB] * outer[:SUB] + fade[:, SUB:] * outer[SUB:]
        held = entering(hloc[i], pre[i], hin[...])
        dbc_ref[at, :states] = mm(grad, readout, precision=HIGH)
        dbc_ref[at, states:] = mm(grad.T, inject, precision=HIGH) + mm(
            jnp.exp(level_x) * og[at], held, NT, HIGH
        )


def conv_back(grad, csc, usc, taps, cols_ref):
    csc[0:BLOCK] = grad
    pre = taps[0:1] * csc[3 : 3 + BLOCK]
    for k in range(1, 4):
        pre = pre + taps[k : k + 1] * csc[3 - k : 3 - k + BLOCK]
    for k in range(4):
        cols_ref[k : k + 1] += jnp.sum(grad * usc[5 + k : 5 + k + BLOCK], axis=0, keepdims=True)
    cols_ref[4:5] += jnp.sum(grad, axis=0, keepdims=True)
    csc[BLOCK : BLOCK + 8] = grad[0:8]
    return pre


def join_body(inner, states, s_ref, co, delta, lx, dx, draw, og, y, z, dbc, hloc, pre, gloc, gin, hin, u, prior,
              uh, taps, rate, skip, mg_ref, tail_ref, head_ref, keep_ref, give_ref, rg_ref, cols_ref, sig_ref,
              col_sc, csc, usc):
    step = pl.program_id(0)
    subs = BLOCK // SUB
    count = pl.num_programs(0)
    b = count - 1 - step

    @pl.when(step == 0)
    def _():
        cols_ref[...] = jnp.zeros_like(cols_ref)
        sig_ref[...] = jnp.zeros_like(sig_ref)
        col_sc[...] = collector(inner)
        csc[BLOCK : BLOCK + 8] = jnp.zeros((8, inner), F32)

    conv = co[...]
    sig = jax.nn.sigmoid(conv)
    act = conv * sig
    x = act[:, :inner]
    delta_x = dx[...]
    ends = []
    zeds = []
    inject_grads = []
    for i in range(subs):
        at = slice(i * SUB, (i + 1) * SUB)
        n = b * subs + i + 1
        level_x = lx[at]
        later = gloc[n] + jnp.exp(pre[subs * count][0:1] - pre[n][0:1]) * gin[...]
        fade = jnp.exp(level_x[SUB - 1 : SUB] - level_x)
        zeds.append(z[at] + fade * mm(act[at, inner : inner + states], later, precision=HIGH))
        inject_grads.append(dbc[at, :states] + mm(fade * delta_x[at] * x[at], later, NT, HIGH))
        held = entering(hloc[n], pre[n], hin[...])
        ends.append(jnp.sum(later * held, axis=0, keepdims=True))
    zed = jnp.concatenate(zeds, axis=0)
    inject_grad = jnp.concatenate(inject_grads, axis=0)
    half = count // 2
    rows = pl.ds(pl.multiple_of((b % half) * BLOCK, BLOCK), BLOCK)

    @pl.when(b // half == s_ref[CORE])
    def _():
        keep_ref[rows, :states] = inject_grad
        keep_ref[rows, states:] = dbc[:, states:]

    @pl.when(b // half != s_ref[CORE])
    def _():
        give_ref[rows, :states] = inject_grad
        give_ref[rows, states:] = dbc[:, states:]

    g = og[...]
    ends = jnp.concatenate(ends + [jnp.zeros((8 - subs, inner), F32)], axis=0)
    sums = mm(three(jnp.concatenate([x * zed, g * y[...], ends], axis=0)), col_sc[...])
    direct, read, ends = sums[:BLOCK], sums[BLOCK : 2 * BLOCK], sums[2 * BLOCK :]
    dlt = delta[...]
    q = running(triangle(False), read - dlt * direct)
    q = jnp.concatenate([q[i * SUB : (i + 1) * SUB] + ends[i : i + 1] for i in range(subs)], axis=0)
    rg = (direct + rate[...] * q) * valid_rows(s_ref, b) * jax.nn.sigmoid(draw[...])
    rg = jnp.where(head_lanes(inner), rg, 0.0)
    rg_ref[...] = rg
    cols_ref[0:1] += jnp.sum(rg, axis=0, keepdims=True)
    cols_ref[1:2] += jnp.sum(dlt * q, axis=0, keepdims=True)

    usc[0:8] = jnp.where(b == 0, uh[...], prior[...])
    usc[8 : 8 + BLOCK] = u[...]
    grad = (delta_x * zed + skip[...] * g) * slope(conv[:, :inner], sig[:, :inner])
    pre_grad = conv_back(grad, csc, usc, taps, sig_ref)
    mg_ref[...] = pre_grad.astype(BF16)
    head_ref[...] = grad[0:8]

    @pl.when(step == 0)
    def _():
        tail_ref[...] = pre_grad[BLOCK - 8 :]


def early_body(parts, s_ref, left1, right1, left2, right2, *outs):
    j = pl.program_id(0)
    width = right1.shape[1]
    first = mm(left1[...], right1[...], TN)
    second = mm(left2[...], right2[...], TN)
    for k in range(parts):

        @pl.when(j == k)
        def _():
            outs[k][:, :width] = first
            outs[k][:, width:] = second


def late_body(parts, s_ref, left, right1, right2, small, *outs):
    j = pl.program_id(0)
    width = right1.shape[1]
    rows = left.shape[1]
    first = mm(left[...], right1[...], TN)
    second = mm(left[...], right2[...], TN)
    for k in range(parts):

        @pl.when(j == k)
        def _():
            outs[k][:rows, :width] = first
            outs[k][:rows, width:] = second
            outs[k][rows:] = small[...]


def deal(s_ref, b, quarter, value, outs):
    place = b // quarter
    rows = pl.ds(pl.multiple_of((b % quarter) * BLOCK, BLOCK), BLOCK)
    at = (place % 2 != s_ref[CORE]).astype(jnp.int32) * 2 + (place // 2 != s_ref[LO]).astype(jnp.int32)
    for k in range(4):

        @pl.when(at == k)
        def _():
            outs[k][rows] = value


def feature_body(parts, quarter, s_ref, own, near, far, ggrad, mg, rg, dbc, dbc_other, co, u, prior, uh, ahead,
                 taps, *rest):
    ws1 = rest[:parts]
    ws2 = rest[parts : 2 * parts]
    outs = rest[2 * parts : 2 * parts + 4]
    xg_ref, cols_ref, state_ref, whole_sc, csc, usc = rest[2 * parts + 4 :]
    step = pl.program_id(0)
    count = pl.num_programs(0)
    b = count - 1 - step
    inner = ggrad.shape[1]
    shard = ws1[0].shape[0]

    @pl.when(step == 0)
    def _():
        cols_ref[...] = jnp.zeros_like(cols_ref)
        state_ref[...] = jnp.zeros_like(state_ref)
        csc[BLOCK : BLOCK + 8] = jnp.where(s_ref[HASNEXT] > 0, ahead[...], 0.0)

    usc[0:8] = jnp.where(b == 0, uh[...], prior[...])
    usc[8 : 8 + BLOCK] = u[...]
    conv = co[...]
    grad = jnp.where(b // (count // 2) == s_ref[CORE], dbc[...], dbc_other[...])
    grad = grad * slope(conv, jax.nn.sigmoid(conv))
    pre = conv_back(grad, csc, usc, taps, state_ref)
    pre = jnp.where(s_ref[CORE] > 0, pltpu.roll(pre, 64, 1), pre)
    lane = lax.broadcasted_iota(jnp.int32, (BLOCK, 128), 1)
    xg = jnp.where(lane < HEAD0, pre, rg[...]).astype(BF16)
    xg_ref[...] = xg
    for j in range(parts):
        at = lanes_of(s_ref, j, shard)
        whole_sc[:, at] = (
            mm(ggrad[...], ws2[j][:, :inner], NT)
            + mm(mg[...], ws1[j][:, :inner], NT)
            + mm(xg, ws1[j][:, -128:], NT)
        )
    value = whole_sc[...]
    scaled = normalize(pick(s_ref, b, quarter, own[...], near[...], far[...]), 1.0)[0]
    cols_ref[0:1] += jnp.sum(value * scaled, axis=0, keepdims=True)
    deal(s_ref, b, quarter, value, outs)


def branch_body(parts, quarter, s_ref, gated, *rest):
    ws2 = rest[:parts]
    outs = rest[parts : parts + 4]
    whole_sc = rest[parts + 4]
    inner = gated.shape[1]
    shard = ws2[0].shape[0]
    for j in range(parts):
        whole_sc[:, lanes_of(s_ref, j, shard)] = mm(gated[...], ws2[j][:, inner:], NT)
    deal(s_ref, pl.program_id(0), quarter, whole_sc[...], outs)


def per_device(
    hidden, lengths, cotangent, norm_gain, proj_main, proj_state, proj_delta, conv_main, conv_state,
    bias_main, bias_state, delta_bias, log_rate, skip_gain, gate_gain, proj_out,
):
    _, steps, model = hidden.shape
    hidden, cotangent = hidden[0], cotangent[0]
    dps, ctxs, tps = lax.axis_size("dp"), lax.axis_size("ctx"), lax.axis_size("tp")
    dp, z, core = lax.axis_index("dp"), lax.axis_index("ctx"), lax.axis_index("tp")
    lo, hi = z % 2, z // 2
    pairs = ctxs // 2
    tokens = 2 * steps
    count = tokens // BLOCK
    quarter = count // 4
    inner = bias_main.shape[0] // 2
    heads = delta_bias.shape[0] // 2
    states = bias_state.shape[0] // 2
    wide = inner + 2 * states

    def swap(value):
        return lax.ppermute(value, "tp", [(0, 1), (1, 0)])

    def across(value, j):
        return lax.ppermute(value, "ctx", [(i, i ^ j) for i in range(ctxs)])

    def along(value, step):
        return lax.ppermute(
            value, "ctx", [(i, i + step) for i in range(ctxs) if 0 <= i + step < ctxs]
        )

    def spread(value, j):
        return lax.ppermute(value, "dp", [(i, i ^ j) for i in range(dps)])

    def mine(value, axis, size):
        return lax.dynamic_slice_in_dim(value, lo * size, size, axis)

    def piece(value, at, size):
        return lax.dynamic_slice_in_dim(value, at * size, size, 0)

    apart = proj_main.shape[0] % 128 == 0
    parts = dps if apart else 1
    shard = proj_main.shape[0] * (dps // parts)

    def gathered(value):
        if not apart:
            return [lax.all_gather(value, "dp", axis=0, tiled=True)]
        return [value] + [spread(value, j) for j in range(1, dps)]

    scalars = jnp.stack(
        [lo, core, hi * tokens, lengths[0], (hi > 0).astype(jnp.int32), (hi < pairs - 1).astype(jnp.int32)]
        + [dp ^ j if apart else 0 * dp for j in range(parts)]
    ).astype(jnp.int32)

    state_own = lax.dynamic_slice_in_dim(proj_state, lo * states + core * (states // 2), states // 2, 1)
    delta_own = mine(proj_delta, 1, heads)
    main_part = mine(proj_main, 2, inner)
    first = jnp.concatenate(
        [main_part[:, 1], proj_state, state_own, delta_own,
         jnp.zeros((proj_main.shape[0], 64 - heads), BF16)], axis=1
    )
    halfway = steps // 2
    near = across(piece(hidden, core, halfway), 1)
    far = swap(near)
    edge, _ = lax.optimization_barrier((hidden[steps - 16 :], first))
    halo = jnp.where(lo == 0, along(edge, 1), along(edge, 2))
    ws1 = gathered(first)
    ws1, near, main_gate, out_later, cot_later = lax.optimization_barrier(
        (ws1, near, main_part[:, 0], proj_out, cotangent)
    )
    second = jnp.concatenate([main_gate, mine(out_later, 1, inner)], axis=1)
    cot_near = across(piece(cot_later, core, halfway), 1)
    ws2 = gathered(second)

    def over_sequences(pieces):
        return [spread(pieces[j], j) for j in range(1, parts)]

    def chunks(pieces, got, extra=0):
        total = pieces[0]
        rows = total.shape[0] - extra
        if not apart:
            shared = [lax.psum(total[rows:], "dp")] if extra else []
            total = jnp.concatenate(
                [lax.psum_scatter(total[:rows], "dp", scatter_dimension=0, tiled=True)] + shared
            )
            rows = total.shape[0] - extra
        for part in got:
            total = total + part
        size = rows // ctxs

        def chunk(j):
            part = piece(total, z ^ j, size)
            return jnp.concatenate([part, total[rows:]]) if extra else part

        return [chunk(j) for j in range(ctxs)]

    def over_positions(cut):
        return [across(cut[j], j) for j in range(1, ctxs)]

    def settled(cut, got, extra=0):
        own, opposite = cut[0], got[0]
        for j in range(2, ctxs):
            if j % 2 == 0:
                own = own + got[j - 1]
            else:
                opposite = opposite + got[j - 1]
        size = own.shape[0] - extra
        own, opposite = jnp.where(lo == 0, own, opposite), jnp.where(lo == 0, opposite, own)
        return (own[:size], opposite[:size]), (own[size:], opposite[size:])

    taps_x = jnp.concatenate([mine(conv_main, 1, inner), conv_state], axis=1)
    bias_x = jnp.concatenate([mine(bias_main, 0, inner), bias_state])[None]
    rate_own = -jnp.exp(mine(log_rate, 0, heads))

    def in_heads(value):
        return jnp.pad(value, (HEAD0, 128 - HEAD0 - heads))[None]

    rate_row = in_heads(rate_own)
    dbias_row = in_heads(mine(delta_bias, 0, heads))
    skip_row = jnp.repeat(mine(skip_gain, 0, heads), inner // heads)[None]
    ggain_row = mine(gate_gain, 0, inner)[None]
    gain_row = norm_gain[None]
    own_spec = pl.BlockSpec(
        (BLOCK, model), lambda b, s: (jnp.clip(b - s[LO] * 2 * quarter, 0, 2 * quarter - 1), 0)
    )
    part_spec = pl.BlockSpec((BLOCK, model), lambda b, s: (b % quarter, 0))
    subs = BLOCK // SUB
    last = count * subs
    state_block = pl.BlockSpec((subs, states, inner), lambda b, s: (b, 0, 0))
    pre_block = pl.BlockSpec((subs, 8, inner), lambda b, s: (b, 0, 0))

    normed, u, uh, conv, draw, delta, level, level_x, delta_x, hloc, pre, own_end = grid_call(
        functools.partial(front_body, parts, inner, states, quarter),
        (count,),
        [own_spec, part_spec, part_spec, whole((16, model)), whole((1, model)), whole((4, wide)),
         whole((1, wide)), whole((1, 128)), whole((1, 128))] + [whole((shard, wide + 128))] * parts,
        [rows_spec(model), rows_spec(wide), whole((8, wide)), rows_spec(wide), rows_spec(128), rows_spec(128),
         rows_spec(128), rows_spec(inner), rows_spec(inner), whole((last + 1, states, inner)),
         whole((last + 1, 8, inner)), whole((states, inner))],
        [shaped((tokens, model), BF16), shaped((tokens, wide)), shaped((8, wide)), shaped((tokens, wide)),
         shaped((tokens, 128)), shaped((tokens, 128)), shaped((tokens, 128)), shaped((tokens, inner)),
         shaped((tokens, inner)), shaped((last + 1, states, inner)), shaped((last + 1, 8, inner)), shaped((states, inner))],
        [pltpu.VMEM((16, model), BF16), pltpu.VMEM((8 + BLOCK, wide), F32), pltpu.VMEM((states, inner), F32),
         pltpu.VMEM((8, inner), F32), pltpu.VMEM((384, inner), BF16)],
        name="front",
    )(scalars, hidden, near, far, halo, gain_row, taps_x, bias_x, dbias_row, rate_row, *ws1)

    cot_near, own_end = lax.optimization_barrier((cot_near, own_end))
    cot_far = swap(cot_near)
    growth = jnp.exp(pre[last][0:1])
    carried = jnp.zeros_like(own_end)
    sending = own_end
    for hop in range(pairs - 1):
        carried = along(sending, 2)
        if hop < pairs - 2:
            sending = own_end + growth * carried

    (inside,) = grid_call(
        functools.partial(within_body, inner, states),
        (count,),
        [rows_spec(wide), rows_spec(128), rows_spec(inner), rows_spec(inner)],
        [rows_spec(inner)],
        [shaped((tokens, inner))],
        name="within",
    )(scalars, conv, level, level_x, delta_x)

    gate, gated_grad, branch_grad = grid_call(
        functools.partial(gates_body, parts, quarter),
        (count,),
        [rows_spec(model), own_spec, part_spec, part_spec] + [whole((shard, 2 * inner))] * parts,
        [rows_spec(inner), rows_spec(inner), rows_spec(model)],
        [shaped((tokens, inner)), shaped((tokens, inner)), shaped((tokens, model), BF16)],
        name="gates",
    )(scalars, normed, cotangent, cot_near, cot_far, *ws2)

    y, sums = grid_call(
        functools.partial(output_body, inner, states),
        (count,),
        [rows_spec(wide), rows_spec(inner), rows_spec(inner), rows_spec(inner), rows_spec(inner), state_block,
         pre_block, whole((states, inner)), whole((1, inner)), whole((1, inner))],
        [rows_spec(inner), pl.BlockSpec((16, BLOCK), lambda b, s: (0, b))],
        [shaped((tokens, inner)), shaped((16, tokens))],
        name="output",
    )(scalars, conv, level_x, inside, gate, gated_grad, hloc, pre, carried, skip_row, ggain_row)

    sums = sums + swap(sums)
    more_sums = across(sums, 1)

    def back(width, rows=BLOCK):
        return pl.BlockSpec((rows, width), lambda b, s: (count - 1 - b, 0))

    back_sums = pl.BlockSpec((16, BLOCK), lambda b, s: (0, count - 1 - b))
    gated, gate_grad, out_grad, gloc, own_start, turn_cols = grid_call(
        functools.partial(turn_body, inner, states, 2 * tps * inner),
        (count,),
        [back(wide), back(inner), back(inner), back(inner), back(inner),
         back_sums, back_sums, whole((1, inner)), whole((1, inner))],
        [back(inner), back(inner), back(inner), whole((last + 1, states, inner)), whole((states, inner)),
         whole((8, inner))],
        [shaped((tokens, inner), BF16), shaped((tokens, inner), BF16), shaped((tokens, inner)),
         shaped((last + 1, states, inner)), shaped((states, inner)), shaped((8, inner))],
        [pltpu.VMEM((states, inner), F32)],
        name="turn",
    )(scalars, conv, level_x, y, gate, gated_grad, sums, more_sums, skip_row, ggain_row)

    returned = jnp.zeros_like(own_start)
    sending = own_start
    for hop in range(pairs - 1):
        returned = along(sending, -2)
        if hop < pairs - 2:
            sending = own_start + growth * returned

    turned = pl.BlockSpec((tokens, shard), lambda j, s: (0, s[SLOT0 + j]))
    early = grid_call(
        functools.partial(early_body, parts),
        (parts,),
        [turned, whole((tokens, inner)), turned, whole((tokens, inner))],
        [whole((shard, 2 * inner))] * parts,
        [shaped((shard, 2 * inner))] * parts,
        name="grad_early",
    )(scalars, normed, gate_grad, branch_grad, gated)

    early, out_grad = lax.optimization_barrier((early, out_grad))
    early_got = over_sequences(early)

    zed, dbc = grid_call(
        functools.partial(back_body, inner, states),
        (count,),
        [rows_spec(wide), rows_spec(128), rows_spec(inner), rows_spec(inner), rows_spec(inner), state_block,
         pre_block, whole((states, inner))],
        [rows_spec(inner), rows_spec(2 * states)],
        [shaped((tokens, inner)), shaped((tokens, 2 * states))],
        name="back",
    )(scalars, conv, level, level_x, delta_x, out_grad, hloc, pre, carried)

    all_states = whole((last + 1, states, inner))
    all_pre = whole((last + 1, 8, inner))
    per = BLOCK // 8
    half_rows = tokens // 2

    def back_lanes(width, lanes):
        return [
            pl.BlockSpec((BLOCK, width), lambda b, s: (count - 1 - b, lanes(s))),
            pl.BlockSpec((8, width), lambda b, s: (jnp.maximum((count - 1 - b) * per - 1, 0), lanes(s))),
            pl.BlockSpec((8, width), lambda b, s: (0, lanes(s))),
        ]

    def table(rows, width, lanes):
        return pl.BlockSpec((rows, width), lambda b, s: (0, lanes(s)))

    signal_pre, tail, head, dbc_keep, dbc_give, raw_grad, head_cols, signal_cols = grid_call(
        functools.partial(join_body, inner, states),
        (count,),
        [back(wide), back(128), back(inner), back(inner), back(128), back(inner), back(inner), back(inner),
         back(2 * states), all_states, all_pre, all_states, whole((states, inner)), whole((states, inner))]
        + back_lanes(inner, lambda s: 0)
        + [table(4, inner, lambda s: 0), whole((1, 128)), whole((1, inner))],
        [back(inner), whole((8, inner)), whole((8, inner)), whole((half_rows, 2 * states)),
         whole((half_rows, 2 * states)), back(128), whole((8, 128)), whole((8, inner))],
        [shaped((tokens, inner), BF16), shaped((8, inner)), shaped((8, inner)), shaped((half_rows, 2 * states)),
         shaped((half_rows, 2 * states)), shaped((tokens, 128)), shaped((8, 128)), shaped((8, inner))],
        [pltpu.VMEM((3 * inner, 128), BF16), pltpu.VMEM((BLOCK + 8, inner), F32),
         pltpu.VMEM((BLOCK + 8, inner), F32)],
        name="join",
    )(scalars, conv, delta, level_x, delta_x, draw, out_grad, y, zed, dbc, hloc, pre, gloc, returned, carried,
      u, u, uh, taps_x, rate_row, skip_row)

    ahead = jnp.where(hi < pairs - 1, along(head, -2), 0.0)
    for k in range(3):
        tail = tail + taps_x[k, :inner] * jnp.concatenate([jnp.zeros((5 + k, inner), F32), ahead[: 3 - k]])
    signal_pre = lax.dynamic_update_slice_in_dim(signal_pre, tail.astype(BF16), tokens - 8, 0)

    dbc = dbc_keep + swap(dbc_give)
    dbc_back = across(lax.dynamic_slice_in_dim(dbc, (1 - lo) * states, states, 1), 1)
    gated_later, early_got, _ = lax.optimization_barrier((gated, early_got, dbc))
    branch = grid_call(
        functools.partial(branch_body, parts, quarter),
        (count,),
        [rows_spec(inner)] + [whole((shard, 2 * inner))] * parts,
        [whole((halfway, model))] * 4,
        [shaped((halfway, model))] * 4,
        [pltpu.VMEM((BLOCK, model), F32)],
        name="branch",
    )(scalars, gated_later, *ws2)

    def over_cores(dealt):
        return dealt[0] + swap(dealt[2]), dealt[1] + swap(dealt[3])

    branch_mine, branch_theirs = over_cores(branch)

    dbc = mine(dbc, 1, states) + dbc_back
    dbc_other = swap(dbc)
    head_rows = jnp.where(core == 0, dbc[:8], dbc_other[:8])
    head_conv = lax.dynamic_slice(conv, (0, inner + lo * states), (8, states))
    state_ahead = along(head_rows * slope(head_conv, jax.nn.sigmoid(head_conv)), -2)
    early_cut = chunks(early, early_got)
    branch_theirs, early_cut, state_ahead = lax.optimization_barrier((branch_theirs, early_cut, state_ahead))
    branch_back = across(branch_theirs, 1)
    early_far = over_positions(early_cut)

    def back_own(b, s):
        return jnp.clip(count - 1 - b - s[LO] * 2 * quarter, 0, 2 * quarter - 1), 0

    def state_lanes(s):
        return inner // states + s[LO]

    back_part = pl.BlockSpec((BLOCK, model), lambda b, s: ((count - 1 - b) % quarter, 0))
    back_half = pl.BlockSpec((BLOCK, states), lambda b, s: ((count - 1 - b) % (count // 2), 0))
    state_side = back_lanes(states, state_lanes)
    *feature, extra_pre, feature_cols, state_cols = grid_call(
        functools.partial(feature_body, parts, quarter),
        (count,),
        [pl.BlockSpec((BLOCK, model), back_own), back_part, back_part, back(inner), back(inner), back(128),
         back_half, back_half, state_side[0]] + state_side
        + [whole((8, states)), table(4, states, state_lanes)]
        + [whole((shard, wide + 128))] * parts + [whole((shard, 2 * inner))] * parts,
        [whole((halfway, model))] * 4 + [back(128), whole((8, model)), whole((8, states))],
        [shaped((halfway, model))] * 4 + [shaped((tokens, 128), BF16), shaped((8, model)), shaped((8, states))],
        [pltpu.VMEM((BLOCK, model), F32), pltpu.VMEM((BLOCK + 8, states), F32),
         pltpu.VMEM((BLOCK + 8, states), F32)],
        name="feature",
    )(scalars, hidden, near, far, gate_grad, signal_pre, raw_grad, dbc, dbc_other, conv, u, u, uh, state_ahead,
      taps_x, *ws1, *ws2)
    feature_mine, feature_theirs = over_cores(feature)

    folds = model // inner
    small = jnp.concatenate(
        [
            jnp.concatenate([signal_cols, state_cols], axis=1),
            jnp.concatenate([turn_cols[:2], head_cols[:2]], axis=1),
            jnp.pad(feature_cols[0].reshape(folds, inner), ((0, 6 - folds), (0, 128))),
        ]
    )
    late = grid_call(
        functools.partial(late_body, parts),
        (parts,),
        [turned, whole((tokens, inner)), whole((tokens, 128)), whole((16, inner + 128))],
        [whole((shard + 16, inner + 128))] * parts,
        [shaped((shard + 16, inner + 128))] * parts,
        name="grad_late",
    )(scalars, normed, signal_pre, extra_pre, small)
    late, feature_theirs, early_far, branch_back = lax.optimization_barrier(
        (late, feature_theirs, early_far, branch_back)
    )
    early_sum, _ = settled(early_cut, early_far)
    late_got, feature_back = lax.optimization_barrier((over_sequences(late), across(feature_theirs, 1)))
    late_cut = chunks(late, late_got, 16)
    late_sum, small_sum = settled(late_cut, over_positions(late_cut), 16)

    def both_halves(value):
        other = swap(value)
        return jnp.where(core == 0, jnp.concatenate([value, other]), jnp.concatenate([other, value]))

    residual = piece(hidden, core, halfway).astype(F32)
    place = z * steps + core * halfway + lax.broadcasted_iota(jnp.int32, (halfway, 1), 0)
    valid = (place < lengths[0]).astype(F32)
    mixed = both_halves((residual + valid * (branch_mine + branch_back)).astype(BF16))

    feature_grad = feature_mine + feature_back
    inverse = lax.rsqrt(jnp.mean(residual * residual, axis=1, keepdims=True) + EPSILON)
    scaled_own = residual * inverse
    scaled_grad = feature_grad * norm_gain
    upstream = piece(cotangent, core, halfway).astype(F32)
    grad_hidden = both_halves(
        upstream + inverse * (scaled_grad - scaled_own * jnp.mean(scaled_grad * scaled_own, axis=1, keepdims=True))
    )

    def side_by_side(pair):
        return jnp.concatenate(pair, axis=-1)

    signal_small = side_by_side([part[:, :inner] for part in small_sum])
    state_small = side_by_side([part[:8, inner:] for part in small_sum])
    heads_small = [part[8:10, inner + HEAD0 : inner + HEAD0 + heads] for part in small_sum]
    rate_all = -jnp.exp(log_rate)
    skip_sum = signal_small[9].reshape(2 * heads, inner // heads).sum(axis=1)
    gain_here = (small_sum[0] + small_sum[1])[10 : 10 + folds, :inner].reshape(model)
    state_here = jnp.stack([part[:, inner : inner + HEAD0] for part in late_sum])
    gain_there, state_there = swap(gain_here), swap(state_here)
    gain_size = model // (dps * ctxs)
    gain_sum = piece(gain_here + gain_there, dp * ctxs + z, gain_size)
    in_order = jnp.where(
        core == 0, jnp.stack([state_here, state_there], 1), jnp.stack([state_there, state_here], 1)
    )
    state_sum = jnp.transpose(in_order, (2, 0, 1, 3)).reshape(-1, 2 * states)
    main_sum = jnp.stack(
        [side_by_side([part[:, :inner] for part in early_sum]), side_by_side([part[:, :inner] for part in late_sum])],
        axis=1,
    )
    delta_sum = side_by_side([part[:, inner + HEAD0 : inner + HEAD0 + heads] for part in late_sum])

    return (
        mixed[None],
        grad_hidden[None],
        gain_sum,
        main_sum,
        state_sum,
        delta_sum,
        signal_small[:4],
        state_small[:4],
        signal_small[4],
        state_small[4],
        side_by_side([part[0] for part in heads_small]),
        side_by_side([part[1] for part in heads_small]) * rate_all,
        skip_sum,
        signal_small[8],
        side_by_side([part[:, inner:] for part in early_sum]),
    )


def solution(mesh):
    in_specs = (
        P("dp", "ctx", None), P("dp"), P("dp", "ctx", None), P(), P("dp", None, "tp"), P("dp", None),
        P("dp", "tp"), P(None, "tp"), P(), P("tp"), P(), P("tp"), P("tp"), P("tp"), P("tp"), P("dp", "tp"),
    )
    out_specs = (
        P("dp", "ctx", None), P("dp", "ctx", None), P(("dp", "ctx")), P(("dp", "ctx"), None, "tp"),
        P(("dp", "ctx"), None), P(("dp", "ctx"), "tp"), P(None, "tp"), P(), P("tp"), P(), P("tp"), P("tp"),
        P("tp"), P("tp"), P(("dp", "ctx"), "tp"),
    )
    return jax.shard_map(
        per_device, mesh=mesh, in_specs=in_specs, out_specs=out_specs, check_vma=False
    )
```

time: 439 us -> 308 us (0.70)
  blocking collectives: 102 us -> 0 us
  waiting for transfers between devices: 49.5 us -> 89.4 us
  Pallas kernels: 141 us -> 112 us
  starting transfers between devices: 71.1 us -> 48.4 us
  local copies, waits for them, and re-layouts: 36 us -> 26 us
  other arithmetic: 34.1 us -> 27.8 us
    unnamed x1 -> x0, blocking collectives: 99.3 us -> none
    ppermute x18 -> x12, waiting for transfers between devices: 16.7 us -> 41.9 us  [spread(): return lax.ppermute(value, 'dp', [(i, i ^ j) for i in range(dps)])]
    ppermute x18 -> x12, starting transfers between devices: 34 us -> 14.8 us  [across(): return lax.ppermute(value, 'ctx', [(i, i ^ j) for i in range(ctxs)])]
    pallas_call x8 -> x4, Pallas kernels: 49.8 us -> 33.7 us  [the longest x1 11.5 us: per_device(): grid_call(functools.partial(feature_body, parts, quarter), (count,), [pl....]
    squeeze x7 -> x2, local copies, waits for them, and re-layouts: 9.54 us -> 0.15 us  [per_device(): part[1]]
    ppermute x18 -> x12, waiting for transfers between devices: 29.6 us -> 38.6 us  [across(): return lax.ppermute(value, 'ctx', [(i, i ^ j) for i in range(ctxs)])]
    ppermute x18 -> x12, starting transfers between devices: 23.1 us -> 15.1 us  [spread(): return lax.ppermute(value, 'dp', [(i, i ^ j) for i in range(dps)])]
    ppermute x5 -> x6, waiting for transfers between devices: 0.01 us -> 6.93 us  [along(): lax.ppermute(value, 'ctx', [(i, i + step) for i in range(ctxs) if 0 <= i...]
  transfers between devices with their start and end apart: 51 -> 43, of which waited for: 12 -> 14; matrix products, arithmetic and copies ran while one was open for 12% -> 12% of each run, Pallas kernels for 24% -> 27%
where the time goes in v2:
time: 308 us; the launch traced here: 305 us
  Pallas kernels  112 us (36%)
  waiting for transfers between devices  89.4 us (29%)
  starting transfers between devices  48.4 us (16%)
  other arithmetic  27.8 us (9%)
  local copies, waits for them, and re-layouts  26 us (8%)
    ppermute x12, waiting for transfers between devices, spread(): return lax.ppermute(value, 'dp', [(i, i ^ j) for i in range(dps)])  41.9 us
    ppermute x12, waiting for transfers between devices, across(): return lax.ppermute(value, 'ctx', [(i, i ^ j) for i in range(ctxs)])  38.6 us
    pallas_call x1, Pallas kernels, per_device(): grid_call(functools.partial(join_body, inner, states), (count,), [back(wi...  16.4 us
    ppermute x6, starting transfers between devices, along(): lax.ppermute(value, 'ctx', [(i, i + step) for i in range(ctxs) if 0 <= i...  16.3 us
    pallas_call x1, Pallas kernels, per_device(): grid_call(functools.partial(front_body, parts, inner, states, quarter), (...  15.3 us
    ppermute x12, starting transfers between devices, spread(): return lax.ppermute(value, 'dp', [(i, i ^ j) for i in range(dps)])  15.1 us
    ppermute x12, starting transfers between devices, across(): return lax.ppermute(value, 'ctx', [(i, i ^ j) for i in range(ctxs)])  14.8 us
    pallas_call x1, Pallas kernels, per_device(): grid_call(functools.partial(feature_body, parts, quarter), (count,), [pl....  11.5 us
  transfers between devices with their start and end apart: 43, of which 14 were waited for; matrix products, arithmetic and copies ran while one was open for 12% of the time, Pallas kernels for 27%

profile of v2, /device:TPU:0, one launch (start us, length us, event | category | flops | bytes accessed | tf_op | source)
XLA Modules:
  0.0 305.3 jit_solution(2413776326595697872)
XLA Ops:
  2.2 3.4 %constant_dynamic-slice_fusion.17 = (bf16[256,1,512]{2,1,0:T(2,128)(2,1)}, bf16[256,1,512]{2,1,0:T(2,128)(2,1)S(1)}) fusion(bf16[256,2,1024]{2,1,0:T(2,128)(2,1)} %param.20, s32[]{:T(128)S(6)} %select_n.157, s32[]{:T(128)S(6)} %add.252), kind=kLoop, calls=%fused_computation.74 | loop fusion | bytes 1048584 | tf_op jit(solution)/shard_map/slice | solution.py:594
  5.7 1.9 concatenate.114.rest_0_
  7.6 3.9 %collective-permute-start.2 = (bf16[256,896]{1,0:T(8,128)(2,1)}, bf16[256,896]{1,0:T(8,128)(2,1)}, u32[]{:S(2)}, u32[]{:S(2)}) collective-permute-start(bf16[256,896]{1,0:T(8,128)(2,1)} %concatenate.114.rest_0_), channel_id=1, source_target_pairs={{0,24},{8,16},{16,8},{24,0},{1,25},{9,17},{17,9},{25,1},{2,26},{10... | collective-permute-start | bytes 1376264 | tf_op jit(solution)/shard_map/ppermute | solution.py:558
  12.3 2.1 collective-permute-start.3
  14.3 4.5 %collective-permute-start.6 = (bf16[16,1024]{1,0:T(8,128)(2,1)S(1)}, bf16[16,1024]{1,0:T(8,128)(2,1)S(1)}, u32[]{:S(2)}, u32[]{:S(2)}) collective-permute-start(bf16[16,1024]{1,0:T(8,128)(2,1)S(1)} %slice_bitcast_fusion.2), channel_id=1, source_target_pairs={{0,4},{2,6},{1,5},{3,7},{8,12},{10,14},{9,13},{11,15},{16,20},{18,... | collective-permute-start | bytes 98312 | tf_op jit(solution)/shard_map/ppermute | solution.py:553
  22.8 1.3 pad_maximum_fusion.8.taps
  24.1 3.0 collective-permute-start.5
  27.2 5.0 %collective-permute-done.1.rest_2_ = bf16[256,896]{1,0:T(8,128)(2,1)} collective-permute-done((bf16[256,896]{1,0:T(8,128)(2,1)}, bf16[256,896]{1,0:T(8,128)(2,1)}, u32[]{:S(2)}, u32[]{:S(2)}) %collective-permute-start.1) | collective-permute-done | bytes 458784 | tf_op jit(solution)/shard_map/ppermute | solution.py:558
  33.3 1.5 collective-permute-start.7
  38.1 1.7 collective-permute-start.11
  39.9 1.3 collective-permute-start.10
  42.5 15.3 %front.1 = (bf16[1024,1024]{1,0:T(8,128)(2,1)}, f32[1024,768]{1,0:T(8,128)}, f32[8,768]{1,0:T(8,128)}, f32[1024,768]{1,0:T(8,128)}, f32[1024,128]{1,0:T(8,128)},...) custom-call(s32[10]{0:T(128)} %stack.79.s_ref, ...), custom_call_target="tpu_custom_call" | custom-call | tf_op jit(solution)/shard_map/front/pallas_call | solution.py:657
  57.8 4.5 %collective-permute-start.12 = (f32[128,512]{1,0:T(8,128)}, f32[128,512]{1,0:T(8,128)S(1)}, u32[]{:S(2)}, u32[]{:S(2)}) collective-permute-start(f32[128,512]{1,0:T(8,128)} %get-tuple-element.126), channel_id=1, source_target_pairs={{0,4},{2,6},{1,5},{3,7},{8,12},{10,14},{9,13},{11,15},{16,20},{18,... | collective-permute-start | bytes 786440 | tf_op jit(solution)/shard_map/ppermute | solution.py:553
  63.8 7.8 %within.1.yw = f32[1024,512]{1,0:T(8,128)} custom-call(s32[10]{0:T(128)} %stack.79.s_ref, f32[1024,768]{1,0:T(8,128)} %get-tuple-element.112.co, f32[1024,128]{1,0:T(8,128)} %get-tuple-element.114.lev, f32[1024,512]{1,0:T(8,128)} %get-tuple-element.113.lx, f32[1024,512]{1,0:T(8,128)} %get-tuple-element.115.dx), custom_call_target="tpu_custom_call" | custom-call | tf_op jit(solution)/shard_map/within/pallas_call | solution.py:683
  72.8 8.5 %gates.1 = (f32[1024,512]{1,0:T(8,128)}, f32[1024,512]{1,0:T(8,128)}, bf16[1024,1024]{1,0:T(8,128)(2,1)}) custom-call(s32[10]{0:T(128)} %stack.79.s_ref, bf16[1024,1024]{1,0:T(8,128)(2,1)} %get-tuple-element.116.normed.left1.left, bf16[512,1024]{1,0:T(8,128)(2,1)} %bitcast.70, bf16[256,1024]{1,0:T(8,128)(2,1)} %collective-permute-done.7.near, ...), custom_call_target="tpu_custom_call" | custom-call | tf_op jit(solution)/shard_map/gates/pallas_call | solution.py:692
  81.9 8.5 %output.1 = (f32[1024,512]{1,0:T(8,128)}, f32[16,1024]{1,0:T(8,128)}) custom-call(s32[10]{0:T(128)} %stack.79.s_ref, f32[1024,768]{1,0:T(8,128)} %get-tuple-element.112.co, f32[1024,512]{1,0:T(8,128)} %get-tuple-element.113.lx, f32[1024,512]{1,0:T(8,128)} %within.1.yw, f32[1024,512]{1,0:T(8,128)} %get-tuple-element.122.gate, ...), custom_call_target="tpu_custom_call" | custom-call | tf_op jit(solution)/shard_map/output/pallas_call | solution.py:701
  93.5 3.6 %collective-permute-done.14.more = f32[16,1024]{1,0:T(8,128)S(1)} collective-permute-done((f32[16,1024]{1,0:T(8,128)S(1)}, f32[16,1024]{1,0:T(8,128)S(1)}, u32[]{:S(2)}, u32[]{:S(2)}) %collective-permute-start.14) | collective-permute-done | bytes 65568 | tf_op jit(solution)/shard_map/ppermute | solution.py:550
  97.7 10.2 %turn.1 = (bf16[1024,512]{1,0:T(8,128)(2,1)}, bf16[1024,512]{1,0:T(8,128)(2,1)}, f32[1024,512]{1,0:T(8,128)}, f32[9,128,512]{2,1,0:T(8,128)}, f32[128,512]{1,0:T(8,128)}, /*index=5*/f32[8,512]{1,0:T(8,128)}) custom-call(s32[10]{0:T(128)} %stack.79.s_ref, f32[1024,768]{1,0:T(8,128)} %get-tuple-element.112.co, f32[1024,512]{1,0:T(8,128)} %get-tuple-element.113.lx, ...), custom_call_target="tpu_custom_call" | custom-call | tf_op jit(solution)/shard_map/turn/pallas_call | solution.py:718
  107.9 1.5 collective-permute-start.18
  109.4 8.4 %grad_early.1 = (f32[256,1024]{1,0:T(8,128)}, f32[256,1024]{1,0:T(8,128)}, f32[256,1024]{1,0:T(8,128)}, f32[256,1024]{1,0:T(8,128)}) custom-call(s32[10]{0:T(128)} %stack.79.s_ref, bf16[1024,1024]{1,0:T(8,128)(2,1)} %get-tuple-element.116.normed.left1.left, bf16[1024,512]{1,0:T(8,128)(2,1)} %get-tuple-element.130.right1.ggrad, ...), custom_call_target="tpu_custom_call" | custom-call | tf_op jit(solution)/shard_map/grad_early/pallas_call | solution.py:739
  117.8 1.5 collective-permute-start.15
  121.3 11.3 %back.1 = (f32[1024,512]{1,0:T(8,128)}, f32[1024,256]{1,0:T(8,128)}) custom-call(s32[10]{0:T(128)} %stack.79.s_ref, f32[1024,768]{1,0:T(8,128)} %get-tuple-element.112.co, f32[1024,128]{1,0:T(8,128)} %get-tuple-element.114.lev, f32[1024,512]{1,0:T(8,128)} %get-tuple-element.113.lx, f32[1024,512]{1,0:T(8,128)} %get-tuple-element.115.dx, ...), custom_call_target="tpu_custom_call" | custom-call | tf_op jit(solution)/shard_map/back/pallas_call | solution.py:751
  133.3 16.4 %join.1 = (bf16[1024,512]{1,0:T(8,128)(2,1)}, f32[8,512]{1,0:T(8,128)}, f32[8,512]{1,0:T(8,128)}, f32[512,256]{1,0:T(8,128)}, f32[512,256]{1,0:T(8,128)}, /*inde...) custom-call(s32[10]{0:T(128)} %stack.79.s_ref, f32[1024,768]{1,0:T(8,128)} %get-tuple-element.112.co, ...), custom_call_target="tpu_custom_call" | custom-call | tf_op jit(solution)/shard_map/join/pallas_call | solution.py:776
  149.9 1.3 collective-permute-start.21
  153.8 3.1 %collective-permute-done.21 = f32[8,512]{1,0:T(8,128)S(1)} collective-permute-done((f32[8,512]{1,0:T(8,128)}, f32[8,512]{1,0:T(8,128)S(1)}, u32[]{:S(2)}, u32[]{:S(2)}) %collective-permute-start.21) | collective-permute-done | bytes 16416 | tf_op jit(solution)/shard_map/ppermute | solution.py:553
  157.0 8.9 %collective-permute-done.16 = f32[256,1024]{1,0:T(8,128)} collective-permute-done((f32[256,1024]{1,0:T(8,128)}, f32[256,1024]{1,0:T(8,128)}, u32[]{:S(2)}, u32[]{:S(2)}) %collective-permute-start.16) | collective-permute-done | bytes 1048608 | tf_op jit(solution)/shard_map/ppermute | solution.py:558
  165.9 7.0 %branch.1 = (f32[256,1024]{1,0:T(8,128)}, f32[256,1024]{1,0:T(8,128)}, f32[256,1024]{1,0:T(8,128)}, f32[256,1024]{1,0:T(8,128)}) custom-call(s32[10]{0:T(128)} %stack.79.s_ref, bf16[1024,512]{1,0:T(8,128)(2,1)} %get-tuple-element.151.right2.gated, bf16[256,1024]{1,0:T(8,128)(2,1)} %copy-done.2, bf16[256,1024]{1,0:T(8,128)(2,1)} %copy-done.6, ...), custom_call_target="tpu_custom_call" | custom-call | tf_op jit(solution)/shard_map/branch/pallas_call | solution.py:801
  175.1 1.9 add_add_fusion
  177.9 1.5 collective-permute-start.25
  180.5 3.8 %collective-permute-done.25.ahead = f32[8,128]{1,0:T(8,128)S(1)} collective-permute-done((f32[8,128]{1,0:T(8,128)S(1)}, f32[8,128]{1,0:T(8,128)S(1)}, u32[]{:S(2)}, u32[]{:S(2)}) %collective-permute-start.25) | collective-permute-done | bytes 4128 | tf_op jit(solution)/shard_map/ppermute | solution.py:553
  184.9 11.5 %feature.1 = (f32[256,1024]{1,0:T(8,128)}, f32[256,1024]{1,0:T(8,128)}, f32[256,1024]{1,0:T(8,128)}, f32[256,1024]{1,0:T(8,128)}, bf16[1024,128]{1,0:T(8,128)(2,...) custom-call(s32[10]{0:T(128)} %stack.79.s_ref, bf16[512,1024]{1,0:T(8,128)(2,1)} %bitcast.68, ...), custom_call_target="tpu_custom_call" | custom-call | tf_op jit(solution)/shard_map/feature/pallas_call | solution.py:835
  197.3 1.3 collective-permute-start.27
  198.6 3.0 collective-permute-start.29
  203.9 1.3 select_maximum_fusion.small
  205.2 6.8 %grad_late.1 = (f32[272,640]{1,0:T(8,128)}, f32[272,640]{1,0:T(8,128)}, f32[272,640]{1,0:T(8,128)}, f32[272,640]{1,0:T(8,128)}) custom-call(s32[10]{0:T(128)} %stack.79.s_ref, bf16[1024,1024]{1,0:T(8,128)(2,1)} %get-tuple-element.116.normed.left1.left, bf16[1024,512]{1,0:T(8,128)(2,1)} %fusion.11.mg.right1, bf16[1024,128]{1,0:T(8,128)(2,1)} %get-tuple-element.165.right2, ...), custom_call_target="tpu_custom_call" | custom-call | tf_op jit(solution)/shard_map/grad_late/pallas_call | solution.py:859
  212.1 1.5 add.225
  213.6 25.5 %collective-permute-done.27 = f32[64,1024]{1,0:T(8,128)} collective-permute-done((f32[64,1024]{1,0:T(8,128)}, f32[64,1024]{1,0:T(8,128)}, u32[]{:S(2)}, u32[]{:S(2)}) %collective-permute-start.27) | collective-permute-done | bytes 262176 | tf_op jit(solution)/shard_map/ppermute | solution.py:550
  239.9 1.4 collective-permute-start.34
  241.3 1.5 collective-permute-start.35
  244.8 12.9 %collective-permute-done.33 = f32[272,640]{1,0:T(8,128)S(1)} collective-permute-done((f32[272,640]{1,0:T(8,128)S(1)}, f32[272,640]{1,0:T(8,128)S(1)}, u32[]{:S(2)}, u32[]{:S(2)}) %collective-permute-start.33) | collective-permute-done | bytes 696352 | tf_op jit(solution)/shard_map/ppermute | solution.py:558
  258.0 14.4 %collective-permute-done.35 = f32[272,640]{1,0:T(8,128)S(1)} collective-permute-done((f32[272,640]{1,0:T(8,128)S(1)}, f32[272,640]{1,0:T(8,128)S(1)}, u32[]{:S(2)}, u32[]{:S(2)}) %collective-permute-start.35) | collective-permute-done | bytes 696352 | tf_op jit(solution)/shard_map/ppermute | solution.py:558
  272.8 2.9 collective-permute-start.38
  275.8 1.5 collective-permute-start.40
  278.9 1.7 fusion.5
  281.2 6.3 %collective-permute-done.38 = f32[80,640]{1,0:T(8,128)S(1)} collective-permute-done((f32[80,640]{1,0:T(8,128)S(1)}, f32[80,640]{1,0:T(8,128)S(1)}, u32[]{:S(2)}, u32[]{:S(2)}) %collective-permute-start.38) | collective-permute-done | bytes 204832 | tf_op jit(solution)/shard_map/ppermute | solution.py:550
  287.4 3.2 %collective-permute-done.40 = f32[80,640]{1,0:T(8,128)S(1)} collective-permute-done((f32[80,640]{1,0:T(8,128)S(1)}, f32[80,640]{1,0:T(8,128)S(1)}, u32[]{:S(2)}, u32[]{:S(2)}) %collective-permute-start.40) | collective-permute-done | bytes 204832 | tf_op jit(solution)/shard_map/ppermute | solution.py:550
  300.5 1.5 maximum_select_fusion.1
  302.0 3.3 %maximum_select_fusion = f32[1,512,1024]{2,1,0:T(8,128)} fusion(f32[1,256,1024]{2,1,0:T(8,128)} %bitcast.27, f32[1,256,1024]{2,1,0:T(8,128)S(1)} %bitcast.69, pred[]{:T(512)S(6)} %eq.6), kind=kLoop, calls=%fused_computation | loop fusion | flops 1572864 | bytes 4194305 | tf_op jit(solution)/shard_map/jit(_where)/select_n | solution.py:877
  (223 shorter events, 46.8 us)
Async XLA Ops:
  0.6 37.4 %copy-start = (bf16[256,1024]{1,0:T(8,128)(2,1)S(1)}, bf16[256,1024]{1,0:T(8,128)(2,1)}, u32[]{:S(2)}) copy-start(bf16[256,1024]{1,0:T(8,128)(2,1)} %param.31) | copy-start | bytes 1572868
  7.6 16.5 %collective-permute-start.2 = (bf16[256,896]{1,0:T(8,128)(2,1)}, bf16[256,896]{1,0:T(8,128)(2,1)}, u32[]{:S(2)}, u32[]{:S(2)}) collective-permute-start(bf16[256,896]{1,0:T(8,128)(2,1)} %concatenate.114.rest_0_), channel_id=1, source_target_pairs={{0,24},{8,16},{16,8},{24,0},{1,25},{9,17},{17,9},{25,1},{2,26},{10... | collective-permute-start | bytes 1376264 | tf_op jit(solution)/shard_map/ppermute | solution.py:558
  11.5 20.7 %collective-permute-start.1 = (bf16[256,896]{1,0:T(8,128)(2,1)}, bf16[256,896]{1,0:T(8,128)(2,1)}, u32[]{:S(2)}, u32[]{:S(2)}) collective-permute-start(bf16[256,896]{1,0:T(8,128)(2,1)} %concatenate.114.rest_0_), channel_id=1, source_target_pairs={{0,16},{8,24},{16,0},{24,8},{1,17},{9,25},{17,1},{25,9},{2,18},{10... | collective-permute-start | bytes 1376264 | tf_op jit(solution)/shard_map/ppermute | solution.py:558
  12.0 20.5 %collective-permute-start = (bf16[256,896]{1,0:T(8,128)(2,1)}, bf16[256,896]{1,0:T(8,128)(2,1)}, u32[]{:S(2)}, u32[]{:S(2)}) collective-permute-start(bf16[256,896]{1,0:T(8,128)(2,1)} %concatenate.114.rest_0_), channel_id=1, source_target_pairs={{0,8},{8,0},{16,24},{24,16},{1,9},{9,1},{17,25},{25,17},{2,10},{10... | collective-permute-start | bytes 1376264 | tf_op jit(solution)/shard_map/ppermute | solution.py:558
  12.3 20.2 %collective-permute-start.3 = (bf16[256,1024]{1,0:T(8,128)(2,1)S(1)}, bf16[256,1024]{1,0:T(8,128)(2,1)}, u32[]{:S(2)}, u32[]{:S(2)}) collective-permute-start(bf16[256,1024]{1,0:T(8,128)(2,1)S(1)} %get-tuple-element.245), channel_id=1, source_target_pairs={{0,2},{2,0},{4,6},{6,4},{1,3},{3,1},{5,7},{7,5},{8,10},{10,8},{12,... | collective-permute-start | bytes 1572872 | tf_op jit(solution)/shard_map/ppermute | solution.py:550
  14.3 23.0 %collective-permute-start.6 = (bf16[16,1024]{1,0:T(8,128)(2,1)S(1)}, bf16[16,1024]{1,0:T(8,128)(2,1)S(1)}, u32[]{:S(2)}, u32[]{:S(2)}) collective-permute-start(bf16[16,1024]{1,0:T(8,128)(2,1)S(1)} %slice_bitcast_fusion.2), channel_id=1, source_target_pairs={{0,4},{2,6},{1,5},{3,7},{8,12},{10,14},{9,13},{11,15},{16,20},{18,... | collective-permute-start | bytes 98312 | tf_op jit(solution)/shard_map/ppermute | solution.py:553
  24.1 13.2 %collective-permute-start.5 = (bf16[16,1024]{1,0:T(8,128)(2,1)S(1)}, bf16[16,1024]{1,0:T(8,128)(2,1)S(1)}, u32[]{:S(2)}, u32[]{:S(2)}) collective-permute-start(bf16[16,1024]{1,0:T(8,128)(2,1)S(1)} %slice_bitcast_fusion.2), channel_id=1, source_target_pairs={{0,2},{2,4},{4,6},{1,3},{3,5},{5,7},{8,10},{10,12},{12,14},{9,11},... | collective-permute-start | bytes 98312 | tf_op jit(solution)/shard_map/ppermute | solution.py:553
  33.3 24.4 %collective-permute-start.7 = (bf16[256,1024]{1,0:T(8,128)(2,1)}, bf16[256,1024]{1,0:T(8,128)(2,1)}, u32[]{:S(2)}, u32[]{:S(2)}) collective-permute-start(bf16[256,1024]{1,0:T(8,128)(2,1)} %constant_dynamic-slice_fusion.13), channel_id=1, source_target_pairs={{0,2},{2,0},{4,6},{6,4},{1,3},{3,1},{5,7},{7,5},{8,10},{10,8},{12,... | collective-permute-start | bytes 1572872 | tf_op jit(solution)/shard_map/ppermute | solution.py:550
  34.8 6.8 %collective-permute-start.4 = (bf16[256,1024]{1,0:T(8,128)(2,1)}, bf16[256,1024]{1,0:T(8,128)(2,1)S(1)}, u32[]{:S(2)}, u32[]{:S(2)}) collective-permute-start(bf16[256,1024]{1,0:T(8,128)(2,1)} %collective-permute-done.3.near), channel_id=1, source_target_pairs={{0,1},{1,0},{2,3},{3,2},{4,5},{5,4},{6,7},{7,6},{8,9},{9,8},{10,11... | collective-permute-start | bytes 1572872 | tf_op jit(solution)/shard_map/ppermute | solution.py:547
  38.1 33.5 %copy-start.2 = (bf16[256,1024]{1,0:T(8,128)(2,1)}, bf16[256,1024]{1,0:T(8,128)(2,1)S(1)}, u32[]{:S(2)}) copy-start(bf16[256,1024]{1,0:T(8,128)(2,1)S(1)} %pad_maximum_fusion.rest_0_.rest_4_) | copy-start | bytes 1572868
  38.1 33.5 %collective-permute-start.11 = (bf16[256,1024]{1,0:T(8,128)(2,1)S(1)}, bf16[256,1024]{1,0:T(8,128)(2,1)S(1)}, u32[]{:S(2)}, u32[]{:S(2)}) collective-permute-start(bf16[256,1024]{1,0:T(8,128)(2,1)S(1)} %pad_maximum_fusion.rest_0_.rest_4_), channel_id=1, source_target_pairs={{0,24},{8,16},{16,8},{24,0},{1,25},{9,17},{17,9},{25,1},{2,26},{10... | collective-permute-start | bytes 1572872 | tf_op jit(solution)/shard_map/ppermute | solution.py:558
  39.9 31.7 %collective-permute-start.10 = (bf16[256,1024]{1,0:T(8,128)(2,1)S(1)}, bf16[256,1024]{1,0:T(8,128)(2,1)S(1)}, u32[]{:S(2)}, u32[]{:S(2)}) collective-permute-start(bf16[256,1024]{1,0:T(8,128)(2,1)S(1)} %pad_maximum_fusion.rest_0_.rest_4_), channel_id=1, source_target_pairs={{0,16},{8,24},{16,0},{24,8},{1,17},{9,25},{17,1},{25,9},{2,18},{10... | collective-permute-start | bytes 1572872 | tf_op jit(solution)/shard_map/ppermute | solution.py:558
  41.2 30.5 %collective-permute-start.9 = (bf16[256,1024]{1,0:T(8,128)(2,1)S(1)}, bf16[256,1024]{1,0:T(8,128)(2,1)S(1)}, u32[]{:S(2)}, u32[]{:S(2)}) collective-permute-start(bf16[256,1024]{1,0:T(8,128)(2,1)S(1)} %pad_maximum_fusion.rest_0_.rest_4_), channel_id=1, source_target_pairs={{0,8},{8,0},{16,24},{24,16},{1,9},{9,1},{17,25},{25,17},{2,10},{10... | collective-permute-start | bytes 1572872 | tf_op jit(solution)/shard_map/ppermute | solution.py:558
  57.8 13.9 %collective-permute-start.8 = (bf16[256,1024]{1,0:T(8,128)(2,1)}, bf16[256,1024]{1,0:T(8,128)(2,1)}, u32[]{:S(2)}, u32[]{:S(2)}) collective-permute-start(bf16[256,1024]{1,0:T(8,128)(2,1)} %collective-permute-done.7.near), channel_id=1, source_target_pairs={{0,1},{1,0},{2,3},{3,2},{4,5},{5,4},{6,7},{7,6},{8,9},{9,8},{10,11... | collective-permute-start | bytes 1572872 | tf_op jit(solution)/shard_map/ppermute | solution.py:547
  57.8 23.4 %collective-permute-start.12 = (f32[128,512]{1,0:T(8,128)}, f32[128,512]{1,0:T(8,128)S(1)}, u32[]{:S(2)}, u32[]{:S(2)}) collective-permute-start(f32[128,512]{1,0:T(8,128)} %get-tuple-element.126), channel_id=1, source_target_pairs={{0,4},{2,6},{1,5},{3,7},{8,12},{10,14},{9,13},{11,15},{16,20},{18,... | collective-permute-start | bytes 786440 | tf_op jit(solution)/shard_map/ppermute | solution.py:553
  90.4 1.5 collective-permute-start.13
  92.7 4.3 %collective-permute-start.14 = (f32[16,1024]{1,0:T(8,128)S(1)}, f32[16,1024]{1,0:T(8,128)S(1)}, u32[]{:S(2)}, u32[]{:S(2)}) collective-permute-start(f32[16,1024]{1,0:T(8,128)S(1)} %add.204.sums), channel_id=1, source_target_pairs={{0,2},{2,0},{4,6},{6,4},{1,3},{3,1},{5,7},{7,5},{8,10},{10,8},{12,... | collective-permute-start | bytes 196616 | tf_op jit(solution)/shard_map/ppermute | solution.py:550
  107.9 24.7 %collective-permute-start.18 = (f32[128,512]{1,0:T(8,128)}, f32[128,512]{1,0:T(8,128)S(1)}, u32[]{:S(2)}, u32[]{:S(2)}) collective-permute-start(f32[128,512]{1,0:T(8,128)} %get-tuple-element.146), channel_id=1, source_target_pairs={{4,0},{6,2},{5,1},{7,3},{12,8},{14,10},{13,9},{15,11},{20,16},{22,... | collective-permute-start | bytes 786440 | tf_op jit(solution)/shard_map/ppermute | solution.py:553
  117.8 39.2 %collective-permute-start.15 = (f32[256,1024]{1,0:T(8,128)}, f32[256,1024]{1,0:T(8,128)S(1)}, u32[]{:S(2)}, u32[]{:S(2)}) collective-permute-start(f32[256,1024]{1,0:T(8,128)} %get-tuple-element.137), channel_id=1, source_target_pairs={{0,8},{8,0},{16,24},{24,16},{1,9},{9,1},{17,25},{25,17},{2,10},{10... | collective-permute-start | bytes 3145736 | tf_op jit(solution)/shard_map/ppermute | solution.py:558
  119.3 46.6 %collective-permute-start.16 = (f32[256,1024]{1,0:T(8,128)}, f32[256,1024]{1,0:T(8,128)}, u32[]{:S(2)}, u32[]{:S(2)}) collective-permute-start(f32[256,1024]{1,0:T(8,128)} %get-tuple-element.138), channel_id=1, source_target_pairs={{0,16},{8,24},{16,0},{24,8},{1,17},{9,25},{17,1},{25,9},{2,18},{10... | collective-permute-start | bytes 3145736 | tf_op jit(solution)/shard_map/ppermute | solution.py:558
  120.1 45.9 %collective-permute-start.17 = (f32[256,1024]{1,0:T(8,128)}, f32[256,1024]{1,0:T(8,128)}, u32[]{:S(2)}, u32[]{:S(2)}) collective-permute-start(f32[256,1024]{1,0:T(8,128)} %get-tuple-element.139), channel_id=1, source_target_pairs={{0,24},{8,16},{16,8},{24,0},{1,25},{9,17},{17,9},{25,1},{2,26},{10... | collective-permute-start | bytes 3145736 | tf_op jit(solution)/shard_map/ppermute | solution.py:558
  149.7 2.2 collective-permute-start.19
  149.9 7.0 %collective-permute-start.21 = (f32[8,512]{1,0:T(8,128)}, f32[8,512]{1,0:T(8,128)S(1)}, u32[]{:S(2)}, u32[]{:S(2)}) collective-permute-start(f32[8,512]{1,0:T(8,128)} %get-tuple-element.156), channel_id=1, source_target_pairs={{4,0},{6,2},{5,1},{7,3},{12,8},{14,10},{13,9},{15,11},{20,16},{22,... | collective-permute-start | bytes 49160 | tf_op jit(solution)/shard_map/ppermute | solution.py:553
  153.1 20.5 %collective-permute-start.22 = (f32[512,128]{1,0:T(8,128)S(1)}, f32[512,128]{1,0:T(8,128)}, u32[]{:S(2)}, u32[]{:S(2)}) collective-permute-start(f32[512,128]{1,0:T(8,128)S(1)} %constant_dynamic-slice_fusion.11), channel_id=1, source_target_pairs={{0,2},{2,0},{4,6},{6,4},{1,3},{3,1},{5,7},{7,5},{8,10},{10,8},{12,... | collective-permute-start | bytes 786440 | tf_op jit(solution)/shard_map/ppermute | solution.py:550
  172.9 7.4 %collective-permute-start.24 = (f32[256,1024]{1,0:T(8,128)}, f32[256,1024]{1,0:T(8,128)S(1)}, u32[]{:S(2)}, u32[]{:S(2)}) collective-permute-start(f32[256,1024]{1,0:T(8,128)} %get-tuple-element.159), channel_id=1, source_target_pairs={{0,1},{1,0},{2,3},{3,2},{4,5},{5,4},{6,7},{7,6},{8,9},{9,8},{10,11... | collective-permute-start | bytes 3145736 | tf_op jit(solution)/shard_map/ppermute | solution.py:547
  174.5 2.5 collective-permute-start.23
  177.9 6.4 %collective-permute-start.25 = (f32[8,128]{1,0:T(8,128)S(1)}, f32[8,128]{1,0:T(8,128)S(1)}, u32[]{:S(2)}, u32[]{:S(2)}) collective-permute-start(f32[8,128]{1,0:T(8,128)S(1)} %fusion.16), channel_id=1, source_target_pairs={{4,0},{6,2},{5,1},{7,3},{12,8},{14,10},{13,9},{15,11},{20,16},{22,... | collective-permute-start | bytes 12296 | tf_op jit(solution)/shard_map/ppermute | solution.py:553
  196.4 15.6 %collective-permute-start.26 = (f32[256,1024]{1,0:T(8,128)}, f32[256,1024]{1,0:T(8,128)}, u32[]{:S(2)}, u32[]{:S(2)}) collective-permute-start(f32[256,1024]{1,0:T(8,128)} %get-tuple-element.176), channel_id=1, source_target_pairs={{0,1},{1,0},{2,3},{3,2},{4,5},{5,4},{6,7},{7,6},{8,9},{9,8},{10,11... | collective-permute-start | bytes 3145736 | tf_op jit(solution)/shard_map/ppermute | solution.py:547
  196.5 42.5 %collective-permute-start.30 = (f32[256,1024]{1,0:T(8,128)S(1)}, f32[256,1024]{1,0:T(8,128)}, u32[]{:S(2)}, u32[]{:S(2)}) collective-permute-start(f32[256,1024]{1,0:T(8,128)S(1)} %add.213), channel_id=1, source_target_pairs={{0,2},{2,0},{4,6},{6,4},{1,3},{3,1},{5,7},{7,5},{8,10},{10,8},{12,... | collective-permute-start | bytes 3145736 | tf_op jit(solution)/shard_map/ppermute | solution.py:550
  197.3 41.8 %collective-permute-start.27 = (f32[64,1024]{1,0:T(8,128)}, f32[64,1024]{1,0:T(8,128)}, u32[]{:S(2)}, u32[]{:S(2)}) collective-permute-start(f32[64,1024]{1,0:T(8,128)} %get-tuple-element.177), channel_id=1, source_target_pairs={{0,2},{2,0},{4,6},{6,4},{1,3},{3,1},{5,7},{7,5},{8,10},{10,8},{12,... | collective-permute-start | bytes 786440 | tf_op jit(solution)/shard_map/ppermute | solution.py:550
  198.6 40.4 %collective-permute-start.28 = (f32[64,1024]{1,0:T(8,128)S(1)}, f32[64,1024]{1,0:T(8,128)}, u32[]{:S(2)}, u32[]{:S(2)}) collective-permute-start(f32[64,1024]{1,0:T(8,128)S(1)} %copy-done.22), channel_id=1, source_target_pairs={{0,4},{2,6},{4,0},{6,2},{1,5},{3,7},{5,1},{7,3},{8,12},{10,14},{12... | collective-permute-start | bytes 786440 | tf_op jit(solution)/shard_map/ppermute | solution.py:550
  198.6 40.4 %collective-permute-start.29 = (f32[64,1024]{1,0:T(8,128)S(1)}, f32[64,1024]{1,0:T(8,128)}, u32[]{:S(2)}, u32[]{:S(2)}) collective-permute-start(f32[64,1024]{1,0:T(8,128)S(1)} %get-tuple-element.179), channel_id=1, source_target_pairs={{0,6},{2,4},{4,2},{6,0},{1,7},{3,5},{5,3},{7,1},{8,14},{10,12},{12... | collective-permute-start | bytes 786440 | tf_op jit(solution)/shard_map/ppermute | solution.py:550
  212.0 29.3 %copy-start.33 = (f32[272,640]{1,0:T(8,128)S(1)}, f32[272,640]{1,0:T(8,128)}, u32[]{:S(2)}) copy-start(f32[272,640]{1,0:T(8,128)} %get-tuple-element.186) | copy-start | bytes 2088964
  213.6 44.2 %copy-start.31 = (f32[256,1024]{1,0:T(8,128)S(1)}, f32[256,1024]{1,0:T(8,128)}, u32[]{:S(2)}) copy-start(f32[256,1024]{1,0:T(8,128)} %get-tuple-element.153) | copy-start | bytes 3145732
  213.6 58.9 %copy-start.17 = (f32[272,640]{1,0:T(8,128)S(1)}, f32[272,640]{1,0:T(8,128)}, u32[]{:S(2)}) copy-start(f32[272,640]{1,0:T(8,128)} %get-tuple-element.189) | copy-start | bytes 2088964
  239.1 33.4 %collective-permute-start.36 = (f32[256,1024]{1,0:T(8,128)S(1)}, f32[256,1024]{1,0:T(8,128)S(1)}, u32[]{:S(2)}, u32[]{:S(2)}) collective-permute-start(f32[256,1024]{1,0:T(8,128)S(1)} %add.225), channel_id=1, source_target_pairs={{0,2},{2,0},{4,6},{6,4},{1,3},{3,1},{5,7},{7,5},{8,10},{10,8},{12,... | collective-permute-start | bytes 3145736 | tf_op jit(solution)/shard_map/ppermute | solution.py:550
  239.2 38.1 %collective-permute-start.32 = (f32[256,1024]{1,0:T(8,128)S(1)}, f32[256,1024]{1,0:T(8,128)S(1)}, u32[]{:S(2)}, u32[]{:S(2)}) collective-permute-start(f32[256,1024]{1,0:T(8,128)S(1)} %copy-done.32), channel_id=1, source_target_pairs={{0,1},{1,0},{2,3},{3,2},{4,5},{5,4},{6,7},{7,6},{8,9},{9,8},{10,11... | collective-permute-start | bytes 3145736 | tf_op jit(solution)/shard_map/ppermute | solution.py:547
  239.3 18.5 %collective-permute-start.33 = (f32[272,640]{1,0:T(8,128)S(1)}, f32[272,640]{1,0:T(8,128)S(1)}, u32[]{:S(2)}, u32[]{:S(2)}) collective-permute-start(f32[272,640]{1,0:T(8,128)S(1)} %copy-done.35), channel_id=1, source_target_pairs={{0,8},{8,0},{16,24},{24,16},{1,9},{9,1},{17,25},{25,17},{2,10},{10... | collective-permute-start | bytes 2088968 | tf_op jit(solution)/shard_map/ppermute | solution.py:558
  239.9 18.1 %collective-permute-start.34 = (f32[272,640]{1,0:T(8,128)S(1)}, f32[272,640]{1,0:T(8,128)S(1)}, u32[]{:S(2)}, u32[]{:S(2)}) collective-permute-start(f32[272,640]{1,0:T(8,128)S(1)} %copy-done.34), channel_id=1, source_target_pairs={{0,16},{8,24},{16,0},{24,8},{1,17},{9,25},{17,1},{25,9},{2,18},{10... | collective-permute-start | bytes 2088968 | tf_op jit(solution)/shard_map/ppermute | solution.py:558
  241.3 31.2 %collective-permute-start.35 = (f32[272,640]{1,0:T(8,128)S(1)}, f32[272,640]{1,0:T(8,128)S(1)}, u32[]{:S(2)}, u32[]{:S(2)}) collective-permute-start(f32[272,640]{1,0:T(8,128)S(1)} %copy-done.33), channel_id=1, source_target_pairs={{0,24},{8,16},{16,8},{24,0},{1,25},{9,17},{17,9},{25,1},{2,26},{10... | collective-permute-start | bytes 2088968 | tf_op jit(solution)/shard_map/ppermute | solution.py:558
  257.7 20.0 %collective-permute-start.20 = (f32[256,1024]{1,0:T(8,128)S(1)}, f32[256,1024]{1,0:T(8,128)S(1)}, u32[]{:S(2)}, u32[]{:S(2)}) collective-permute-start(f32[256,1024]{1,0:T(8,128)S(1)} %copy-done.31), channel_id=1, source_target_pairs={{0,1},{1,0},{2,3},{3,2},{4,5},{5,4},{6,7},{7,6},{8,9},{9,8},{10,11... | collective-permute-start | bytes 3145736 | tf_op jit(solution)/shard_map/ppermute | solution.py:547
  272.8 14.6 %collective-permute-start.38 = (f32[80,640]{1,0:T(8,128)S(1)}, f32[80,640]{1,0:T(8,128)S(1)}, u32[]{:S(2)}, u32[]{:S(2)}) collective-permute-start(f32[80,640]{1,0:T(8,128)S(1)} %get-tuple-element.275), channel_id=1, source_target_pairs={{0,4},{2,6},{4,0},{6,2},{1,5},{3,7},{5,1},{7,3},{8,12},{10,14},{12... | collective-permute-start | bytes 614408 | tf_op jit(solution)/shard_map/ppermute | solution.py:550
  275.8 11.7 %collective-permute-start.39 = (f32[80,640]{1,0:T(8,128)S(1)}, f32[80,640]{1,0:T(8,128)S(1)}, u32[]{:S(2)}, u32[]{:S(2)}) collective-permute-start(f32[80,640]{1,0:T(8,128)S(1)} %get-tuple-element.276), channel_id=1, source_target_pairs={{0,2},{2,0},{4,6},{6,4},{1,3},{3,1},{5,7},{7,5},{8,10},{10,8},{12,... | collective-permute-start | bytes 614408 | tf_op jit(solution)/shard_map/ppermute | solution.py:550
  275.8 14.8 %collective-permute-start.40 = (f32[80,640]{1,0:T(8,128)S(1)}, f32[80,640]{1,0:T(8,128)S(1)}, u32[]{:S(2)}, u32[]{:S(2)}) collective-permute-start(f32[80,640]{1,0:T(8,128)S(1)} %get-tuple-element.277), channel_id=1, source_target_pairs={{0,6},{2,4},{4,2},{6,0},{1,7},{3,5},{5,3},{7,1},{8,14},{10,12},{12... | collective-permute-start | bytes 614408 | tf_op jit(solution)/shard_map/ppermute | solution.py:550
  280.6 19.9 %collective-permute-start.31 = (bf16[256,1024]{1,0:T(8,128)(2,1)S(1)}, bf16[256,1024]{1,0:T(8,128)(2,1)S(1)}, u32[]{:S(2)}, u32[]{:S(2)}) collective-permute-start(bf16[256,1024]{1,0:T(8,128)(2,1)S(1)} %get-tuple-element.261), channel_id=1, source_target_pairs={{0,1},{1,0},{2,3},{3,2},{4,5},{5,4},{6,7},{7,6},{8,9},{9,8},{10,11... | collective-permute-start | bytes 1572872 | tf_op jit(solution)/shard_map/ppermute | solution.py:547
  280.7 21.3 %collective-permute-start.37 = (f32[256,1024]{1,0:T(8,128)S(1)}, f32[256,1024]{1,0:T(8,128)}, u32[]{:S(2)}, u32[]{:S(2)}) collective-permute-start(f32[256,1024]{1,0:T(8,128)S(1)} %get-tuple-element.260), channel_id=1, source_target_pairs={{0,1},{1,0},{2,3},{3,2},{4,5},{5,4},{6,7},{7,6},{8,9},{9,8},{10,11... | collective-permute-start | bytes 3145736 | tf_op jit(solution)/shard_map/ppermute | solution.py:547
  292.4 5.6 %collective-permute-start.41 = (f32[1024]{0:T(1024)S(1)}, f32[1024]{0:T(1024)S(1)}, u32[]{:S(2)}, u32[]{:S(2)}) collective-permute-start(f32[1024]{0:T(1024)S(1)} %bitcast.79), channel_id=1, source_target_pairs={{0,1},{1,0},{2,3},{3,2},{4,5},{5,4},{6,7},{7,6},{8,9},{9,8},{10,11... | collective-permute-start | bytes 12296 | tf_op jit(solution)/shard_map/ppermute | solution.py:547
  292.5 6.1 %collective-permute-start.42 = (f32[2,64,64]{2,1,0:T(8,128)S(1)}, f32[2,64,64]{2,1,0:T(8,128)}, u32[]{:S(2)}, u32[]{:S(2)}) collective-permute-start(f32[2,64,64]{2,1,0:T(8,128)S(1)} %get-tuple-element.274), channel_id=1, source_target_pairs={{0,1},{1,0},{2,3},{3,2},{4,5},{5,4},{6,7},{7,6},{8,9},{9,8},{10,11... | collective-permute-start | bytes 98312 | tf_op jit(solution)/shard_map/ppermute | solution.py:547
  (32 other events, 320.4 us)

commit v3 on v2

--- a/solution.py
+++ b/solution.py
@@ -14,6 +14,7 @@
 HIGHEST = lax.Precision.HIGHEST
 F32 = jnp.float32
 BF16 = jnp.bfloat16
+F16 = jnp.float16
 NN = (((1,), (0,)), ((), ()))
 NT = (((1,), (1,)), ((), ()))
 TN = (((0,), (0,)), ((), ()))
@@ -25,7 +26,7 @@
     return lax.dot_general(a, b, dims, precision=precision, preferred_element_type=F32)
 
 
-def grid_call(body, grid, in_specs, out_specs, out_shape, scratch=(), name=None):
+def grid_call(body, grid, in_specs, out_specs, out_shape, scratch=(), name=None, limit=None):
     return pl.pallas_call(
         body,
         grid_spec=pltpu.PrefetchScalarGridSpec(
@@ -36,12 +37,17 @@
             scratch_shapes=list(scratch),
         ),
         out_shape=out_shape,
-        compiler_params=pltpu.CompilerParams(dimension_semantics=("arbitrary",) * len(grid)
+        compiler_params=pltpu.CompilerParams(
+            dimension_semantics=("arbitrary",) * len(grid), vmem_limit_bytes=limit
         ),
         name=name,
     )
 
 
+def streamed(*arrays):
+    return [pltpu.with_memory_space_constraint(array, pltpu.HBM) for array in arrays]
+
+
 def rows_spec(width, rows=BLOCK, lane=0):
     return pl.BlockSpec((rows, width), lambda b, s: (b, lane))
 
@@ -52,6 +58,10 @@
 
 def shaped(shape, dtype=F32):
     return jax.ShapeDtypeStruct(shape, dtype)
+
+
+def kept(shape, dtype=F32):
+    return pltpu.HBM(shape, dtype)
 
 
 def slope(v, sig):
@@ -271,14 +281,14 @@
     sum_ref[8:16] = mm(ones, three(gg[...] * ggain[...] * product), NT)
 
 
-def turn_body(inner, states, total, s_ref, co, lx, y, gate, gg, sums, more, skip, ggain,
+def turn_body(inner, states, total, s_ref, co, lx, y, gate, gg, sums, sums1, sums2, sums3, skip, ggain,
               gated_ref, ggrad_ref, og_ref, gloc_ref, start_ref, cols_ref, chain):
     step = pl.program_id(0)
     conv = co[...]
     act = conv * jax.nn.sigmoid(conv)
     x = act[:, :inner]
     readout_t = act[:, inner + states :].T
-    both = (sums[...] + more[...]).T
+    both = (sums[...] + sums1[...] + sums2[...] + sums3[...]).T
     ginv = lax.rsqrt(both[:, 0:1] / total + EPSILON)
     dot = ginv * both[:, 8:9] / total
     g = gate[...]
@@ -361,28 +371,15 @@
     return pre
 
 
-def join_body(inner, states, s_ref, co, delta, lx, dx, draw, og, y, z, dbc, hloc, pre, gloc, gin, hin, u, prior,
-              uh, taps, rate, skip, mg_ref, tail_ref, head_ref, keep_ref, give_ref, rg_ref, cols_ref, sig_ref,
-              col_sc, csc, usc):
-    step = pl.program_id(0)
+def meet_body(inner, states, s_ref, co, lx, dx, z, dbc, hloc, pre, gloc, gin, hin, zed_ref, ends_ref, keep_ref,
+              give_ref):
     subs = BLOCK // SUB
     count = pl.num_programs(0)
-    b = count - 1 - step
-
-    @pl.when(step == 0)
-    def _():
-        cols_ref[...] = jnp.zeros_like(cols_ref)
-        sig_ref[...] = jnp.zeros_like(sig_ref)
-        col_sc[...] = collector(inner)
-        csc[BLOCK : BLOCK + 8] = jnp.zeros((8, inner), F32)
-
+    b = pl.program_id(0)
     conv = co[...]
-    sig = jax.nn.sigmoid(conv)
-    act = conv * sig
-    x = act[:, :inner]
-    delta_x = dx[...]
+    act = conv * jax.nn.sigmoid(conv)
+    source = dx[...] * act[:, :inner]
     ends = []
-    zeds = []
     inject_grads = []
     for i in range(subs):
         at = slice(i * SUB, (i + 1) * SUB)
@@ -390,11 +387,10 @@
         level_x = lx[at]
         later = gloc[n] + jnp.exp(pre[subs * count][0:1] - pre[n][0:1]) * gin[...]
         fade = jnp.exp(level_x[SUB - 1 : SUB] - level_x)
-        zeds.append(z[at] + fade * mm(act[at, inner : inner + states], later, precision=HIGH))
-        inject_grads.append(dbc[at, :states] + mm(fade * delta_x[at] * x[at], later, NT, HIGH))
-        held = entering(hloc[n], pre[n], hin[...])
-        ends.append(jnp.sum(later * held, axis=0, keepdims=True))
-    zed = jnp.concatenate(zeds, axis=0)
+        zed_ref[at] = z[at] + fade * mm(act[at, inner : inner + states], later, precision=HIGH)
+        inject_grads.append(dbc[at, :states] + mm(fade * source[at], later, NT, HIGH))
+        ends.append(jnp.sum(later * entering(hloc[n], pre[n], hin[...]), axis=0, keepdims=True))
+    ends_ref[...] = jnp.concatenate(ends + [jnp.zeros((8 - subs, inner), F32)], axis=0)
     inject_grad = jnp.concatenate(inject_grads, axis=0)
     half = count // 2
     rows = pl.ds(pl.multiple_of((b % half) * BLOCK, BLOCK), BLOCK)
@@ -409,8 +405,28 @@
         give_ref[rows, :states] = inject_grad
         give_ref[rows, states:] = dbc[:, states:]
 
+
+def join_body(inner, s_ref, co, delta, dx, draw, og, y, zed_in, ends_in, u, prior, uh, taps, rate, skip, mg_ref,
+              tail_ref, head_ref, rg_ref, cols_ref, sig_ref, col_sc, csc, usc):
+    step = pl.program_id(0)
+    subs = BLOCK // SUB
+    count = pl.num_programs(0)
+    b = count - 1 - step
+
+    @pl.when(step == 0)
+    def _():
+        cols_ref[...] = jnp.zeros_like(cols_ref)
+        sig_ref[...] = jnp.zeros_like(sig_ref)
+        col_sc[...] = collector(inner)
+        csc[BLOCK : BLOCK + 8] = jnp.zeros((8, inner), F32)
+
+    conv = co[...]
+    sig = jax.nn.sigmoid(conv)
+    x = conv * sig
+    delta_x = dx[...]
+    zed = zed_in[...]
+    ends = ends_in[...]
     g = og[...]
-    ends = jnp.concatenate(ends + [jnp.zeros((8 - subs, inner), F32)], axis=0)
     sums = mm(three(jnp.concatenate([x * zed, g * y[...], ends], axis=0)), col_sc[...])
     direct, read, ends = sums[:BLOCK], sums[BLOCK : 2 * BLOCK], sums[2 * BLOCK :]
     dlt = delta[...]
@@ -424,7 +440,7 @@
 
     usc[0:8] = jnp.where(b == 0, uh[...], prior[...])
     usc[8 : 8 + BLOCK] = u[...]
-    grad = (delta_x * zed + skip[...] * g) * slope(conv[:, :inner], sig[:, :inner])
+    grad = (delta_x * zed + skip[...] * g) * slope(conv, sig)
     pre_grad = conv_back(grad, csc, usc, taps, sig_ref)
     mg_ref[...] = pre_grad.astype(BF16)
     head_ref[...] = grad[0:8]
@@ -434,32 +450,55 @@
         tail_ref[...] = pre_grad[BLOCK - 8 :]
 
 
-def early_body(parts, s_ref, left1, right1, left2, right2, *outs):
+def exponents(peak):
+    return jnp.clip(jnp.ceil(jnp.log(jnp.maximum(peak, 1e-36)) * 1.4426950408889634) - 14.0, -100.0, 100.0)
+
+
+def packed(value, power, inverse, riders=()):
+    rows = [(value * inverse).astype(F16), jnp.broadcast_to(power, (16, value.shape[1])).astype(F16)]
+    for more in riders:
+        each = exponents(jnp.abs(more))
+        rows += [(more * jnp.exp2(-each)).astype(F16), each.astype(F16)]
+    return jnp.concatenate(rows)
+
+
+def unpacked(sent, counts=()):
+    rows = sent.shape[0] - 16 - 2 * sum(counts)
+    power = sent[rows : rows + 1].astype(F32)
+    more = []
+    at = rows + 16
+    for size in counts:
+        more.append(sent[at : at + size].astype(F32) * jnp.exp2(sent[at + size : at + 2 * size].astype(F32)))
+        at += 2 * size
+    return sent[:rows].astype(F32) * jnp.exp2(power), power, more
+
+
+def grads_body(parts, pairs, s_ref, *refs):
+    inputs = 1 + max(max(pair) for pair in pairs)
+    outs, scale, peak = refs[inputs : inputs + parts], refs[inputs + parts], refs[inputs + parts + 1]
     j = pl.program_id(0)
-    width = right1.shape[1]
-    first = mm(left1[...], right1[...], TN)
-    second = mm(left2[...], right2[...], TN)
-    for k in range(parts):
-
-        @pl.when(j == k)
-        def _():
-            outs[k][:, :width] = first
-            outs[k][:, width:] = second
-
-
-def late_body(parts, s_ref, left, right1, right2, small, *outs):
-    j = pl.program_id(0)
-    width = right1.shape[1]
-    rows = left.shape[1]
-    first = mm(left[...], right1[...], TN)
-    second = mm(left[...], right2[...], TN)
-    for k in range(parts):
-
-        @pl.when(j == k)
-        def _():
-            outs[k][:rows, :width] = first
-            outs[k][:rows, width:] = second
-            outs[k][rows:] = small[...]
+
+    @pl.when(j == 0)
+    def _():
+        peak[...] = jnp.zeros_like(peak)
+
+    at = 0
+    for left, right in pairs:
+        value = mm(refs[left][...], refs[right][...], TN)
+        lanes = slice(at, at + value.shape[1])
+        at += value.shape[1]
+        peak[0:1, lanes] = jnp.maximum(peak[0:1, lanes], jnp.max(jnp.abs(value), axis=0, keepdims=True))
+        for k in range(parts):
+
+            @pl.when(j == k)
+            def _():
+                outs[k][:, lanes] = value
+
+    @pl.when(j == parts - 1)
+    def _():
+        power = exponents(peak[...])
+        scale[0:8] = jnp.broadcast_to(power[0:1], (8, at))
+        scale[8:16] = jnp.broadcast_to(jnp.exp2(-power[0:1]), (8, at))
 
 
 def deal(s_ref, b, quarter, value, outs):
@@ -587,51 +626,43 @@
     halfway = steps // 2
     near = across(piece(hidden, core, halfway), 1)
     far = swap(near)
-    edge, _ = lax.optimization_barrier((hidden[steps - 16 :], first))
-    halo = jnp.where(lo == 0, along(edge, 1), along(edge, 2))
     ws1 = gathered(first)
-    ws1, near, main_gate, out_later, cot_later = lax.optimization_barrier(
-        (ws1, near, main_part[:, 0], proj_out, cotangent)
-    )
-    second = jnp.concatenate([main_gate, mine(out_later, 1, inner)], axis=1)
-    cot_near = across(piece(cot_later, core, halfway), 1)
-    ws2 = gathered(second)
-
-    def over_sequences(pieces):
-        return [spread(pieces[j], j) for j in range(1, parts)]
-
-    def chunks(pieces, got, extra=0):
-        total = pieces[0]
-        rows = total.shape[0] - extra
+
+    def over_sequences(pieces, scale, riders=()):
+        return [spread(packed(pieces[j], scale[0:1], scale[8:9], riders), j) for j in range(1, parts)]
+
+    def chunks(pieces, scale, got, riders=()):
+        total, power = pieces[0], scale[0:1]
         if not apart:
-            shared = [lax.psum(total[rows:], "dp")] if extra else []
-            total = jnp.concatenate(
-                [lax.psum_scatter(total[:rows], "dp", scatter_dimension=0, tiled=True)] + shared
-            )
-            rows = total.shape[0] - extra
-        for part in got:
-            total = total + part
-        size = rows // ctxs
-
-        def chunk(j):
-            part = piece(total, z ^ j, size)
-            return jnp.concatenate([part, total[rows:]]) if extra else part
-
-        return [chunk(j) for j in range(ctxs)]
+            total = lax.psum_scatter(total, "dp", scatter_dimension=0, tiled=True)
+            power = exponents(jnp.max(jnp.abs(total), axis=0, keepdims=True))
+            riders = [lax.psum(value, "dp") for value in riders]
+        for sent in got:
+            value, other, more = unpacked(sent, [rider.shape[0] for rider in riders])
+            total, power = total + value, jnp.maximum(power, other)
+            riders = [one + two for one, two in zip(riders, more)]
+        power = power + (parts - 1).bit_length()
+        size = total.shape[0] // ctxs
+        rows = [piece(total, z ^ j, size) for j in range(ctxs)]
+        return rows[:1] + [packed(value, power, jnp.exp2(-power), riders) for value in rows[1:]], riders
 
     def over_positions(cut):
         return [across(cut[j], j) for j in range(1, ctxs)]
 
-    def settled(cut, got, extra=0):
-        own, opposite = cut[0], got[0]
+    def settled(own, got):
+        opposite = got[0]
         for j in range(2, ctxs):
             if j % 2 == 0:
                 own = own + got[j - 1]
             else:
                 opposite = opposite + got[j - 1]
-        size = own.shape[0] - extra
-        own, opposite = jnp.where(lo == 0, own, opposite), jnp.where(lo == 0, opposite, own)
-        return (own[:size], opposite[:size]), (own[size:], opposite[size:])
+        return jnp.where(lo == 0, own, opposite), jnp.where(lo == 0, opposite, own)
+
+    def decoded(got, counts=()):
+        return [unpacked(sent, counts)[0] for sent in got]
+
+    def ridden(got, counts):
+        return [unpacked(sent, counts)[2][0] for sent in got]
 
     taps_x = jnp.concatenate([mine(conv_main, 1, inner), conv_state], axis=1)
     bias_x = jnp.concatenate([mine(bias_main, 0, inner), bias_state])[None]
@@ -645,6 +676,22 @@
     skip_row = jnp.repeat(mine(skip_gain, 0, heads), inner // heads)[None]
     ggain_row = mine(gate_gain, 0, inner)[None]
     gain_row = norm_gain[None]
+    edge, scalars, taps_x, bias_x, rate_row, dbias_row, _ = lax.optimization_barrier(
+        (hidden[steps - 16 :], scalars, taps_x, bias_x, rate_row, dbias_row, first)
+    )
+    route = [
+        ((z0 - 1) * tps + c, (z0 + c) * tps + c) for z0 in range(2, ctxs, 2) for c in range(2)
+    ]
+    edge = lax.ppermute(edge, ("ctx", "tp"), route)
+    halo = jnp.where(core == lo, edge, swap(edge))
+
+    ws1, near, main_gate, out_later, cot_later = lax.optimization_barrier(
+        (ws1, near, main_part[:, 0], proj_out, cotangent)
+    )
+    second = jnp.concatenate([main_gate, mine(out_later, 1, inner)], axis=1)
+    ws2 = gathered(second)
+    cot_near = across(piece(cot_later, core, halfway), 1)
+
     own_spec = pl.BlockSpec(
         (BLOCK, model), lambda b, s: (jnp.clip(b - s[LO] * 2 * quarter, 0, 2 * quarter - 1), 0)
     )
@@ -687,7 +734,8 @@
         [rows_spec(inner)],
         [shaped((tokens, inner))],
         name="within",
-    )(scalars, conv, level, level_x, delta_x)
+        limit=20 << 20,
+    )(scalars, *streamed(conv, level, level_x, delta_x))
 
     gate, gated_grad, branch_grad = grid_call(
         functools.partial(gates_body, parts, quarter),
@@ -696,7 +744,8 @@
         [rows_spec(inner), rows_spec(inner), rows_spec(model)],
         [shaped((tokens, inner)), shaped((tokens, inner)), shaped((tokens, model), BF16)],
         name="gates",
-    )(scalars, normed, cotangent, cot_near, cot_far, *ws2)
+        limit=20 << 20,
+    )(scalars, *streamed(normed, cotangent, cot_near, cot_far, *ws2))
 
     y, sums = grid_call(
         functools.partial(output_body, inner, states),
@@ -706,10 +755,11 @@
         [rows_spec(inner), pl.BlockSpec((16, BLOCK), lambda b, s: (0, b))],
         [shaped((tokens, inner)), shaped((16, tokens))],
         name="output",
-    )(scalars, conv, level_x, inside, gate, gated_grad, hloc, pre, carried, skip_row, ggain_row)
-
-    sums = sums + swap(sums)
-    more_sums = across(sums, 1)
+        limit=20 << 20,
+    )(scalars, *streamed(conv, level_x), inside, gate, gated_grad, *streamed(hloc), pre, carried, skip_row, ggain_row)
+
+    corner = [(n, ((n // tps) ^ 1) * tps + (n % tps + 1) % tps) for n in range(ctxs * tps)]
+    all_sums = [sums, swap(sums), across(sums, 1), lax.ppermute(sums, ("ctx", "tp"), corner)]
 
     def back(width, rows=BLOCK):
         return pl.BlockSpec((rows, width), lambda b, s: (count - 1 - b, 0))
@@ -719,14 +769,15 @@
         functools.partial(turn_body, inner, states, 2 * tps * inner),
         (count,),
         [back(wide), back(inner), back(inner), back(inner), back(inner),
-         back_sums, back_sums, whole((1, inner)), whole((1, inner))],
+         back_sums, back_sums, back_sums, back_sums, whole((1, inner)), whole((1, inner))],
         [back(inner), back(inner), back(inner), whole((last + 1, states, inner)), whole((states, inner)),
          whole((8, inner))],
-        [shaped((tokens, inner), BF16), shaped((tokens, inner), BF16), shaped((tokens, inner)),
-         shaped((last + 1, states, inner)), shaped((states, inner)), shaped((8, inner))],
+        [kept((tokens, inner), BF16), kept((tokens, inner), BF16), kept((tokens, inner)),
+         kept((last + 1, states, inner)), shaped((states, inner)), shaped((8, inner))],
         [pltpu.VMEM((states, inner), F32)],
         name="turn",
-    )(scalars, conv, level_x, y, gate, gated_grad, sums, more_sums, skip_row, ggain_row)
+        limit=20 << 20,
+    )(scalars, *streamed(conv, level_x), y, gate, gated_grad, *all_sums, skip_row, ggain_row)
 
     returned = jnp.zeros_like(own_start)
     sending = own_start
@@ -736,17 +787,28 @@
             sending = own_start + growth * returned
 
     turned = pl.BlockSpec((tokens, shard), lambda j, s: (0, s[SLOT0 + j]))
-    early = grid_call(
-        functools.partial(early_body, parts),
-        (parts,),
-        [turned, whole((tokens, inner)), turned, whole((tokens, inner))],
-        [whole((shard, 2 * inner))] * parts,
-        [shaped((shard, 2 * inner))] * parts,
-        name="grad_early",
-    )(scalars, normed, gate_grad, branch_grad, gated)
-
+    dealt_specs = [whole((halfway, model))] * 4
+    dealt_shapes = [shaped((halfway, model))] * 4
+    def grads(lefts, rights, name):
+        sources = []
+        for left, right in zip(lefts, rights):
+            sources += [left, right]
+        width = sum(right.shape[1] for right in rights)
+        specs = [turned if n % 2 == 0 else whole(source.shape) for n, source in enumerate(sources)]
+        *pieces, scale = grid_call(
+            functools.partial(grads_body, parts, [(n, n + 1) for n in range(0, len(sources), 2)]),
+            (parts,),
+            specs,
+            [whole((shard, width))] * parts + [whole((16, width))],
+            [shaped((shard, width))] * parts + [shaped((16, width))],
+            [pltpu.VMEM((8, width), F32)],
+            name=name,
+        )(scalars, *sources)
+        return pieces, scale
+
+    early, early_scale = grads([normed, branch_grad], [gate_grad, gated], "grad_early")
+    early_got = over_sequences(early, early_scale)
     early, out_grad = lax.optimization_barrier((early, out_grad))
-    early_got = over_sequences(early)
 
     zed, dbc = grid_call(
         functools.partial(back_body, inner, states),
@@ -758,6 +820,23 @@
         name="back",
     )(scalars, conv, level, level_x, delta_x, out_grad, hloc, pre, carried)
 
+    gated_later, zed = lax.optimization_barrier((gated, zed))
+    branch = grid_call(
+        functools.partial(branch_body, parts, quarter),
+        (count,),
+        [rows_spec(inner)] + [whole((shard, 2 * inner))] * parts,
+        dealt_specs,
+        dealt_shapes,
+        [pltpu.VMEM((BLOCK, model), F32)],
+        name="branch",
+    )(scalars, gated_later, *ws2)
+
+    returned, early_got, branch = lax.optimization_barrier((returned, early_got, branch))
+    front_rows = halfway // 2
+    branch_give = swap(branch[3])
+    branch_theirs = [branch[1][:front_rows] + branch_give[:front_rows], branch[1][front_rows:] + branch_give[front_rows:]]
+    returned, branch_theirs = lax.optimization_barrier((returned, branch_theirs))
+    branch_back = [across(branch_theirs[0], 1)]
     all_states = whole((last + 1, states, inner))
     all_pre = whole((last + 1, 8, inner))
     per = BLOCK // 8
@@ -773,56 +852,55 @@
     def table(rows, width, lanes):
         return pl.BlockSpec((rows, width), lambda b, s: (0, lanes(s)))
 
-    signal_pre, tail, head, dbc_keep, dbc_give, raw_grad, head_cols, signal_cols = grid_call(
-        functools.partial(join_body, inner, states),
+    zed, ends, dbc_keep, dbc_give = grid_call(
+        functools.partial(meet_body, inner, states),
         (count,),
-        [back(wide), back(128), back(inner), back(inner), back(128), back(inner), back(inner), back(inner),
-         back(2 * states), all_states, all_pre, all_states, whole((states, inner)), whole((states, inner))]
+        [rows_spec(wide), rows_spec(inner), rows_spec(inner), rows_spec(inner), rows_spec(2 * states), all_states,
+         all_pre, all_states, whole((states, inner)), whole((states, inner))],
+        [rows_spec(inner), rows_spec(inner, 8), whole((half_rows, 2 * states)), whole((half_rows, 2 * states))],
+        [shaped((tokens, inner)), shaped((8 * count, inner)), shaped((half_rows, 2 * states)),
+         shaped((half_rows, 2 * states))],
+        name="meet",
+        limit=20 << 20,
+    )(scalars, *streamed(conv, level_x, delta_x, zed, dbc, hloc, pre, gloc), returned, carried)
+
+    zed, ends, dbc_keep, dbc_give, branch_back = lax.optimization_barrier((zed, ends, dbc_keep, dbc_give, branch_back))
+    early_cut, _ = chunks(early, early_scale, early_got)
+    early_far = over_positions(early_cut)
+    signal_pre, tail, head, raw_grad, head_cols, signal_cols = grid_call(
+        functools.partial(join_body, inner),
+        (count,),
+        [back(inner), back(128), back(inner), back(128), back(inner), back(inner), back(inner), back(inner, 8)]
         + back_lanes(inner, lambda s: 0)
         + [table(4, inner, lambda s: 0), whole((1, 128)), whole((1, inner))],
-        [back(inner), whole((8, inner)), whole((8, inner)), whole((half_rows, 2 * states)),
-         whole((half_rows, 2 * states)), back(128), whole((8, 128)), whole((8, inner))],
-        [shaped((tokens, inner), BF16), shaped((8, inner)), shaped((8, inner)), shaped((half_rows, 2 * states)),
-         shaped((half_rows, 2 * states)), shaped((tokens, 128)), shaped((8, 128)), shaped((8, inner))],
+        [back(inner), whole((8, inner)), whole((8, inner)), back(128), whole((8, 128)), whole((8, inner))],
+        [shaped((tokens, inner), BF16), shaped((8, inner)), shaped((8, inner)), shaped((tokens, 128)),
+         shaped((8, 128)), shaped((8, inner))],
         [pltpu.VMEM((3 * inner, 128), BF16), pltpu.VMEM((BLOCK + 8, inner), F32),
          pltpu.VMEM((BLOCK + 8, inner), F32)],
         name="join",
-    )(scalars, conv, delta, level_x, delta_x, draw, out_grad, y, zed, dbc, hloc, pre, gloc, returned, carried,
-      u, u, uh, taps_x, rate_row, skip_row)
+        limit=20 << 20,
+    )(scalars, *streamed(conv, delta, delta_x, draw, out_grad, y), zed, ends, *streamed(u, u), uh, taps_x, rate_row, skip_row)
+
+    head, early_far = lax.optimization_barrier((head, early_far))
 
     ahead = jnp.where(hi < pairs - 1, along(head, -2), 0.0)
     for k in range(3):
         tail = tail + taps_x[k, :inner] * jnp.concatenate([jnp.zeros((5 + k, inner), F32), ahead[: 3 - k]])
     signal_pre = lax.dynamic_update_slice_in_dim(signal_pre, tail.astype(BF16), tokens - 8, 0)
 
+    signal_small = jnp.concatenate([signal_cols, turn_cols])
+    signal, signal_scale = grads([normed], [signal_pre], "grad_signal")
+    signal_got = over_sequences(signal, signal_scale, [signal_small])
+
     dbc = dbc_keep + swap(dbc_give)
     dbc_back = across(lax.dynamic_slice_in_dim(dbc, (1 - lo) * states, states, 1), 1)
-    gated_later, early_got, _ = lax.optimization_barrier((gated, early_got, dbc))
-    branch = grid_call(
-        functools.partial(branch_body, parts, quarter),
-        (count,),
-        [rows_spec(inner)] + [whole((shard, 2 * inner))] * parts,
-        [whole((halfway, model))] * 4,
-        [shaped((halfway, model))] * 4,
-        [pltpu.VMEM((BLOCK, model), F32)],
-        name="branch",
-    )(scalars, gated_later, *ws2)
-
-    def over_cores(dealt):
-        return dealt[0] + swap(dealt[2]), dealt[1] + swap(dealt[3])
-
-    branch_mine, branch_theirs = over_cores(branch)
-
+    branch_later, dbc_back = lax.optimization_barrier((branch_theirs[1], dbc_back))
     dbc = mine(dbc, 1, states) + dbc_back
     dbc_other = swap(dbc)
     head_rows = jnp.where(core == 0, dbc[:8], dbc_other[:8])
     head_conv = lax.dynamic_slice(conv, (0, inner + lo * states), (8, states))
     state_ahead = along(head_rows * slope(head_conv, jax.nn.sigmoid(head_conv)), -2)
-    early_cut = chunks(early, early_got)
-    branch_theirs, early_cut, state_ahead = lax.optimization_barrier((branch_theirs, early_cut, state_ahead))
-    branch_back = across(branch_theirs, 1)
-    early_far = over_positions(early_cut)
-
     def back_own(b, s):
         return jnp.clip(count - 1 - b - s[LO] * 2 * quarter, 0, 2 * quarter - 1), 0
 
@@ -839,38 +917,40 @@
          back_half, back_half, state_side[0]] + state_side
         + [whole((8, states)), table(4, states, state_lanes)]
         + [whole((shard, wide + 128))] * parts + [whole((shard, 2 * inner))] * parts,
-        [whole((halfway, model))] * 4 + [back(128), whole((8, model)), whole((8, states))],
-        [shaped((halfway, model))] * 4 + [shaped((tokens, 128), BF16), shaped((8, model)), shaped((8, states))],
+        dealt_specs + [back(128), whole((8, model)), whole((8, states))],
+        dealt_shapes + [shaped((tokens, 128), BF16), shaped((8, model)), shaped((8, states))],
         [pltpu.VMEM((BLOCK, model), F32), pltpu.VMEM((BLOCK + 8, states), F32),
          pltpu.VMEM((BLOCK + 8, states), F32)],
         name="feature",
     )(scalars, hidden, near, far, gate_grad, signal_pre, raw_grad, dbc, dbc_other, conv, u, u, uh, state_ahead,
       taps_x, *ws1, *ws2)
-    feature_mine, feature_theirs = over_cores(feature)
-
-    folds = model // inner
-    small = jnp.concatenate(
-        [
-            jnp.concatenate([signal_cols, state_cols], axis=1),
-            jnp.concatenate([turn_cols[:2], head_cols[:2]], axis=1),
-            jnp.pad(feature_cols[0].reshape(folds, inner), ((0, 6 - folds), (0, 128))),
-        ]
-    )
-    late = grid_call(
-        functools.partial(late_body, parts),
-        (parts,),
-        [turned, whole((tokens, inner)), whole((tokens, 128)), whole((16, inner + 128))],
-        [whole((shard + 16, inner + 128))] * parts,
-        [shaped((shard + 16, inner + 128))] * parts,
-        name="grad_late",
-    )(scalars, normed, signal_pre, extra_pre, small)
-    late, feature_theirs, early_far, branch_back = lax.optimization_barrier(
-        (late, feature_theirs, early_far, branch_back)
-    )
-    early_sum, _ = settled(early_cut, early_far)
-    late_got, feature_back = lax.optimization_barrier((over_sequences(late), across(feature_theirs, 1)))
-    late_cut = chunks(late, late_got, 16)
-    late_sum, small_sum = settled(late_cut, over_positions(late_cut), 16)
+    feature, branch_rest, signal_got = lax.optimization_barrier((feature, across(branch_later, 1), signal_got))
+    branch_back = jnp.concatenate(branch_back + [branch_rest])
+    feature_theirs = feature[1] + swap(feature[3])
+    feature_mine = feature[0] + swap(feature[2])
+
+    folds = model // 128
+    extra_small = jnp.concatenate(
+        [state_cols, head_cols, feature_cols[0].reshape(folds, 128), jnp.zeros((16 - folds % 16, 128), F32)]
+    )
+    extra, extra_scale = grads([normed], [extra_pre], "grad_extra")
+    extra, feature_theirs = lax.optimization_barrier((extra, feature_theirs))
+    feature_power = exponents(jnp.max(jnp.abs(feature_theirs), axis=0, keepdims=True))
+    feature_back = across(packed(feature_theirs, feature_power, jnp.exp2(-feature_power)), 1)
+    extra_got = over_sequences(extra, extra_scale, [extra_small])
+    extra_got, feature_back = lax.optimization_barrier((extra_got, feature_back))
+    signal_got, extra_got = lax.optimization_barrier((signal_got, extra_got))
+    signal_cut, (signal_here,) = chunks(signal, signal_scale, signal_got, [signal_small])
+    signal_far = over_positions(signal_cut)
+    extra_cut, (extra_here,) = chunks(extra, extra_scale, extra_got, [extra_small])
+    extra_far = over_positions(extra_cut)
+    early_sum = settled(early_cut[0], decoded(early_far))
+    signal_sum = settled(signal_cut[0], decoded(signal_far, [16]))
+    signal_small = settled(signal_here, ridden(signal_far, [16]))
+    extra_rows = extra_small.shape[0]
+    extra_sum = settled(extra_cut[0], decoded(extra_far, [extra_rows]))
+    extra_small = settled(extra_here, ridden(extra_far, [extra_rows]))
+    feature_back = unpacked(feature_back)[0]
 
     def both_halves(value):
         other = swap(value)
@@ -879,7 +959,7 @@
     residual = piece(hidden, core, halfway).astype(F32)
     place = z * steps + core * halfway + lax.broadcasted_iota(jnp.int32, (halfway, 1), 0)
     valid = (place < lengths[0]).astype(F32)
-    mixed = both_halves((residual + valid * (branch_mine + branch_back)).astype(BF16))
+    mixed = both_halves((residual + valid * (branch[0] + swap(branch[2]) + branch_back)).astype(BF16))
 
     feature_grad = feature_mine + feature_back
     inverse = lax.rsqrt(jnp.mean(residual * residual, axis=1, keepdims=True) + EPSILON)
@@ -893,13 +973,13 @@
     def side_by_side(pair):
         return jnp.concatenate(pair, axis=-1)
 
-    signal_small = side_by_side([part[:, :inner] for part in small_sum])
-    state_small = side_by_side([part[:8, inner:] for part in small_sum])
-    heads_small = [part[8:10, inner + HEAD0 : inner + HEAD0 + heads] for part in small_sum]
+    signal_small = side_by_side(signal_small)
+    state_small = side_by_side([part[:8] for part in extra_small])
+    heads_small = [part[8:10, HEAD0 : HEAD0 + heads] for part in extra_small]
     rate_all = -jnp.exp(log_rate)
     skip_sum = signal_small[9].reshape(2 * heads, inner // heads).sum(axis=1)
-    gain_here = (small_sum[0] + small_sum[1])[10 : 10 + folds, :inner].reshape(model)
-    state_here = jnp.stack([part[:, inner : inner + HEAD0] for part in late_sum])
+    gain_here = (extra_small[0] + extra_small[1])[16 : 16 + folds].reshape(model)
+    state_here = jnp.stack([part[:, :HEAD0] for part in extra_sum])
     gain_there, state_there = swap(gain_here), swap(state_here)
     gain_size = model // (dps * ctxs)
     gain_sum = piece(gain_here + gain_there, dp * ctxs + z, gain_size)
@@ -907,11 +987,8 @@
         core == 0, jnp.stack([state_here, state_there], 1), jnp.stack([state_there, state_here], 1)
     )
     state_sum = jnp.transpose(in_order, (2, 0, 1, 3)).reshape(-1, 2 * states)
-    main_sum = jnp.stack(
-        [side_by_side([part[:, :inner] for part in early_sum]), side_by_side([part[:, :inner] for part in late_sum])],
-        axis=1,
-    )
-    delta_sum = side_by_side([part[:, inner + HEAD0 : inner + HEAD0 + heads] for part in late_sum])
+    main_sum = jnp.stack([side_by_side([part[:, :inner] for part in early_sum]), side_by_side(signal_sum)], axis=1)
+    delta_sum = side_by_side([part[:, HEAD0 : HEAD0 + heads] for part in extra_sum])
 
     return (
         mixed[None],

time: 308 us -> 276 us (0.90)
  waiting for transfers between devices: 89.4 us -> 46.7 us
  other arithmetic: 27.8 us -> 39.6 us
  local copies, waits for them, and re-layouts: 26 us -> 20.1 us
  starting transfers between devices: 48.4 us -> 53.5 us
    ppermute x12 -> x16, waiting for transfers between devices: 38.6 us -> 14.2 us  [across(): return lax.ppermute(value, 'ctx', [(i, i ^ j) for i in range(ctxs)])]
    ppermute x12 -> x15, waiting for transfers between devices: 41.9 us -> 20.8 us  [spread(): return lax.ppermute(value, 'dp', [(i, i ^ j) for i in range(dps)])]
    ppermute x12 -> x16, starting transfers between devices: 14.8 us -> 23 us  [across(): return lax.ppermute(value, 'ctx', [(i, i ^ j) for i in range(ctxs)])]
    ppermute x6 -> x4, starting transfers between devices: 16.3 us -> 9.04 us  [along(): lax.ppermute(value, 'ctx', [(i, i + step) for i in range(ctxs) if 0 <= i...]
    convert_element_type x0 -> x18, other arithmetic: none -> 6.88 us  [the longest x7 4.18 us: packed(): (value * inverse).astype(F16)]
    pallas_call x3 -> x5, Pallas kernels: 31.7 us -> 38 us  [the longest x3 20 us: grads(): grid_call(functools.partial(grads_body, parts, [(n, n + 1) for n in range...]
    exp2 x0 -> x10, other arithmetic: none -> 6.12 us  [the longest x7 4.38 us: unpacked(): return (sent[:rows].astype(F32) * jnp.exp2(power), power, more)]
    ppermute x12 -> x15, starting transfers between devices: 15.1 us -> 18.6 us  [spread(): return lax.ppermute(value, 'dp', [(i, i ^ j) for i in range(dps)])]
  transfers between devices with their start and end apart: 43 -> 51, of which waited for: 14 -> 15; matrix products, arithmetic and copies ran while one was open for 12% -> 15% of each run, Pallas kernels for 27% -> 32%
where the time goes in v3:
time: 276 us; the launch traced here: 274 us
  Pallas kernels  112 us (41%)
  starting transfers between devices  53.5 us (19%)
  waiting for transfers between devices  46.7 us (17%)
  other arithmetic  39.6 us (14%)
  local copies, waits for them, and re-layouts  20.1 us (7%)
    ppermute x16, starting transfers between devices, across(): return lax.ppermute(value, 'ctx', [(i, i ^ j) for i in range(ctxs)])  23 us
    ppermute x15, waiting for transfers between devices, spread(): return lax.ppermute(value, 'dp', [(i, i ^ j) for i in range(dps)])  20.8 us
    pallas_call x3, Pallas kernels, grads(): grid_call(functools.partial(grads_body, parts, [(n, n + 1) for n in range...  20 us
    ppermute x15, starting transfers between devices, spread(): return lax.ppermute(value, 'dp', [(i, i ^ j) for i in range(dps)])  18.6 us
    pallas_call x1, Pallas kernels, per_device(): grid_call(functools.partial(front_body, parts, inner, states, quarter), (...  15.3 us
    ppermute x16, waiting for transfers between devices, across(): return lax.ppermute(value, 'ctx', [(i, i ^ j) for i in range(ctxs)])  14.2 us
    pallas_call x1, Pallas kernels, per_device(): grid_call(functools.partial(feature_body, parts, quarter), (count,), [pl....  11.3 us
    pallas_call x1, Pallas kernels, per_device(): grid_call(functools.partial(back_body, inner, states), (count,), [rows_sp...  11.3 us
  transfers between devices with their start and end apart: 51, of which 15 were waited for; matrix products, arithmetic and copies ran while one was open for 15% of the time, Pallas kernels for 32%

profile of v3, /device:TPU:0, one launch (start us, length us, event | category | flops | bytes accessed | tf_op | source)
XLA Modules:
  0.0 274.0 jit_solution(13218409991269315743)
XLA Ops:
  1.6 3.4 %constant_dynamic-slice_fusion.7 = (bf16[256,1,512]{2,1,0:T(2,128)(2,1)}, bf16[256,1,512]{2,1,0:T(2,128)(2,1)S(1)}) fusion(bf16[256,2,1024]{2,1,0:T(2,128)(2,1)} %param.20, s32[]{:T(128)S(6)} %select_n.189, s32[]{:T(128)S(6)} %add.341), kind=kLoop, calls=%fused_computation.156 | loop fusion | bytes 1048584 | tf_op jit(solution)/shard_map/slice | solution.py:689
  6.1 3.9 %collective-permute-start.2 = (bf16[256,896]{1,0:T(8,128)(2,1)}, bf16[256,896]{1,0:T(8,128)(2,1)}, u32[]{:S(2)}, u32[]{:S(2)}) collective-permute-start(bf16[256,896]{1,0:T(8,128)(2,1)} %concatenate.161.rest_0_), channel_id=1, source_target_pairs={{0,24},{8,16},{16,8},{24,0},{1,25},{9,17},{17,9},{25,1},{2,26},{10... | collective-permute-start | bytes 1376264 | tf_op jit(solution)/shard_map/ppermute | solution.py:597
  10.8 2.1 collective-permute-start.3
  17.9 3.8 %collective-permute-done.2.rest_3_ = bf16[256,896]{1,0:T(8,128)(2,1)} collective-permute-done((bf16[256,896]{1,0:T(8,128)(2,1)}, bf16[256,896]{1,0:T(8,128)(2,1)}, u32[]{:S(2)}, u32[]{:S(2)}) %collective-permute-start.2) | collective-permute-done | bytes 458784 | tf_op jit(solution)/shard_map/ppermute | solution.py:597
  21.7 9.0 %collective-permute-done.1.rest_2_ = bf16[256,896]{1,0:T(8,128)(2,1)} collective-permute-done((bf16[256,896]{1,0:T(8,128)(2,1)}, bf16[256,896]{1,0:T(8,128)(2,1)}, u32[]{:S(2)}, u32[]{:S(2)}) %collective-permute-start.1) | collective-permute-done | bytes 458784 | tf_op jit(solution)/shard_map/ppermute | solution.py:597
  31.8 1.5 collective-permute-start.7
  35.3 1.7 collective-permute-start.11
  38.9 15.3 %front.1 = (bf16[1024,1024]{1,0:T(8,128)(2,1)}, f32[1024,768]{1,0:T(8,128)}, f32[8,768]{1,0:T(8,128)}, f32[1024,768]{1,0:T(8,128)}, f32[1024,128]{1,0:T(8,128)},...) custom-call(s32[10]{0:T(128)} %stack.79.s_ref, ...), custom_call_target="tpu_custom_call" | custom-call | tf_op jit(solution)/shard_map/front/pallas_call | solution.py:704
  54.2 4.7 %collective-permute-start.12 = (f32[128,512]{1,0:T(8,128)}, f32[128,512]{1,0:T(8,128)S(1)}, u32[]{:S(2)}, u32[]{:S(2)}) collective-permute-start(f32[128,512]{1,0:T(8,128)} %get-tuple-element.166), channel_id=1, source_target_pairs={{0,4},{2,6},{1,5},{3,7},{8,12},{10,14},{9,13},{11,15},{16,20},{18,... | collective-permute-start | bytes 786440 | tf_op jit(solution)/shard_map/ppermute | solution.py:592
  59.2 6.6 %within.1.yw = f32[1024,512]{1,0:T(8,128)S(1)} custom-call(s32[10]{0:T(128)S(1)} %copy-done.10, f32[1024,768]{1,0:T(8,128)} %get-tuple-element.152.co, f32[1024,128]{1,0:T(8,128)} %get-tuple-element.154.lev, f32[1024,512]{1,0:T(8,128)} %get-tuple-element.153.lx, f32[1024,512]{1,0:T(8,128)} %get-tuple-element.155.dx), custom_call_target="tpu_custom_call" | custom-call | tf_op jit(solution)/shard_map/within/pallas_call | solution.py:730
  67.2 6.7 %gates.1 = (f32[1024,512]{1,0:T(8,128)S(1)}, f32[1024,512]{1,0:T(8,128)S(1)}, bf16[1024,1024]{1,0:T(8,128)(2,1)S(1)}) custom-call(s32[10]{0:T(128)S(1)} %copy-done.10, bf16[1024,1024]{1,0:T(8,128)(2,1)} %get-tuple-element.156.normed.refs_0_, bf16[512,1024]{1,0:T(8,128)(2,1)} %bitcast.109, bf16[256,1024]{1,0:T(8,128)(2,1)} %collective-permute-done.7.near, ...), custom_call_target="tpu_custom_call" | custom-call | tf_op jit(solution)/shard_map/gates/pallas_call | solution.py:740
  73.9 1.4 copy-done.6
  75.3 6.4 %output.1 = (f32[1024,512]{1,0:T(8,128)S(1)}, f32[16,1024]{1,0:T(8,128)S(1)}) custom-call(s32[10]{0:T(128)S(1)} %copy-done.10, f32[1024,768]{1,0:T(8,128)} %get-tuple-element.152.co, f32[1024,512]{1,0:T(8,128)} %get-tuple-element.153.lx, f32[1024,512]{1,0:T(8,128)S(1)} %within.1.yw, f32[1024,512]{1,0:T(8,128)S(1)} %get-tuple-element.162.gate, ...), custom_call_target="tpu_custom_call" | custom-call | tf_op jit(solution)/shard_map/output/pallas_call | solution.py:750
  82.3 1.4 collective-permute-start.14
  83.7 2.2 collective-permute-done.15.sums3
  85.9 1.7 collective-permute-done.14.sums2
  87.6 8.8 %turn.1 = (bf16[1024,512]{1,0:T(8,128)(2,1)}, bf16[1024,512]{1,0:T(8,128)(2,1)}, f32[1024,512]{1,0:T(8,128)}, f32[9,128,512]{2,1,0:T(8,128)}, f32[128,512]{1,0:T(8,128)S(1)}, /*index=5*/f32[8,512]{1,0:T(8,128)S(1)}) custom-call(s32[10]{0:T(128)S(1)} %copy-done.10, f32[1024,768]{1,0:T(8,128)} %get-tuple-element.152.co, f32[1024,512]{1,0:T(8,128)} %get-tuple-element.153.lx, ...), custom_call_target="tpu_custom_call" | custom-call | tf_op jit(solution)/shard_map/turn/pallas_call | solution.py:768
  96.4 9.0 %grad_early.1 = (f32[256,1024]{1,0:T(8,128)}, f32[256,1024]{1,0:T(8,128)}, f32[256,1024]{1,0:T(8,128)}, f32[256,1024]{1,0:T(8,128)}, f32[16,1024]{1,0:T(8,128)}) custom-call(s32[10]{0:T(128)} %stack.79.s_ref, bf16[1024,1024]{1,0:T(8,128)(2,1)} %get-tuple-element.156.normed.refs_0_, bf16[1024,512]{1,0:T(8,128)(2,1)} %get-tuple-element.170.refs_1_.ggrad, ...), custom_call_target="tpu_custom_call" | custom-call | tf_op jit(solution)/shard_map/grad_early/pallas_call | solution.py:798
  106.9 2.3 multiply_convert_fusion.1
  109.7 1.8 collective-permute-start.19
  113.3 1.5 collective-permute-start.16
  114.8 11.3 %back.1 = (f32[1024,512]{1,0:T(8,128)}, f32[1024,256]{1,0:T(8,128)}) custom-call(s32[10]{0:T(128)} %stack.79.s_ref, f32[1024,768]{1,0:T(8,128)} %get-tuple-element.152.co, f32[1024,128]{1,0:T(8,128)} %get-tuple-element.154.lev, f32[1024,512]{1,0:T(8,128)} %get-tuple-element.153.lx, f32[1024,512]{1,0:T(8,128)} %get-tuple-element.155.dx, ...), custom_call_target="tpu_custom_call" | custom-call | tf_op jit(solution)/shard_map/back/pallas_call | solution.py:813
  126.1 7.2 %branch.1 = (f32[256,1024]{1,0:T(8,128)}, f32[256,1024]{1,0:T(8,128)}, f32[256,1024]{1,0:T(8,128)}, f32[256,1024]{1,0:T(8,128)}) custom-call(s32[10]{0:T(128)} %stack.79.s_ref, bf16[1024,512]{1,0:T(8,128)(2,1)} %get-tuple-element.181.refs_3_.gated, bf16[256,1024]{1,0:T(8,128)(2,1)} %copy-done.14, bf16[256,1024]{1,0:T(8,128)(2,1)} %copy-done.18, ...), custom_call_target="tpu_custom_call" | custom-call | tf_op jit(solution)/shard_map/branch/pallas_call | solution.py:824
  133.3 3.7 %collective-permute-done.18 = f16[272,1024]{1,0:T(8,128)(2,1)} collective-permute-done((f16[272,1024]{1,0:T(8,128)(2,1)S(1)}, f16[272,1024]{1,0:T(8,128)(2,1)}, u32[]{:S(2)}, u32[]{:S(2)}) %collective-permute-start.18) | collective-permute-done | bytes 557088 | tf_op jit(solution)/shard_map/ppermute | solution.py:597
  137.9 2.0 multiply_add_fusion
  142.6 2.1 collective-permute-start.24
  144.7 1.5 collective-permute-start.23
  146.4 8.2 %meet.1 = (f32[1024,512]{1,0:T(8,128)S(1)}, f32[32,512]{1,0:T(8,128)S(1)}, f32[512,256]{1,0:T(8,128)S(1)}, f32[512,256]{1,0:T(8,128)S(1)}) custom-call(s32[10]{0:T(128)S(1)} %copy-done.11, f32[1024,768]{1,0:T(8,128)} %get-tuple-element.152.co, f32[1024,512]{1,0:T(8,128)} %get-tuple-element.153.lx, f32[1024,512]{1,0:T(8,128)} %get-tuple-element.155.dx, ...), custom_call_target="tpu_custom_call" | custom-call | tf_op jit(solution)/shard_map/meet/pallas_call | solution.py:855
  154.6 8.1 %collective-permute-done.22 = f32[128,1024]{1,0:T(8,128)S(1)} collective-permute-done((f32[128,1024]{1,0:T(8,128)S(1)}, f32[128,1024]{1,0:T(8,128)S(1)}, u32[]{:S(2)}, u32[]{:S(2)}) %collective-permute-start.22) | collective-permute-done | bytes 524320 | tf_op jit(solution)/shard_map/ppermute | solution.py:589
  162.8 9.7 %join.1 = (bf16[1024,512]{1,0:T(8,128)(2,1)S(1)}, f32[8,512]{1,0:T(8,128)S(1)}, f32[8,512]{1,0:T(8,128)S(1)}, f32[1024,128]{1,0:T(8,128)S(1)}, f32[8,128]{1,0:T(8,128)S(1)}, /*index=5*/f32[8,512]{1,0:T(8,128)S(1)}) custom-call(s32[10]{0:T(128)S(1)} %copy-done.11, f32[1024,768]{1,0:T(8,128)} %get-tuple-element.152.co, f32[1024,128]{1,0:T(8,128)} %get-tuple-element.201.delta, ...), custom_call_target="tpu_custom_call" | custom-call | tf_op jit(solution)/shard_map/join/pallas_call | solution.py:870
  177.6 3.2 %collective-permute-done.26 = f32[8,512]{1,0:T(8,128)S(1)} collective-permute-done((f32[8,512]{1,0:T(8,128)S(1)}, f32[8,512]{1,0:T(8,128)S(1)}, u32[]{:S(2)}, u32[]{:S(2)}) %collective-permute-start.26) | collective-permute-done | bytes 16416 | tf_op jit(solution)/shard_map/ppermute | solution.py:592
  181.5 6.1 %grad_signal.1 = (f32[256,512]{1,0:T(8,128)}, f32[256,512]{1,0:T(8,128)}, f32[256,512]{1,0:T(8,128)}, f32[256,512]{1,0:T(8,128)}, f32[16,512]{1,0:T(8,128)}) custom-call(s32[10]{0:T(128)} %stack.79.s_ref, bf16[1024,1024]{1,0:T(8,128)(2,1)} %get-tuple-element.156.normed.refs_0_, bf16[1024,512]{1,0:T(8,128)(2,1)} %fusion.21.mg.refs_1_), custom_call_target="tpu_custom_call" | custom-call | tf_op jit(solution)/shard_map/grad_signal/pallas_call | solution.py:798
  188.4 1.6 multiply_convert_fusion.4
  192.0 1.7 collective-permute-start.34
  196.2 1.6 collective-permute-start.30
  198.5 4.2 %collective-permute-done.30.ahead = f32[8,128]{1,0:T(8,128)S(1)} collective-permute-done((f32[8,128]{1,0:T(8,128)S(1)}, f32[8,128]{1,0:T(8,128)S(1)}, u32[]{:S(2)}, u32[]{:S(2)}) %collective-permute-start.30) | collective-permute-done | bytes 4128 | tf_op jit(solution)/shard_map/ppermute | solution.py:592
  203.2 11.3 %feature.1 = (f32[256,1024]{1,0:T(8,128)}, f32[256,1024]{1,0:T(8,128)}, f32[256,1024]{1,0:T(8,128)}, f32[256,1024]{1,0:T(8,128)}, bf16[1024,128]{1,0:T(8,128)(2,...) custom-call(s32[10]{0:T(128)} %stack.79.s_ref, bf16[512,1024]{1,0:T(8,128)(2,1)} %bitcast.107, ...), custom_call_target="tpu_custom_call" | custom-call | tf_op jit(solution)/shard_map/feature/pallas_call | solution.py:913
  218.1 4.9 %grad_extra.1 = (f32[256,128]{1,0:T(8,128)}, f32[256,128]{1,0:T(8,128)}, f32[256,128]{1,0:T(8,128)}, f32[256,128]{1,0:T(8,128)}, f32[16,128]{1,0:T(8,128)}) custom-call(s32[10]{0:T(128)} %stack.79.s_ref, bf16[1024,1024]{1,0:T(8,128)(2,1)} %get-tuple-element.156.normed.refs_0_, bf16[1024,128]{1,0:T(8,128)(2,1)} %get-tuple-element.234.refs_1_), custom_call_target="tpu_custom_call" | custom-call | tf_op jit(solution)/shard_map/grad_extra/pallas_call | solution.py:798
  224.9 4.0 %collective-permute-start.41 = (f16[272,1024]{1,0:T(8,128)(2,1)S(1)}, f16[272,1024]{1,0:T(8,128)(2,1)S(1)}, u32[]{:S(2)}, u32[]{:S(2)}) collective-permute-start(f16[272,1024]{1,0:T(8,128)(2,1)S(1)} %pad_maximum_fusion.3), channel_id=1, source_target_pairs={{0,2},{2,0},{4,6},{6,4},{1,3},{3,1},{5,7},{7,5},{8,10},{10,8},{12,... | collective-permute-start | bytes 1671176 | tf_op jit(solution)/shard_map/ppermute | solution.py:589
  229.8 1.8 collective-permute-start.40
  233.4 2.5 collective-permute-done.40
  237.4 4.3 %collective-permute-done.41 = f16[272,1024]{1,0:T(8,128)(2,1)S(1)} collective-permute-done((f16[272,1024]{1,0:T(8,128)(2,1)S(1)}, f16[272,1024]{1,0:T(8,128)(2,1)S(1)}, u32[]{:S(2)}, u32[]{:S(2)}) %collective-permute-start.41) | collective-permute-done | bytes 557088 | tf_op jit(solution)/shard_map/ppermute | solution.py:589
  243.6 1.8 collective-permute-start.44
  245.4 1.7 collective-permute-start.43
  252.0 1.6 collective-permute-start.48
  254.2 2.4 collective-permute-start.49
  269.9 2.6 maximum_select_fusion.1
  272.5 1.5 maximum_select_fusion
  (315 shorter events, 63.6 us)
Async XLA Ops:
  6.1 15.6 %collective-permute-start.2 = (bf16[256,896]{1,0:T(8,128)(2,1)}, bf16[256,896]{1,0:T(8,128)(2,1)}, u32[]{:S(2)}, u32[]{:S(2)}) collective-permute-start(bf16[256,896]{1,0:T(8,128)(2,1)} %concatenate.161.rest_0_), channel_id=1, source_target_pairs={{0,24},{8,16},{16,8},{24,0},{1,25},{9,17},{17,9},{25,1},{2,26},{10... | collective-permute-start | bytes 1376264 | tf_op jit(solution)/shard_map/ppermute | solution.py:597
  10.0 20.7 %collective-permute-start.1 = (bf16[256,896]{1,0:T(8,128)(2,1)}, bf16[256,896]{1,0:T(8,128)(2,1)}, u32[]{:S(2)}, u32[]{:S(2)}) collective-permute-start(bf16[256,896]{1,0:T(8,128)(2,1)} %concatenate.161.rest_0_), channel_id=1, source_target_pairs={{0,16},{8,24},{16,0},{24,8},{1,17},{9,25},{17,1},{25,9},{2,18},{10... | collective-permute-start | bytes 1376264 | tf_op jit(solution)/shard_map/ppermute | solution.py:597
  10.5 20.5 %collective-permute-start = (bf16[256,896]{1,0:T(8,128)(2,1)}, bf16[256,896]{1,0:T(8,128)(2,1)}, u32[]{:S(2)}, u32[]{:S(2)}) collective-permute-start(bf16[256,896]{1,0:T(8,128)(2,1)} %concatenate.161.rest_0_), channel_id=1, source_target_pairs={{0,8},{8,0},{16,24},{24,16},{1,9},{9,1},{17,25},{25,17},{2,10},{10... | collective-permute-start | bytes 1376264 | tf_op jit(solution)/shard_map/ppermute | solution.py:597
  10.8 20.2 %collective-permute-start.3 = (bf16[256,1024]{1,0:T(8,128)(2,1)S(1)}, bf16[256,1024]{1,0:T(8,128)(2,1)}, u32[]{:S(2)}, u32[]{:S(2)}) collective-permute-start(bf16[256,1024]{1,0:T(8,128)(2,1)S(1)} %get-tuple-element.321), channel_id=1, source_target_pairs={{0,2},{2,0},{4,6},{6,4},{1,3},{3,1},{5,7},{7,5},{8,10},{10,8},{12,... | collective-permute-start | bytes 1572872 | tf_op jit(solution)/shard_map/ppermute | solution.py:589
  16.1 17.2 %collective-permute-start.5 = (bf16[16,1024]{1,0:T(8,128)(2,1)S(1)}, bf16[16,1024]{1,0:T(8,128)(2,1)S(1)}, u32[]{:S(2)}, u32[]{:S(2)}) collective-permute-start(bf16[16,1024]{1,0:T(8,128)(2,1)S(1)} %slice_bitcast_fusion.2), channel_id=1, source_target_pairs={{2,4},{3,7},{10,12},{11,15},{18,20},{19,23},{26,28},{27,31}} | collective-permute-start | bytes 98312 | tf_op jit(solution)/shard_map/ppermute | solution.py:685
  30.9 7.9 %collective-permute-start.4 = (bf16[256,1024]{1,0:T(8,128)(2,1)}, bf16[256,1024]{1,0:T(8,128)(2,1)}, u32[]{:S(2)}, u32[]{:S(2)}) collective-permute-start(bf16[256,1024]{1,0:T(8,128)(2,1)} %collective-permute-done.3.near), channel_id=1, source_target_pairs={{0,1},{1,0},{2,3},{3,2},{4,5},{5,4},{6,7},{7,6},{8,9},{9,8},{10,11... | collective-permute-start | bytes 1572872 | tf_op jit(solution)/shard_map/ppermute | solution.py:586
  31.8 22.3 %collective-permute-start.7 = (bf16[256,1024]{1,0:T(8,128)(2,1)}, bf16[256,1024]{1,0:T(8,128)(2,1)}, u32[]{:S(2)}, u32[]{:S(2)}) collective-permute-start(bf16[256,1024]{1,0:T(8,128)(2,1)} %constant_dynamic-slice_fusion.4), channel_id=1, source_target_pairs={{0,2},{2,0},{4,6},{6,4},{1,3},{3,1},{5,7},{7,5},{8,10},{10,8},{12,... | collective-permute-start | bytes 1572872 | tf_op jit(solution)/shard_map/ppermute | solution.py:589
  35.3 30.6 %collective-permute-start.11 = (bf16[256,1024]{1,0:T(8,128)(2,1)S(1)}, bf16[256,1024]{1,0:T(8,128)(2,1)S(1)}, u32[]{:S(2)}, u32[]{:S(2)}) collective-permute-start(bf16[256,1024]{1,0:T(8,128)(2,1)S(1)} %pad_maximum_fusion.13.rest_0_.rest_4_), channel_id=1, source_target_pairs={{0,24},{8,16},{16,8},{24,0},{1,25},{9,17},{17,9},{25,1},{2,26},{10... | collective-permute-start | bytes 1572872 | tf_op jit(solution)/shard_map/ppermute | solution.py:597
  37.0 28.9 %collective-permute-start.10 = (bf16[256,1024]{1,0:T(8,128)(2,1)S(1)}, bf16[256,1024]{1,0:T(8,128)(2,1)S(1)}, u32[]{:S(2)}, u32[]{:S(2)}) collective-permute-start(bf16[256,1024]{1,0:T(8,128)(2,1)S(1)} %pad_maximum_fusion.13.rest_0_.rest_4_), channel_id=1, source_target_pairs={{0,16},{8,24},{16,0},{24,8},{1,17},{9,25},{17,1},{25,9},{2,18},{10... | collective-permute-start | bytes 1572872 | tf_op jit(solution)/shard_map/ppermute | solution.py:597
  38.3 27.6 %collective-permute-start.9 = (bf16[256,1024]{1,0:T(8,128)(2,1)S(1)}, bf16[256,1024]{1,0:T(8,128)(2,1)S(1)}, u32[]{:S(2)}, u32[]{:S(2)}) collective-permute-start(bf16[256,1024]{1,0:T(8,128)(2,1)S(1)} %pad_maximum_fusion.13.rest_0_.rest_4_), channel_id=1, source_target_pairs={{0,8},{8,0},{16,24},{24,16},{1,9},{9,1},{17,25},{25,17},{2,10},{10... | collective-permute-start | bytes 1572872 | tf_op jit(solution)/shard_map/ppermute | solution.py:597
  54.1 11.8 %collective-permute-start.8 = (bf16[256,1024]{1,0:T(8,128)(2,1)}, bf16[256,1024]{1,0:T(8,128)(2,1)S(1)}, u32[]{:S(2)}, u32[]{:S(2)}) collective-permute-start(bf16[256,1024]{1,0:T(8,128)(2,1)} %collective-permute-done.7.near), channel_id=1, source_target_pairs={{0,1},{1,0},{2,3},{3,2},{4,5},{5,4},{6,7},{7,6},{8,9},{9,8},{10,11... | collective-permute-start | bytes 1572872 | tf_op jit(solution)/shard_map/ppermute | solution.py:586
  54.2 21.1 %collective-permute-start.12 = (f32[128,512]{1,0:T(8,128)}, f32[128,512]{1,0:T(8,128)S(1)}, u32[]{:S(2)}, u32[]{:S(2)}) collective-permute-start(f32[128,512]{1,0:T(8,128)} %get-tuple-element.166), channel_id=1, source_target_pairs={{0,4},{2,6},{1,5},{3,7},{8,12},{10,14},{9,13},{11,15},{16,20},{18,... | collective-permute-start | bytes 786440 | tf_op jit(solution)/shard_map/ppermute | solution.py:592
  81.7 4.2 %collective-permute-start.15 = (f32[16,1024]{1,0:T(8,128)S(1)}, f32[16,1024]{1,0:T(8,128)S(1)}, u32[]{:S(2)}, u32[]{:S(2)}) collective-permute-start(f32[16,1024]{1,0:T(8,128)S(1)} %get-tuple-element.168.sums), channel_id=1, source_target_pairs={{0,3},{1,2},{2,1},{3,0},{4,7},{5,6},{6,5},{7,4},{8,11},{9,10},{10,... | collective-permute-start | bytes 196616 | tf_op jit(solution)/shard_map/ppermute | solution.py:762
  82.3 5.3 %collective-permute-start.14 = (f32[16,1024]{1,0:T(8,128)S(1)}, f32[16,1024]{1,0:T(8,128)S(1)}, u32[]{:S(2)}, u32[]{:S(2)}) collective-permute-start(f32[16,1024]{1,0:T(8,128)S(1)} %get-tuple-element.168.sums), channel_id=1, source_target_pairs={{0,2},{2,0},{4,6},{6,4},{1,3},{3,1},{5,7},{7,5},{8,10},{10,8},{12,... | collective-permute-start | bytes 196616 | tf_op jit(solution)/shard_map/ppermute | solution.py:589
  83.6 4.0 %collective-permute-start.13 = (f32[16,1024]{1,0:T(8,128)S(1)}, f32[16,1024]{1,0:T(8,128)S(1)}, u32[]{:S(2)}, u32[]{:S(2)}) collective-permute-start(f32[16,1024]{1,0:T(8,128)S(1)} %get-tuple-element.168.sums), channel_id=1, source_target_pairs={{0,1},{1,0},{2,3},{3,2},{4,5},{5,4},{6,7},{7,6},{8,9},{9,8},{10,11... | collective-permute-start | bytes 196616 | tf_op jit(solution)/shard_map/ppermute | solution.py:586
  109.7 23.6 %collective-permute-start.19 = (f16[272,1024]{1,0:T(8,128)(2,1)S(1)}, f16[272,1024]{1,0:T(8,128)(2,1)S(1)}, u32[]{:S(2)}, u32[]{:S(2)}) collective-permute-start(f16[272,1024]{1,0:T(8,128)(2,1)S(1)} %get-tuple-element.378), channel_id=1, source_target_pairs={{0,24},{8,16},{16,8},{24,0},{1,25},{9,17},{17,9},{25,1},{2,26},{10... | collective-permute-start | bytes 1671176 | tf_op jit(solution)/shard_map/ppermute | solution.py:597
  111.5 25.6 %collective-permute-start.18 = (f16[272,1024]{1,0:T(8,128)(2,1)S(1)}, f16[272,1024]{1,0:T(8,128)(2,1)}, u32[]{:S(2)}, u32[]{:S(2)}) collective-permute-start(f16[272,1024]{1,0:T(8,128)(2,1)S(1)} %get-tuple-element.379), channel_id=1, source_target_pairs={{0,16},{8,24},{16,0},{24,8},{1,17},{9,25},{17,1},{25,9},{2,18},{10... | collective-permute-start | bytes 1671176 | tf_op jit(solution)/shard_map/ppermute | solution.py:597
  112.7 24.3 %collective-permute-start.17 = (f16[272,1024]{1,0:T(8,128)(2,1)S(1)}, f16[272,1024]{1,0:T(8,128)(2,1)}, u32[]{:S(2)}, u32[]{:S(2)}) collective-permute-start(f16[272,1024]{1,0:T(8,128)(2,1)S(1)} %get-tuple-element.380), channel_id=1, source_target_pairs={{0,8},{8,0},{16,24},{24,16},{1,9},{9,1},{17,25},{25,17},{2,10},{10... | collective-permute-start | bytes 1671176 | tf_op jit(solution)/shard_map/ppermute | solution.py:597
  113.3 20.0 %collective-permute-start.16 = (f32[128,512]{1,0:T(8,128)S(1)}, f32[128,512]{1,0:T(8,128)S(1)}, u32[]{:S(2)}, u32[]{:S(2)}) collective-permute-start(f32[128,512]{1,0:T(8,128)S(1)} %get-tuple-element.169), channel_id=1, source_target_pairs={{4,0},{6,2},{5,1},{7,3},{12,8},{14,10},{13,9},{15,11},{20,16},{22,... | collective-permute-start | bytes 786440 | tf_op jit(solution)/shard_map/ppermute | solution.py:592
  137.1 3.0 %collective-permute-start.21 = (f32[256,1024]{1,0:T(8,128)}, f32[256,1024]{1,0:T(8,128)S(1)}, u32[]{:S(2)}, u32[]{:S(2)}) collective-permute-start(f32[256,1024]{1,0:T(8,128)} %get-tuple-element.193), channel_id=1, source_target_pairs={{0,1},{1,0},{2,3},{3,2},{4,5},{5,4},{6,7},{7,6},{8,9},{9,8},{10,11... | collective-permute-start | bytes 3145736 | tf_op jit(solution)/shard_map/ppermute | solution.py:586
  141.0 21.7 %collective-permute-start.22 = (f32[128,1024]{1,0:T(8,128)S(1)}, f32[128,1024]{1,0:T(8,128)S(1)}, u32[]{:S(2)}, u32[]{:S(2)}) collective-permute-start(f32[128,1024]{1,0:T(8,128)S(1)} %get-tuple-element.199), channel_id=1, source_target_pairs={{0,2},{2,0},{4,6},{6,4},{1,3},{3,1},{5,7},{7,5},{8,10},{10,8},{12,... | collective-permute-start | bytes 1572872 | tf_op jit(solution)/shard_map/ppermute | solution.py:589
  141.8 31.6 %collective-permute-start.25 = (f16[80,1024]{1,0:T(8,128)(2,1)S(1)}, f16[80,1024]{1,0:T(8,128)(2,1)}, u32[]{:S(2)}, u32[]{:S(2)}) collective-permute-start(f16[80,1024]{1,0:T(8,128)(2,1)S(1)} %get-tuple-element.375), channel_id=1, source_target_pairs={{0,6},{2,4},{4,2},{6,0},{1,7},{3,5},{5,3},{7,1},{8,14},{10,12},{12... | collective-permute-start | bytes 491528 | tf_op jit(solution)/shard_map/ppermute | solution.py:589
  142.6 30.7 %collective-permute-start.24 = (f16[80,1024]{1,0:T(8,128)(2,1)S(1)}, f16[80,1024]{1,0:T(8,128)(2,1)}, u32[]{:S(2)}, u32[]{:S(2)}) collective-permute-start(f16[80,1024]{1,0:T(8,128)(2,1)S(1)} %get-tuple-element.376), channel_id=1, source_target_pairs={{0,4},{2,6},{4,0},{6,2},{1,5},{3,7},{5,1},{7,3},{8,12},{10,14},{12... | collective-permute-start | bytes 491528 | tf_op jit(solution)/shard_map/ppermute | solution.py:589
  144.7 28.6 %collective-permute-start.23 = (f16[80,1024]{1,0:T(8,128)(2,1)S(1)}, f16[80,1024]{1,0:T(8,128)(2,1)}, u32[]{:S(2)}, u32[]{:S(2)}) collective-permute-start(f16[80,1024]{1,0:T(8,128)(2,1)S(1)} %get-tuple-element.377), channel_id=1, source_target_pairs={{0,2},{2,0},{4,6},{6,4},{1,3},{3,1},{5,7},{7,5},{8,10},{10,8},{12,... | collective-permute-start | bytes 491528 | tf_op jit(solution)/shard_map/ppermute | solution.py:589
  174.2 6.6 %collective-permute-start.26 = (f32[8,512]{1,0:T(8,128)S(1)}, f32[8,512]{1,0:T(8,128)S(1)}, u32[]{:S(2)}, u32[]{:S(2)}) collective-permute-start(f32[8,512]{1,0:T(8,128)S(1)} %get-tuple-element.214), channel_id=1, source_target_pairs={{4,0},{6,2},{5,1},{7,3},{12,8},{14,10},{13,9},{15,11},{20,16},{22,... | collective-permute-start | bytes 49160 | tf_op jit(solution)/shard_map/ppermute | solution.py:592
  177.6 10.8 %collective-permute-start.28 = (f32[512,128]{1,0:T(8,128)S(1)}, f32[512,128]{1,0:T(8,128)S(1)}, u32[]{:S(2)}, u32[]{:S(2)}) collective-permute-start(f32[512,128]{1,0:T(8,128)S(1)} %constant_dynamic-slice_fusion.2), channel_id=1, source_target_pairs={{0,2},{2,0},{4,6},{6,4},{1,3},{3,1},{5,7},{7,5},{8,10},{10,8},{12,... | collective-permute-start | bytes 786440 | tf_op jit(solution)/shard_map/ppermute | solution.py:589
  188.4 7.1 %collective-permute-start.29 = (f32[512,128]{1,0:T(8,128)S(1)}, f32[512,128]{1,0:T(8,128)S(1)}, u32[]{:S(2)}, u32[]{:S(2)}) collective-permute-start(f32[512,128]{1,0:T(8,128)S(1)} %dynamic-slice_add_fusion.dbc), channel_id=1, source_target_pairs={{0,1},{1,0},{2,3},{3,2},{4,5},{5,4},{6,7},{7,6},{8,9},{9,8},{10,11... | collective-permute-start | bytes 786440 | tf_op jit(solution)/shard_map/ppermute | solution.py:586
  190.8 23.9 %collective-permute-start.31 = (f32[128,1024]{1,0:T(8,128)}, f32[128,1024]{1,0:T(8,128)S(1)}, u32[]{:S(2)}, u32[]{:S(2)}) collective-permute-start(f32[128,1024]{1,0:T(8,128)} %get-tuple-element.224), channel_id=1, source_target_pairs={{0,2},{2,0},{4,6},{6,4},{1,3},{3,1},{5,7},{7,5},{8,10},{10,8},{12,... | collective-permute-start | bytes 1572872 | tf_op jit(solution)/shard_map/ppermute | solution.py:589
  192.0 22.6 %collective-permute-start.34 = (f16[304,512]{1,0:T(8,128)(2,1)}, f16[304,512]{1,0:T(8,128)(2,1)}, u32[]{:S(2)}, u32[]{:S(2)}) collective-permute-start(f16[304,512]{1,0:T(8,128)(2,1)} %get-tuple-element.370), channel_id=1, source_target_pairs={{0,24},{8,16},{16,8},{24,0},{1,25},{9,17},{17,9},{25,1},{2,26},{10... | collective-permute-start | bytes 933896 | tf_op jit(solution)/shard_map/ppermute | solution.py:597
  193.7 21.0 %collective-permute-start.33 = (f16[304,512]{1,0:T(8,128)(2,1)}, f16[304,512]{1,0:T(8,128)(2,1)}, u32[]{:S(2)}, u32[]{:S(2)}) collective-permute-start(f16[304,512]{1,0:T(8,128)(2,1)} %get-tuple-element.371), channel_id=1, source_target_pairs={{0,16},{8,24},{16,0},{24,8},{1,17},{9,25},{17,1},{25,9},{2,18},{10... | collective-permute-start | bytes 933896 | tf_op jit(solution)/shard_map/ppermute | solution.py:597
  194.9 19.7 %collective-permute-start.32 = (f16[304,512]{1,0:T(8,128)(2,1)S(1)}, f16[304,512]{1,0:T(8,128)(2,1)}, u32[]{:S(2)}, u32[]{:S(2)}) collective-permute-start(f16[304,512]{1,0:T(8,128)(2,1)S(1)} %get-tuple-element.372), channel_id=1, source_target_pairs={{0,8},{8,0},{16,24},{24,16},{1,9},{9,1},{17,25},{25,17},{2,10},{10... | collective-permute-start | bytes 933896 | tf_op jit(solution)/shard_map/ppermute | solution.py:597
  196.2 6.5 %collective-permute-start.30 = (f32[8,128]{1,0:T(8,128)S(1)}, f32[8,128]{1,0:T(8,128)S(1)}, u32[]{:S(2)}, u32[]{:S(2)}) collective-permute-start(f32[8,128]{1,0:T(8,128)S(1)} %fusion.26), channel_id=1, source_target_pairs={{4,0},{6,2},{5,1},{7,3},{12,8},{14,10},{13,9},{15,11},{20,16},{22,... | collective-permute-start | bytes 12296 | tf_op jit(solution)/shard_map/ppermute | solution.py:592
  202.7 49.3 %collective-permute-start.20 = (f32[256,1024]{1,0:T(8,128)}, f32[256,1024]{1,0:T(8,128)S(1)}, u32[]{:S(2)}, u32[]{:S(2)}) collective-permute-start(f32[256,1024]{1,0:T(8,128)} %get-tuple-element.187), channel_id=1, source_target_pairs={{0,1},{1,0},{2,3},{3,2},{4,5},{5,4},{6,7},{7,6},{8,9},{9,8},{10,11... | collective-permute-start | bytes 3145736 | tf_op jit(solution)/shard_map/ppermute | solution.py:586
  214.6 8.5 %collective-permute-start.37 = (f32[256,1024]{1,0:T(8,128)}, f32[256,1024]{1,0:T(8,128)}, u32[]{:S(2)}, u32[]{:S(2)}) collective-permute-start(f32[256,1024]{1,0:T(8,128)} %get-tuple-element.240), channel_id=1, source_target_pairs={{0,1},{1,0},{2,3},{3,2},{4,5},{5,4},{6,7},{7,6},{8,9},{9,8},{10,11... | collective-permute-start | bytes 3145736 | tf_op jit(solution)/shard_map/ppermute | solution.py:586
  224.9 16.7 %collective-permute-start.41 = (f16[272,1024]{1,0:T(8,128)(2,1)S(1)}, f16[272,1024]{1,0:T(8,128)(2,1)S(1)}, u32[]{:S(2)}, u32[]{:S(2)}) collective-permute-start(f16[272,1024]{1,0:T(8,128)(2,1)S(1)} %pad_maximum_fusion.3), channel_id=1, source_target_pairs={{0,2},{2,0},{4,6},{6,4},{1,3},{3,1},{5,7},{7,5},{8,10},{10,8},{12,... | collective-permute-start | bytes 1671176 | tf_op jit(solution)/shard_map/ppermute | solution.py:589
  229.8 6.1 %collective-permute-start.40 = (f16[336,128]{1,0:T(8,128)(2,1)S(1)}, f16[336,128]{1,0:T(8,128)(2,1)S(1)}, u32[]{:S(2)}, u32[]{:S(2)}) collective-permute-start(f16[336,128]{1,0:T(8,128)(2,1)S(1)} %get-tuple-element.384), channel_id=1, source_target_pairs={{0,24},{8,16},{16,8},{24,0},{1,25},{9,17},{17,9},{25,1},{2,26},{10... | collective-permute-start | bytes 258056 | tf_op jit(solution)/shard_map/ppermute | solution.py:597
  231.6 5.1 %collective-permute-start.39 = (f16[336,128]{1,0:T(8,128)(2,1)S(1)}, f16[336,128]{1,0:T(8,128)(2,1)S(1)}, u32[]{:S(2)}, u32[]{:S(2)}) collective-permute-start(f16[336,128]{1,0:T(8,128)(2,1)S(1)} %get-tuple-element.385), channel_id=1, source_target_pairs={{0,16},{8,24},{16,0},{24,8},{1,17},{9,25},{17,1},{25,9},{2,18},{10... | collective-permute-start | bytes 258056 | tf_op jit(solution)/shard_map/ppermute | solution.py:597
  232.9 4.5 %collective-permute-start.38 = (f16[336,128]{1,0:T(8,128)(2,1)S(1)}, f16[336,128]{1,0:T(8,128)(2,1)S(1)}, u32[]{:S(2)}, u32[]{:S(2)}) collective-permute-start(f16[336,128]{1,0:T(8,128)(2,1)S(1)} %get-tuple-element.386), channel_id=1, source_target_pairs={{0,8},{8,0},{16,24},{24,16},{1,9},{9,1},{17,25},{25,17},{2,10},{10... | collective-permute-start | bytes 258056 | tf_op jit(solution)/shard_map/ppermute | solution.py:597
  235.9 14.3 %collective-permute-start.36 = (f32[256,1024]{1,0:T(8,128)S(1)}, f32[256,1024]{1,0:T(8,128)S(1)}, u32[]{:S(2)}, u32[]{:S(2)}) collective-permute-start(f32[256,1024]{1,0:T(8,128)S(1)} %copy-done.51), channel_id=1, source_target_pairs={{0,1},{1,0},{2,3},{3,2},{4,5},{5,4},{6,7},{7,6},{8,9},{9,8},{10,11... | collective-permute-start | bytes 3145736 | tf_op jit(solution)/shard_map/ppermute | solution.py:586
  243.6 10.6 %collective-permute-start.44 = (f16[144,128]{1,0:T(8,128)(2,1)S(1)}, f16[144,128]{1,0:T(8,128)(2,1)S(1)}, u32[]{:S(2)}, u32[]{:S(2)}) collective-permute-start(f16[144,128]{1,0:T(8,128)(2,1)S(1)} %get-tuple-element.381), channel_id=1, source_target_pairs={{0,2},{2,0},{4,6},{6,4},{1,3},{3,1},{5,7},{7,5},{8,10},{10,8},{12,... | collective-permute-start | bytes 110600 | tf_op jit(solution)/shard_map/ppermute | solution.py:589
  245.4 11.2 %collective-permute-start.45 = (f16[144,128]{1,0:T(8,128)(2,1)S(1)}, f16[144,128]{1,0:T(8,128)(2,1)S(1)}, u32[]{:S(2)}, u32[]{:S(2)}) collective-permute-start(f16[144,128]{1,0:T(8,128)(2,1)S(1)} %get-tuple-element.382), channel_id=1, source_target_pairs={{0,6},{2,4},{4,2},{6,0},{1,7},{3,5},{5,3},{7,1},{8,14},{10,12},{12... | collective-permute-start | bytes 110600 | tf_op jit(solution)/shard_map/ppermute | solution.py:589
  245.4 11.2 %collective-permute-start.43 = (f16[144,128]{1,0:T(8,128)(2,1)S(1)}, f16[144,128]{1,0:T(8,128)(2,1)S(1)}, u32[]{:S(2)}, u32[]{:S(2)}) collective-permute-start(f16[144,128]{1,0:T(8,128)(2,1)S(1)} %get-tuple-element.383), channel_id=1, source_target_pairs={{0,4},{2,6},{4,0},{6,2},{1,5},{3,7},{5,1},{7,3},{8,12},{10,14},{12... | collective-permute-start | bytes 110600 | tf_op jit(solution)/shard_map/ppermute | solution.py:589
  250.3 12.5 %collective-permute-start.47 = (f16[112,512]{1,0:T(8,128)(2,1)}, f16[112,512]{1,0:T(8,128)(2,1)}, u32[]{:S(2)}, u32[]{:S(2)}) collective-permute-start(f16[112,512]{1,0:T(8,128)(2,1)} %get-tuple-element.367), channel_id=1, source_target_pairs={{0,4},{2,6},{4,0},{6,2},{1,5},{3,7},{5,1},{7,3},{8,12},{10,14},{12... | collective-permute-start | bytes 344072 | tf_op jit(solution)/shard_map/ppermute | solution.py:589
  252.0 11.5 %collective-permute-start.48 = (f16[112,512]{1,0:T(8,128)(2,1)}, f16[112,512]{1,0:T(8,128)(2,1)}, u32[]{:S(2)}, u32[]{:S(2)}) collective-permute-start(f16[112,512]{1,0:T(8,128)(2,1)} %get-tuple-element.368), channel_id=1, source_target_pairs={{0,2},{2,0},{4,6},{6,4},{1,3},{3,1},{5,7},{7,5},{8,10},{10,8},{12,... | collective-permute-start | bytes 344072 | tf_op jit(solution)/shard_map/ppermute | solution.py:589
  254.2 10.0 %collective-permute-start.49 = (f16[112,512]{1,0:T(8,128)(2,1)}, f16[112,512]{1,0:T(8,128)(2,1)}, u32[]{:S(2)}, u32[]{:S(2)}) collective-permute-start(f16[112,512]{1,0:T(8,128)(2,1)} %get-tuple-element.369), channel_id=1, source_target_pairs={{0,6},{2,4},{4,2},{6,0},{1,7},{3,5},{5,3},{7,1},{8,14},{10,12},{12... | collective-permute-start | bytes 344072 | tf_op jit(solution)/shard_map/ppermute | solution.py:589
  258.4 2.9 %collective-permute-start.50 = (f32[2,64,64]{2,1,0:T(8,128)S(1)}, f32[2,64,64]{2,1,0:T(8,128)S(1)}, u32[]{:S(2)}, u32[]{:S(2)}) collective-permute-start(f32[2,64,64]{2,1,0:T(8,128)S(1)} %get-tuple-element.366), channel_id=1, source_target_pairs={{0,1},{1,0},{2,3},{3,2},{4,5},{5,4},{6,7},{7,6},{8,9},{9,8},{10,11... | collective-permute-start | bytes 98312 | tf_op jit(solution)/shard_map/ppermute | solution.py:586
  260.7 9.2 %collective-permute-start.35 = (bf16[256,1024]{1,0:T(8,128)(2,1)S(1)}, bf16[256,1024]{1,0:T(8,128)(2,1)}, u32[]{:S(2)}, u32[]{:S(2)}) collective-permute-start(bf16[256,1024]{1,0:T(8,128)(2,1)S(1)} %get-tuple-element.342), channel_id=1, source_target_pairs={{0,1},{1,0},{2,3},{3,2},{4,5},{5,4},{6,7},{7,6},{8,9},{9,8},{10,11... | collective-permute-start | bytes 1572872 | tf_op jit(solution)/shard_map/ppermute | solution.py:586
  261.3 11.2 %collective-permute-start.42 = (f32[256,1024]{1,0:T(8,128)S(1)}, f32[256,1024]{1,0:T(8,128)S(1)}, u32[]{:S(2)}, u32[]{:S(2)}) collective-permute-start(f32[256,1024]{1,0:T(8,128)S(1)} %get-tuple-element.341), channel_id=1, source_target_pairs={{0,1},{1,0},{2,3},{3,2},{4,5},{5,4},{6,7},{7,6},{8,9},{9,8},{10,11... | collective-permute-start | bytes 3145736 | tf_op jit(solution)/shard_map/ppermute | solution.py:586
  (57 other events, 550.7 us)

commit v4 on v3

--- a/solution.py
+++ b/solution.py
@@ -19,6 +19,7 @@
 NT = (((1,), (1,)), ((), ()))
 TN = (((0,), (0,)), ((), ()))
 HEAD0 = 64
+STEP = 16
 LO, CORE, BASE, LENGTH, HASPREV, HASNEXT, SLOT0 = range(7)
 
 
@@ -92,8 +93,8 @@
     return (position < s_ref[LENGTH]).astype(F32)
 
 
-def expander(inner):
-    lane = lax.broadcasted_iota(jnp.int32, (384, inner), 0) % 128 - HEAD0
+def expander(inner, shift=0):
+    lane = lax.broadcasted_iota(jnp.int32, (384, inner), 0) % 128 - HEAD0 - shift
     head = lax.broadcasted_iota(jnp.int32, (384, inner), 1) // 64
     return (lane == head).astype(F32).astype(BF16)
 
@@ -160,9 +161,8 @@
 def front_body(parts, inner, states, quarter, s_ref, own, near, far, halo, gain, taps, bias, dbias, rate,
                *rest):
     ws = rest[:parts]
-    (normed_ref, u_ref, uh_ref, co_ref, draw_ref, delta_ref, lev_ref, lx_ref, dx_ref, hloc_ref,
-     pre_ref, end_ref) = rest[parts : parts + 12]
-    hsc, usc, state, pre, esc = rest[parts + 12 :]
+    normed_ref, u_ref, uh_ref, co_ref, hd_ref, hloc_ref, pre_ref, end_ref = rest[parts : parts + 8]
+    hsc, usc, state, pre, esc = rest[parts + 8 :]
     b = pl.program_id(0)
     wide = inner + 2 * states
     shard = ws[0].shape[0]
@@ -195,16 +195,13 @@
         conv = conv + taps[k : k + 1] * usc[5 + k : 5 + k + BLOCK]
     co_ref[...] = conv
     raw = u[:, wide:] + dbias[...]
-    draw_ref[...] = raw
     delta = jnp.where(head_lanes(inner), jnp.maximum(raw, 0.0) + jnp.log1p(jnp.exp(-jnp.abs(raw))), 0.0)
     delta = delta * valid_rows(s_ref, b)
-    delta_ref[...] = delta
     level = running(triangle(True), delta * rate[...])
-    lev_ref[...] = level
+    raw = jnp.where(head_lanes(inner), raw, 0.0)
+    hd_ref[...] = level + pltpu.roll(delta, STEP, 1) + pltpu.roll(raw, 2 * STEP, 1)
     both = mm(jnp.concatenate([three(level), three(delta)], axis=0), esc[...])
     level_x, delta_x = both[:BLOCK], both[BLOCK:]
-    lx_ref[...] = level_x
-    dx_ref[...] = delta_x
     act = conv * jax.nn.sigmoid(conv)
     source = delta_x * act[:, :inner]
     inject_t = act[:, inner : inner + states].T
@@ -226,11 +223,21 @@
         pre_ref[n + 1] = pre[...]
 
 
-def within_body(inner, states, s_ref, co, lev, lx, dx, yw_ref):
+def start_expanders(inner, *scs):
+    @pl.when(pl.program_id(0) == 0)
+    def _():
+        for shift, sc in scs:
+            sc[...] = expander(inner, shift)
+
+
+def within_body(inner, states, s_ref, co, hd, yw_ref, lsc, dsc):
+    start_expanders(inner, (0, lsc), (STEP, dsc))
     conv = co[...]
     act = conv * jax.nn.sigmoid(conv)
-    xs = dx[...] * act[:, :inner]
-    level = lev[...]
+    level = hd[...]
+    exact = three(level)
+    lx = mm(exact, lsc[...])
+    xs = mm(exact, dsc[...]) * act[:, :inner]
     keep = lax.broadcasted_iota(jnp.int32, (SUB, SUB), 0) >= lax.broadcasted_iota(jnp.int32, (SUB, SUB), 1)
     for i in range(BLOCK // SUB):
         at = slice(i * SUB, (i + 1) * SUB)
@@ -266,7 +273,9 @@
     return hloc + jnp.exp(pre[0:1]) * hin
 
 
-def output_body(inner, states, s_ref, co, lx, yw, gate, gg, hloc, pre, hin, skip, ggain, y_ref, sum_ref):
+def output_body(inner, states, s_ref, co, hd, yw, gate, gg, hloc, pre, hin, skip, ggain, y_ref, sum_ref, lsc):
+    start_expanders(inner, (0, lsc))
+    lx = mm(three(hd[...]), lsc[...])
     conv = co[...]
     act = conv * jax.nn.sigmoid(conv)
     for i in range(BLOCK // SUB):
@@ -281,8 +290,10 @@
     sum_ref[8:16] = mm(ones, three(gg[...] * ggain[...] * product), NT)
 
 
-def turn_body(inner, states, total, s_ref, co, lx, y, gate, gg, sums, sums1, sums2, sums3, skip, ggain,
-              gated_ref, ggrad_ref, og_ref, gloc_ref, start_ref, cols_ref, chain):
+def turn_body(inner, states, total, s_ref, co, hd, y, gate, gg, sums, sums1, sums2, sums3, skip, ggain,
+              gated_ref, ggrad_ref, og_ref, gloc_ref, start_ref, cols_ref, chain, lsc):
+    start_expanders(inner, (0, lsc))
+    lx = mm(three(hd[...]), lsc[...])
     step = pl.program_id(0)
     conv = co[...]
     act = conv * jax.nn.sigmoid(conv)
@@ -327,11 +338,14 @@
         start_ref[...] = chain[...]
 
 
-def back_body(inner, states, s_ref, co, lev, lx, dx, og, hloc, pre, hin, z_ref, dbc_ref):
+def back_body(inner, states, s_ref, co, hd, og, hloc, pre, hin, z_ref, dbc_ref, lsc, dsc):
+    start_expanders(inner, (0, lsc), (STEP, dsc))
     conv = co[...]
     act = conv * jax.nn.sigmoid(conv)
-    xs = dx[...] * act[:, :inner]
-    level = lev[...]
+    level = hd[...]
+    exact = three(level)
+    lx = mm(exact, lsc[...])
+    xs = mm(exact, dsc[...]) * act[:, :inner]
     keep = lax.broadcasted_iota(jnp.int32, (SUB, SUB), 1) >= lax.broadcasted_iota(jnp.int32, (SUB, SUB), 0)
     for i in range(BLOCK // SUB):
         at = slice(i * SUB, (i + 1) * SUB)
@@ -371,14 +385,17 @@
     return pre
 
 
-def meet_body(inner, states, s_ref, co, lx, dx, z, dbc, hloc, pre, gloc, gin, hin, zed_ref, ends_ref, keep_ref,
-              give_ref):
+def meet_body(inner, states, s_ref, co, hd, z, dbc, hloc, pre, gloc, gin, hin, zed_ref, ends_ref, keep_ref,
+              give_ref, lsc, dsc):
+    start_expanders(inner, (0, lsc), (STEP, dsc))
+    exact = three(hd[...])
+    lx = mm(exact, lsc[...])
     subs = BLOCK // SUB
     count = pl.num_programs(0)
     b = pl.program_id(0)
     conv = co[...]
     act = conv * jax.nn.sigmoid(conv)
-    source = dx[...] * act[:, :inner]
+    source = mm(exact, dsc[...]) * act[:, :inner]
     ends = []
     inject_grads = []
     for i in range(subs):
@@ -406,8 +423,9 @@
         give_ref[rows, states:] = dbc[:, states:]
 
 
-def join_body(inner, s_ref, co, delta, dx, draw, og, y, zed_in, ends_in, u, prior, uh, taps, rate, skip, mg_ref,
-              tail_ref, head_ref, rg_ref, cols_ref, sig_ref, col_sc, csc, usc):
+def join_body(inner, s_ref, co, hd, og, y, zed_in, ends_in, u, prior, uh, taps, rate, skip, mg_ref,
+              tail_ref, head_ref, rg_ref, cols_ref, sig_ref, col_sc, csc, usc, dsc):
+    start_expanders(inner, (STEP, dsc))
     step = pl.program_id(0)
     subs = BLOCK // SUB
     count = pl.num_programs(0)
@@ -423,16 +441,18 @@
     conv = co[...]
     sig = jax.nn.sigmoid(conv)
     x = conv * sig
-    delta_x = dx[...]
+    packed_heads = hd[...]
+    delta_x = mm(three(packed_heads), dsc[...])
     zed = zed_in[...]
     ends = ends_in[...]
     g = og[...]
     sums = mm(three(jnp.concatenate([x * zed, g * y[...], ends], axis=0)), col_sc[...])
     direct, read, ends = sums[:BLOCK], sums[BLOCK : 2 * BLOCK], sums[2 * BLOCK :]
-    dlt = delta[...]
+    dlt = jnp.where(head_lanes(inner), pltpu.roll(packed_heads, 128 - STEP, 1), 0.0)
+    draw = pltpu.roll(packed_heads, 128 - 2 * STEP, 1)
     q = running(triangle(False), read - dlt * direct)
     q = jnp.concatenate([q[i * SUB : (i + 1) * SUB] + ends[i : i + 1] for i in range(subs)], axis=0)
-    rg = (direct + rate[...] * q) * valid_rows(s_ref, b) * jax.nn.sigmoid(draw[...])
+    rg = (direct + rate[...] * q) * valid_rows(s_ref, b) * jax.nn.sigmoid(draw)
     rg = jnp.where(head_lanes(inner), rg, 0.0)
     rg_ref[...] = rg
     cols_ref[0:1] += jnp.sum(rg, axis=0, keepdims=True)
@@ -475,7 +495,8 @@
 
 def grads_body(parts, pairs, s_ref, *refs):
     inputs = 1 + max(max(pair) for pair in pairs)
-    outs, scale, peak = refs[inputs : inputs + parts], refs[inputs + parts], refs[inputs + parts + 1]
+    outs = refs[inputs : inputs + parts]
+    powers, inverse, peak = refs[inputs + parts :]
     j = pl.program_id(0)
 
     @pl.when(j == 0)
@@ -497,8 +518,8 @@
     @pl.when(j == parts - 1)
     def _():
         power = exponents(peak[...])
-        scale[0:8] = jnp.broadcast_to(power[0:1], (8, at))
-        scale[8:16] = jnp.broadcast_to(jnp.exp2(-power[0:1]), (8, at))
+        powers[...] = jnp.broadcast_to(power[0:1], (16, at))
+        inverse[...] = jnp.exp2(-power[0:1])
 
 
 def deal(s_ref, b, quarter, value, outs):
@@ -628,11 +649,14 @@
     far = swap(near)
     ws1 = gathered(first)
 
-    def over_sequences(pieces, scale, riders=()):
-        return [spread(packed(pieces[j], scale[0:1], scale[8:9], riders), j) for j in range(1, parts)]
-
-    def chunks(pieces, scale, got, riders=()):
-        total, power = pieces[0], scale[0:1]
+    def payloads(pieces, scale, riders=()):
+        return [packed(pieces[j], scale[0], scale[1], riders) for j in range(1, parts)]
+
+    def over_sequences(payload):
+        return [spread(payload[j - 1], j) for j in range(1, parts)]
+
+    def totalled(pieces, scale, got, riders=()):
+        total, power = pieces[0], scale[0][0:1]
         if not apart:
             total = lax.psum_scatter(total, "dp", scatter_dimension=0, tiled=True)
             power = exponents(jnp.max(jnp.abs(total), axis=0, keepdims=True))
@@ -641,10 +665,12 @@
             value, other, more = unpacked(sent, [rider.shape[0] for rider in riders])
             total, power = total + value, jnp.maximum(power, other)
             riders = [one + two for one, two in zip(riders, more)]
-        power = power + (parts - 1).bit_length()
-        size = total.shape[0] // ctxs
-        rows = [piece(total, z ^ j, size) for j in range(ctxs)]
-        return rows[:1] + [packed(value, power, jnp.exp2(-power), riders) for value in rows[1:]], riders
+        return total, power + (parts - 1).bit_length(), riders
+
+    def chunks(totals, power, riders=()):
+        size = totals[0].shape[0] // ctxs
+        rows = [jnp.concatenate([piece(total, z ^ j, size) for total in totals], axis=1) for j in range(ctxs)]
+        return rows[:1] + [packed(value, power, jnp.exp2(-power), riders) for value in rows[1:]]
 
     def over_positions(cut):
         return [across(cut[j], j) for j in range(1, ctxs)]
@@ -701,17 +727,16 @@
     state_block = pl.BlockSpec((subs, states, inner), lambda b, s: (b, 0, 0))
     pre_block = pl.BlockSpec((subs, 8, inner), lambda b, s: (b, 0, 0))
 
-    normed, u, uh, conv, draw, delta, level, level_x, delta_x, hloc, pre, own_end = grid_call(
+    normed, u, uh, conv, per_head, hloc, pre, own_end = grid_call(
         functools.partial(front_body, parts, inner, states, quarter),
         (count,),
         [own_spec, part_spec, part_spec, whole((16, model)), whole((1, model)), whole((4, wide)),
          whole((1, wide)), whole((1, 128)), whole((1, 128))] + [whole((shard, wide + 128))] * parts,
-        [rows_spec(model), rows_spec(wide), whole((8, wide)), rows_spec(wide), rows_spec(128), rows_spec(128),
-         rows_spec(128), rows_spec(inner), rows_spec(inner), whole((last + 1, states, inner)),
-         whole((last + 1, 8, inner)), whole((states, inner))],
+        [rows_spec(model), rows_spec(wide), whole((8, wide)), rows_spec(wide), rows_spec(128),
+         whole((last + 1, states, inner)), whole((last + 1, 8, inner)), whole((states, inner))],
         [shaped((tokens, model), BF16), shaped((tokens, wide)), shaped((8, wide)), shaped((tokens, wide)),
-         shaped((tokens, 128)), shaped((tokens, 128)), shaped((tokens, 128)), shaped((tokens, inner)),
-         shaped((tokens, inner)), shaped((last + 1, states, inner)), shaped((last + 1, 8, inner)), shaped((states, inner))],
+         shaped((tokens, 128)), shaped((last + 1, states, inner)), shaped((last + 1, 8, inner)),
+         shaped((states, inner))],
         [pltpu.VMEM((16, model), BF16), pltpu.VMEM((8 + BLOCK, wide), F32), pltpu.VMEM((states, inner), F32),
          pltpu.VMEM((8, inner), F32), pltpu.VMEM((384, inner), BF16)],
         name="front",
@@ -730,12 +755,13 @@
     (inside,) = grid_call(
         functools.partial(within_body, inner, states),
         (count,),
-        [rows_spec(wide), rows_spec(128), rows_spec(inner), rows_spec(inner)],
+        [rows_spec(wide), rows_spec(128)],
         [rows_spec(inner)],
         [shaped((tokens, inner))],
+        [pltpu.VMEM((384, inner), BF16)] * 2,
         name="within",
         limit=20 << 20,
-    )(scalars, *streamed(conv, level, level_x, delta_x))
+    )(scalars, *streamed(conv, per_head))
 
     gate, gated_grad, branch_grad = grid_call(
         functools.partial(gates_body, parts, quarter),
@@ -750,13 +776,14 @@
     y, sums = grid_call(
         functools.partial(output_body, inner, states),
         (count,),
-        [rows_spec(wide), rows_spec(inner), rows_spec(inner), rows_spec(inner), rows_spec(inner), state_block,
+        [rows_spec(wide), rows_spec(128), rows_spec(inner), rows_spec(inner), rows_spec(inner), state_block,
          pre_block, whole((states, inner)), whole((1, inner)), whole((1, inner))],
         [rows_spec(inner), pl.BlockSpec((16, BLOCK), lambda b, s: (0, b))],
         [shaped((tokens, inner)), shaped((16, tokens))],
+        [pltpu.VMEM((384, inner), BF16)],
         name="output",
         limit=20 << 20,
-    )(scalars, *streamed(conv, level_x), inside, gate, gated_grad, *streamed(hloc), pre, carried, skip_row, ggain_row)
+    )(scalars, *streamed(conv, per_head), inside, gate, gated_grad, *streamed(hloc), pre, carried, skip_row, ggain_row)
 
     corner = [(n, ((n // tps) ^ 1) * tps + (n % tps + 1) % tps) for n in range(ctxs * tps)]
     all_sums = [sums, swap(sums), across(sums, 1), lax.ppermute(sums, ("ctx", "tp"), corner)]
@@ -768,16 +795,16 @@
     gated, gate_grad, out_grad, gloc, own_start, turn_cols = grid_call(
         functools.partial(turn_body, inner, states, 2 * tps * inner),
         (count,),
-        [back(wide), back(inner), back(inner), back(inner), back(inner),
+        [back(wide), back(128), back(inner), back(inner), back(inner),
          back_sums, back_sums, back_sums, back_sums, whole((1, inner)), whole((1, inner))],
         [back(inner), back(inner), back(inner), whole((last + 1, states, inner)), whole((states, inner)),
          whole((8, inner))],
         [kept((tokens, inner), BF16), kept((tokens, inner), BF16), kept((tokens, inner)),
          kept((last + 1, states, inner)), shaped((states, inner)), shaped((8, inner))],
-        [pltpu.VMEM((states, inner), F32)],
+        [pltpu.VMEM((states, inner), F32), pltpu.VMEM((384, inner), BF16)],
         name="turn",
         limit=20 << 20,
-    )(scalars, *streamed(conv, level_x), y, gate, gated_grad, *all_sums, skip_row, ggain_row)
+    )(scalars, *streamed(conv, per_head), y, gate, gated_grad, *all_sums, skip_row, ggain_row)
 
     returned = jnp.zeros_like(own_start)
     sending = own_start
@@ -795,30 +822,30 @@
             sources += [left, right]
         width = sum(right.shape[1] for right in rights)
         specs = [turned if n % 2 == 0 else whole(source.shape) for n, source in enumerate(sources)]
-        *pieces, scale = grid_call(
+        *pieces, powers, inverse = grid_call(
             functools.partial(grads_body, parts, [(n, n + 1) for n in range(0, len(sources), 2)]),
             (parts,),
             specs,
-            [whole((shard, width))] * parts + [whole((16, width))],
-            [shaped((shard, width))] * parts + [shaped((16, width))],
+            [whole((shard, width))] * parts + [whole((16, width)), whole((1, width))],
+            [shaped((shard, width))] * parts + [shaped((16, width)), shaped((1, width))],
             [pltpu.VMEM((8, width), F32)],
             name=name,
         )(scalars, *sources)
-        return pieces, scale
+        return pieces, (powers, inverse)
 
     early, early_scale = grads([normed, branch_grad], [gate_grad, gated], "grad_early")
-    early_got = over_sequences(early, early_scale)
+    early_got = over_sequences(payloads(early, early_scale))
     early, out_grad = lax.optimization_barrier((early, out_grad))
 
     zed, dbc = grid_call(
         functools.partial(back_body, inner, states),
         (count,),
-        [rows_spec(wide), rows_spec(128), rows_spec(inner), rows_spec(inner), rows_spec(inner), state_block,
-         pre_block, whole((states, inner))],
+        [rows_spec(wide), rows_spec(128), rows_spec(inner), state_block, pre_block, whole((states, inner))],
         [rows_spec(inner), rows_spec(2 * states)],
         [shaped((tokens, inner)), shaped((tokens, 2 * states))],
+        [pltpu.VMEM((384, inner), BF16)] * 2,
         name="back",
-    )(scalars, conv, level, level_x, delta_x, out_grad, hloc, pre, carried)
+    )(scalars, conv, per_head, out_grad, hloc, pre, carried)
 
     gated_later, zed = lax.optimization_barrier((gated, zed))
     branch = grid_call(
@@ -832,7 +859,7 @@
     )(scalars, gated_later, *ws2)
 
     returned, early_got, branch = lax.optimization_barrier((returned, early_got, branch))
-    front_rows = halfway // 2
+    front_rows = halfway // 4
     branch_give = swap(branch[3])
     branch_theirs = [branch[1][:front_rows] + branch_give[:front_rows], branch[1][front_rows:] + branch_give[front_rows:]]
     returned, branch_theirs = lax.optimization_barrier((returned, branch_theirs))
@@ -855,52 +882,61 @@
     zed, ends, dbc_keep, dbc_give = grid_call(
         functools.partial(meet_body, inner, states),
         (count,),
-        [rows_spec(wide), rows_spec(inner), rows_spec(inner), rows_spec(inner), rows_spec(2 * states), all_states,
+        [rows_spec(wide), rows_spec(128), rows_spec(inner), rows_spec(2 * states), all_states,
          all_pre, all_states, whole((states, inner)), whole((states, inner))],
         [rows_spec(inner), rows_spec(inner, 8), whole((half_rows, 2 * states)), whole((half_rows, 2 * states))],
         [shaped((tokens, inner)), shaped((8 * count, inner)), shaped((half_rows, 2 * states)),
          shaped((half_rows, 2 * states))],
+        [pltpu.VMEM((384, inner), BF16)] * 2,
         name="meet",
         limit=20 << 20,
-    )(scalars, *streamed(conv, level_x, delta_x, zed, dbc, hloc, pre, gloc), returned, carried)
+    )(scalars, *streamed(conv, per_head, zed, dbc, hloc, pre, gloc), returned, carried)
 
     zed, ends, dbc_keep, dbc_give, branch_back = lax.optimization_barrier((zed, ends, dbc_keep, dbc_give, branch_back))
-    early_cut, _ = chunks(early, early_scale, early_got)
+    early_total, early_power, _ = totalled(early, early_scale, early_got)
+    early_cut = chunks([early_total], early_power)
     early_far = over_positions(early_cut)
     signal_pre, tail, head, raw_grad, head_cols, signal_cols = grid_call(
         functools.partial(join_body, inner),
         (count,),
-        [back(inner), back(128), back(inner), back(128), back(inner), back(inner), back(inner), back(inner, 8)]
+        [back(inner), back(128), back(inner), back(inner), back(inner), back(inner, 8)]
         + back_lanes(inner, lambda s: 0)
         + [table(4, inner, lambda s: 0), whole((1, 128)), whole((1, inner))],
         [back(inner), whole((8, inner)), whole((8, inner)), back(128), whole((8, 128)), whole((8, inner))],
         [shaped((tokens, inner), BF16), shaped((8, inner)), shaped((8, inner)), shaped((tokens, 128)),
          shaped((8, 128)), shaped((8, inner))],
         [pltpu.VMEM((3 * inner, 128), BF16), pltpu.VMEM((BLOCK + 8, inner), F32),
-         pltpu.VMEM((BLOCK + 8, inner), F32)],
+         pltpu.VMEM((BLOCK + 8, inner), F32), pltpu.VMEM((384, inner), BF16)],
         name="join",
         limit=20 << 20,
-    )(scalars, *streamed(conv, delta, delta_x, draw, out_grad, y), zed, ends, *streamed(u, u), uh, taps_x, rate_row, skip_row)
+    )(scalars, *streamed(conv, per_head, out_grad, y), zed, ends, *streamed(u, u), uh, taps_x, rate_row, skip_row)
 
     head, early_far = lax.optimization_barrier((head, early_far))
-
-    ahead = jnp.where(hi < pairs - 1, along(head, -2), 0.0)
+    early_sum = settled(early_cut[0], decoded(early_far))
+    out_sum = jnp.concatenate([part[:, inner:] for part in early_sum], axis=1)
+    gate_sum = jnp.concatenate([part[:, :inner] for part in early_sum], axis=1)
+
+    ahead, out_sum, gate_sum = lax.optimization_barrier((along(head, -2), out_sum, gate_sum))
+    ahead = jnp.where(hi < pairs - 1, ahead, 0.0)
     for k in range(3):
         tail = tail + taps_x[k, :inner] * jnp.concatenate([jnp.zeros((5 + k, inner), F32), ahead[: 3 - k]])
     signal_pre = lax.dynamic_update_slice_in_dim(signal_pre, tail.astype(BF16), tokens - 8, 0)
 
+    dbc = dbc_keep + swap(dbc_give)
+    signal_pre, dbc = lax.optimization_barrier((signal_pre, dbc))
+    dbc_back = across(lax.dynamic_slice_in_dim(dbc, (1 - lo) * states, states, 1), 1)
     signal_small = jnp.concatenate([signal_cols, turn_cols])
     signal, signal_scale = grads([normed], [signal_pre], "grad_signal")
-    signal_got = over_sequences(signal, signal_scale, [signal_small])
-
-    dbc = dbc_keep + swap(dbc_give)
-    dbc_back = across(lax.dynamic_slice_in_dim(dbc, (1 - lo) * states, states, 1), 1)
-    branch_later, dbc_back = lax.optimization_barrier((branch_theirs[1], dbc_back))
+    signal, dbc_back = lax.optimization_barrier((signal, dbc_back))
+    signal_payload = payloads(signal, signal_scale, [signal_small])
+
     dbc = mine(dbc, 1, states) + dbc_back
     dbc_other = swap(dbc)
     head_rows = jnp.where(core == 0, dbc[:8], dbc_other[:8])
     head_conv = lax.dynamic_slice(conv, (0, inner + lo * states), (8, states))
     state_ahead = along(head_rows * slope(head_conv, jax.nn.sigmoid(head_conv)), -2)
+    branch_later, state_ahead, signal_payload = lax.optimization_barrier((branch_theirs[1], state_ahead, signal_payload))
+    signal_got = over_sequences(signal_payload)
     def back_own(b, s):
         return jnp.clip(count - 1 - b - s[LO] * 2 * quarter, 0, 2 * quarter - 1), 0
 
@@ -931,25 +967,20 @@
 
     folds = model // 128
     extra_small = jnp.concatenate(
-        [state_cols, head_cols, feature_cols[0].reshape(folds, 128), jnp.zeros((16 - folds % 16, 128), F32)]
+        [state_cols[:5], head_cols[:2], jnp.zeros((1, 128), F32), feature_cols[0].reshape(folds, 128)]
     )
     extra, extra_scale = grads([normed], [extra_pre], "grad_extra")
     extra, feature_theirs = lax.optimization_barrier((extra, feature_theirs))
     feature_power = exponents(jnp.max(jnp.abs(feature_theirs), axis=0, keepdims=True))
     feature_back = across(packed(feature_theirs, feature_power, jnp.exp2(-feature_power)), 1)
-    extra_got = over_sequences(extra, extra_scale, [extra_small])
+    signal_total, signal_power, (signal_here,) = totalled(signal, signal_scale, signal_got, [signal_small])
+    extra_got = over_sequences(payloads(extra, extra_scale, [extra_small]))
     extra_got, feature_back = lax.optimization_barrier((extra_got, feature_back))
-    signal_got, extra_got = lax.optimization_barrier((signal_got, extra_got))
-    signal_cut, (signal_here,) = chunks(signal, signal_scale, signal_got, [signal_small])
-    signal_far = over_positions(signal_cut)
-    extra_cut, (extra_here,) = chunks(extra, extra_scale, extra_got, [extra_small])
-    extra_far = over_positions(extra_cut)
-    early_sum = settled(early_cut[0], decoded(early_far))
-    signal_sum = settled(signal_cut[0], decoded(signal_far, [16]))
-    signal_small = settled(signal_here, ridden(signal_far, [16]))
-    extra_rows = extra_small.shape[0]
-    extra_sum = settled(extra_cut[0], decoded(extra_far, [extra_rows]))
-    extra_small = settled(extra_here, ridden(extra_far, [extra_rows]))
+    extra_total, extra_power, (extra_here,) = totalled(extra, extra_scale, extra_got, [extra_small])
+    late_power = jnp.concatenate([signal_power, extra_power], axis=1)
+    small_here = jnp.concatenate([signal_here, extra_here], axis=1)
+    late_cut = chunks([signal_total, extra_total], late_power, [small_here])
+    late_far = over_positions(late_cut)
     feature_back = unpacked(feature_back)[0]
 
     def both_halves(value):
@@ -970,16 +1001,20 @@
         upstream + inverse * (scaled_grad - scaled_own * jnp.mean(scaled_grad * scaled_own, axis=1, keepdims=True))
     )
 
+    mixed, grad_hidden, late_far = lax.optimization_barrier((mixed, grad_hidden, late_far))
+    late_sum = settled(late_cut[0], decoded(late_far, [16]))
+    small_sum = settled(small_here, ridden(late_far, [16]))
+
     def side_by_side(pair):
         return jnp.concatenate(pair, axis=-1)
 
-    signal_small = side_by_side(signal_small)
-    state_small = side_by_side([part[:8] for part in extra_small])
-    heads_small = [part[8:10, HEAD0 : HEAD0 + heads] for part in extra_small]
+    signal_small = side_by_side([part[:, :inner] for part in small_sum])
+    state_small = side_by_side([part[:8, inner:] for part in small_sum])
+    heads_small = [part[5:7, inner + HEAD0 : inner + HEAD0 + heads] for part in small_sum]
     rate_all = -jnp.exp(log_rate)
     skip_sum = signal_small[9].reshape(2 * heads, inner // heads).sum(axis=1)
-    gain_here = (extra_small[0] + extra_small[1])[16 : 16 + folds].reshape(model)
-    state_here = jnp.stack([part[:, :HEAD0] for part in extra_sum])
+    gain_here = (small_sum[0] + small_sum[1])[8 : 8 + folds, inner:].reshape(model)
+    state_here = jnp.stack([part[:, inner : inner + HEAD0] for part in late_sum])
     gain_there, state_there = swap(gain_here), swap(state_here)
     gain_size = model // (dps * ctxs)
     gain_sum = piece(gain_here + gain_there, dp * ctxs + z, gain_size)
@@ -987,8 +1022,8 @@
         core == 0, jnp.stack([state_here, state_there], 1), jnp.stack([state_there, state_here], 1)
     )
     state_sum = jnp.transpose(in_order, (2, 0, 1, 3)).reshape(-1, 2 * states)
-    main_sum = jnp.stack([side_by_side([part[:, :inner] for part in early_sum]), side_by_side(signal_sum)], axis=1)
-    delta_sum = side_by_side([part[:, HEAD0 : HEAD0 + heads] for part in extra_sum])
+    main_sum = jnp.stack([gate_sum, side_by_side([part[:, :inner] for part in late_sum])], axis=1)
+    delta_sum = side_by_side([part[:, inner + HEAD0 : inner + HEAD0 + heads] for part in late_sum])
 
     return (
         mixed[None],
@@ -1005,7 +1040,7 @@
         side_by_side([part[1] for part in heads_small]) * rate_all,
         skip_sum,
         signal_small[8],
-        side_by_side([part[:, inner:] for part in early_sum]),
+        out_sum,
     )
 
 

time: 276 us -> 262 us (0.949)
  other arithmetic: 39.6 us -> 29.4 us
  starting transfers between devices: 53.5 us -> 49 us
    ppermute x16 -> x13, starting transfers between devices: 23 us -> 18.5 us  [across(): return lax.ppermute(value, 'ctx', [(i, i ^ j) for i in range(ctxs)])]
    exp2 x7, other arithmetic: 4.38 us -> 0.12 us  [unpacked(): return (sent[:rows].astype(F32) * jnp.exp2(power), power, more)]
    ppermute x16 -> x13, waiting for transfers between devices: 14.2 us -> 15.9 us  [across(): return lax.ppermute(value, 'ctx', [(i, i ^ j) for i in range(ctxs)])]
  transfers between devices with their start and end apart: 51 -> 48, of which waited for: 15 -> 17; matrix products, arithmetic and copies ran while one was open for 15% -> 11% of each run, Pallas kernels for 32% -> 34%
where the time goes in v4:
time: 262 us; the launch traced here: 260 us
  Pallas kernels  112 us (43%)
  waiting for transfers between devices  49.3 us (19%)
  starting transfers between devices  49 us (19%)
  other arithmetic  29.4 us (11%)
  local copies, waits for them, and re-layouts  18.1 us (7%)
    ppermute x15, waiting for transfers between devices, spread(): return lax.ppermute(value, 'dp', [(i, i ^ j) for i in range(dps)])  22 us
    pallas_call x3, Pallas kernels, grads(): grid_call(functools.partial(grads_body, parts, [(n, n + 1) for n in range...  20.1 us
    ppermute x15, starting transfers between devices, spread(): return lax.ppermute(value, 'dp', [(i, i ^ j) for i in range(dps)])  18.6 us
    ppermute x13, starting transfers between devices, across(): return lax.ppermute(value, 'ctx', [(i, i ^ j) for i in range(ctxs)])  18.5 us
    ppermute x13, waiting for transfers between devices, across(): return lax.ppermute(value, 'ctx', [(i, i ^ j) for i in range(ctxs)])  15.9 us
    pallas_call x1, Pallas kernels, per_device(): grid_call(functools.partial(front_body, parts, inner, states, quarter), (...  14.6 us
    pallas_call x1, Pallas kernels, per_device(): grid_call(functools.partial(back_body, inner, states), (count,), [rows_sp...  11.5 us
    pallas_call x1, Pallas kernels, per_device(): grid_call(functools.partial(feature_body, parts, quarter), (count,), [pl....  11.4 us
  transfers between devices with their start and end apart: 48, of which 17 were waited for; matrix products, arithmetic and copies ran while one was open for 11% of the time, Pallas kernels for 34%

profile of v4, /device:TPU:0, one launch (start us, length us, event | category | flops | bytes accessed | tf_op | source)
XLA Modules:
  0.0 260.3 jit_solution(11141292184711024128)
XLA Ops:
  1.6 3.3 %constant_dynamic-slice_fusion.15 = (bf16[256,1,512]{2,1,0:T(2,128)(2,1)}, bf16[256,1,512]{2,1,0:T(2,128)(2,1)S(1)}) fusion(bf16[256,2,1024]{2,1,0:T(2,128)(2,1)} %param.20, s32[]{:T(128)S(6)} %select_n.151, s32[]{:T(128)S(6)} %add.325), kind=kLoop, calls=%fused_computation.145 | loop fusion | bytes 1048584 | tf_op jit(solution)/shard_map/slice | solution.py:715
  6.1 3.9 %collective-permute-start.2 = (bf16[256,896]{1,0:T(8,128)(2,1)}, bf16[256,896]{1,0:T(8,128)(2,1)}, u32[]{:S(2)}, u32[]{:S(2)}) collective-permute-start(bf16[256,896]{1,0:T(8,128)(2,1)} %concatenate.146.rest_0_), channel_id=1, source_target_pairs={{0,24},{8,16},{16,8},{24,0},{1,25},{9,17},{17,9},{25,1},{2,26},{10... | collective-permute-start | bytes 1376264 | tf_op jit(solution)/shard_map/ppermute | solution.py:618
  10.7 2.1 collective-permute-start.3
  18.0 3.7 %collective-permute-done.2.rest_3_ = bf16[256,896]{1,0:T(8,128)(2,1)} collective-permute-done((bf16[256,896]{1,0:T(8,128)(2,1)}, bf16[256,896]{1,0:T(8,128)(2,1)}, u32[]{:S(2)}, u32[]{:S(2)}) %collective-permute-start.2) | collective-permute-done | bytes 458784 | tf_op jit(solution)/shard_map/ppermute | solution.py:618
  21.7 9.0 %collective-permute-done.1.rest_2_ = bf16[256,896]{1,0:T(8,128)(2,1)} collective-permute-done((bf16[256,896]{1,0:T(8,128)(2,1)}, bf16[256,896]{1,0:T(8,128)(2,1)}, u32[]{:S(2)}, u32[]{:S(2)}) %collective-permute-start.1) | collective-permute-done | bytes 458784 | tf_op jit(solution)/shard_map/ppermute | solution.py:618
  31.8 1.6 collective-permute-start.7
  35.3 1.7 collective-permute-start.11
  38.9 14.6 %front.1 = (bf16[1024,1024]{1,0:T(8,128)(2,1)}, f32[1024,768]{1,0:T(8,128)}, f32[8,768]{1,0:T(8,128)}, f32[1024,768]{1,0:T(8,128)}, f32[1024,128]{1,0:T(8,128)},...) custom-call(s32[10]{0:T(128)} %stack.79.s_ref, bf16[512,1024]{1,0:T(8,128)(2,1)} %bitcast.90, ...), custom_call_target="tpu_custom_call" | custom-call | tf_op jit(solution)/shard_map/front/pallas_call | solution.py:730
  53.6 4.7 %collective-permute-start.12 = (f32[128,512]{1,0:T(8,128)}, f32[128,512]{1,0:T(8,128)S(1)}, u32[]{:S(2)}, u32[]{:S(2)}) collective-permute-start(f32[128,512]{1,0:T(8,128)} %get-tuple-element.175), channel_id=1, source_target_pairs={{0,4},{2,6},{1,5},{3,7},{8,12},{10,14},{9,13},{11,15},{16,20},{18,... | collective-permute-start | bytes 786440 | tf_op jit(solution)/shard_map/ppermute | solution.py:613
  58.6 6.9 %within.1.yw = f32[1024,512]{1,0:T(8,128)S(1)} custom-call(s32[10]{0:T(128)S(1)} %copy-done.10, f32[1024,768]{1,0:T(8,128)} %get-tuple-element.163.co, f32[1024,128]{1,0:T(8,128)} %get-tuple-element.164.hd), custom_call_target="tpu_custom_call" | custom-call | tf_op jit(solution)/shard_map/within/pallas_call | solution.py:755
  66.9 6.7 %gates.1 = (f32[1024,512]{1,0:T(8,128)S(1)}, f32[1024,512]{1,0:T(8,128)S(1)}, bf16[1024,1024]{1,0:T(8,128)(2,1)S(1)}) custom-call(s32[10]{0:T(128)S(1)} %copy-done.10, bf16[1024,1024]{1,0:T(8,128)(2,1)} %get-tuple-element.165.normed.refs_0_, bf16[512,1024]{1,0:T(8,128)(2,1)} %bitcast.92, bf16[256,1024]{1,0:T(8,128)(2,1)} %collective-permute-done.7.near, ...), custom_call_target="tpu_custom_call" | custom-call | tf_op jit(solution)/shard_map/gates/pallas_call | solution.py:766
  74.9 6.5 %output.1 = (f32[1024,512]{1,0:T(8,128)S(1)}, f32[16,1024]{1,0:T(8,128)S(1)}) custom-call(s32[10]{0:T(128)S(1)} %copy-done.10, f32[1024,768]{1,0:T(8,128)} %get-tuple-element.163.co, f32[1024,128]{1,0:T(8,128)} %get-tuple-element.164.hd, f32[1024,512]{1,0:T(8,128)S(1)} %within.1.yw, f32[1024,512]{1,0:T(8,128)S(1)} %get-tuple-element.171.gate, ...), custom_call_target="tpu_custom_call" | custom-call | tf_op jit(solution)/shard_map/output/pallas_call | solution.py:776
  81.9 1.4 collective-permute-start.14
  83.3 2.2 collective-permute-done.15.sums3
  85.6 1.7 collective-permute-done.14.sums2
  87.3 8.6 %turn.1 = (bf16[1024,512]{1,0:T(8,128)(2,1)}, bf16[1024,512]{1,0:T(8,128)(2,1)}, f32[1024,512]{1,0:T(8,128)}, f32[9,128,512]{2,1,0:T(8,128)}, f32[128,512]{1,0:T(8,128)S(1)}, /*index=5*/f32[8,512]{1,0:T(8,128)S(1)}) custom-call(s32[10]{0:T(128)S(1)} %copy-done.10, f32[1024,768]{1,0:T(8,128)} %get-tuple-element.163.co, f32[1024,128]{1,0:T(8,128)} %get-tuple-element.164.hd, ...), custom_call_target="tpu_custom_call" | custom-call | tf_op jit(solution)/shard_map/turn/pallas_call | solution.py:795
  95.9 9.0 %grad_early.1 = (f32[256,1024]{1,0:T(8,128)}, f32[256,1024]{1,0:T(8,128)}, f32[256,1024]{1,0:T(8,128)}, f32[256,1024]{1,0:T(8,128)}, f32[16,1024]{1,0:T(8,128)}, /*index=5*/f32[1,1024]{1,0:T(1,128)}) custom-call(s32[10]{0:T(128)} %stack.79.s_ref, bf16[1024,1024]{1,0:T(8,128)(2,1)} %get-tuple-element.165.normed.refs_0_, ...), custom_call_target="tpu_custom_call" | custom-call | tf_op jit(solution)/shard_map/grad_early/pallas_call | solution.py:825
  105.8 2.2 multiply_convert_fusion.1
  109.3 1.7 collective-permute-start.19
  112.8 1.5 collective-permute-start.16
  114.3 11.5 %back.1 = (f32[1024,512]{1,0:T(8,128)}, f32[1024,256]{1,0:T(8,128)}) custom-call(s32[10]{0:T(128)} %stack.79.s_ref, f32[1024,768]{1,0:T(8,128)} %get-tuple-element.163.co, f32[1024,128]{1,0:T(8,128)} %get-tuple-element.164.hd, f32[1024,512]{1,0:T(8,128)} %get-tuple-element.189.og, f32[9,128,512]{2,1,0:T(8,128)} %get-tuple-element.173.hloc, ...), custom_call_target="tpu_custom_call" | custom-call | tf_op jit(solution)/shard_map/back/pallas_call | solution.py:840
  125.8 7.3 %branch.1 = (f32[256,1024]{1,0:T(8,128)}, f32[256,1024]{1,0:T(8,128)}, f32[256,1024]{1,0:T(8,128)}, f32[256,1024]{1,0:T(8,128)}) custom-call(s32[10]{0:T(128)} %stack.79.s_ref, bf16[1024,512]{1,0:T(8,128)(2,1)} %get-tuple-element.191.refs_3_.gated, bf16[256,1024]{1,0:T(8,128)(2,1)} %copy-done.14, bf16[256,1024]{1,0:T(8,128)(2,1)} %copy-done.18, ...), custom_call_target="tpu_custom_call" | custom-call | tf_op jit(solution)/shard_map/branch/pallas_call | solution.py:851
  133.0 3.7 %collective-permute-done.18 = f16[272,1024]{1,0:T(8,128)(2,1)} collective-permute-done((f16[272,1024]{1,0:T(8,128)(2,1)S(1)}, f16[272,1024]{1,0:T(8,128)(2,1)}, u32[]{:S(2)}, u32[]{:S(2)}) %collective-permute-start.18) | collective-permute-done | bytes 557088 | tf_op jit(solution)/shard_map/ppermute | solution.py:618
  137.7 1.8 multiply_add_fusion
  141.5 2.1 collective-permute-start.24
  143.6 1.5 collective-permute-start.23
  145.1 8.3 %meet.1 = (f32[1024,512]{1,0:T(8,128)S(1)}, f32[32,512]{1,0:T(8,128)S(1)}, f32[512,256]{1,0:T(8,128)S(1)}, f32[512,256]{1,0:T(8,128)S(1)}) custom-call(s32[10]{0:T(128)S(1)} %copy-done.11, f32[1024,768]{1,0:T(8,128)} %get-tuple-element.163.co, f32[1024,128]{1,0:T(8,128)} %get-tuple-element.164.hd, f32[1024,512]{1,0:T(8,128)} %get-tuple-element.198.z, ...), custom_call_target="tpu_custom_call" | custom-call | tf_op jit(solution)/shard_map/meet/pallas_call | solution.py:882
  154.2 10.0 %join.1 = (bf16[1024,512]{1,0:T(8,128)(2,1)S(1)}, f32[8,512]{1,0:T(8,128)S(1)}, f32[8,512]{1,0:T(8,128)S(1)}, f32[1024,128]{1,0:T(8,128)S(1)}, f32[8,128]{1,0:T(8,128)S(1)}, /*index=5*/f32[8,512]{1,0:T(8,128)S(1)}) custom-call(s32[10]{0:T(128)S(1)} %copy-done.11, f32[1024,768]{1,0:T(8,128)} %get-tuple-element.163.co, f32[1024,128]{1,0:T(8,128)} %get-tuple-element.164.hd, ...), custom_call_target="tpu_custom_call" | custom-call | tf_op jit(solution)/shard_map/join/pallas_call | solution.py:899
  166.6 4.5 %collective-permute-done.26 = f32[8,512]{1,0:T(8,128)S(1)} collective-permute-done((f32[8,512]{1,0:T(8,128)S(1)}, f32[8,512]{1,0:T(8,128)S(1)}, u32[]{:S(2)}, u32[]{:S(2)}) %collective-permute-start.26) | collective-permute-done | bytes 16416 | tf_op jit(solution)/shard_map/ppermute | solution.py:613
  172.4 6.1 %grad_signal.1 = (f32[256,512]{1,0:T(8,128)}, f32[256,512]{1,0:T(8,128)}, f32[256,512]{1,0:T(8,128)}, f32[256,512]{1,0:T(8,128)}, f32[16,512]{1,0:T(8,128)}, /*index=5*/f32[1,512]{1,0:T(1,128)}) custom-call(s32[10]{0:T(128)} %stack.79.s_ref, bf16[1024,1024]{1,0:T(8,128)(2,1)} %get-tuple-element.165.normed.refs_0_, bf16[1024,512]{1,0:T(8,128)(2,1)} %fusion.20.refs_1_.mg), custom_call_target="tpu_custom_call" | custom-call | tf_op jit(solution)/shard_map/grad_signal/pallas_call | solution.py:825
  179.4 1.6 multiply_convert_fusion.4
  181.7 1.6 collective-permute-start.30
  184.4 3.7 %collective-permute-done.30.ahead = f32[8,128]{1,0:T(8,128)S(1)} collective-permute-done((f32[8,128]{1,0:T(8,128)S(1)}, f32[8,128]{1,0:T(8,128)S(1)}, u32[]{:S(2)}, u32[]{:S(2)}) %collective-permute-start.30) | collective-permute-done | bytes 4128 | tf_op jit(solution)/shard_map/ppermute | solution.py:613
  188.1 1.6 collective-permute-start.31
  189.8 1.5 collective-permute-start.32
  193.3 11.4 %feature.1 = (f32[256,1024]{1,0:T(8,128)}, f32[256,1024]{1,0:T(8,128)}, f32[256,1024]{1,0:T(8,128)}, f32[256,1024]{1,0:T(8,128)}, bf16[1024,128]{1,0:T(8,128)(2,...) custom-call(s32[10]{0:T(128)} %stack.79.s_ref, bf16[512,1024]{1,0:T(8,128)(2,1)} %bitcast.91, ...), custom_call_target="tpu_custom_call" | custom-call | tf_op jit(solution)/shard_map/feature/pallas_call | solution.py:949
  204.8 1.4 collective-permute-done.33
  207.8 5.0 %grad_extra.1 = (f32[256,128]{1,0:T(8,128)}, f32[256,128]{1,0:T(8,128)}, f32[256,128]{1,0:T(8,128)}, f32[256,128]{1,0:T(8,128)}, f32[16,128]{1,0:T(8,128)}, /*index=5*/f32[1,128]{1,0:T(1,128)}) custom-call(s32[10]{0:T(128)} %stack.79.s_ref, bf16[1024,1024]{1,0:T(8,128)(2,1)} %get-tuple-element.165.normed.refs_0_, bf16[1024,128]{1,0:T(8,128)(2,1)} %get-tuple-element.257.refs_1_), custom_call_target="tpu_custom_call" | custom-call | tf_op jit(solution)/shard_map/grad_extra/pallas_call | solution.py:825
  217.1 1.7 collective-permute-start.41
  219.9 1.6 collective-permute-start.40
  221.5 1.4 collective-permute-start.39
  223.5 1.9 collective-permute-done.40
  225.4 1.6 collective-permute-done.39
  227.3 4.9 %collective-permute-done.41 = f16[272,1024]{1,0:T(8,128)(2,1)S(1)} collective-permute-done((f16[272,1024]{1,0:T(8,128)(2,1)S(1)}, f16[272,1024]{1,0:T(8,128)(2,1)S(1)}, u32[]{:S(2)}, u32[]{:S(2)}) %collective-permute-start.41) | collective-permute-done | bytes 557088 | tf_op jit(solution)/shard_map/ppermute | solution.py:610
  235.2 1.8 collective-permute-start.45
  239.6 1.5 maximum_select_fusion.1
  241.1 1.6 maximum_select_fusion
  243.8 7.5 %collective-permute-done.44 = f16[112,640]{1,0:T(8,128)(2,1)S(1)} collective-permute-done((f16[112,640]{1,0:T(8,128)(2,1)S(1)}, f16[112,640]{1,0:T(8,128)(2,1)S(1)}, u32[]{:S(2)}, u32[]{:S(2)}) %collective-permute-start.44) | collective-permute-done | bytes 143392 | tf_op jit(solution)/shard_map/ppermute | solution.py:610
  (302 shorter events, 54.5 us)
Async XLA Ops:
  6.1 15.6 %collective-permute-start.2 = (bf16[256,896]{1,0:T(8,128)(2,1)}, bf16[256,896]{1,0:T(8,128)(2,1)}, u32[]{:S(2)}, u32[]{:S(2)}) collective-permute-start(bf16[256,896]{1,0:T(8,128)(2,1)} %concatenate.146.rest_0_), channel_id=1, source_target_pairs={{0,24},{8,16},{16,8},{24,0},{1,25},{9,17},{17,9},{25,1},{2,26},{10... | collective-permute-start | bytes 1376264 | tf_op jit(solution)/shard_map/ppermute | solution.py:618
  10.0 20.7 %collective-permute-start.1 = (bf16[256,896]{1,0:T(8,128)(2,1)}, bf16[256,896]{1,0:T(8,128)(2,1)}, u32[]{:S(2)}, u32[]{:S(2)}) collective-permute-start(bf16[256,896]{1,0:T(8,128)(2,1)} %concatenate.146.rest_0_), channel_id=1, source_target_pairs={{0,16},{8,24},{16,0},{24,8},{1,17},{9,25},{17,1},{25,9},{2,18},{10... | collective-permute-start | bytes 1376264 | tf_op jit(solution)/shard_map/ppermute | solution.py:618
  10.5 20.5 %collective-permute-start = (bf16[256,896]{1,0:T(8,128)(2,1)}, bf16[256,896]{1,0:T(8,128)(2,1)}, u32[]{:S(2)}, u32[]{:S(2)}) collective-permute-start(bf16[256,896]{1,0:T(8,128)(2,1)} %concatenate.146.rest_0_), channel_id=1, source_target_pairs={{0,8},{8,0},{16,24},{24,16},{1,9},{9,1},{17,25},{25,17},{2,10},{10... | collective-permute-start | bytes 1376264 | tf_op jit(solution)/shard_map/ppermute | solution.py:618
  10.7 20.2 %collective-permute-start.3 = (bf16[256,1024]{1,0:T(8,128)(2,1)S(1)}, bf16[256,1024]{1,0:T(8,128)(2,1)}, u32[]{:S(2)}, u32[]{:S(2)}) collective-permute-start(bf16[256,1024]{1,0:T(8,128)(2,1)S(1)} %get-tuple-element.339), channel_id=1, source_target_pairs={{0,2},{2,0},{4,6},{6,4},{1,3},{3,1},{5,7},{7,5},{8,10},{10,8},{12,... | collective-permute-start | bytes 1572872 | tf_op jit(solution)/shard_map/ppermute | solution.py:610
  16.2 17.1 %collective-permute-start.5 = (bf16[16,1024]{1,0:T(8,128)(2,1)S(1)}, bf16[16,1024]{1,0:T(8,128)(2,1)S(1)}, u32[]{:S(2)}, u32[]{:S(2)}) collective-permute-start(bf16[16,1024]{1,0:T(8,128)(2,1)S(1)} %slice_bitcast_fusion.2), channel_id=1, source_target_pairs={{2,4},{3,7},{10,12},{11,15},{18,20},{19,23},{26,28},{27,31}} | collective-permute-start | bytes 98312 | tf_op jit(solution)/shard_map/ppermute | solution.py:711
  30.9 8.0 %collective-permute-start.4 = (bf16[256,1024]{1,0:T(8,128)(2,1)}, bf16[256,1024]{1,0:T(8,128)(2,1)}, u32[]{:S(2)}, u32[]{:S(2)}) collective-permute-start(bf16[256,1024]{1,0:T(8,128)(2,1)} %collective-permute-done.3.near), channel_id=1, source_target_pairs={{0,1},{1,0},{2,3},{3,2},{4,5},{5,4},{6,7},{7,6},{8,9},{9,8},{10,11... | collective-permute-start | bytes 1572872 | tf_op jit(solution)/shard_map/ppermute | solution.py:607
  31.8 21.8 %collective-permute-start.7 = (bf16[256,1024]{1,0:T(8,128)(2,1)}, bf16[256,1024]{1,0:T(8,128)(2,1)}, u32[]{:S(2)}, u32[]{:S(2)}) collective-permute-start(bf16[256,1024]{1,0:T(8,128)(2,1)} %constant_dynamic-slice_fusion.12), channel_id=1, source_target_pairs={{0,2},{2,0},{4,6},{6,4},{1,3},{3,1},{5,7},{7,5},{8,10},{10,8},{12,... | collective-permute-start | bytes 1572872 | tf_op jit(solution)/shard_map/ppermute | solution.py:610
  33.4 1.2 collective-permute-start.6
  35.3 30.2 %collective-permute-start.11 = (bf16[256,1024]{1,0:T(8,128)(2,1)S(1)}, bf16[256,1024]{1,0:T(8,128)(2,1)S(1)}, u32[]{:S(2)}, u32[]{:S(2)}) collective-permute-start(bf16[256,1024]{1,0:T(8,128)(2,1)S(1)} %pad_maximum_fusion.13.rest_0_.rest_4_), channel_id=1, source_target_pairs={{0,24},{8,16},{16,8},{24,0},{1,25},{9,17},{17,9},{25,1},{2,26},{10... | collective-permute-start | bytes 1572872 | tf_op jit(solution)/shard_map/ppermute | solution.py:618
  37.0 28.5 %collective-permute-start.10 = (bf16[256,1024]{1,0:T(8,128)(2,1)S(1)}, bf16[256,1024]{1,0:T(8,128)(2,1)S(1)}, u32[]{:S(2)}, u32[]{:S(2)}) collective-permute-start(bf16[256,1024]{1,0:T(8,128)(2,1)S(1)} %pad_maximum_fusion.13.rest_0_.rest_4_), channel_id=1, source_target_pairs={{0,16},{8,24},{16,0},{24,8},{1,17},{9,25},{17,1},{25,9},{2,18},{10... | collective-permute-start | bytes 1572872 | tf_op jit(solution)/shard_map/ppermute | solution.py:618
  38.3 27.2 %collective-permute-start.9 = (bf16[256,1024]{1,0:T(8,128)(2,1)S(1)}, bf16[256,1024]{1,0:T(8,128)(2,1)S(1)}, u32[]{:S(2)}, u32[]{:S(2)}) collective-permute-start(bf16[256,1024]{1,0:T(8,128)(2,1)S(1)} %pad_maximum_fusion.13.rest_0_.rest_4_), channel_id=1, source_target_pairs={{0,8},{8,0},{16,24},{24,16},{1,9},{9,1},{17,25},{25,17},{2,10},{10... | collective-permute-start | bytes 1572872 | tf_op jit(solution)/shard_map/ppermute | solution.py:618
  53.6 12.0 %collective-permute-start.8 = (bf16[256,1024]{1,0:T(8,128)(2,1)}, bf16[256,1024]{1,0:T(8,128)(2,1)S(1)}, u32[]{:S(2)}, u32[]{:S(2)}) collective-permute-start(bf16[256,1024]{1,0:T(8,128)(2,1)} %collective-permute-done.7.near), channel_id=1, source_target_pairs={{0,1},{1,0},{2,3},{3,2},{4,5},{5,4},{6,7},{7,6},{8,9},{9,8},{10,11... | collective-permute-start | bytes 1572872 | tf_op jit(solution)/shard_map/ppermute | solution.py:607
  53.6 21.3 %collective-permute-start.12 = (f32[128,512]{1,0:T(8,128)}, f32[128,512]{1,0:T(8,128)S(1)}, u32[]{:S(2)}, u32[]{:S(2)}) collective-permute-start(f32[128,512]{1,0:T(8,128)} %get-tuple-element.175), channel_id=1, source_target_pairs={{0,4},{2,6},{1,5},{3,7},{8,12},{10,14},{9,13},{11,15},{16,20},{18,... | collective-permute-start | bytes 786440 | tf_op jit(solution)/shard_map/ppermute | solution.py:613
  81.4 4.2 %collective-permute-start.15 = (f32[16,1024]{1,0:T(8,128)S(1)}, f32[16,1024]{1,0:T(8,128)S(1)}, u32[]{:S(2)}, u32[]{:S(2)}) collective-permute-start(f32[16,1024]{1,0:T(8,128)S(1)} %get-tuple-element.177.sums), channel_id=1, source_target_pairs={{0,3},{1,2},{2,1},{3,0},{4,7},{5,6},{6,5},{7,4},{8,11},{9,10},{10,... | collective-permute-start | bytes 196616 | tf_op jit(solution)/shard_map/ppermute | solution.py:789
  81.9 5.4 %collective-permute-start.14 = (f32[16,1024]{1,0:T(8,128)S(1)}, f32[16,1024]{1,0:T(8,128)S(1)}, u32[]{:S(2)}, u32[]{:S(2)}) collective-permute-start(f32[16,1024]{1,0:T(8,128)S(1)} %get-tuple-element.177.sums), channel_id=1, source_target_pairs={{0,2},{2,0},{4,6},{6,4},{1,3},{3,1},{5,7},{7,5},{8,10},{10,8},{12,... | collective-permute-start | bytes 196616 | tf_op jit(solution)/shard_map/ppermute | solution.py:610
  83.3 4.0 %collective-permute-start.13 = (f32[16,1024]{1,0:T(8,128)S(1)}, f32[16,1024]{1,0:T(8,128)S(1)}, u32[]{:S(2)}, u32[]{:S(2)}) collective-permute-start(f32[16,1024]{1,0:T(8,128)S(1)} %get-tuple-element.177.sums), channel_id=1, source_target_pairs={{0,1},{1,0},{2,3},{3,2},{4,5},{5,4},{6,7},{7,6},{8,9},{9,8},{10,11... | collective-permute-start | bytes 196616 | tf_op jit(solution)/shard_map/ppermute | solution.py:607
  109.3 23.7 %collective-permute-start.19 = (f16[272,1024]{1,0:T(8,128)(2,1)}, f16[272,1024]{1,0:T(8,128)(2,1)}, u32[]{:S(2)}, u32[]{:S(2)}) collective-permute-start(f16[272,1024]{1,0:T(8,128)(2,1)} %get-tuple-element.401), channel_id=1, source_target_pairs={{0,24},{8,16},{16,8},{24,0},{1,25},{9,17},{17,9},{25,1},{2,26},{10... | collective-permute-start | bytes 1671176 | tf_op jit(solution)/shard_map/ppermute | solution.py:618
  111.0 25.8 %collective-permute-start.18 = (f16[272,1024]{1,0:T(8,128)(2,1)S(1)}, f16[272,1024]{1,0:T(8,128)(2,1)}, u32[]{:S(2)}, u32[]{:S(2)}) collective-permute-start(f16[272,1024]{1,0:T(8,128)(2,1)S(1)} %get-tuple-element.402), channel_id=1, source_target_pairs={{0,16},{8,24},{16,0},{24,8},{1,17},{9,25},{17,1},{25,9},{2,18},{10... | collective-permute-start | bytes 1671176 | tf_op jit(solution)/shard_map/ppermute | solution.py:618
  112.2 24.6 %collective-permute-start.17 = (f16[272,1024]{1,0:T(8,128)(2,1)S(1)}, f16[272,1024]{1,0:T(8,128)(2,1)}, u32[]{:S(2)}, u32[]{:S(2)}) collective-permute-start(f16[272,1024]{1,0:T(8,128)(2,1)S(1)} %get-tuple-element.403), channel_id=1, source_target_pairs={{0,8},{8,0},{16,24},{24,16},{1,9},{9,1},{17,25},{25,17},{2,10},{10... | collective-permute-start | bytes 1671176 | tf_op jit(solution)/shard_map/ppermute | solution.py:618
  112.8 20.3 %collective-permute-start.16 = (f32[128,512]{1,0:T(8,128)S(1)}, f32[128,512]{1,0:T(8,128)S(1)}, u32[]{:S(2)}, u32[]{:S(2)}) collective-permute-start(f32[128,512]{1,0:T(8,128)S(1)} %get-tuple-element.178), channel_id=1, source_target_pairs={{4,0},{6,2},{5,1},{7,3},{12,8},{14,10},{13,9},{15,11},{20,16},{22,... | collective-permute-start | bytes 786440 | tf_op jit(solution)/shard_map/ppermute | solution.py:613
  136.8 2.9 %collective-permute-start.21 = (f32[256,1024]{1,0:T(8,128)}, f32[256,1024]{1,0:T(8,128)S(1)}, u32[]{:S(2)}, u32[]{:S(2)}) collective-permute-start(f32[256,1024]{1,0:T(8,128)} %get-tuple-element.203), channel_id=1, source_target_pairs={{0,1},{1,0},{2,3},{3,2},{4,5},{5,4},{6,7},{7,6},{8,9},{9,8},{10,11... | collective-permute-start | bytes 3145736 | tf_op jit(solution)/shard_map/ppermute | solution.py:607
  139.9 13.6 %collective-permute-start.22 = (f32[64,1024]{1,0:T(8,128)S(1)}, f32[64,1024]{1,0:T(8,128)S(1)}, u32[]{:S(2)}, u32[]{:S(2)}) collective-permute-start(f32[64,1024]{1,0:T(8,128)S(1)} %slice_add_fusion.1), channel_id=1, source_target_pairs={{0,2},{2,0},{4,6},{6,4},{1,3},{3,1},{5,7},{7,5},{8,10},{10,8},{12,... | collective-permute-start | bytes 786440 | tf_op jit(solution)/shard_map/ppermute | solution.py:610
  140.6 23.6 %collective-permute-start.25 = (f16[80,1024]{1,0:T(8,128)(2,1)S(1)}, f16[80,1024]{1,0:T(8,128)(2,1)S(1)}, u32[]{:S(2)}, u32[]{:S(2)}) collective-permute-start(f16[80,1024]{1,0:T(8,128)(2,1)S(1)} %get-tuple-element.398), channel_id=1, source_target_pairs={{0,6},{2,4},{4,2},{6,0},{1,7},{3,5},{5,3},{7,1},{8,14},{10,12},{12... | collective-permute-start | bytes 491528 | tf_op jit(solution)/shard_map/ppermute | solution.py:610
  141.5 22.7 %collective-permute-start.24 = (f16[80,1024]{1,0:T(8,128)(2,1)S(1)}, f16[80,1024]{1,0:T(8,128)(2,1)S(1)}, u32[]{:S(2)}, u32[]{:S(2)}) collective-permute-start(f16[80,1024]{1,0:T(8,128)(2,1)S(1)} %get-tuple-element.399), channel_id=1, source_target_pairs={{0,4},{2,6},{4,0},{6,2},{1,5},{3,7},{5,1},{7,3},{8,12},{10,14},{12... | collective-permute-start | bytes 491528 | tf_op jit(solution)/shard_map/ppermute | solution.py:610
  143.6 20.6 %collective-permute-start.23 = (f16[80,1024]{1,0:T(8,128)(2,1)S(1)}, f16[80,1024]{1,0:T(8,128)(2,1)S(1)}, u32[]{:S(2)}, u32[]{:S(2)}) collective-permute-start(f16[80,1024]{1,0:T(8,128)(2,1)S(1)} %get-tuple-element.400), channel_id=1, source_target_pairs={{0,2},{2,0},{4,6},{6,4},{1,3},{3,1},{5,7},{7,5},{8,10},{10,8},{12,... | collective-permute-start | bytes 491528 | tf_op jit(solution)/shard_map/ppermute | solution.py:610
  164.4 6.7 %collective-permute-start.26 = (f32[8,512]{1,0:T(8,128)S(1)}, f32[8,512]{1,0:T(8,128)S(1)}, u32[]{:S(2)}, u32[]{:S(2)}) collective-permute-start(f32[8,512]{1,0:T(8,128)S(1)} %get-tuple-element.222), channel_id=1, source_target_pairs={{4,0},{6,2},{5,1},{7,3},{12,8},{14,10},{13,9},{15,11},{20,16},{22,... | collective-permute-start | bytes 49160 | tf_op jit(solution)/shard_map/ppermute | solution.py:613
  165.7 6.0 %collective-permute-start.27 = (f32[512,256]{1,0:T(8,128)S(1)}, f32[512,256]{1,0:T(8,128)S(1)}, u32[]{:S(2)}, u32[]{:S(2)}) collective-permute-start(f32[512,256]{1,0:T(8,128)S(1)} %get-tuple-element.228), channel_id=1, source_target_pairs={{0,1},{1,0},{2,3},{3,2},{4,5},{5,4},{6,7},{7,6},{8,9},{9,8},{10,11... | collective-permute-start | bytes 1572872 | tf_op jit(solution)/shard_map/ppermute | solution.py:607
  171.9 7.4 %collective-permute-start.28 = (f32[512,128]{1,0:T(8,128)S(1)}, f32[512,128]{1,0:T(8,128)S(1)}, u32[]{:S(2)}, u32[]{:S(2)}) collective-permute-start(f32[512,128]{1,0:T(8,128)S(1)} %constant_dynamic-slice_fusion.10), channel_id=1, source_target_pairs={{0,2},{2,0},{4,6},{6,4},{1,3},{3,1},{5,7},{7,5},{8,10},{10,8},{12,... | collective-permute-start | bytes 786440 | tf_op jit(solution)/shard_map/ppermute | solution.py:610
  179.3 1.7 collective-permute-start.29
  181.7 6.4 %collective-permute-start.30 = (f32[8,128]{1,0:T(8,128)S(1)}, f32[8,128]{1,0:T(8,128)S(1)}, u32[]{:S(2)}, u32[]{:S(2)}) collective-permute-start(f32[8,128]{1,0:T(8,128)S(1)} %fusion.26), channel_id=1, source_target_pairs={{4,0},{6,2},{5,1},{7,3},{12,8},{14,10},{13,9},{15,11},{20,16},{22,... | collective-permute-start | bytes 12296 | tf_op jit(solution)/shard_map/ppermute | solution.py:613
  188.1 18.8 %collective-permute-start.31 = (f32[192,1024]{1,0:T(8,128)S(1)}, f32[192,1024]{1,0:T(8,128)S(1)}, u32[]{:S(2)}, u32[]{:S(2)}) collective-permute-start(f32[192,1024]{1,0:T(8,128)S(1)} %slice_add_fusion), channel_id=1, source_target_pairs={{0,2},{2,0},{4,6},{6,4},{1,3},{3,1},{5,7},{7,5},{8,10},{10,8},{12,... | collective-permute-start | bytes 2359304 | tf_op jit(solution)/shard_map/ppermute | solution.py:610
  189.8 15.0 %collective-permute-start.32 = (f16[304,512]{1,0:T(8,128)(2,1)}, f16[304,512]{1,0:T(8,128)(2,1)}, u32[]{:S(2)}, u32[]{:S(2)}) collective-permute-start(f16[304,512]{1,0:T(8,128)(2,1)} %get-tuple-element.251), channel_id=1, source_target_pairs={{0,8},{8,0},{16,24},{24,16},{1,9},{9,1},{17,25},{25,17},{2,10},{10... | collective-permute-start | bytes 933896 | tf_op jit(solution)/shard_map/ppermute | solution.py:618
  191.2 15.0 %collective-permute-start.33 = (f16[304,512]{1,0:T(8,128)(2,1)}, f16[304,512]{1,0:T(8,128)(2,1)}, u32[]{:S(2)}, u32[]{:S(2)}) collective-permute-start(f16[304,512]{1,0:T(8,128)(2,1)} %get-tuple-element.252), channel_id=1, source_target_pairs={{0,16},{8,24},{16,0},{24,8},{1,17},{9,25},{17,1},{25,9},{2,18},{10... | collective-permute-start | bytes 933896 | tf_op jit(solution)/shard_map/ppermute | solution.py:618
  191.9 14.4 %collective-permute-start.34 = (f16[304,512]{1,0:T(8,128)(2,1)}, f16[304,512]{1,0:T(8,128)(2,1)}, u32[]{:S(2)}, u32[]{:S(2)}) collective-permute-start(f16[304,512]{1,0:T(8,128)(2,1)} %get-tuple-element.253), channel_id=1, source_target_pairs={{0,24},{8,16},{16,8},{24,0},{1,25},{9,17},{17,9},{25,1},{2,26},{10... | collective-permute-start | bytes 933896 | tf_op jit(solution)/shard_map/ppermute | solution.py:618
  206.9 9.6 %collective-permute-start.37 = (f32[256,1024]{1,0:T(8,128)}, f32[256,1024]{1,0:T(8,128)S(1)}, u32[]{:S(2)}, u32[]{:S(2)}) collective-permute-start(f32[256,1024]{1,0:T(8,128)} %get-tuple-element.263), channel_id=1, source_target_pairs={{0,1},{1,0},{2,3},{3,2},{4,5},{5,4},{6,7},{7,6},{8,9},{9,8},{10,11... | collective-permute-start | bytes 3145736 | tf_op jit(solution)/shard_map/ppermute | solution.py:607
  214.3 17.9 %collective-permute-start.36 = (f32[256,1024]{1,0:T(8,128)}, f32[256,1024]{1,0:T(8,128)S(1)}, u32[]{:S(2)}, u32[]{:S(2)}) collective-permute-start(f32[256,1024]{1,0:T(8,128)} %get-tuple-element.256), channel_id=1, source_target_pairs={{0,1},{1,0},{2,3},{3,2},{4,5},{5,4},{6,7},{7,6},{8,9},{9,8},{10,11... | collective-permute-start | bytes 3145736 | tf_op jit(solution)/shard_map/ppermute | solution.py:607
  217.1 15.1 %collective-permute-start.41 = (f16[272,1024]{1,0:T(8,128)(2,1)S(1)}, f16[272,1024]{1,0:T(8,128)(2,1)S(1)}, u32[]{:S(2)}, u32[]{:S(2)}) collective-permute-start(f16[272,1024]{1,0:T(8,128)(2,1)S(1)} %pad_maximum_fusion.3), channel_id=1, source_target_pairs={{0,2},{2,0},{4,6},{6,4},{1,3},{3,1},{5,7},{7,5},{8,10},{10,8},{12,... | collective-permute-start | bytes 1671176 | tf_op jit(solution)/shard_map/ppermute | solution.py:610
  219.9 5.5 %collective-permute-start.40 = (f16[304,128]{1,0:T(8,128)(2,1)S(1)}, f16[304,128]{1,0:T(8,128)(2,1)S(1)}, u32[]{:S(2)}, u32[]{:S(2)}) collective-permute-start(f16[304,128]{1,0:T(8,128)(2,1)S(1)} %get-tuple-element.404), channel_id=1, source_target_pairs={{0,24},{8,16},{16,8},{24,0},{1,25},{9,17},{17,9},{25,1},{2,26},{10... | collective-permute-start | bytes 233480 | tf_op jit(solution)/shard_map/ppermute | solution.py:618
  221.5 5.5 %collective-permute-start.39 = (f16[304,128]{1,0:T(8,128)(2,1)S(1)}, f16[304,128]{1,0:T(8,128)(2,1)S(1)}, u32[]{:S(2)}, u32[]{:S(2)}) collective-permute-start(f16[304,128]{1,0:T(8,128)(2,1)S(1)} %get-tuple-element.405), channel_id=1, source_target_pairs={{0,16},{8,24},{16,0},{24,8},{1,17},{9,25},{17,1},{25,9},{2,18},{10... | collective-permute-start | bytes 233480 | tf_op jit(solution)/shard_map/ppermute | solution.py:618
  222.9 4.5 %collective-permute-start.38 = (f16[304,128]{1,0:T(8,128)(2,1)S(1)}, f16[304,128]{1,0:T(8,128)(2,1)S(1)}, u32[]{:S(2)}, u32[]{:S(2)}) collective-permute-start(f16[304,128]{1,0:T(8,128)(2,1)S(1)} %get-tuple-element.406), channel_id=1, source_target_pairs={{0,8},{8,0},{16,24},{24,16},{1,9},{9,1},{17,25},{25,17},{2,10},{10... | collective-permute-start | bytes 233480 | tf_op jit(solution)/shard_map/ppermute | solution.py:618
  225.4 8.1 %collective-permute-start.20 = (f32[256,1024]{1,0:T(8,128)S(1)}, f32[256,1024]{1,0:T(8,128)S(1)}, u32[]{:S(2)}, u32[]{:S(2)}) collective-permute-start(f32[256,1024]{1,0:T(8,128)S(1)} %copy-done.51), channel_id=1, source_target_pairs={{0,1},{1,0},{2,3},{3,2},{4,5},{5,4},{6,7},{7,6},{8,9},{9,8},{10,11... | collective-permute-start | bytes 3145736 | tf_op jit(solution)/shard_map/ppermute | solution.py:607
  234.2 5.4 %collective-permute-start.35 = (bf16[256,1024]{1,0:T(8,128)(2,1)S(1)}, bf16[256,1024]{1,0:T(8,128)(2,1)S(1)}, u32[]{:S(2)}, u32[]{:S(2)}) collective-permute-start(bf16[256,1024]{1,0:T(8,128)(2,1)S(1)} %get-tuple-element.359), channel_id=1, source_target_pairs={{0,1},{1,0},{2,3},{3,2},{4,5},{5,4},{6,7},{7,6},{8,9},{9,8},{10,11... | collective-permute-start | bytes 1572872 | tf_op jit(solution)/shard_map/ppermute | solution.py:607
  234.3 6.8 %collective-permute-start.42 = (f32[256,1024]{1,0:T(8,128)S(1)}, f32[256,1024]{1,0:T(8,128)S(1)}, u32[]{:S(2)}, u32[]{:S(2)}) collective-permute-start(f32[256,1024]{1,0:T(8,128)S(1)} %get-tuple-element.358), channel_id=1, source_target_pairs={{0,1},{1,0},{2,3},{3,2},{4,5},{5,4},{6,7},{7,6},{8,9},{9,8},{10,11... | collective-permute-start | bytes 3145736 | tf_op jit(solution)/shard_map/ppermute | solution.py:607
  235.2 8.6 %collective-permute-start.45 = (f16[112,640]{1,0:T(8,128)(2,1)S(1)}, f16[112,640]{1,0:T(8,128)(2,1)S(1)}, u32[]{:S(2)}, u32[]{:S(2)}) collective-permute-start(f16[112,640]{1,0:T(8,128)(2,1)S(1)} %get-tuple-element.381), channel_id=1, source_target_pairs={{0,6},{2,4},{4,2},{6,0},{1,7},{3,5},{5,3},{7,1},{8,14},{10,12},{12... | collective-permute-start | bytes 430088 | tf_op jit(solution)/shard_map/ppermute | solution.py:610
  237.0 14.3 %collective-permute-start.44 = (f16[112,640]{1,0:T(8,128)(2,1)S(1)}, f16[112,640]{1,0:T(8,128)(2,1)S(1)}, u32[]{:S(2)}, u32[]{:S(2)}) collective-permute-start(f16[112,640]{1,0:T(8,128)(2,1)S(1)} %get-tuple-element.382), channel_id=1, source_target_pairs={{0,4},{2,6},{4,0},{6,2},{1,5},{3,7},{5,1},{7,3},{8,12},{10,14},{12... | collective-permute-start | bytes 430088 | tf_op jit(solution)/shard_map/ppermute | solution.py:610
  238.3 12.9 %collective-permute-start.43 = (f16[112,640]{1,0:T(8,128)(2,1)S(1)}, f16[112,640]{1,0:T(8,128)(2,1)S(1)}, u32[]{:S(2)}, u32[]{:S(2)}) collective-permute-start(f16[112,640]{1,0:T(8,128)(2,1)S(1)} %get-tuple-element.383), channel_id=1, source_target_pairs={{0,2},{2,0},{4,6},{6,4},{1,3},{3,1},{5,7},{7,5},{8,10},{10,8},{12,... | collective-permute-start | bytes 430088 | tf_op jit(solution)/shard_map/ppermute | solution.py:610
  254.2 4.5 %collective-permute-start.46 = (f32[1024]{0:T(1024)S(1)}, f32[1024]{0:T(1024)S(1)}, u32[]{:S(2)}, u32[]{:S(2)}) collective-permute-start(f32[1024]{0:T(1024)S(1)} %get-tuple-element.392), channel_id=1, source_target_pairs={{0,1},{1,0},{2,3},{3,2},{4,5},{5,4},{6,7},{7,6},{8,9},{9,8},{10,11... | collective-permute-start | bytes 12296 | tf_op jit(solution)/shard_map/ppermute | solution.py:607
  254.4 4.9 %collective-permute-start.47 = (f32[2,64,64]{2,1,0:T(8,128)S(1)}, f32[2,64,64]{2,1,0:T(8,128)S(1)}, u32[]{:S(2)}, u32[]{:S(2)}) collective-permute-start(f32[2,64,64]{2,1,0:T(8,128)S(1)} %get-tuple-element.380), channel_id=1, source_target_pairs={{0,1},{1,0},{2,3},{3,2},{4,5},{5,4},{6,7},{7,6},{8,9},{9,8},{10,11... | collective-permute-start | bytes 98312 | tf_op jit(solution)/shard_map/ppermute | solution.py:607
  (54 other events, 558.9 us)

commit v5 on v4

--- a/solution.py
+++ b/solution.py
@@ -162,7 +162,7 @@
                *rest):
     ws = rest[:parts]
     normed_ref, u_ref, uh_ref, co_ref, hd_ref, hloc_ref, pre_ref, end_ref = rest[parts : parts + 8]
-    hsc, usc, state, pre, esc = rest[parts + 8 :]
+    hsc, usc, state, pre, esc, wsc = rest[parts + 8 :]
     b = pl.program_id(0)
     wide = inner + 2 * states
     shard = ws[0].shape[0]
@@ -171,9 +171,9 @@
     @pl.when(b == 0)
     def _():
         hsc[...] = normalize(halo[...], gain[...])[1]
-        edge = jnp.zeros((16, wide), F32)
         for j in range(parts):
-            edge += mm(hsc[:, lanes_of(s_ref, j, shard)], ws[j][:, :wide])
+            wsc[lanes_of(s_ref, j, shard)] = ws[j][...]
+        edge = mm(hsc[...], wsc[:, :wide])
         edge = jnp.where(s_ref[HASPREV] > 0, edge[8:], 0.0)
         usc[0:8] = edge
         uh_ref[...] = edge
@@ -185,9 +185,7 @@
     def _():
         usc[0:8] = usc[BLOCK : BLOCK + 8]
 
-    u = jnp.zeros((BLOCK, wide + 128), F32)
-    for j in range(parts):
-        u += mm(normed_ref[:, lanes_of(s_ref, j, shard)], ws[j][...])
+    u = mm(normed_ref[...], wsc[...])
     usc[8 : 8 + BLOCK] = u[:, :wide]
     u_ref[...] = u[:, :wide]
     conv = bias[...] + taps[0:1] * usc[5 : 5 + BLOCK]
@@ -211,14 +209,13 @@
         fresh = mm(inject_t[:, at], jnp.exp(last - level_x[at]) * source[at], precision=HIGH)
         before = state[...]
         n = b * (BLOCK // SUB) + i
-        hloc_ref[n] = before
+        hloc_ref[i] = before
         pre_ref[n] = pre[...]
         state[...] = jnp.exp(last) * before + fresh
         pre[...] = pre[...] + last
 
     @pl.when(b == pl.num_programs(0) - 1)
     def _():
-        hloc_ref[n + 1] = state[...]
         end_ref[...] = state[...]
         pre_ref[n + 1] = pre[...]
 
@@ -253,20 +250,20 @@
 
 def gates_body(parts, quarter, s_ref, normed, own, near, far, *rest):
     ws = rest[:parts]
-    gate_ref, gg_ref, bg_ref = rest[parts:]
+    gate_ref, gg_ref, bg_ref, wsc = rest[parts:]
     b = pl.program_id(0)
     shard = ws[0].shape[0]
     inner = gate_ref.shape[1]
     up = pick(s_ref, b, quarter, own[...], near[...], far[...])
     bg_ref[...] = (up.astype(F32) * valid_rows(s_ref, b)).astype(BF16)
-    gate = jnp.zeros(gate_ref.shape, F32)
-    gg = jnp.zeros(gg_ref.shape, F32)
-    for j in range(parts):
-        at = lanes_of(s_ref, j, shard)
-        gate += mm(normed[:, at], ws[j][:, :inner])
-        gg += mm(bg_ref[:, at], ws[j][:, inner:])
-    gate_ref[...] = gate
-    gg_ref[...] = gg
+
+    @pl.when(b == 0)
+    def _():
+        for j in range(parts):
+            wsc[lanes_of(s_ref, j, shard)] = ws[j][...]
+
+    gate_ref[...] = mm(normed[...], wsc[:, :inner])
+    gg_ref[...] = mm(bg_ref[...], wsc[:, inner:])
 
 
 def entering(hloc, pre, hin):
@@ -325,8 +322,7 @@
     for i in reversed(range(BLOCK // SUB)):
         at = slice(i * SUB, (i + 1) * SUB)
         held = chain[...]
-        n = b * (BLOCK // SUB) + i
-        gloc_ref[n + 1] = held
+        gloc_ref[i] = held
         level_x = lx[at]
         chain[...] = jnp.exp(level_x[SUB - 1 : SUB]) * held + mm(
             readout_t[:, at], jnp.exp(level_x) * og[at], precision=HIGH
@@ -334,7 +330,6 @@
 
     @pl.when(b == 0)
     def _():
-        gloc_ref[0] = chain[...]
         start_ref[...] = chain[...]
 
 
@@ -385,7 +380,7 @@
     return pre
 
 
-def meet_body(inner, states, s_ref, co, hd, z, dbc, hloc, pre, gloc, gin, hin, zed_ref, ends_ref, keep_ref,
+def meet_body(inner, states, s_ref, co, hd, z, dbc, hloc, hnext, hend, pre, gloc, gin, hin, zed_ref, ends_ref, keep_ref,
               give_ref, lsc, dsc):
     start_expanders(inner, (0, lsc), (STEP, dsc))
     exact = three(hd[...])
@@ -402,11 +397,12 @@
         at = slice(i * SUB, (i + 1) * SUB)
         n = b * subs + i + 1
         level_x = lx[at]
-        later = gloc[n] + jnp.exp(pre[subs * count][0:1] - pre[n][0:1]) * gin[...]
+        later = gloc[i] + jnp.exp(pre[subs * count][0:1] - pre[n][0:1]) * gin[...]
+        after = hloc[i + 1] if i < subs - 1 else jnp.where(b == count - 1, hend[...], hnext[0])
         fade = jnp.exp(level_x[SUB - 1 : SUB] - level_x)
         zed_ref[at] = z[at] + fade * mm(act[at, inner : inner + states], later, precision=HIGH)
         inject_grads.append(dbc[at, :states] + mm(fade * source[at], later, NT, HIGH))
-        ends.append(jnp.sum(later * entering(hloc[n], pre[n], hin[...]), axis=0, keepdims=True))
+        ends.append(jnp.sum(later * entering(after, pre[n], hin[...]), axis=0, keepdims=True))
     ends_ref[...] = jnp.concatenate(ends + [jnp.zeros((8 - subs, inner), F32)], axis=0)
     inject_grad = jnp.concatenate(inject_grads, axis=0)
     half = count // 2
@@ -585,6 +581,31 @@
     deal(s_ref, pl.program_id(0), quarter, whole_sc[...], outs)
 
 
+def finish_body(inner, s_ref, first, second, rate, taps_ref, bias_ref, gain_ref, staps_ref, sbias_ref, raw_ref,
+                rate_ref, skip_ref, norm_ref):
+    both = (first, second)
+    heads = inner // 64
+    lane = lax.broadcasted_iota(jnp.int32, (8, 128), 1)
+    pairs, skips = [], []
+    for n, part in enumerate(both):
+        at = slice(n * inner, (n + 1) * inner)
+        taps_ref[:, at] = part[0:4, :inner]
+        bias_ref[:, at] = part[4:5, :inner]
+        gain_ref[:, at] = part[8:9, :inner]
+        here = slice(n * 128, (n + 1) * 128)
+        staps_ref[:, here] = part[0:4, inner:]
+        sbias_ref[:, here] = part[4:5, inner:]
+        turn = (128 - HEAD0 + n * heads) % 128
+        pairs.append(pltpu.roll(part[0:8, inner:], turn, 1))
+        skips.append(pltpu.roll(mm(three(part[8:16, :inner]), collector(inner)), turn, 1))
+    values = jnp.where(lane < heads, pairs[0], pairs[1])
+    skip = jnp.where(lane < heads, skips[0], skips[1])
+    raw_ref[...] = values[5:6, : 2 * heads]
+    rate_ref[...] = values[6:7, : 2 * heads] * rate[...]
+    skip_ref[...] = skip[1:2, : 2 * heads]
+    norm_ref[...] = first[8:16, inner:] + second[8:16, inner:]
+
+
 def per_device(
     hidden, lengths, cotangent, norm_gain, proj_main, proj_state, proj_delta, conv_main, conv_state,
     bias_main, bias_state, delta_bias, log_rate, skip_gain, gate_gain, proj_out,
@@ -711,9 +732,8 @@
     edge = lax.ppermute(edge, ("ctx", "tp"), route)
     halo = jnp.where(core == lo, edge, swap(edge))
 
-    ws1, near, main_gate, out_later, cot_later = lax.optimization_barrier(
-        (ws1, near, main_part[:, 0], proj_out, cotangent)
-    )
+    near, cot_later = lax.optimization_barrier((near, cotangent))
+    ws1, near, main_gate, out_later = lax.optimization_barrier((ws1, near, main_part[:, 0], proj_out))
     second = jnp.concatenate([main_gate, mine(out_later, 1, inner)], axis=1)
     ws2 = gathered(second)
     cot_near = across(piece(cot_later, core, halfway), 1)
@@ -733,12 +753,12 @@
         [own_spec, part_spec, part_spec, whole((16, model)), whole((1, model)), whole((4, wide)),
          whole((1, wide)), whole((1, 128)), whole((1, 128))] + [whole((shard, wide + 128))] * parts,
         [rows_spec(model), rows_spec(wide), whole((8, wide)), rows_spec(wide), rows_spec(128),
-         whole((last + 1, states, inner)), whole((last + 1, 8, inner)), whole((states, inner))],
+         state_block, whole((last + 1, 8, inner)), whole((states, inner))],
         [shaped((tokens, model), BF16), shaped((tokens, wide)), shaped((8, wide)), shaped((tokens, wide)),
-         shaped((tokens, 128)), shaped((last + 1, states, inner)), shaped((last + 1, 8, inner)),
+         shaped((tokens, 128)), shaped((last, states, inner)), shaped((last + 1, 8, inner)),
          shaped((states, inner))],
         [pltpu.VMEM((16, model), BF16), pltpu.VMEM((8 + BLOCK, wide), F32), pltpu.VMEM((states, inner), F32),
-         pltpu.VMEM((8, inner), F32), pltpu.VMEM((384, inner), BF16)],
+         pltpu.VMEM((8, inner), F32), pltpu.VMEM((384, inner), BF16), pltpu.VMEM((model, wide + 128), BF16)],
         name="front",
     )(scalars, hidden, near, far, halo, gain_row, taps_x, bias_x, dbias_row, rate_row, *ws1)
 
@@ -769,6 +789,7 @@
         [rows_spec(model), own_spec, part_spec, part_spec] + [whole((shard, 2 * inner))] * parts,
         [rows_spec(inner), rows_spec(inner), rows_spec(model)],
         [shaped((tokens, inner)), shaped((tokens, inner)), shaped((tokens, model), BF16)],
+        [pltpu.VMEM((model, 2 * inner), BF16)],
         name="gates",
         limit=20 << 20,
     )(scalars, *streamed(normed, cotangent, cot_near, cot_far, *ws2))
@@ -797,10 +818,11 @@
         (count,),
         [back(wide), back(128), back(inner), back(inner), back(inner),
          back_sums, back_sums, back_sums, back_sums, whole((1, inner)), whole((1, inner))],
-        [back(inner), back(inner), back(inner), whole((last + 1, states, inner)), whole((states, inner)),
+        [back(inner), back(inner), back(inner),
+         pl.BlockSpec((subs, states, inner), lambda b, s: (count - 1 - b, 0, 0)), whole((states, inner)),
          whole((8, inner))],
-        [kept((tokens, inner), BF16), kept((tokens, inner), BF16), kept((tokens, inner)),
-         kept((last + 1, states, inner)), shaped((states, inner)), shaped((8, inner))],
+        [shaped((tokens, inner), BF16), shaped((tokens, inner), BF16), kept((tokens, inner)),
+         kept((last, states, inner)), shaped((states, inner)), shaped((8, inner))],
         [pltpu.VMEM((states, inner), F32), pltpu.VMEM((384, inner), BF16)],
         name="turn",
         limit=20 << 20,
@@ -816,7 +838,7 @@
     turned = pl.BlockSpec((tokens, shard), lambda j, s: (0, s[SLOT0 + j]))
     dealt_specs = [whole((halfway, model))] * 4
     dealt_shapes = [shaped((halfway, model))] * 4
-    def grads(lefts, rights, name):
+    def grads(lefts, rights, name, limit=None):
         sources = []
         for left, right in zip(lefts, rights):
             sources += [left, right]
@@ -830,10 +852,11 @@
             [shaped((shard, width))] * parts + [shaped((16, width)), shaped((1, width))],
             [pltpu.VMEM((8, width), F32)],
             name=name,
+            limit=limit,
         )(scalars, *sources)
         return pieces, (powers, inverse)
 
-    early, early_scale = grads([normed, branch_grad], [gate_grad, gated], "grad_early")
+    early, early_scale = grads(streamed(normed, branch_grad), [gate_grad, gated], "grad_early", 20 << 20)
     early_got = over_sequences(payloads(early, early_scale))
     early, out_grad = lax.optimization_barrier((early, out_grad))
 
@@ -864,7 +887,6 @@
     branch_theirs = [branch[1][:front_rows] + branch_give[:front_rows], branch[1][front_rows:] + branch_give[front_rows:]]
     returned, branch_theirs = lax.optimization_barrier((returned, branch_theirs))
     branch_back = [across(branch_theirs[0], 1)]
-    all_states = whole((last + 1, states, inner))
     all_pre = whole((last + 1, 8, inner))
     per = BLOCK // 8
     half_rows = tokens // 2
@@ -882,15 +904,16 @@
     zed, ends, dbc_keep, dbc_give = grid_call(
         functools.partial(meet_body, inner, states),
         (count,),
-        [rows_spec(wide), rows_spec(128), rows_spec(inner), rows_spec(2 * states), all_states,
-         all_pre, all_states, whole((states, inner)), whole((states, inner))],
+        [rows_spec(wide), rows_spec(128), rows_spec(inner), rows_spec(2 * states), state_block,
+         pl.BlockSpec((1, states, inner), lambda b, s: (jnp.minimum((b + 1) * subs, last - 1), 0, 0)),
+         whole((states, inner)), all_pre, state_block, whole((states, inner)), whole((states, inner))],
         [rows_spec(inner), rows_spec(inner, 8), whole((half_rows, 2 * states)), whole((half_rows, 2 * states))],
         [shaped((tokens, inner)), shaped((8 * count, inner)), shaped((half_rows, 2 * states)),
          shaped((half_rows, 2 * states))],
         [pltpu.VMEM((384, inner), BF16)] * 2,
         name="meet",
         limit=20 << 20,
-    )(scalars, *streamed(conv, per_head, zed, dbc, hloc, pre, gloc), returned, carried)
+    )(scalars, *streamed(conv, per_head, zed, dbc, hloc, hloc), own_end, *streamed(pre, gloc), returned, carried)
 
     zed, ends, dbc_keep, dbc_give, branch_back = lax.optimization_barrier((zed, ends, dbc_keep, dbc_give, branch_back))
     early_total, early_power, _ = totalled(early, early_scale, early_got)
@@ -926,7 +949,7 @@
     signal_pre, dbc = lax.optimization_barrier((signal_pre, dbc))
     dbc_back = across(lax.dynamic_slice_in_dim(dbc, (1 - lo) * states, states, 1), 1)
     signal_small = jnp.concatenate([signal_cols, turn_cols])
-    signal, signal_scale = grads([normed], [signal_pre], "grad_signal")
+    signal, signal_scale = grads(streamed(normed), streamed(signal_pre), "grad_signal", 20 << 20)
     signal, dbc_back = lax.optimization_barrier((signal, dbc_back))
     signal_payload = payloads(signal, signal_scale, [signal_small])
 
@@ -958,8 +981,9 @@
         [pltpu.VMEM((BLOCK, model), F32), pltpu.VMEM((BLOCK + 8, states), F32),
          pltpu.VMEM((BLOCK + 8, states), F32)],
         name="feature",
-    )(scalars, hidden, near, far, gate_grad, signal_pre, raw_grad, dbc, dbc_other, conv, u, u, uh, state_ahead,
-      taps_x, *ws1, *ws2)
+        limit=24 << 20,
+    )(scalars, *streamed(hidden, near, far, gate_grad, signal_pre, raw_grad), dbc, dbc_other, *streamed(conv, u, u), uh,
+      state_ahead, taps_x, *streamed(*ws1, *ws2))
     feature, branch_rest, signal_got = lax.optimization_barrier((feature, across(branch_later, 1), signal_got))
     branch_back = jnp.concatenate(branch_back + [branch_rest])
     feature_theirs = feature[1] + swap(feature[3])
@@ -969,10 +993,11 @@
     extra_small = jnp.concatenate(
         [state_cols[:5], head_cols[:2], jnp.zeros((1, 128), F32), feature_cols[0].reshape(folds, 128)]
     )
-    extra, extra_scale = grads([normed], [extra_pre], "grad_extra")
-    extra, feature_theirs = lax.optimization_barrier((extra, feature_theirs))
     feature_power = exponents(jnp.max(jnp.abs(feature_theirs), axis=0, keepdims=True))
-    feature_back = across(packed(feature_theirs, feature_power, jnp.exp2(-feature_power)), 1)
+    feature_payload = packed(feature_theirs, feature_power, jnp.exp2(-feature_power))
+    extra_pre, feature_payload = lax.optimization_barrier((extra_pre, feature_payload))
+    extra, extra_scale = grads(streamed(normed), [extra_pre], "grad_extra", 20 << 20)
+    feature_back = across(feature_payload, 1)
     signal_total, signal_power, (signal_here,) = totalled(signal, signal_scale, signal_got, [signal_small])
     extra_got = over_sequences(payloads(extra, extra_scale, [extra_small]))
     extra_got, feature_back = lax.optimization_barrier((extra_got, feature_back))
@@ -980,6 +1005,7 @@
     late_power = jnp.concatenate([signal_power, extra_power], axis=1)
     small_here = jnp.concatenate([signal_here, extra_here], axis=1)
     late_cut = chunks([signal_total, extra_total], late_power, [small_here])
+    feature_back, late_cut = lax.optimization_barrier((feature_back, late_cut))
     late_far = over_positions(late_cut)
     feature_back = unpacked(feature_back)[0]
 
@@ -1008,12 +1034,19 @@
     def side_by_side(pair):
         return jnp.concatenate(pair, axis=-1)
 
-    signal_small = side_by_side([part[:, :inner] for part in small_sum])
-    state_small = side_by_side([part[:8, inner:] for part in small_sum])
-    heads_small = [part[5:7, inner + HEAD0 : inner + HEAD0 + heads] for part in small_sum]
-    rate_all = -jnp.exp(log_rate)
-    skip_sum = signal_small[9].reshape(2 * heads, inner // heads).sum(axis=1)
-    gain_here = (small_sum[0] + small_sum[1])[8 : 8 + folds, inner:].reshape(model)
+    taps_sum, bias_sum, ggain_sum, state_taps, state_bias, raw_sum, rate_sum, skip_sum, gain_here = grid_call(
+        functools.partial(finish_body, inner),
+        (1,),
+        [whole((16, inner + 128)), whole((16, inner + 128)), whole((1, 2 * heads))],
+        [whole((4, 2 * inner)), whole((1, 2 * inner)), whole((1, 2 * inner)), whole((4, 2 * states)),
+         whole((1, 2 * states)), whole((1, 2 * heads)), whole((1, 2 * heads)), whole((1, 2 * heads)),
+         whole((8, 128))],
+        [shaped((4, 2 * inner)), shaped((1, 2 * inner)), shaped((1, 2 * inner)), shaped((4, 2 * states)),
+         shaped((1, 2 * states)), shaped((1, 2 * heads)), shaped((1, 2 * heads)), shaped((1, 2 * heads)),
+         shaped((8, 128))],
+        name="finish",
+    )(scalars, *small_sum, -jnp.exp(log_rate)[None])
+    gain_here = gain_here.reshape(model)
     state_here = jnp.stack([part[:, inner : inner + HEAD0] for part in late_sum])
     gain_there, state_there = swap(gain_here), swap(state_here)
     gain_size = model // (dps * ctxs)
@@ -1032,14 +1065,14 @@
         main_sum,
         state_sum,
         delta_sum,
-        signal_small[:4],
-        state_small[:4],
-        signal_small[4],
-        state_small[4],
-        side_by_side([part[0] for part in heads_small]),
-        side_by_side([part[1] for part in heads_small]) * rate_all,
-        skip_sum,
-        signal_small[8],
+        taps_sum,
+        state_taps,
+        bias_sum[0],
+        state_bias[0],
+        raw_sum[0],
+        rate_sum[0],
+        skip_sum[0],
+        ggain_sum[0],
         out_sum,
     )
 

time: 262 us -> 241 us (0.920)
  other arithmetic: 29.4 us -> 21 us
  Pallas kernels: 112 us -> 105 us
  waiting for transfers between devices: 49.3 us -> 45.2 us
    ppermute x15, waiting for transfers between devices: 22 us -> 13.1 us  [spread(): return lax.ppermute(value, 'dp', [(i, i ^ j) for i in range(dps)])]
    pallas_call x3, Pallas kernels: 20.1 us -> 14.8 us  [grads(): grid_call(functools.partial(grads_body, parts, [(n, n + 1) for n in range...]
    ppermute x13, waiting for transfers between devices: 15.9 us -> 20.4 us  [across(): return lax.ppermute(value, 'ctx', [(i, i ^ j) for i in range(ctxs)])]
    convert_element_type x6, other arithmetic: 4.14 us -> 0.94 us  [packed(): (value * inverse).astype(F16)]
    concatenate x6 -> x1, other arithmetic: 3.56 us -> 0.6 us  [side_by_side(): return jnp.concatenate(pair, axis=-1)]
    unnamed x113 -> x103, local copies, waits for them, and re-layouts: 6.78 us -> 8.22 us
  transfers between devices with their start and end apart: 48 -> 48, of which waited for: 17 -> 18; matrix products, arithmetic and copies ran while one was open for 11% -> 10% of each run, Pallas kernels for 34% -> 34%
where the time goes in v5:
time: 241 us; the launch traced here: 240 us
  Pallas kernels  105 us (44%)
  starting transfers between devices  48 us (20%)
  waiting for transfers between devices  45.2 us (19%)
  other arithmetic  21 us (9%)
  local copies, waits for them, and re-layouts  18.5 us (8%)
  between operations  2.53 us (1%)
    ppermute x13, waiting for transfers between devices, across(): return lax.ppermute(value, 'ctx', [(i, i ^ j) for i in range(ctxs)])  20.4 us
    ppermute x15, starting transfers between devices, spread(): return lax.ppermute(value, 'dp', [(i, i ^ j) for i in range(dps)])  18.6 us
    ppermute x13, starting transfers between devices, across(): return lax.ppermute(value, 'ctx', [(i, i ^ j) for i in range(ctxs)])  15.9 us
    pallas_call x3, Pallas kernels, grads(): grid_call(functools.partial(grads_body, parts, [(n, n + 1) for n in range...  14.8 us
    pallas_call x1, Pallas kernels, per_device(): grid_call(functools.partial(front_body, parts, inner, states, quarter), (...  14 us
    ppermute x15, waiting for transfers between devices, spread(): return lax.ppermute(value, 'dp', [(i, i ^ j) for i in range(dps)])  13.1 us
    pallas_call x1, Pallas kernels, per_device(): grid_call(functools.partial(back_body, inner, states), (count,), [rows_sp...  11.6 us
    pallas_call x1, Pallas kernels, per_device(): grid_call(functools.partial(join_body, inner), (count,), [back(inner), ba...  10 us
  transfers between devices with their start and end apart: 48, of which 18 were waited for; matrix products, arithmetic and copies ran while one was open for 10% of the time, Pallas kernels for 34%

profile of v5, /device:TPU:0, one launch (start us, length us, event | category | flops | bytes accessed | tf_op | source)
XLA Modules:
  0.0 239.9 jit_solution(750648560694909947)
XLA Ops:
  1.7 3.3 %constant_dynamic-slice_fusion.15 = (bf16[256,1,512]{2,1,0:T(2,128)(2,1)}, bf16[256,1,512]{2,1,0:T(2,128)(2,1)S(1)}) fusion(bf16[256,2,1024]{2,1,0:T(2,128)(2,1)} %param.20, s32[]{:T(128)S(6)} %select_n.151, s32[]{:T(128)S(6)} %add.319), kind=kLoop, calls=%fused_computation.137 | loop fusion | bytes 1048584 | tf_op jit(solution)/shard_map/slice | solution.py:736
  6.1 3.9 %collective-permute-start.2 = (bf16[256,896]{1,0:T(8,128)(2,1)}, bf16[256,896]{1,0:T(8,128)(2,1)}, u32[]{:S(2)}, u32[]{:S(2)}) collective-permute-start(bf16[256,896]{1,0:T(8,128)(2,1)} %concatenate.134.rest_0_), channel_id=1, source_target_pairs={{0,24},{8,16},{16,8},{24,0},{1,25},{9,17},{17,9},{25,1},{2,26},{10... | collective-permute-start | bytes 1376264 | tf_op jit(solution)/shard_map/ppermute | solution.py:639
  10.7 2.2 collective-permute-start.3
  17.1 7.0 %collective-permute-done.3.near = bf16[256,1024]{1,0:T(8,128)(2,1)} collective-permute-done((bf16[256,1024]{1,0:T(8,128)(2,1)S(1)}, bf16[256,1024]{1,0:T(8,128)(2,1)}, u32[]{:S(2)}, u32[]{:S(2)}) %collective-permute-start.3) | collective-permute-done | bytes 524320 | tf_op jit(solution)/shard_map/ppermute | solution.py:631
  25.0 1.7 collective-permute-start.7
  28.4 2.2 collective-permute-done.1.rest_2_
  31.1 1.5 collective-permute-start.11
  32.6 1.5 collective-permute-start.10
  34.6 14.0 %front.1 = (bf16[1024,1024]{1,0:T(8,128)(2,1)}, f32[1024,768]{1,0:T(8,128)}, f32[8,768]{1,0:T(8,128)}, f32[1024,768]{1,0:T(8,128)}, f32[1024,128]{1,0:T(8,128)},...) custom-call(s32[10]{0:T(128)} %stack.79.s_ref, bf16[512,1024]{1,0:T(8,128)(2,1)} %bitcast.92, ...), custom_call_target="tpu_custom_call" | custom-call | tf_op jit(solution)/shard_map/front/pallas_call | solution.py:750
  48.7 4.7 %collective-permute-start.12 = (f32[128,512]{1,0:T(8,128)}, f32[128,512]{1,0:T(8,128)S(1)}, u32[]{:S(2)}, u32[]{:S(2)}) collective-permute-start(f32[128,512]{1,0:T(8,128)} %get-tuple-element.188.hend), channel_id=1, source_target_pairs={{0,4},{2,6},{1,5},{3,7},{8,12},{10,14},{9,13},{11,15},{16,20},{18,... | collective-permute-start | bytes 786440 | tf_op jit(solution)/shard_map/ppermute | solution.py:634
  53.7 6.9 %within.1.yw = f32[1024,512]{1,0:T(8,128)S(1)} custom-call(s32[10]{0:T(128)S(1)} %copy-done.13, f32[1024,768]{1,0:T(8,128)} %get-tuple-element.176.co, f32[1024,128]{1,0:T(8,128)} %get-tuple-element.177.hd), custom_call_target="tpu_custom_call" | custom-call | tf_op jit(solution)/shard_map/within/pallas_call | solution.py:775
  61.9 6.6 %gates.1 = (f32[1024,512]{1,0:T(8,128)S(1)}, f32[1024,512]{1,0:T(8,128)S(1)}, bf16[1024,1024]{1,0:T(8,128)(2,1)S(1)}) custom-call(s32[10]{0:T(128)S(1)} %copy-done.13, bf16[1024,1024]{1,0:T(8,128)(2,1)} %get-tuple-element.178.normed.refs_0_, bf16[512,1024]{1,0:T(8,128)(2,1)} %bitcast.94, bf16[256,1024]{1,0:T(8,128)(2,1)} %collective-permute-done.7.near, ...), custom_call_target="tpu_custom_call" | custom-call | tf_op jit(solution)/shard_map/gates/pallas_call | solution.py:786
  68.5 1.3 copy-done.8
  69.9 6.5 %output.1 = (f32[1024,512]{1,0:T(8,128)S(1)}, f32[16,1024]{1,0:T(8,128)S(1)}) custom-call(s32[10]{0:T(128)S(1)} %copy-done.13, f32[1024,768]{1,0:T(8,128)} %get-tuple-element.176.co, f32[1024,128]{1,0:T(8,128)} %get-tuple-element.177.hd, f32[1024,512]{1,0:T(8,128)S(1)} %within.1.yw, f32[1024,512]{1,0:T(8,128)S(1)} %get-tuple-element.184.gate, ...), custom_call_target="tpu_custom_call" | custom-call | tf_op jit(solution)/shard_map/output/pallas_call | solution.py:797
  76.4 1.7 collective-permute-start.15
  78.5 2.1 collective-permute-done.15.sums3
  80.6 1.8 collective-permute-done.14.sums2
  83.8 7.8 %turn.1 = (bf16[1024,512]{1,0:T(8,128)(2,1)S(1)}, bf16[1024,512]{1,0:T(8,128)(2,1)S(1)}, f32[1024,512]{1,0:T(8,128)}, f32[8,128,512]{2,1,0:T(8,128)}, f32[128,512]{1,0:T(8,128)S(1)}, /*index=5*/f32[8,512]{1,0:T(8,128)S(1)}) custom-call(s32[10]{0:T(128)S(1)} %copy-done.14, f32[1024,768]{1,0:T(8,128)} %get-tuple-element.176.co, ...), custom_call_target="tpu_custom_call" | custom-call | tf_op jit(solution)/shard_map/turn/pallas_call | solution.py:816
  91.7 6.3 %grad_early.1 = (f32[256,1024]{1,0:T(8,128)S(1)}, f32[256,1024]{1,0:T(8,128)S(1)}, f32[256,1024]{1,0:T(8,128)S(1)}, f32[256,1024]{1,0:T(8,128)S(1)}, f32[16,1024]{1,0:T(8,128)S(1)}, /*index=5*/f32[1,1024]{1,0:T(1,128)S(1)}) custom-call(s32[10]{0:T(128)S(1)} %copy-done.14, bf16[1024,1024]{1,0:T(8,128)(2,1)} %get-tuple-element.178.normed.refs_0_, ...), custom_call_target="tpu_custom_call" | custom-call | tf_op jit(solution)/shard_map/grad_early/pallas_call | solution.py:847
  99.0 1.7 collective-permute-start.19
  102.5 1.5 collective-permute-start.16
  104.0 11.6 %back.1 = (f32[1024,512]{1,0:T(8,128)}, f32[1024,256]{1,0:T(8,128)}) custom-call(s32[10]{0:T(128)} %stack.79.s_ref, f32[1024,768]{1,0:T(8,128)} %get-tuple-element.176.co, f32[1024,128]{1,0:T(8,128)} %get-tuple-element.177.hd, f32[1024,512]{1,0:T(8,128)} %get-tuple-element.202.og, f32[8,128,512]{2,1,0:T(8,128)} %get-tuple-element.186.hloc.hnext, ...), custom_call_target="tpu_custom_call" | custom-call | tf_op jit(solution)/shard_map/back/pallas_call | solution.py:863
  115.6 6.9 %branch.1 = (f32[256,1024]{1,0:T(8,128)}, f32[256,1024]{1,0:T(8,128)}, f32[256,1024]{1,0:T(8,128)}, f32[256,1024]{1,0:T(8,128)}) custom-call(s32[10]{0:T(128)} %stack.79.s_ref, bf16[1024,512]{1,0:T(8,128)(2,1)} %copy-done.5, bf16[256,1024]{1,0:T(8,128)(2,1)} %copy-done.23, bf16[256,1024]{1,0:T(8,128)(2,1)} %copy-done.27, bf16[256,1024]{1,0:T(8,128)(2,1)} %copy-done.26, ...), custom_call_target="tpu_custom_call" | custom-call | tf_op jit(solution)/shard_map/branch/pallas_call | solution.py:874
  122.5 3.5 %collective-permute-done.18 = f16[272,1024]{1,0:T(8,128)(2,1)} collective-permute-done((f16[272,1024]{1,0:T(8,128)(2,1)S(1)}, f16[272,1024]{1,0:T(8,128)(2,1)}, u32[]{:S(2)}, u32[]{:S(2)}) %collective-permute-start.18) | collective-permute-done | bytes 557088 | tf_op jit(solution)/shard_map/ppermute | solution.py:639
  126.8 1.8 multiply_add_fusion
  129.9 2.0 collective-permute-start.22
  132.1 1.5 collective-permute-start.24
  133.6 2.9 %collective-permute-start.23 = (f16[80,1024]{1,0:T(8,128)(2,1)S(1)}, f16[80,1024]{1,0:T(8,128)(2,1)S(1)}, u32[]{:S(2)}, u32[]{:S(2)}) collective-permute-start(f16[80,1024]{1,0:T(8,128)(2,1)S(1)} %get-tuple-element.416), channel_id=1, source_target_pairs={{0,2},{2,0},{4,6},{6,4},{1,3},{3,1},{5,7},{7,5},{8,10},{10,8},{12,... | collective-permute-start | bytes 491528 | tf_op jit(solution)/shard_map/ppermute | solution.py:631
  136.6 7.8 %meet.1 = (f32[1024,512]{1,0:T(8,128)S(1)}, f32[32,512]{1,0:T(8,128)S(1)}, f32[512,256]{1,0:T(8,128)S(1)}, f32[512,256]{1,0:T(8,128)S(1)}) custom-call(s32[10]{0:T(128)S(1)} %copy-done.15, f32[1024,768]{1,0:T(8,128)} %get-tuple-element.176.co, f32[1024,128]{1,0:T(8,128)} %get-tuple-element.177.hd, f32[1024,512]{1,0:T(8,128)} %get-tuple-element.211.z, ...), custom_call_target="tpu_custom_call" | custom-call | tf_op jit(solution)/shard_map/meet/pallas_call | solution.py:904
  145.1 10.0 %join.1 = (bf16[1024,512]{1,0:T(8,128)(2,1)S(1)}, f32[8,512]{1,0:T(8,128)S(1)}, f32[8,512]{1,0:T(8,128)S(1)}, f32[1024,128]{1,0:T(8,128)S(1)}, f32[8,128]{1,0:T(8,128)S(1)}, /*index=5*/f32[8,512]{1,0:T(8,128)S(1)}) custom-call(s32[10]{0:T(128)S(1)} %copy-done.15, f32[1024,768]{1,0:T(8,128)} %get-tuple-element.176.co, f32[1024,128]{1,0:T(8,128)} %get-tuple-element.177.hd, ...), custom_call_target="tpu_custom_call" | custom-call | tf_op jit(solution)/shard_map/join/pallas_call | solution.py:922
  157.6 4.4 %collective-permute-done.26 = f32[8,512]{1,0:T(8,128)S(1)} collective-permute-done((f32[8,512]{1,0:T(8,128)S(1)}, f32[8,512]{1,0:T(8,128)S(1)}, u32[]{:S(2)}, u32[]{:S(2)}) %collective-permute-start.26) | collective-permute-done | bytes 16416 | tf_op jit(solution)/shard_map/ppermute | solution.py:634
  162.8 4.7 %grad_signal.1 = (f32[256,512]{1,0:T(8,128)S(1)}, f32[256,512]{1,0:T(8,128)S(1)}, f32[256,512]{1,0:T(8,128)S(1)}, f32[256,512]{1,0:T(8,128)S(1)}, f32[16,512]{1,0:T(8,128)S(1)}, /*index=5*/f32[1,512]{1,0:T(1,128)S(1)}) custom-call(s32[10]{0:T(128)S(1)} %copy-done.15, bf16[1024,1024]{1,0:T(8,128)(2,1)} %get-tuple-element.178.normed.refs_0_, ...), custom_call_target="tpu_custom_call" | custom-call | tf_op jit(solution)/shard_map/grad_signal/pallas_call | solution.py:847
  167.5 1.6 collective-permute-done.28
  171.5 1.6 collective-permute-start.30
  174.1 3.8 %collective-permute-done.30.ahead = f32[8,128]{1,0:T(8,128)S(1)} collective-permute-done((f32[8,128]{1,0:T(8,128)S(1)}, f32[8,128]{1,0:T(8,128)S(1)}, u32[]{:S(2)}, u32[]{:S(2)}) %collective-permute-start.30) | collective-permute-done | bytes 4128 | tf_op jit(solution)/shard_map/ppermute | solution.py:634
  178.3 1.5 collective-permute-start.32
  181.8 9.1 %feature.1 = (f32[256,1024]{1,0:T(8,128)S(1)}, f32[256,1024]{1,0:T(8,128)S(1)}, f32[256,1024]{1,0:T(8,128)S(1)}, f32[256,1024]{1,0:T(8,128)S(1)}, bf16[1024,128]...) custom-call(s32[10]{0:T(128)S(1)} %copy-done.15, bf16[512,1024]{1,0:T(8,128)(2,1)} %bitcast.93, ...), custom_call_target="tpu_custom_call" | custom-call | tf_op jit(solution)/shard_map/feature/pallas_call | solution.py:972
  190.9 3.3 %collective-permute-done.33 = f16[304,512]{1,0:T(8,128)(2,1)} collective-permute-done((f16[304,512]{1,0:T(8,128)(2,1)S(1)}, f16[304,512]{1,0:T(8,128)(2,1)}, u32[]{:S(2)}, u32[]{:S(2)}) %collective-permute-start.33) | collective-permute-done | bytes 311328 | tf_op jit(solution)/shard_map/ppermute | solution.py:639
  194.2 2.3 collective-permute-done.31
  201.0 3.8 %grad_extra.1 = (f32[256,128]{1,0:T(8,128)S(1)}, f32[256,128]{1,0:T(8,128)S(1)}, f32[256,128]{1,0:T(8,128)S(1)}, f32[256,128]{1,0:T(8,128)S(1)}, f32[16,128]{1,0:T(8,128)S(1)}, /*index=5*/f32[1,128]{1,0:T(1,128)S(1)}) custom-call(s32[10]{0:T(128)S(1)} %copy-done.15, bf16[1024,1024]{1,0:T(8,128)(2,1)} %get-tuple-element.178.normed.refs_0_, ...), custom_call_target="tpu_custom_call" | custom-call | tf_op jit(solution)/shard_map/grad_extra/pallas_call | solution.py:847
  205.0 1.7 collective-permute-start.40
  208.6 2.2 collective-permute-done.40
  212.4 2.0 collective-permute-done.41
  219.0 3.4 %collective-permute-start.45 = (f16[112,640]{1,0:T(8,128)(2,1)S(1)}, f16[112,640]{1,0:T(8,128)(2,1)S(1)}, u32[]{:S(2)}, u32[]{:S(2)}) collective-permute-start(f16[112,640]{1,0:T(8,128)(2,1)S(1)} %get-tuple-element.295), channel_id=1, source_target_pairs={{0,6},{2,4},{4,2},{6,0},{1,7},{3,5},{5,3},{7,1},{8,14},{10,12},{12... | collective-permute-start | bytes 430088 | tf_op jit(solution)/shard_map/ppermute | solution.py:631
  222.5 2.6 %maximum_select_fusion.1 = bf16[512,1024]{1,0:T(8,128)(2,1)} fusion(bf16[256,1024]{1,0:T(8,128)(2,1)} %collective-permute-done.35, bf16[256,1024]{1,0:T(8,128)(2,1)S(1)} %get-tuple-element.381, pred[]{:T(512)S(6)} %eq.8), kind=kLoop, calls=%fused_computation.14 | loop fusion | flops 4718592 | bytes 2097153 | tf_op jit(solution)/shard_map/jit(_where)/select_n | solution.py:1014
  225.1 1.5 maximum_select_fusion
  226.6 5.6 %collective-permute-done.44 = f16[112,640]{1,0:T(8,128)(2,1)S(1)} collective-permute-done((f16[112,640]{1,0:T(8,128)(2,1)S(1)}, f16[112,640]{1,0:T(8,128)(2,1)S(1)}, u32[]{:S(2)}, u32[]{:S(2)}) %collective-permute-start.44) | collective-permute-done | bytes 143392 | tf_op jit(solution)/shard_map/ppermute | solution.py:631
  233.2 2.6 %finish.1 = (f32[4,1024]{1,0:T(4,128)}, f32[1,1024]{1,0:T(1,128)}, f32[1,1024]{1,0:T(1,128)}, f32[4,256]{1,0:T(4,128)}, f32[1,256]{1,0:T(1,128)}, /*index=5*/f32...) custom-call(s32[10]{0:T(128)} %stack.79.s_ref, f32[16,640]{1,0:T(8,128)} %get-tuple-element.387.first, ...), custom_call_target="tpu_custom_call" | custom-call | tf_op jit(solution)/shard_map/finish/pallas_call | solution.py:1037
  (281 shorter events, 45.2 us)
Async XLA Ops:
  6.1 22.3 %collective-permute-start.2 = (bf16[256,896]{1,0:T(8,128)(2,1)}, bf16[256,896]{1,0:T(8,128)(2,1)}, u32[]{:S(2)}, u32[]{:S(2)}) collective-permute-start(bf16[256,896]{1,0:T(8,128)(2,1)} %concatenate.134.rest_0_), channel_id=1, source_target_pairs={{0,24},{8,16},{16,8},{24,0},{1,25},{9,17},{17,9},{25,1},{2,26},{10... | collective-permute-start | bytes 1376264 | tf_op jit(solution)/shard_map/ppermute | solution.py:639
  10.0 20.7 %collective-permute-start.1 = (bf16[256,896]{1,0:T(8,128)(2,1)}, bf16[256,896]{1,0:T(8,128)(2,1)}, u32[]{:S(2)}, u32[]{:S(2)}) collective-permute-start(bf16[256,896]{1,0:T(8,128)(2,1)} %concatenate.134.rest_0_), channel_id=1, source_target_pairs={{0,16},{8,24},{16,0},{24,8},{1,17},{9,25},{17,1},{25,9},{2,18},{10... | collective-permute-start | bytes 1376264 | tf_op jit(solution)/shard_map/ppermute | solution.py:639
  10.5 20.5 %collective-permute-start = (bf16[256,896]{1,0:T(8,128)(2,1)}, bf16[256,896]{1,0:T(8,128)(2,1)}, u32[]{:S(2)}, u32[]{:S(2)}) collective-permute-start(bf16[256,896]{1,0:T(8,128)(2,1)} %concatenate.134.rest_0_), channel_id=1, source_target_pairs={{0,8},{8,0},{16,24},{24,16},{1,9},{9,1},{17,25},{25,17},{2,10},{10... | collective-permute-start | bytes 1376264 | tf_op jit(solution)/shard_map/ppermute | solution.py:639
  10.7 13.4 %collective-permute-start.3 = (bf16[256,1024]{1,0:T(8,128)(2,1)S(1)}, bf16[256,1024]{1,0:T(8,128)(2,1)}, u32[]{:S(2)}, u32[]{:S(2)}) collective-permute-start(bf16[256,1024]{1,0:T(8,128)(2,1)S(1)} %get-tuple-element.365), channel_id=1, source_target_pairs={{0,2},{2,0},{4,6},{6,4},{1,3},{3,1},{5,7},{7,5},{8,10},{10,8},{12,... | collective-permute-start | bytes 1572872 | tf_op jit(solution)/shard_map/ppermute | solution.py:631
  16.4 0.7 collective-permute-start.5
  17.0 7.9 %collective-permute-start.6 = (bf16[16,1024]{1,0:T(8,128)(2,1)S(1)}, bf16[16,1024]{1,0:T(8,128)(2,1)S(1)}, u32[]{:S(2)}, u32[]{:S(2)}) collective-permute-start(bf16[16,1024]{1,0:T(8,128)(2,1)S(1)} %collective-permute-done.5), channel_id=1, source_target_pairs={{0,1},{1,0},{2,3},{3,2},{4,5},{5,4},{6,7},{7,6},{8,9},{9,8},{10,11... | collective-permute-start | bytes 98312 | tf_op jit(solution)/shard_map/ppermute | solution.py:628
  24.1 10.5 %collective-permute-start.4 = (bf16[256,1024]{1,0:T(8,128)(2,1)}, bf16[256,1024]{1,0:T(8,128)(2,1)}, u32[]{:S(2)}, u32[]{:S(2)}) collective-permute-start(bf16[256,1024]{1,0:T(8,128)(2,1)} %collective-permute-done.3.near), channel_id=1, source_target_pairs={{0,1},{1,0},{2,3},{3,2},{4,5},{5,4},{6,7},{7,6},{8,9},{9,8},{10,11... | collective-permute-start | bytes 1572872 | tf_op jit(solution)/shard_map/ppermute | solution.py:628
  25.0 23.7 %collective-permute-start.7 = (bf16[256,1024]{1,0:T(8,128)(2,1)}, bf16[256,1024]{1,0:T(8,128)(2,1)}, u32[]{:S(2)}, u32[]{:S(2)}) collective-permute-start(bf16[256,1024]{1,0:T(8,128)(2,1)} %constant_dynamic-slice_fusion.12), channel_id=1, source_target_pairs={{0,2},{2,0},{4,6},{6,4},{1,3},{3,1},{5,7},{7,5},{8,10},{10,8},{12,... | collective-permute-start | bytes 1572872 | tf_op jit(solution)/shard_map/ppermute | solution.py:631
  31.1 29.6 %collective-permute-start.11 = (bf16[256,1024]{1,0:T(8,128)(2,1)S(1)}, bf16[256,1024]{1,0:T(8,128)(2,1)S(1)}, u32[]{:S(2)}, u32[]{:S(2)}) collective-permute-start(bf16[256,1024]{1,0:T(8,128)(2,1)S(1)} %pad_maximum_fusion.13.rest_0_.rest_4_), channel_id=1, source_target_pairs={{0,24},{8,16},{16,8},{24,0},{1,25},{9,17},{17,9},{25,1},{2,26},{10... | collective-permute-start | bytes 1572872 | tf_op jit(solution)/shard_map/ppermute | solution.py:639
  32.6 28.1 %collective-permute-start.10 = (bf16[256,1024]{1,0:T(8,128)(2,1)S(1)}, bf16[256,1024]{1,0:T(8,128)(2,1)S(1)}, u32[]{:S(2)}, u32[]{:S(2)}) collective-permute-start(bf16[256,1024]{1,0:T(8,128)(2,1)S(1)} %pad_maximum_fusion.13.rest_0_.rest_4_), channel_id=1, source_target_pairs={{0,16},{8,24},{16,0},{24,8},{1,17},{9,25},{17,1},{25,9},{2,18},{10... | collective-permute-start | bytes 1572872 | tf_op jit(solution)/shard_map/ppermute | solution.py:639
  34.1 26.6 %collective-permute-start.9 = (bf16[256,1024]{1,0:T(8,128)(2,1)S(1)}, bf16[256,1024]{1,0:T(8,128)(2,1)S(1)}, u32[]{:S(2)}, u32[]{:S(2)}) collective-permute-start(bf16[256,1024]{1,0:T(8,128)(2,1)S(1)} %pad_maximum_fusion.13.rest_0_.rest_4_), channel_id=1, source_target_pairs={{0,8},{8,0},{16,24},{24,16},{1,9},{9,1},{17,25},{25,17},{2,10},{10... | collective-permute-start | bytes 1572872 | tf_op jit(solution)/shard_map/ppermute | solution.py:639
  48.6 12.0 %collective-permute-start.8 = (bf16[256,1024]{1,0:T(8,128)(2,1)}, bf16[256,1024]{1,0:T(8,128)(2,1)S(1)}, u32[]{:S(2)}, u32[]{:S(2)}) collective-permute-start(bf16[256,1024]{1,0:T(8,128)(2,1)} %collective-permute-done.7.near), channel_id=1, source_target_pairs={{0,1},{1,0},{2,3},{3,2},{4,5},{5,4},{6,7},{7,6},{8,9},{9,8},{10,11... | collective-permute-start | bytes 1572872 | tf_op jit(solution)/shard_map/ppermute | solution.py:628
  48.7 21.1 %collective-permute-start.12 = (f32[128,512]{1,0:T(8,128)}, f32[128,512]{1,0:T(8,128)S(1)}, u32[]{:S(2)}, u32[]{:S(2)}) collective-permute-start(f32[128,512]{1,0:T(8,128)} %get-tuple-element.188.hend), channel_id=1, source_target_pairs={{0,4},{2,6},{1,5},{3,7},{8,12},{10,14},{9,13},{11,15},{16,20},{18,... | collective-permute-start | bytes 786440 | tf_op jit(solution)/shard_map/ppermute | solution.py:634
  76.4 4.2 %collective-permute-start.15 = (f32[16,1024]{1,0:T(8,128)S(1)}, f32[16,1024]{1,0:T(8,128)S(1)}, u32[]{:S(2)}, u32[]{:S(2)}) collective-permute-start(f32[16,1024]{1,0:T(8,128)S(1)} %get-tuple-element.190.sums), channel_id=1, source_target_pairs={{0,3},{1,2},{2,1},{3,0},{4,7},{5,6},{6,5},{7,4},{8,11},{9,10},{10,... | collective-permute-start | bytes 196616 | tf_op jit(solution)/shard_map/ppermute | solution.py:810
  78.1 4.3 %collective-permute-start.14 = (f32[16,1024]{1,0:T(8,128)S(1)}, f32[16,1024]{1,0:T(8,128)S(1)}, u32[]{:S(2)}, u32[]{:S(2)}) collective-permute-start(f32[16,1024]{1,0:T(8,128)S(1)} %get-tuple-element.190.sums), channel_id=1, source_target_pairs={{0,2},{2,0},{4,6},{6,4},{1,3},{3,1},{5,7},{7,5},{8,10},{10,8},{12,... | collective-permute-start | bytes 196616 | tf_op jit(solution)/shard_map/ppermute | solution.py:631
  78.4 4.0 %collective-permute-start.13 = (f32[16,1024]{1,0:T(8,128)S(1)}, f32[16,1024]{1,0:T(8,128)S(1)}, u32[]{:S(2)}, u32[]{:S(2)}) collective-permute-start(f32[16,1024]{1,0:T(8,128)S(1)} %get-tuple-element.190.sums), channel_id=1, source_target_pairs={{0,1},{1,0},{2,3},{3,2},{4,5},{5,4},{6,7},{7,6},{8,9},{9,8},{10,11... | collective-permute-start | bytes 196616 | tf_op jit(solution)/shard_map/ppermute | solution.py:628
  99.0 23.6 %collective-permute-start.19 = (f16[272,1024]{1,0:T(8,128)(2,1)S(1)}, f16[272,1024]{1,0:T(8,128)(2,1)}, u32[]{:S(2)}, u32[]{:S(2)}) collective-permute-start(f16[272,1024]{1,0:T(8,128)(2,1)S(1)} %get-tuple-element.417), channel_id=1, source_target_pairs={{0,24},{8,16},{16,8},{24,0},{1,25},{9,17},{17,9},{25,1},{2,26},{10... | collective-permute-start | bytes 1671176 | tf_op jit(solution)/shard_map/ppermute | solution.py:639
  100.7 25.3 %collective-permute-start.18 = (f16[272,1024]{1,0:T(8,128)(2,1)S(1)}, f16[272,1024]{1,0:T(8,128)(2,1)}, u32[]{:S(2)}, u32[]{:S(2)}) collective-permute-start(f16[272,1024]{1,0:T(8,128)(2,1)S(1)} %get-tuple-element.418), channel_id=1, source_target_pairs={{0,16},{8,24},{16,0},{24,8},{1,17},{9,25},{17,1},{25,9},{2,18},{10... | collective-permute-start | bytes 1671176 | tf_op jit(solution)/shard_map/ppermute | solution.py:639
  102.0 24.0 %collective-permute-start.17 = (f16[272,1024]{1,0:T(8,128)(2,1)S(1)}, f16[272,1024]{1,0:T(8,128)(2,1)}, u32[]{:S(2)}, u32[]{:S(2)}) collective-permute-start(f16[272,1024]{1,0:T(8,128)(2,1)S(1)} %get-tuple-element.419), channel_id=1, source_target_pairs={{0,8},{8,0},{16,24},{24,16},{1,9},{9,1},{17,25},{25,17},{2,10},{10... | collective-permute-start | bytes 1671176 | tf_op jit(solution)/shard_map/ppermute | solution.py:639
  102.5 20.0 %collective-permute-start.16 = (f32[128,512]{1,0:T(8,128)S(1)}, f32[128,512]{1,0:T(8,128)S(1)}, u32[]{:S(2)}, u32[]{:S(2)}) collective-permute-start(f32[128,512]{1,0:T(8,128)S(1)} %get-tuple-element.191), channel_id=1, source_target_pairs={{4,0},{6,2},{5,1},{7,3},{12,8},{14,10},{13,9},{15,11},{20,16},{22,... | collective-permute-start | bytes 786440 | tf_op jit(solution)/shard_map/ppermute | solution.py:634
  126.0 2.9 %collective-permute-start.21 = (f32[256,1024]{1,0:T(8,128)}, f32[256,1024]{1,0:T(8,128)S(1)}, u32[]{:S(2)}, u32[]{:S(2)}) collective-permute-start(f32[256,1024]{1,0:T(8,128)} %get-tuple-element.216), channel_id=1, source_target_pairs={{0,1},{1,0},{2,3},{3,2},{4,5},{5,4},{6,7},{7,6},{8,9},{9,8},{10,11... | collective-permute-start | bytes 3145736 | tf_op jit(solution)/shard_map/ppermute | solution.py:628
  129.9 14.5 %collective-permute-start.22 = (f32[64,1024]{1,0:T(8,128)S(1)}, f32[64,1024]{1,0:T(8,128)S(1)}, u32[]{:S(2)}, u32[]{:S(2)}) collective-permute-start(f32[64,1024]{1,0:T(8,128)S(1)} %slice_add_fusion.1), channel_id=1, source_target_pairs={{0,2},{2,0},{4,6},{6,4},{1,3},{3,1},{5,7},{7,5},{8,10},{10,8},{12,... | collective-permute-start | bytes 786440 | tf_op jit(solution)/shard_map/ppermute | solution.py:631
  132.1 23.1 %collective-permute-start.25 = (f16[80,1024]{1,0:T(8,128)(2,1)S(1)}, f16[80,1024]{1,0:T(8,128)(2,1)S(1)}, u32[]{:S(2)}, u32[]{:S(2)}) collective-permute-start(f16[80,1024]{1,0:T(8,128)(2,1)S(1)} %get-tuple-element.414), channel_id=1, source_target_pairs={{0,6},{2,4},{4,2},{6,0},{1,7},{3,5},{5,3},{7,1},{8,14},{10,12},{12... | collective-permute-start | bytes 491528 | tf_op jit(solution)/shard_map/ppermute | solution.py:631
  132.1 23.1 %collective-permute-start.24 = (f16[80,1024]{1,0:T(8,128)(2,1)S(1)}, f16[80,1024]{1,0:T(8,128)(2,1)S(1)}, u32[]{:S(2)}, u32[]{:S(2)}) collective-permute-start(f16[80,1024]{1,0:T(8,128)(2,1)S(1)} %get-tuple-element.415), channel_id=1, source_target_pairs={{0,4},{2,6},{4,0},{6,2},{1,5},{3,7},{5,1},{7,3},{8,12},{10,14},{12... | collective-permute-start | bytes 491528 | tf_op jit(solution)/shard_map/ppermute | solution.py:631
  133.6 21.6 %collective-permute-start.23 = (f16[80,1024]{1,0:T(8,128)(2,1)S(1)}, f16[80,1024]{1,0:T(8,128)(2,1)S(1)}, u32[]{:S(2)}, u32[]{:S(2)}) collective-permute-start(f16[80,1024]{1,0:T(8,128)(2,1)S(1)} %get-tuple-element.416), channel_id=1, source_target_pairs={{0,2},{2,0},{4,6},{6,4},{1,3},{3,1},{5,7},{7,5},{8,10},{10,8},{12,... | collective-permute-start | bytes 491528 | tf_op jit(solution)/shard_map/ppermute | solution.py:631
  155.4 6.5 %collective-permute-start.26 = (f32[8,512]{1,0:T(8,128)S(1)}, f32[8,512]{1,0:T(8,128)S(1)}, u32[]{:S(2)}, u32[]{:S(2)}) collective-permute-start(f32[8,512]{1,0:T(8,128)S(1)} %get-tuple-element.235), channel_id=1, source_target_pairs={{4,0},{6,2},{5,1},{7,3},{12,8},{14,10},{13,9},{15,11},{20,16},{22,... | collective-permute-start | bytes 49160 | tf_op jit(solution)/shard_map/ppermute | solution.py:634
  156.7 5.9 %collective-permute-start.27 = (f32[512,256]{1,0:T(8,128)S(1)}, f32[512,256]{1,0:T(8,128)S(1)}, u32[]{:S(2)}, u32[]{:S(2)}) collective-permute-start(f32[512,256]{1,0:T(8,128)S(1)} %get-tuple-element.241), channel_id=1, source_target_pairs={{0,1},{1,0},{2,3},{3,2},{4,5},{5,4},{6,7},{7,6},{8,9},{9,8},{10,11... | collective-permute-start | bytes 1572872 | tf_op jit(solution)/shard_map/ppermute | solution.py:628
  162.7 6.5 %collective-permute-start.28 = (f32[512,128]{1,0:T(8,128)S(1)}, f32[512,128]{1,0:T(8,128)S(1)}, u32[]{:S(2)}, u32[]{:S(2)}) collective-permute-start(f32[512,128]{1,0:T(8,128)S(1)} %constant_dynamic-slice_fusion.10), channel_id=1, source_target_pairs={{0,2},{2,0},{4,6},{6,4},{1,3},{3,1},{5,7},{7,5},{8,10},{10,8},{12,... | collective-permute-start | bytes 786440 | tf_op jit(solution)/shard_map/ppermute | solution.py:631
  169.2 1.6 collective-permute-start.29
  171.5 6.4 %collective-permute-start.30 = (f32[8,128]{1,0:T(8,128)S(1)}, f32[8,128]{1,0:T(8,128)S(1)}, u32[]{:S(2)}, u32[]{:S(2)}) collective-permute-start(f32[8,128]{1,0:T(8,128)S(1)} %fusion.21), channel_id=1, source_target_pairs={{4,0},{6,2},{5,1},{7,3},{12,8},{14,10},{13,9},{15,11},{20,16},{22,... | collective-permute-start | bytes 12296 | tf_op jit(solution)/shard_map/ppermute | solution.py:634
  177.9 18.6 %collective-permute-start.31 = (f32[192,1024]{1,0:T(8,128)}, f32[192,1024]{1,0:T(8,128)S(1)}, u32[]{:S(2)}, u32[]{:S(2)}) collective-permute-start(f32[192,1024]{1,0:T(8,128)} %slice_add_fusion), channel_id=1, source_target_pairs={{0,2},{2,0},{4,6},{6,4},{1,3},{3,1},{5,7},{7,5},{8,10},{10,8},{12,... | collective-permute-start | bytes 2359304 | tf_op jit(solution)/shard_map/ppermute | solution.py:631
  178.3 12.6 %collective-permute-start.32 = (f16[304,512]{1,0:T(8,128)(2,1)}, f16[304,512]{1,0:T(8,128)(2,1)}, u32[]{:S(2)}, u32[]{:S(2)}) collective-permute-start(f16[304,512]{1,0:T(8,128)(2,1)} %get-tuple-element.264), channel_id=1, source_target_pairs={{0,8},{8,0},{16,24},{24,16},{1,9},{9,1},{17,25},{25,17},{2,10},{10... | collective-permute-start | bytes 933896 | tf_op jit(solution)/shard_map/ppermute | solution.py:639
  179.8 14.5 %collective-permute-start.33 = (f16[304,512]{1,0:T(8,128)(2,1)S(1)}, f16[304,512]{1,0:T(8,128)(2,1)}, u32[]{:S(2)}, u32[]{:S(2)}) collective-permute-start(f16[304,512]{1,0:T(8,128)(2,1)S(1)} %get-tuple-element.265), channel_id=1, source_target_pairs={{0,16},{8,24},{16,0},{24,8},{1,17},{9,25},{17,1},{25,9},{2,18},{10... | collective-permute-start | bytes 933896 | tf_op jit(solution)/shard_map/ppermute | solution.py:639
  180.5 13.7 %collective-permute-start.34 = (f16[304,512]{1,0:T(8,128)(2,1)S(1)}, f16[304,512]{1,0:T(8,128)(2,1)}, u32[]{:S(2)}, u32[]{:S(2)}) collective-permute-start(f16[304,512]{1,0:T(8,128)(2,1)S(1)} %get-tuple-element.266), channel_id=1, source_target_pairs={{0,24},{8,16},{16,8},{24,0},{1,25},{9,17},{17,9},{25,1},{2,26},{10... | collective-permute-start | bytes 933896 | tf_op jit(solution)/shard_map/ppermute | solution.py:639
  196.6 2.7 %collective-permute-start.37 = (f32[256,1024]{1,0:T(8,128)S(1)}, f32[256,1024]{1,0:T(8,128)S(1)}, u32[]{:S(2)}, u32[]{:S(2)}) collective-permute-start(f32[256,1024]{1,0:T(8,128)S(1)} %get-tuple-element.272), channel_id=1, source_target_pairs={{0,1},{1,0},{2,3},{3,2},{4,5},{5,4},{6,7},{7,6},{8,9},{9,8},{10,11... | collective-permute-start | bytes 3145736 | tf_op jit(solution)/shard_map/ppermute | solution.py:628
  196.6 18.8 %collective-permute-start.20 = (f32[256,1024]{1,0:T(8,128)S(1)}, f32[256,1024]{1,0:T(8,128)S(1)}, u32[]{:S(2)}, u32[]{:S(2)}) collective-permute-start(f32[256,1024]{1,0:T(8,128)S(1)} %copy-done.45), channel_id=1, source_target_pairs={{0,1},{1,0},{2,3},{3,2},{4,5},{5,4},{6,7},{7,6},{8,9},{9,8},{10,11... | collective-permute-start | bytes 3145736 | tf_op jit(solution)/shard_map/ppermute | solution.py:628
  199.7 14.7 %collective-permute-start.41 = (f16[272,1024]{1,0:T(8,128)(2,1)S(1)}, f16[272,1024]{1,0:T(8,128)(2,1)S(1)}, u32[]{:S(2)}, u32[]{:S(2)}) collective-permute-start(f16[272,1024]{1,0:T(8,128)(2,1)S(1)} %pad_maximum_fusion.3), channel_id=1, source_target_pairs={{0,2},{2,0},{4,6},{6,4},{1,3},{3,1},{5,7},{7,5},{8,10},{10,8},{12,... | collective-permute-start | bytes 1671176 | tf_op jit(solution)/shard_map/ppermute | solution.py:631
  205.0 5.8 %collective-permute-start.40 = (f16[304,128]{1,0:T(8,128)(2,1)S(1)}, f16[304,128]{1,0:T(8,128)(2,1)S(1)}, u32[]{:S(2)}, u32[]{:S(2)}) collective-permute-start(f16[304,128]{1,0:T(8,128)(2,1)S(1)} %get-tuple-element.420), channel_id=1, source_target_pairs={{0,24},{8,16},{16,8},{24,0},{1,25},{9,17},{17,9},{25,1},{2,26},{10... | collective-permute-start | bytes 233480 | tf_op jit(solution)/shard_map/ppermute | solution.py:639
  206.7 5.0 %collective-permute-start.39 = (f16[304,128]{1,0:T(8,128)(2,1)S(1)}, f16[304,128]{1,0:T(8,128)(2,1)S(1)}, u32[]{:S(2)}, u32[]{:S(2)}) collective-permute-start(f16[304,128]{1,0:T(8,128)(2,1)S(1)} %get-tuple-element.421), channel_id=1, source_target_pairs={{0,16},{8,24},{16,0},{24,8},{1,17},{9,25},{17,1},{25,9},{2,18},{10... | collective-permute-start | bytes 233480 | tf_op jit(solution)/shard_map/ppermute | solution.py:639
  208.0 4.4 %collective-permute-start.38 = (f16[304,128]{1,0:T(8,128)(2,1)S(1)}, f16[304,128]{1,0:T(8,128)(2,1)S(1)}, u32[]{:S(2)}, u32[]{:S(2)}) collective-permute-start(f16[304,128]{1,0:T(8,128)(2,1)S(1)} %get-tuple-element.422), channel_id=1, source_target_pairs={{0,8},{8,0},{16,24},{24,16},{1,9},{9,1},{17,25},{25,17},{2,10},{10... | collective-permute-start | bytes 233480 | tf_op jit(solution)/shard_map/ppermute | solution.py:639
  210.8 4.1 %collective-permute-start.36 = (f32[256,1024]{1,0:T(8,128)S(1)}, f32[256,1024]{1,0:T(8,128)S(1)}, u32[]{:S(2)}, u32[]{:S(2)}) collective-permute-start(f32[256,1024]{1,0:T(8,128)S(1)} %get-tuple-element.269), channel_id=1, source_target_pairs={{0,1},{1,0},{2,3},{3,2},{4,5},{5,4},{6,7},{7,6},{8,9},{9,8},{10,11... | collective-permute-start | bytes 3145736 | tf_op jit(solution)/shard_map/ppermute | solution.py:628
  217.0 8.1 %collective-permute-start.42 = (f32[256,1024]{1,0:T(8,128)S(1)}, f32[256,1024]{1,0:T(8,128)S(1)}, u32[]{:S(2)}, u32[]{:S(2)}) collective-permute-start(f32[256,1024]{1,0:T(8,128)S(1)} %get-tuple-element.380), channel_id=1, source_target_pairs={{0,1},{1,0},{2,3},{3,2},{4,5},{5,4},{6,7},{7,6},{8,9},{9,8},{10,11... | collective-permute-start | bytes 3145736 | tf_op jit(solution)/shard_map/ppermute | solution.py:628
  217.0 5.4 %collective-permute-start.35 = (bf16[256,1024]{1,0:T(8,128)(2,1)S(1)}, bf16[256,1024]{1,0:T(8,128)(2,1)}, u32[]{:S(2)}, u32[]{:S(2)}) collective-permute-start(bf16[256,1024]{1,0:T(8,128)(2,1)S(1)} %get-tuple-element.381), channel_id=1, source_target_pairs={{0,1},{1,0},{2,3},{3,2},{4,5},{5,4},{6,7},{7,6},{8,9},{9,8},{10,11... | collective-permute-start | bytes 1572872 | tf_op jit(solution)/shard_map/ppermute | solution.py:628
  218.1 8.5 %collective-permute-start.43 = (f16[112,640]{1,0:T(8,128)(2,1)S(1)}, f16[112,640]{1,0:T(8,128)(2,1)S(1)}, u32[]{:S(2)}, u32[]{:S(2)}) collective-permute-start(f16[112,640]{1,0:T(8,128)(2,1)S(1)} %get-tuple-element.293), channel_id=1, source_target_pairs={{0,2},{2,0},{4,6},{6,4},{1,3},{3,1},{5,7},{7,5},{8,10},{10,8},{12,... | collective-permute-start | bytes 430088 | tf_op jit(solution)/shard_map/ppermute | solution.py:631
  218.4 13.7 %collective-permute-start.44 = (f16[112,640]{1,0:T(8,128)(2,1)S(1)}, f16[112,640]{1,0:T(8,128)(2,1)S(1)}, u32[]{:S(2)}, u32[]{:S(2)}) collective-permute-start(f16[112,640]{1,0:T(8,128)(2,1)S(1)} %get-tuple-element.294), channel_id=1, source_target_pairs={{0,4},{2,6},{4,0},{6,2},{1,5},{3,7},{5,1},{7,3},{8,12},{10,14},{12... | collective-permute-start | bytes 430088 | tf_op jit(solution)/shard_map/ppermute | solution.py:631
  219.0 13.1 %collective-permute-start.45 = (f16[112,640]{1,0:T(8,128)(2,1)S(1)}, f16[112,640]{1,0:T(8,128)(2,1)S(1)}, u32[]{:S(2)}, u32[]{:S(2)}) collective-permute-start(f16[112,640]{1,0:T(8,128)(2,1)S(1)} %get-tuple-element.295), channel_id=1, source_target_pairs={{0,6},{2,4},{4,2},{6,0},{1,7},{3,5},{5,3},{7,1},{8,14},{10,12},{12... | collective-permute-start | bytes 430088 | tf_op jit(solution)/shard_map/ppermute | solution.py:631
  235.8 2.6 %collective-permute-start.46 = (f32[1024]{0:T(1024)}, f32[1024]{0:T(1024)S(1)}, u32[]{:S(2)}, u32[]{:S(2)}) collective-permute-start(f32[1024]{0:T(1024)} %bitcast.121), channel_id=1, source_target_pairs={{0,1},{1,0},{2,3},{3,2},{4,5},{5,4},{6,7},{7,6},{8,9},{9,8},{10,11... | collective-permute-start | bytes 12296 | tf_op jit(solution)/shard_map/ppermute | solution.py:628
  235.9 3.0 %collective-permute-start.47 = (f32[2,64,64]{2,1,0:T(8,128)S(1)}, f32[2,64,64]{2,1,0:T(8,128)S(1)}, u32[]{:S(2)}, u32[]{:S(2)}) collective-permute-start(f32[2,64,64]{2,1,0:T(8,128)S(1)} %get-tuple-element.403), channel_id=1, source_target_pairs={{0,1},{1,0},{2,3},{3,2},{4,5},{5,4},{6,7},{7,6},{8,9},{9,8},{10,11... | collective-permute-start | bytes 98312 | tf_op jit(solution)/shard_map/ppermute | solution.py:628
  (49 other events, 483.2 us)

commit v6 on v5

--- a/solution.py
+++ b/solution.py
@@ -788,7 +788,7 @@
         (count,),
         [rows_spec(model), own_spec, part_spec, part_spec] + [whole((shard, 2 * inner))] * parts,
         [rows_spec(inner), rows_spec(inner), rows_spec(model)],
-        [shaped((tokens, inner)), shaped((tokens, inner)), shaped((tokens, model), BF16)],
+        [shaped((tokens, inner)), shaped((tokens, inner)), kept((tokens, model), BF16)],
         [pltpu.VMEM((model, 2 * inner), BF16)],
         name="gates",
         limit=20 << 20,

time: 241 us -> 240 us (level)
    unnamed x103 -> x101, local copies, waits for them, and re-layouts: 8.22 us -> 6.87 us
where the time goes in v6:
time: 240 us; the launch traced here: 239 us
  Pallas kernels  105 us (44%)
  starting transfers between devices  48 us (20%)
  waiting for transfers between devices  45.2 us (19%)
  other arithmetic  21 us (9%)
  local copies, waits for them, and re-layouts  17.2 us (7%)
  between operations  2.53 us (1%)
    ppermute x13, waiting for transfers between devices, across(): return lax.ppermute(value, 'ctx', [(i, i ^ j) for i in range(ctxs)])  20.3 us
    ppermute x15, starting transfers between devices, spread(): return lax.ppermute(value, 'dp', [(i, i ^ j) for i in range(dps)])  18.6 us
    ppermute x13, starting transfers between devices, across(): return lax.ppermute(value, 'ctx', [(i, i ^ j) for i in range(ctxs)])  15.9 us
    pallas_call x3, Pallas kernels, grads(): grid_call(functools.partial(grads_body, parts, [(n, n + 1) for n in range...  14.8 us
    pallas_call x1, Pallas kernels, per_device(): grid_call(functools.partial(front_body, parts, inner, states, quarter), (...  14 us
    ppermute x15, waiting for transfers between devices, spread(): return lax.ppermute(value, 'dp', [(i, i ^ j) for i in range(dps)])  13.1 us
    pallas_call x1, Pallas kernels, per_device(): grid_call(functools.partial(back_body, inner, states), (count,), [rows_sp...  11.6 us
    pallas_call x1, Pallas kernels, per_device(): grid_call(functools.partial(join_body, inner), (count,), [back(inner), ba...  10 us
  transfers between devices with their start and end apart: 48, of which 18 were waited for; matrix products, arithmetic and copies ran while one was open for 10% of the time, Pallas kernels for 34%

profile of v6, /device:TPU:0, one launch (start us, length us, event | category | flops | bytes accessed | tf_op | source)
XLA Modules:
  0.0 239.1 jit_solution(15008052857750145244)
XLA Ops:
  1.7 3.3 %constant_dynamic-slice_fusion.15 = (bf16[256,1,512]{2,1,0:T(2,128)(2,1)}, bf16[256,1,512]{2,1,0:T(2,128)(2,1)S(1)}) fusion(bf16[256,2,1024]{2,1,0:T(2,128)(2,1)} %param.20, s32[]{:T(128)S(6)} %select_n.151, s32[]{:T(128)S(6)} %add.319), kind=kLoop, calls=%fused_computation.137 | loop fusion | bytes 1048584 | tf_op jit(solution)/shard_map/slice | solution.py:736
  6.1 3.9 %collective-permute-start.2 = (bf16[256,896]{1,0:T(8,128)(2,1)}, bf16[256,896]{1,0:T(8,128)(2,1)}, u32[]{:S(2)}, u32[]{:S(2)}) collective-permute-start(bf16[256,896]{1,0:T(8,128)(2,1)} %concatenate.134.rest_0_), channel_id=1, source_target_pairs={{0,24},{8,16},{16,8},{24,0},{1,25},{9,17},{17,9},{25,1},{2,26},{10... | collective-permute-start | bytes 1376264 | tf_op jit(solution)/shard_map/ppermute | solution.py:639
  10.7 2.2 collective-permute-start.3
  17.1 7.0 %collective-permute-done.3.near = bf16[256,1024]{1,0:T(8,128)(2,1)} collective-permute-done((bf16[256,1024]{1,0:T(8,128)(2,1)S(1)}, bf16[256,1024]{1,0:T(8,128)(2,1)}, u32[]{:S(2)}, u32[]{:S(2)}) %collective-permute-start.3) | collective-permute-done | bytes 524320 | tf_op jit(solution)/shard_map/ppermute | solution.py:631
  25.0 1.7 collective-permute-start.7
  28.4 2.2 collective-permute-done.1.rest_2_
  31.1 1.5 collective-permute-start.11
  32.6 1.5 collective-permute-start.10
  34.6 14.0 %front.1 = (bf16[1024,1024]{1,0:T(8,128)(2,1)}, f32[1024,768]{1,0:T(8,128)}, f32[8,768]{1,0:T(8,128)}, f32[1024,768]{1,0:T(8,128)}, f32[1024,128]{1,0:T(8,128)},...) custom-call(s32[10]{0:T(128)} %stack.79.s_ref, bf16[512,1024]{1,0:T(8,128)(2,1)} %bitcast.92, ...), custom_call_target="tpu_custom_call" | custom-call | tf_op jit(solution)/shard_map/front/pallas_call | solution.py:750
  48.7 4.7 %collective-permute-start.12 = (f32[128,512]{1,0:T(8,128)}, f32[128,512]{1,0:T(8,128)S(1)}, u32[]{:S(2)}, u32[]{:S(2)}) collective-permute-start(f32[128,512]{1,0:T(8,128)} %get-tuple-element.188.hend), channel_id=1, source_target_pairs={{0,4},{2,6},{1,5},{3,7},{8,12},{10,14},{9,13},{11,15},{16,20},{18,... | collective-permute-start | bytes 786440 | tf_op jit(solution)/shard_map/ppermute | solution.py:634
  53.7 6.9 %within.1.yw = f32[1024,512]{1,0:T(8,128)S(1)} custom-call(s32[10]{0:T(128)S(1)} %copy-done.12, f32[1024,768]{1,0:T(8,128)} %get-tuple-element.176.co, f32[1024,128]{1,0:T(8,128)} %get-tuple-element.177.hd), custom_call_target="tpu_custom_call" | custom-call | tf_op jit(solution)/shard_map/within/pallas_call | solution.py:775
  61.9 7.1 %gates.1 = (f32[1024,512]{1,0:T(8,128)S(1)}, f32[1024,512]{1,0:T(8,128)S(1)}, bf16[1024,1024]{1,0:T(8,128)(2,1)}) custom-call(s32[10]{0:T(128)S(1)} %copy-done.12, bf16[1024,1024]{1,0:T(8,128)(2,1)} %get-tuple-element.178.normed.refs_0_, bf16[512,1024]{1,0:T(8,128)(2,1)} %bitcast.94, bf16[256,1024]{1,0:T(8,128)(2,1)} %collective-permute-done.7.near, ...), custom_call_target="tpu_custom_call" | custom-call | tf_op jit(solution)/shard_map/gates/pallas_call | solution.py:786
  69.1 6.5 %output.1 = (f32[1024,512]{1,0:T(8,128)S(1)}, f32[16,1024]{1,0:T(8,128)S(1)}) custom-call(s32[10]{0:T(128)S(1)} %copy-done.12, f32[1024,768]{1,0:T(8,128)} %get-tuple-element.176.co, f32[1024,128]{1,0:T(8,128)} %get-tuple-element.177.hd, f32[1024,512]{1,0:T(8,128)S(1)} %within.1.yw, f32[1024,512]{1,0:T(8,128)S(1)} %get-tuple-element.184.gate, ...), custom_call_target="tpu_custom_call" | custom-call | tf_op jit(solution)/shard_map/output/pallas_call | solution.py:797
  75.6 1.7 collective-permute-start.15
  77.6 2.2 collective-permute-done.15.sums3
  79.8 1.8 collective-permute-done.14.sums2
  83.0 7.8 %turn.1 = (bf16[1024,512]{1,0:T(8,128)(2,1)S(1)}, bf16[1024,512]{1,0:T(8,128)(2,1)S(1)}, f32[1024,512]{1,0:T(8,128)}, f32[8,128,512]{2,1,0:T(8,128)}, f32[128,512]{1,0:T(8,128)S(1)}, /*index=5*/f32[8,512]{1,0:T(8,128)S(1)}) custom-call(s32[10]{0:T(128)S(1)} %copy-done.13, f32[1024,768]{1,0:T(8,128)} %get-tuple-element.176.co, ...), custom_call_target="tpu_custom_call" | custom-call | tf_op jit(solution)/shard_map/turn/pallas_call | solution.py:816
  90.9 6.3 %grad_early.1 = (f32[256,1024]{1,0:T(8,128)S(1)}, f32[256,1024]{1,0:T(8,128)S(1)}, f32[256,1024]{1,0:T(8,128)S(1)}, f32[256,1024]{1,0:T(8,128)S(1)}, f32[16,1024]{1,0:T(8,128)S(1)}, /*index=5*/f32[1,1024]{1,0:T(1,128)S(1)}) custom-call(s32[10]{0:T(128)S(1)} %copy-done.13, bf16[1024,1024]{1,0:T(8,128)(2,1)} %get-tuple-element.178.normed.refs_0_, ...), custom_call_target="tpu_custom_call" | custom-call | tf_op jit(solution)/shard_map/grad_early/pallas_call | solution.py:847
  98.1 1.7 collective-permute-start.19
  101.7 1.5 collective-permute-start.16
  103.2 11.6 %back.1 = (f32[1024,512]{1,0:T(8,128)}, f32[1024,256]{1,0:T(8,128)}) custom-call(s32[10]{0:T(128)} %stack.79.s_ref, f32[1024,768]{1,0:T(8,128)} %get-tuple-element.176.co, f32[1024,128]{1,0:T(8,128)} %get-tuple-element.177.hd, f32[1024,512]{1,0:T(8,128)} %get-tuple-element.202.og, f32[8,128,512]{2,1,0:T(8,128)} %get-tuple-element.186.hloc.hnext, ...), custom_call_target="tpu_custom_call" | custom-call | tf_op jit(solution)/shard_map/back/pallas_call | solution.py:863
  114.8 6.9 %branch.1 = (f32[256,1024]{1,0:T(8,128)}, f32[256,1024]{1,0:T(8,128)}, f32[256,1024]{1,0:T(8,128)}, f32[256,1024]{1,0:T(8,128)}) custom-call(s32[10]{0:T(128)} %stack.79.s_ref, bf16[1024,512]{1,0:T(8,128)(2,1)} %copy-done.5, bf16[256,1024]{1,0:T(8,128)(2,1)} %copy-done.22, bf16[256,1024]{1,0:T(8,128)(2,1)} %copy-done.26, bf16[256,1024]{1,0:T(8,128)(2,1)} %copy-done.25, ...), custom_call_target="tpu_custom_call" | custom-call | tf_op jit(solution)/shard_map/branch/pallas_call | solution.py:874
  121.7 3.5 %collective-permute-done.18 = f16[272,1024]{1,0:T(8,128)(2,1)} collective-permute-done((f16[272,1024]{1,0:T(8,128)(2,1)S(1)}, f16[272,1024]{1,0:T(8,128)(2,1)}, u32[]{:S(2)}, u32[]{:S(2)}) %collective-permute-start.18) | collective-permute-done | bytes 557088 | tf_op jit(solution)/shard_map/ppermute | solution.py:639
  126.0 1.8 multiply_add_fusion
  129.1 2.0 collective-permute-start.22
  131.3 1.5 collective-permute-start.24
  132.8 2.9 %collective-permute-start.23 = (f16[80,1024]{1,0:T(8,128)(2,1)S(1)}, f16[80,1024]{1,0:T(8,128)(2,1)S(1)}, u32[]{:S(2)}, u32[]{:S(2)}) collective-permute-start(f16[80,1024]{1,0:T(8,128)(2,1)S(1)} %get-tuple-element.416), channel_id=1, source_target_pairs={{0,2},{2,0},{4,6},{6,4},{1,3},{3,1},{5,7},{7,5},{8,10},{10,8},{12,... | collective-permute-start | bytes 491528 | tf_op jit(solution)/shard_map/ppermute | solution.py:631
  135.8 7.8 %meet.1 = (f32[1024,512]{1,0:T(8,128)S(1)}, f32[32,512]{1,0:T(8,128)S(1)}, f32[512,256]{1,0:T(8,128)S(1)}, f32[512,256]{1,0:T(8,128)S(1)}) custom-call(s32[10]{0:T(128)S(1)} %copy-done.14, f32[1024,768]{1,0:T(8,128)} %get-tuple-element.176.co, f32[1024,128]{1,0:T(8,128)} %get-tuple-element.177.hd, f32[1024,512]{1,0:T(8,128)} %get-tuple-element.211.z, ...), custom_call_target="tpu_custom_call" | custom-call | tf_op jit(solution)/shard_map/meet/pallas_call | solution.py:904
  144.3 10.0 %join.1 = (bf16[1024,512]{1,0:T(8,128)(2,1)S(1)}, f32[8,512]{1,0:T(8,128)S(1)}, f32[8,512]{1,0:T(8,128)S(1)}, f32[1024,128]{1,0:T(8,128)S(1)}, f32[8,128]{1,0:T(8,128)S(1)}, /*index=5*/f32[8,512]{1,0:T(8,128)S(1)}) custom-call(s32[10]{0:T(128)S(1)} %copy-done.14, f32[1024,768]{1,0:T(8,128)} %get-tuple-element.176.co, f32[1024,128]{1,0:T(8,128)} %get-tuple-element.177.hd, ...), custom_call_target="tpu_custom_call" | custom-call | tf_op jit(solution)/shard_map/join/pallas_call | solution.py:922
  156.7 4.4 %collective-permute-done.26 = f32[8,512]{1,0:T(8,128)S(1)} collective-permute-done((f32[8,512]{1,0:T(8,128)S(1)}, f32[8,512]{1,0:T(8,128)S(1)}, u32[]{:S(2)}, u32[]{:S(2)}) %collective-permute-start.26) | collective-permute-done | bytes 16416 | tf_op jit(solution)/shard_map/ppermute | solution.py:634
  162.0 4.7 %grad_signal.1 = (f32[256,512]{1,0:T(8,128)S(1)}, f32[256,512]{1,0:T(8,128)S(1)}, f32[256,512]{1,0:T(8,128)S(1)}, f32[256,512]{1,0:T(8,128)S(1)}, f32[16,512]{1,0:T(8,128)S(1)}, /*index=5*/f32[1,512]{1,0:T(1,128)S(1)}) custom-call(s32[10]{0:T(128)S(1)} %copy-done.14, bf16[1024,1024]{1,0:T(8,128)(2,1)} %get-tuple-element.178.normed.refs_0_, ...), custom_call_target="tpu_custom_call" | custom-call | tf_op jit(solution)/shard_map/grad_signal/pallas_call | solution.py:847
  166.7 1.6 collective-permute-done.28
  168.7 1.3 collective-permute-done.29.dbc_other
  170.7 1.6 collective-permute-start.30
  173.2 3.8 %collective-permute-done.30.ahead = f32[8,128]{1,0:T(8,128)S(1)} collective-permute-done((f32[8,128]{1,0:T(8,128)S(1)}, f32[8,128]{1,0:T(8,128)S(1)}, u32[]{:S(2)}, u32[]{:S(2)}) %collective-permute-start.30) | collective-permute-done | bytes 4128 | tf_op jit(solution)/shard_map/ppermute | solution.py:634
  177.5 1.5 collective-permute-start.32
  181.0 9.1 %feature.1 = (f32[256,1024]{1,0:T(8,128)S(1)}, f32[256,1024]{1,0:T(8,128)S(1)}, f32[256,1024]{1,0:T(8,128)S(1)}, f32[256,1024]{1,0:T(8,128)S(1)}, bf16[1024,128]...) custom-call(s32[10]{0:T(128)S(1)} %copy-done.14, bf16[512,1024]{1,0:T(8,128)(2,1)} %bitcast.93, ...), custom_call_target="tpu_custom_call" | custom-call | tf_op jit(solution)/shard_map/feature/pallas_call | solution.py:972
  190.1 3.3 %collective-permute-done.33 = f16[304,512]{1,0:T(8,128)(2,1)} collective-permute-done((f16[304,512]{1,0:T(8,128)(2,1)S(1)}, f16[304,512]{1,0:T(8,128)(2,1)}, u32[]{:S(2)}, u32[]{:S(2)}) %collective-permute-start.33) | collective-permute-done | bytes 311328 | tf_op jit(solution)/shard_map/ppermute | solution.py:639
  193.4 2.3 collective-permute-done.31
  200.2 3.8 %grad_extra.1 = (f32[256,128]{1,0:T(8,128)S(1)}, f32[256,128]{1,0:T(8,128)S(1)}, f32[256,128]{1,0:T(8,128)S(1)}, f32[256,128]{1,0:T(8,128)S(1)}, f32[16,128]{1,0:T(8,128)S(1)}, /*index=5*/f32[1,128]{1,0:T(1,128)S(1)}) custom-call(s32[10]{0:T(128)S(1)} %copy-done.14, bf16[1024,1024]{1,0:T(8,128)(2,1)} %get-tuple-element.178.normed.refs_0_, ...), custom_call_target="tpu_custom_call" | custom-call | tf_op jit(solution)/shard_map/grad_extra/pallas_call | solution.py:847
  204.2 1.7 collective-permute-start.40
  207.8 2.2 collective-permute-done.40
  211.6 1.9 collective-permute-done.41
  218.2 3.4 %collective-permute-start.45 = (f16[112,640]{1,0:T(8,128)(2,1)S(1)}, f16[112,640]{1,0:T(8,128)(2,1)S(1)}, u32[]{:S(2)}, u32[]{:S(2)}) collective-permute-start(f16[112,640]{1,0:T(8,128)(2,1)S(1)} %get-tuple-element.295), channel_id=1, source_target_pairs={{0,6},{2,4},{4,2},{6,0},{1,7},{3,5},{5,3},{7,1},{8,14},{10,12},{12... | collective-permute-start | bytes 430088 | tf_op jit(solution)/shard_map/ppermute | solution.py:631
  221.6 2.6 %maximum_select_fusion.1 = bf16[512,1024]{1,0:T(8,128)(2,1)} fusion(bf16[256,1024]{1,0:T(8,128)(2,1)} %collective-permute-done.35, bf16[256,1024]{1,0:T(8,128)(2,1)S(1)} %get-tuple-element.381, pred[]{:T(512)S(6)} %eq.8), kind=kLoop, calls=%fused_computation.14 | loop fusion | flops 4718592 | bytes 2097153 | tf_op jit(solution)/shard_map/jit(_where)/select_n | solution.py:1014
  224.2 1.5 maximum_select_fusion
  225.7 5.6 %collective-permute-done.44 = f16[112,640]{1,0:T(8,128)(2,1)S(1)} collective-permute-done((f16[112,640]{1,0:T(8,128)(2,1)S(1)}, f16[112,640]{1,0:T(8,128)(2,1)S(1)}, u32[]{:S(2)}, u32[]{:S(2)}) %collective-permute-start.44) | collective-permute-done | bytes 143392 | tf_op jit(solution)/shard_map/ppermute | solution.py:631
  232.3 2.6 %finish.1 = (f32[4,1024]{1,0:T(4,128)}, f32[1,1024]{1,0:T(1,128)}, f32[1,1024]{1,0:T(1,128)}, f32[4,256]{1,0:T(4,128)}, f32[1,256]{1,0:T(1,128)}, /*index=5*/f32...) custom-call(s32[10]{0:T(128)} %stack.79.s_ref, f32[16,640]{1,0:T(8,128)} %get-tuple-element.387.first, ...), custom_call_target="tpu_custom_call" | custom-call | tf_op jit(solution)/shard_map/finish/pallas_call | solution.py:1037
  (279 shorter events, 44.0 us)
Async XLA Ops:
  6.1 22.3 %collective-permute-start.2 = (bf16[256,896]{1,0:T(8,128)(2,1)}, bf16[256,896]{1,0:T(8,128)(2,1)}, u32[]{:S(2)}, u32[]{:S(2)}) collective-permute-start(bf16[256,896]{1,0:T(8,128)(2,1)} %concatenate.134.rest_0_), channel_id=1, source_target_pairs={{0,24},{8,16},{16,8},{24,0},{1,25},{9,17},{17,9},{25,1},{2,26},{10... | collective-permute-start | bytes 1376264 | tf_op jit(solution)/shard_map/ppermute | solution.py:639
  10.0 20.7 %collective-permute-start.1 = (bf16[256,896]{1,0:T(8,128)(2,1)}, bf16[256,896]{1,0:T(8,128)(2,1)}, u32[]{:S(2)}, u32[]{:S(2)}) collective-permute-start(bf16[256,896]{1,0:T(8,128)(2,1)} %concatenate.134.rest_0_), channel_id=1, source_target_pairs={{0,16},{8,24},{16,0},{24,8},{1,17},{9,25},{17,1},{25,9},{2,18},{10... | collective-permute-start | bytes 1376264 | tf_op jit(solution)/shard_map/ppermute | solution.py:639
  10.5 20.5 %collective-permute-start = (bf16[256,896]{1,0:T(8,128)(2,1)}, bf16[256,896]{1,0:T(8,128)(2,1)}, u32[]{:S(2)}, u32[]{:S(2)}) collective-permute-start(bf16[256,896]{1,0:T(8,128)(2,1)} %concatenate.134.rest_0_), channel_id=1, source_target_pairs={{0,8},{8,0},{16,24},{24,16},{1,9},{9,1},{17,25},{25,17},{2,10},{10... | collective-permute-start | bytes 1376264 | tf_op jit(solution)/shard_map/ppermute | solution.py:639
  10.7 13.4 %collective-permute-start.3 = (bf16[256,1024]{1,0:T(8,128)(2,1)S(1)}, bf16[256,1024]{1,0:T(8,128)(2,1)}, u32[]{:S(2)}, u32[]{:S(2)}) collective-permute-start(bf16[256,1024]{1,0:T(8,128)(2,1)S(1)} %get-tuple-element.365), channel_id=1, source_target_pairs={{0,2},{2,0},{4,6},{6,4},{1,3},{3,1},{5,7},{7,5},{8,10},{10,8},{12,... | collective-permute-start | bytes 1572872 | tf_op jit(solution)/shard_map/ppermute | solution.py:631
  16.4 0.7 collective-permute-start.5
  17.0 7.9 %collective-permute-start.6 = (bf16[16,1024]{1,0:T(8,128)(2,1)S(1)}, bf16[16,1024]{1,0:T(8,128)(2,1)S(1)}, u32[]{:S(2)}, u32[]{:S(2)}) collective-permute-start(bf16[16,1024]{1,0:T(8,128)(2,1)S(1)} %collective-permute-done.5), channel_id=1, source_target_pairs={{0,1},{1,0},{2,3},{3,2},{4,5},{5,4},{6,7},{7,6},{8,9},{9,8},{10,11... | collective-permute-start | bytes 98312 | tf_op jit(solution)/shard_map/ppermute | solution.py:628
  24.1 10.5 %collective-permute-start.4 = (bf16[256,1024]{1,0:T(8,128)(2,1)}, bf16[256,1024]{1,0:T(8,128)(2,1)}, u32[]{:S(2)}, u32[]{:S(2)}) collective-permute-start(bf16[256,1024]{1,0:T(8,128)(2,1)} %collective-permute-done.3.near), channel_id=1, source_target_pairs={{0,1},{1,0},{2,3},{3,2},{4,5},{5,4},{6,7},{7,6},{8,9},{9,8},{10,11... | collective-permute-start | bytes 1572872 | tf_op jit(solution)/shard_map/ppermute | solution.py:628
  25.0 23.7 %collective-permute-start.7 = (bf16[256,1024]{1,0:T(8,128)(2,1)}, bf16[256,1024]{1,0:T(8,128)(2,1)}, u32[]{:S(2)}, u32[]{:S(2)}) collective-permute-start(bf16[256,1024]{1,0:T(8,128)(2,1)} %constant_dynamic-slice_fusion.12), channel_id=1, source_target_pairs={{0,2},{2,0},{4,6},{6,4},{1,3},{3,1},{5,7},{7,5},{8,10},{10,8},{12,... | collective-permute-start | bytes 1572872 | tf_op jit(solution)/shard_map/ppermute | solution.py:631
  31.1 29.6 %collective-permute-start.11 = (bf16[256,1024]{1,0:T(8,128)(2,1)S(1)}, bf16[256,1024]{1,0:T(8,128)(2,1)S(1)}, u32[]{:S(2)}, u32[]{:S(2)}) collective-permute-start(bf16[256,1024]{1,0:T(8,128)(2,1)S(1)} %pad_maximum_fusion.13.rest_0_.rest_4_), channel_id=1, source_target_pairs={{0,24},{8,16},{16,8},{24,0},{1,25},{9,17},{17,9},{25,1},{2,26},{10... | collective-permute-start | bytes 1572872 | tf_op jit(solution)/shard_map/ppermute | solution.py:639
  32.6 28.1 %collective-permute-start.10 = (bf16[256,1024]{1,0:T(8,128)(2,1)S(1)}, bf16[256,1024]{1,0:T(8,128)(2,1)S(1)}, u32[]{:S(2)}, u32[]{:S(2)}) collective-permute-start(bf16[256,1024]{1,0:T(8,128)(2,1)S(1)} %pad_maximum_fusion.13.rest_0_.rest_4_), channel_id=1, source_target_pairs={{0,16},{8,24},{16,0},{24,8},{1,17},{9,25},{17,1},{25,9},{2,18},{10... | collective-permute-start | bytes 1572872 | tf_op jit(solution)/shard_map/ppermute | solution.py:639
  34.1 26.6 %collective-permute-start.9 = (bf16[256,1024]{1,0:T(8,128)(2,1)S(1)}, bf16[256,1024]{1,0:T(8,128)(2,1)S(1)}, u32[]{:S(2)}, u32[]{:S(2)}) collective-permute-start(bf16[256,1024]{1,0:T(8,128)(2,1)S(1)} %pad_maximum_fusion.13.rest_0_.rest_4_), channel_id=1, source_target_pairs={{0,8},{8,0},{16,24},{24,16},{1,9},{9,1},{17,25},{25,17},{2,10},{10... | collective-permute-start | bytes 1572872 | tf_op jit(solution)/shard_map/ppermute | solution.py:639
  48.6 12.0 %collective-permute-start.8 = (bf16[256,1024]{1,0:T(8,128)(2,1)}, bf16[256,1024]{1,0:T(8,128)(2,1)S(1)}, u32[]{:S(2)}, u32[]{:S(2)}) collective-permute-start(bf16[256,1024]{1,0:T(8,128)(2,1)} %collective-permute-done.7.near), channel_id=1, source_target_pairs={{0,1},{1,0},{2,3},{3,2},{4,5},{5,4},{6,7},{7,6},{8,9},{9,8},{10,11... | collective-permute-start | bytes 1572872 | tf_op jit(solution)/shard_map/ppermute | solution.py:628
  48.7 20.3 %collective-permute-start.12 = (f32[128,512]{1,0:T(8,128)}, f32[128,512]{1,0:T(8,128)S(1)}, u32[]{:S(2)}, u32[]{:S(2)}) collective-permute-start(f32[128,512]{1,0:T(8,128)} %get-tuple-element.188.hend), channel_id=1, source_target_pairs={{0,4},{2,6},{1,5},{3,7},{8,12},{10,14},{9,13},{11,15},{16,20},{18,... | collective-permute-start | bytes 786440 | tf_op jit(solution)/shard_map/ppermute | solution.py:634
  75.6 4.2 %collective-permute-start.15 = (f32[16,1024]{1,0:T(8,128)S(1)}, f32[16,1024]{1,0:T(8,128)S(1)}, u32[]{:S(2)}, u32[]{:S(2)}) collective-permute-start(f32[16,1024]{1,0:T(8,128)S(1)} %get-tuple-element.190.sums), channel_id=1, source_target_pairs={{0,3},{1,2},{2,1},{3,0},{4,7},{5,6},{6,5},{7,4},{8,11},{9,10},{10,... | collective-permute-start | bytes 196616 | tf_op jit(solution)/shard_map/ppermute | solution.py:810
  77.3 4.3 %collective-permute-start.14 = (f32[16,1024]{1,0:T(8,128)S(1)}, f32[16,1024]{1,0:T(8,128)S(1)}, u32[]{:S(2)}, u32[]{:S(2)}) collective-permute-start(f32[16,1024]{1,0:T(8,128)S(1)} %get-tuple-element.190.sums), channel_id=1, source_target_pairs={{0,2},{2,0},{4,6},{6,4},{1,3},{3,1},{5,7},{7,5},{8,10},{10,8},{12,... | collective-permute-start | bytes 196616 | tf_op jit(solution)/shard_map/ppermute | solution.py:631
  77.6 4.0 %collective-permute-start.13 = (f32[16,1024]{1,0:T(8,128)S(1)}, f32[16,1024]{1,0:T(8,128)S(1)}, u32[]{:S(2)}, u32[]{:S(2)}) collective-permute-start(f32[16,1024]{1,0:T(8,128)S(1)} %get-tuple-element.190.sums), channel_id=1, source_target_pairs={{0,1},{1,0},{2,3},{3,2},{4,5},{5,4},{6,7},{7,6},{8,9},{9,8},{10,11... | collective-permute-start | bytes 196616 | tf_op jit(solution)/shard_map/ppermute | solution.py:628
  98.1 23.6 %collective-permute-start.19 = (f16[272,1024]{1,0:T(8,128)(2,1)S(1)}, f16[272,1024]{1,0:T(8,128)(2,1)}, u32[]{:S(2)}, u32[]{:S(2)}) collective-permute-start(f16[272,1024]{1,0:T(8,128)(2,1)S(1)} %get-tuple-element.417), channel_id=1, source_target_pairs={{0,24},{8,16},{16,8},{24,0},{1,25},{9,17},{17,9},{25,1},{2,26},{10... | collective-permute-start | bytes 1671176 | tf_op jit(solution)/shard_map/ppermute | solution.py:639
  99.9 25.3 %collective-permute-start.18 = (f16[272,1024]{1,0:T(8,128)(2,1)S(1)}, f16[272,1024]{1,0:T(8,128)(2,1)}, u32[]{:S(2)}, u32[]{:S(2)}) collective-permute-start(f16[272,1024]{1,0:T(8,128)(2,1)S(1)} %get-tuple-element.418), channel_id=1, source_target_pairs={{0,16},{8,24},{16,0},{24,8},{1,17},{9,25},{17,1},{25,9},{2,18},{10... | collective-permute-start | bytes 1671176 | tf_op jit(solution)/shard_map/ppermute | solution.py:639
  101.1 24.0 %collective-permute-start.17 = (f16[272,1024]{1,0:T(8,128)(2,1)S(1)}, f16[272,1024]{1,0:T(8,128)(2,1)}, u32[]{:S(2)}, u32[]{:S(2)}) collective-permute-start(f16[272,1024]{1,0:T(8,128)(2,1)S(1)} %get-tuple-element.419), channel_id=1, source_target_pairs={{0,8},{8,0},{16,24},{24,16},{1,9},{9,1},{17,25},{25,17},{2,10},{10... | collective-permute-start | bytes 1671176 | tf_op jit(solution)/shard_map/ppermute | solution.py:639
  101.7 20.0 %collective-permute-start.16 = (f32[128,512]{1,0:T(8,128)S(1)}, f32[128,512]{1,0:T(8,128)S(1)}, u32[]{:S(2)}, u32[]{:S(2)}) collective-permute-start(f32[128,512]{1,0:T(8,128)S(1)} %get-tuple-element.191), channel_id=1, source_target_pairs={{4,0},{6,2},{5,1},{7,3},{12,8},{14,10},{13,9},{15,11},{20,16},{22,... | collective-permute-start | bytes 786440 | tf_op jit(solution)/shard_map/ppermute | solution.py:634
  125.2 2.9 %collective-permute-start.21 = (f32[256,1024]{1,0:T(8,128)}, f32[256,1024]{1,0:T(8,128)S(1)}, u32[]{:S(2)}, u32[]{:S(2)}) collective-permute-start(f32[256,1024]{1,0:T(8,128)} %get-tuple-element.216), channel_id=1, source_target_pairs={{0,1},{1,0},{2,3},{3,2},{4,5},{5,4},{6,7},{7,6},{8,9},{9,8},{10,11... | collective-permute-start | bytes 3145736 | tf_op jit(solution)/shard_map/ppermute | solution.py:628
  129.1 14.5 %collective-permute-start.22 = (f32[64,1024]{1,0:T(8,128)S(1)}, f32[64,1024]{1,0:T(8,128)S(1)}, u32[]{:S(2)}, u32[]{:S(2)}) collective-permute-start(f32[64,1024]{1,0:T(8,128)S(1)} %slice_add_fusion.1), channel_id=1, source_target_pairs={{0,2},{2,0},{4,6},{6,4},{1,3},{3,1},{5,7},{7,5},{8,10},{10,8},{12,... | collective-permute-start | bytes 786440 | tf_op jit(solution)/shard_map/ppermute | solution.py:631
  131.2 23.1 %collective-permute-start.25 = (f16[80,1024]{1,0:T(8,128)(2,1)S(1)}, f16[80,1024]{1,0:T(8,128)(2,1)S(1)}, u32[]{:S(2)}, u32[]{:S(2)}) collective-permute-start(f16[80,1024]{1,0:T(8,128)(2,1)S(1)} %get-tuple-element.414), channel_id=1, source_target_pairs={{0,6},{2,4},{4,2},{6,0},{1,7},{3,5},{5,3},{7,1},{8,14},{10,12},{12... | collective-permute-start | bytes 491528 | tf_op jit(solution)/shard_map/ppermute | solution.py:631
  131.3 23.1 %collective-permute-start.24 = (f16[80,1024]{1,0:T(8,128)(2,1)S(1)}, f16[80,1024]{1,0:T(8,128)(2,1)S(1)}, u32[]{:S(2)}, u32[]{:S(2)}) collective-permute-start(f16[80,1024]{1,0:T(8,128)(2,1)S(1)} %get-tuple-element.415), channel_id=1, source_target_pairs={{0,4},{2,6},{4,0},{6,2},{1,5},{3,7},{5,1},{7,3},{8,12},{10,14},{12... | collective-permute-start | bytes 491528 | tf_op jit(solution)/shard_map/ppermute | solution.py:631
  132.8 21.6 %collective-permute-start.23 = (f16[80,1024]{1,0:T(8,128)(2,1)S(1)}, f16[80,1024]{1,0:T(8,128)(2,1)S(1)}, u32[]{:S(2)}, u32[]{:S(2)}) collective-permute-start(f16[80,1024]{1,0:T(8,128)(2,1)S(1)} %get-tuple-element.416), channel_id=1, source_target_pairs={{0,2},{2,0},{4,6},{6,4},{1,3},{3,1},{5,7},{7,5},{8,10},{10,8},{12,... | collective-permute-start | bytes 491528 | tf_op jit(solution)/shard_map/ppermute | solution.py:631
  154.6 6.5 %collective-permute-start.26 = (f32[8,512]{1,0:T(8,128)S(1)}, f32[8,512]{1,0:T(8,128)S(1)}, u32[]{:S(2)}, u32[]{:S(2)}) collective-permute-start(f32[8,512]{1,0:T(8,128)S(1)} %get-tuple-element.235), channel_id=1, source_target_pairs={{4,0},{6,2},{5,1},{7,3},{12,8},{14,10},{13,9},{15,11},{20,16},{22,... | collective-permute-start | bytes 49160 | tf_op jit(solution)/shard_map/ppermute | solution.py:634
  155.9 5.9 %collective-permute-start.27 = (f32[512,256]{1,0:T(8,128)S(1)}, f32[512,256]{1,0:T(8,128)S(1)}, u32[]{:S(2)}, u32[]{:S(2)}) collective-permute-start(f32[512,256]{1,0:T(8,128)S(1)} %get-tuple-element.241), channel_id=1, source_target_pairs={{0,1},{1,0},{2,3},{3,2},{4,5},{5,4},{6,7},{7,6},{8,9},{9,8},{10,11... | collective-permute-start | bytes 1572872 | tf_op jit(solution)/shard_map/ppermute | solution.py:628
  161.9 6.5 %collective-permute-start.28 = (f32[512,128]{1,0:T(8,128)S(1)}, f32[512,128]{1,0:T(8,128)S(1)}, u32[]{:S(2)}, u32[]{:S(2)}) collective-permute-start(f32[512,128]{1,0:T(8,128)S(1)} %constant_dynamic-slice_fusion.10), channel_id=1, source_target_pairs={{0,2},{2,0},{4,6},{6,4},{1,3},{3,1},{5,7},{7,5},{8,10},{10,8},{12,... | collective-permute-start | bytes 786440 | tf_op jit(solution)/shard_map/ppermute | solution.py:631
  168.4 1.6 collective-permute-start.29
  170.7 6.4 %collective-permute-start.30 = (f32[8,128]{1,0:T(8,128)S(1)}, f32[8,128]{1,0:T(8,128)S(1)}, u32[]{:S(2)}, u32[]{:S(2)}) collective-permute-start(f32[8,128]{1,0:T(8,128)S(1)} %fusion.21), channel_id=1, source_target_pairs={{4,0},{6,2},{5,1},{7,3},{12,8},{14,10},{13,9},{15,11},{20,16},{22,... | collective-permute-start | bytes 12296 | tf_op jit(solution)/shard_map/ppermute | solution.py:634
  177.1 18.6 %collective-permute-start.31 = (f32[192,1024]{1,0:T(8,128)}, f32[192,1024]{1,0:T(8,128)S(1)}, u32[]{:S(2)}, u32[]{:S(2)}) collective-permute-start(f32[192,1024]{1,0:T(8,128)} %slice_add_fusion), channel_id=1, source_target_pairs={{0,2},{2,0},{4,6},{6,4},{1,3},{3,1},{5,7},{7,5},{8,10},{10,8},{12,... | collective-permute-start | bytes 2359304 | tf_op jit(solution)/shard_map/ppermute | solution.py:631
  177.5 12.6 %collective-permute-start.32 = (f16[304,512]{1,0:T(8,128)(2,1)}, f16[304,512]{1,0:T(8,128)(2,1)}, u32[]{:S(2)}, u32[]{:S(2)}) collective-permute-start(f16[304,512]{1,0:T(8,128)(2,1)} %get-tuple-element.264), channel_id=1, source_target_pairs={{0,8},{8,0},{16,24},{24,16},{1,9},{9,1},{17,25},{25,17},{2,10},{10... | collective-permute-start | bytes 933896 | tf_op jit(solution)/shard_map/ppermute | solution.py:639
  178.9 14.5 %collective-permute-start.33 = (f16[304,512]{1,0:T(8,128)(2,1)S(1)}, f16[304,512]{1,0:T(8,128)(2,1)}, u32[]{:S(2)}, u32[]{:S(2)}) collective-permute-start(f16[304,512]{1,0:T(8,128)(2,1)S(1)} %get-tuple-element.265), channel_id=1, source_target_pairs={{0,16},{8,24},{16,0},{24,8},{1,17},{9,25},{17,1},{25,9},{2,18},{10... | collective-permute-start | bytes 933896 | tf_op jit(solution)/shard_map/ppermute | solution.py:639
  179.7 13.7 %collective-permute-start.34 = (f16[304,512]{1,0:T(8,128)(2,1)S(1)}, f16[304,512]{1,0:T(8,128)(2,1)}, u32[]{:S(2)}, u32[]{:S(2)}) collective-permute-start(f16[304,512]{1,0:T(8,128)(2,1)S(1)} %get-tuple-element.266), channel_id=1, source_target_pairs={{0,24},{8,16},{16,8},{24,0},{1,25},{9,17},{17,9},{25,1},{2,26},{10... | collective-permute-start | bytes 933896 | tf_op jit(solution)/shard_map/ppermute | solution.py:639
  195.7 2.7 %collective-permute-start.37 = (f32[256,1024]{1,0:T(8,128)S(1)}, f32[256,1024]{1,0:T(8,128)S(1)}, u32[]{:S(2)}, u32[]{:S(2)}) collective-permute-start(f32[256,1024]{1,0:T(8,128)S(1)} %get-tuple-element.272), channel_id=1, source_target_pairs={{0,1},{1,0},{2,3},{3,2},{4,5},{5,4},{6,7},{7,6},{8,9},{9,8},{10,11... | collective-permute-start | bytes 3145736 | tf_op jit(solution)/shard_map/ppermute | solution.py:628
  195.7 18.8 %collective-permute-start.20 = (f32[256,1024]{1,0:T(8,128)S(1)}, f32[256,1024]{1,0:T(8,128)S(1)}, u32[]{:S(2)}, u32[]{:S(2)}) collective-permute-start(f32[256,1024]{1,0:T(8,128)S(1)} %copy-done.44), channel_id=1, source_target_pairs={{0,1},{1,0},{2,3},{3,2},{4,5},{5,4},{6,7},{7,6},{8,9},{9,8},{10,11... | collective-permute-start | bytes 3145736 | tf_op jit(solution)/shard_map/ppermute | solution.py:628
  198.9 14.7 %collective-permute-start.41 = (f16[272,1024]{1,0:T(8,128)(2,1)S(1)}, f16[272,1024]{1,0:T(8,128)(2,1)S(1)}, u32[]{:S(2)}, u32[]{:S(2)}) collective-permute-start(f16[272,1024]{1,0:T(8,128)(2,1)S(1)} %pad_maximum_fusion.3), channel_id=1, source_target_pairs={{0,2},{2,0},{4,6},{6,4},{1,3},{3,1},{5,7},{7,5},{8,10},{10,8},{12,... | collective-permute-start | bytes 1671176 | tf_op jit(solution)/shard_map/ppermute | solution.py:631
  204.2 5.8 %collective-permute-start.40 = (f16[304,128]{1,0:T(8,128)(2,1)S(1)}, f16[304,128]{1,0:T(8,128)(2,1)S(1)}, u32[]{:S(2)}, u32[]{:S(2)}) collective-permute-start(f16[304,128]{1,0:T(8,128)(2,1)S(1)} %get-tuple-element.420), channel_id=1, source_target_pairs={{0,24},{8,16},{16,8},{24,0},{1,25},{9,17},{17,9},{25,1},{2,26},{10... | collective-permute-start | bytes 233480 | tf_op jit(solution)/shard_map/ppermute | solution.py:639
  205.9 5.0 %collective-permute-start.39 = (f16[304,128]{1,0:T(8,128)(2,1)S(1)}, f16[304,128]{1,0:T(8,128)(2,1)S(1)}, u32[]{:S(2)}, u32[]{:S(2)}) collective-permute-start(f16[304,128]{1,0:T(8,128)(2,1)S(1)} %get-tuple-element.421), channel_id=1, source_target_pairs={{0,16},{8,24},{16,0},{24,8},{1,17},{9,25},{17,1},{25,9},{2,18},{10... | collective-permute-start | bytes 233480 | tf_op jit(solution)/shard_map/ppermute | solution.py:639
  207.2 4.4 %collective-permute-start.38 = (f16[304,128]{1,0:T(8,128)(2,1)S(1)}, f16[304,128]{1,0:T(8,128)(2,1)S(1)}, u32[]{:S(2)}, u32[]{:S(2)}) collective-permute-start(f16[304,128]{1,0:T(8,128)(2,1)S(1)} %get-tuple-element.422), channel_id=1, source_target_pairs={{0,8},{8,0},{16,24},{24,16},{1,9},{9,1},{17,25},{25,17},{2,10},{10... | collective-permute-start | bytes 233480 | tf_op jit(solution)/shard_map/ppermute | solution.py:639
  210.0 4.1 %collective-permute-start.36 = (f32[256,1024]{1,0:T(8,128)S(1)}, f32[256,1024]{1,0:T(8,128)S(1)}, u32[]{:S(2)}, u32[]{:S(2)}) collective-permute-start(f32[256,1024]{1,0:T(8,128)S(1)} %get-tuple-element.269), channel_id=1, source_target_pairs={{0,1},{1,0},{2,3},{3,2},{4,5},{5,4},{6,7},{7,6},{8,9},{9,8},{10,11... | collective-permute-start | bytes 3145736 | tf_op jit(solution)/shard_map/ppermute | solution.py:628
  216.1 8.1 %collective-permute-start.42 = (f32[256,1024]{1,0:T(8,128)S(1)}, f32[256,1024]{1,0:T(8,128)S(1)}, u32[]{:S(2)}, u32[]{:S(2)}) collective-permute-start(f32[256,1024]{1,0:T(8,128)S(1)} %get-tuple-element.380), channel_id=1, source_target_pairs={{0,1},{1,0},{2,3},{3,2},{4,5},{5,4},{6,7},{7,6},{8,9},{9,8},{10,11... | collective-permute-start | bytes 3145736 | tf_op jit(solution)/shard_map/ppermute | solution.py:628
  216.2 5.4 %collective-permute-start.35 = (bf16[256,1024]{1,0:T(8,128)(2,1)S(1)}, bf16[256,1024]{1,0:T(8,128)(2,1)}, u32[]{:S(2)}, u32[]{:S(2)}) collective-permute-start(bf16[256,1024]{1,0:T(8,128)(2,1)S(1)} %get-tuple-element.381), channel_id=1, source_target_pairs={{0,1},{1,0},{2,3},{3,2},{4,5},{5,4},{6,7},{7,6},{8,9},{9,8},{10,11... | collective-permute-start | bytes 1572872 | tf_op jit(solution)/shard_map/ppermute | solution.py:628
  217.2 8.5 %collective-permute-start.43 = (f16[112,640]{1,0:T(8,128)(2,1)S(1)}, f16[112,640]{1,0:T(8,128)(2,1)S(1)}, u32[]{:S(2)}, u32[]{:S(2)}) collective-permute-start(f16[112,640]{1,0:T(8,128)(2,1)S(1)} %get-tuple-element.293), channel_id=1, source_target_pairs={{0,2},{2,0},{4,6},{6,4},{1,3},{3,1},{5,7},{7,5},{8,10},{10,8},{12,... | collective-permute-start | bytes 430088 | tf_op jit(solution)/shard_map/ppermute | solution.py:631
  217.6 13.7 %collective-permute-start.44 = (f16[112,640]{1,0:T(8,128)(2,1)S(1)}, f16[112,640]{1,0:T(8,128)(2,1)S(1)}, u32[]{:S(2)}, u32[]{:S(2)}) collective-permute-start(f16[112,640]{1,0:T(8,128)(2,1)S(1)} %get-tuple-element.294), channel_id=1, source_target_pairs={{0,4},{2,6},{4,0},{6,2},{1,5},{3,7},{5,1},{7,3},{8,12},{10,14},{12... | collective-permute-start | bytes 430088 | tf_op jit(solution)/shard_map/ppermute | solution.py:631
  218.2 13.1 %collective-permute-start.45 = (f16[112,640]{1,0:T(8,128)(2,1)S(1)}, f16[112,640]{1,0:T(8,128)(2,1)S(1)}, u32[]{:S(2)}, u32[]{:S(2)}) collective-permute-start(f16[112,640]{1,0:T(8,128)(2,1)S(1)} %get-tuple-element.295), channel_id=1, source_target_pairs={{0,6},{2,4},{4,2},{6,0},{1,7},{3,5},{5,3},{7,1},{8,14},{10,12},{12... | collective-permute-start | bytes 430088 | tf_op jit(solution)/shard_map/ppermute | solution.py:631
  234.9 2.6 %collective-permute-start.46 = (f32[1024]{0:T(1024)}, f32[1024]{0:T(1024)S(1)}, u32[]{:S(2)}, u32[]{:S(2)}) collective-permute-start(f32[1024]{0:T(1024)} %bitcast.121), channel_id=1, source_target_pairs={{0,1},{1,0},{2,3},{3,2},{4,5},{5,4},{6,7},{7,6},{8,9},{9,8},{10,11... | collective-permute-start | bytes 12296 | tf_op jit(solution)/shard_map/ppermute | solution.py:628
  235.1 3.0 %collective-permute-start.47 = (f32[2,64,64]{2,1,0:T(8,128)S(1)}, f32[2,64,64]{2,1,0:T(8,128)S(1)}, u32[]{:S(2)}, u32[]{:S(2)}) collective-permute-start(f32[2,64,64]{2,1,0:T(8,128)S(1)} %get-tuple-element.403), channel_id=1, source_target_pairs={{0,1},{1,0},{2,3},{3,2},{4,5},{5,4},{6,7},{7,6},{8,9},{9,8},{10,11... | collective-permute-start | bytes 98312 | tf_op jit(solution)/shard_map/ppermute | solution.py:628
  (48 other events, 479.2 us)

commit v7 on v6

--- a/solution.py
+++ b/solution.py
@@ -380,8 +380,8 @@
     return pre
 
 
-def meet_body(inner, states, s_ref, co, hd, z, dbc, hloc, hnext, hend, pre, gloc, gin, hin, zed_ref, ends_ref, keep_ref,
-              give_ref, lsc, dsc):
+def meet_body(inner, states, s_ref, co, hd, z, dbc, hloc, hnext, hend, pre, gloc, gin, hin, og, skip, zed_ref, ends_ref, keep_ref,
+              give_ref, head_ref, lsc, dsc):
     start_expanders(inner, (0, lsc), (STEP, dsc))
     exact = three(hd[...])
     lx = mm(exact, lsc[...])
@@ -390,7 +390,8 @@
     b = pl.program_id(0)
     conv = co[...]
     act = conv * jax.nn.sigmoid(conv)
-    source = mm(exact, dsc[...]) * act[:, :inner]
+    delta_x = mm(exact, dsc[...])
+    source = delta_x * act[:, :inner]
     ends = []
     inject_grads = []
     for i in range(subs):
@@ -403,6 +404,13 @@
         zed_ref[at] = z[at] + fade * mm(act[at, inner : inner + states], later, precision=HIGH)
         inject_grads.append(dbc[at, :states] + mm(fade * source[at], later, NT, HIGH))
         ends.append(jnp.sum(later * entering(after, pre[n], hin[...]), axis=0, keepdims=True))
+
+    @pl.when(b == 0)
+    def _():
+        first = conv[0:8, :inner]
+        grad = delta_x[0:8] * zed_ref[0:8] + skip[...] * og[...]
+        head_ref[...] = grad * slope(first, jax.nn.sigmoid(first))
+
     ends_ref[...] = jnp.concatenate(ends + [jnp.zeros((8 - subs, inner), F32)], axis=0)
     inject_grad = jnp.concatenate(inject_grads, axis=0)
     half = count // 2
@@ -420,7 +428,7 @@
 
 
 def join_body(inner, s_ref, co, hd, og, y, zed_in, ends_in, u, prior, uh, taps, rate, skip, mg_ref,
-              tail_ref, head_ref, rg_ref, cols_ref, sig_ref, col_sc, csc, usc, dsc):
+              tail_ref, rg_ref, cols_ref, sig_ref, col_sc, csc, usc, dsc):
     start_expanders(inner, (STEP, dsc))
     step = pl.program_id(0)
     subs = BLOCK // SUB
@@ -459,7 +467,6 @@
     grad = (delta_x * zed + skip[...] * g) * slope(conv, sig)
     pre_grad = conv_back(grad, csc, usc, taps, sig_ref)
     mg_ref[...] = pre_grad.astype(BF16)
-    head_ref[...] = grad[0:8]
 
     @pl.when(step == 0)
     def _():
@@ -901,32 +908,33 @@
     def table(rows, width, lanes):
         return pl.BlockSpec((rows, width), lambda b, s: (0, lanes(s)))
 
-    zed, ends, dbc_keep, dbc_give = grid_call(
+    zed, ends, dbc_keep, dbc_give, head = grid_call(
         functools.partial(meet_body, inner, states),
         (count,),
         [rows_spec(wide), rows_spec(128), rows_spec(inner), rows_spec(2 * states), state_block,
          pl.BlockSpec((1, states, inner), lambda b, s: (jnp.minimum((b + 1) * subs, last - 1), 0, 0)),
-         whole((states, inner)), all_pre, state_block, whole((states, inner)), whole((states, inner))],
-        [rows_spec(inner), rows_spec(inner, 8), whole((half_rows, 2 * states)), whole((half_rows, 2 * states))],
+         whole((states, inner)), all_pre, state_block, whole((states, inner)), whole((states, inner)), whole((8, inner)), whole((1, inner))],
+        [rows_spec(inner), rows_spec(inner, 8), whole((half_rows, 2 * states)), whole((half_rows, 2 * states)),
+         whole((8, inner))],
         [shaped((tokens, inner)), shaped((8 * count, inner)), shaped((half_rows, 2 * states)),
-         shaped((half_rows, 2 * states))],
+         shaped((half_rows, 2 * states)), shaped((8, inner))],
         [pltpu.VMEM((384, inner), BF16)] * 2,
         name="meet",
         limit=20 << 20,
-    )(scalars, *streamed(conv, per_head, zed, dbc, hloc, hloc), own_end, *streamed(pre, gloc), returned, carried)
+    )(scalars, *streamed(conv, per_head, zed, dbc, hloc, hloc), own_end, *streamed(pre, gloc), returned, carried, *streamed(out_grad), skip_row)
 
     zed, ends, dbc_keep, dbc_give, branch_back = lax.optimization_barrier((zed, ends, dbc_keep, dbc_give, branch_back))
     early_total, early_power, _ = totalled(early, early_scale, early_got)
     early_cut = chunks([early_total], early_power)
     early_far = over_positions(early_cut)
-    signal_pre, tail, head, raw_grad, head_cols, signal_cols = grid_call(
+    signal_pre, tail, raw_grad, head_cols, signal_cols = grid_call(
         functools.partial(join_body, inner),
         (count,),
         [back(inner), back(128), back(inner), back(inner), back(inner), back(inner, 8)]
         + back_lanes(inner, lambda s: 0)
         + [table(4, inner, lambda s: 0), whole((1, 128)), whole((1, inner))],
-        [back(inner), whole((8, inner)), whole((8, inner)), back(128), whole((8, 128)), whole((8, inner))],
-        [shaped((tokens, inner), BF16), shaped((8, inner)), shaped((8, inner)), shaped((tokens, 128)),
+        [back(inner), whole((8, inner)), back(128), whole((8, 128)), whole((8, inner))],
+        [shaped((tokens, inner), BF16), shaped((8, inner)), shaped((tokens, 128)),
          shaped((8, 128)), shaped((8, inner))],
         [pltpu.VMEM((3 * inner, 128), BF16), pltpu.VMEM((BLOCK + 8, inner), F32),
          pltpu.VMEM((BLOCK + 8, inner), F32), pltpu.VMEM((384, inner), BF16)],
@@ -934,7 +942,7 @@
         limit=20 << 20,
     )(scalars, *streamed(conv, per_head, out_grad, y), zed, ends, *streamed(u, u), uh, taps_x, rate_row, skip_row)
 
-    head, early_far = lax.optimization_barrier((head, early_far))
+    tail, early_far = lax.optimization_barrier((tail, early_far))
     early_sum = settled(early_cut[0], decoded(early_far))
     out_sum = jnp.concatenate([part[:, inner:] for part in early_sum], axis=1)
     gate_sum = jnp.concatenate([part[:, :inner] for part in early_sum], axis=1)

time: 240 us -> 240 us (level)
    ppermute x4, waiting for transfers between devices: 8.2 us -> 3.83 us  [along(): lax.ppermute(value, 'ctx', [(i, i + step) for i in range(ctxs) if 0 <= i...]
  transfers between devices with their start and end apart: 48 -> 48, of which waited for: 18 -> 17; matrix products, arithmetic and copies ran while one was open for 10% -> 10% of each run, Pallas kernels for 34% -> 34%
where the time goes in v7:
time: 240 us; the launch traced here: 238 us
  Pallas kernels  105 us (44%)
  starting transfers between devices  47.7 us (20%)
  waiting for transfers between devices  44.3 us (18%)
  other arithmetic  21.2 us (9%)
  local copies, waits for them, and re-layouts  17.2 us (7%)
  between operations  2.56 us (1%)
    ppermute x13, waiting for transfers between devices, across(): return lax.ppermute(value, 'ctx', [(i, i ^ j) for i in range(ctxs)])  22.4 us
    ppermute x15, starting transfers between devices, spread(): return lax.ppermute(value, 'dp', [(i, i ^ j) for i in range(dps)])  18.6 us
    ppermute x13, starting transfers between devices, across(): return lax.ppermute(value, 'ctx', [(i, i ^ j) for i in range(ctxs)])  15.8 us
    pallas_call x3, Pallas kernels, grads(): grid_call(functools.partial(grads_body, parts, [(n, n + 1) for n in range...  14.8 us
    pallas_call x1, Pallas kernels, per_device(): grid_call(functools.partial(front_body, parts, inner, states, quarter), (...  14 us
    ppermute x15, waiting for transfers between devices, spread(): return lax.ppermute(value, 'dp', [(i, i ^ j) for i in range(dps)])  13.4 us
    pallas_call x1, Pallas kernels, per_device(): grid_call(functools.partial(back_body, inner, states), (count,), [rows_sp...  11.6 us
    pallas_call x1, Pallas kernels, per_device(): grid_call(functools.partial(join_body, inner), (count,), [back(inner), ba...  10 us
  transfers between devices with their start and end apart: 48, of which 17 were waited for; matrix products, arithmetic and copies ran while one was open for 10% of the time, Pallas kernels for 34%

profile of v7, /device:TPU:0, one launch (start us, length us, event | category | flops | bytes accessed | tf_op | source)
XLA Modules:
  0.0 238.2 jit_solution(16344728263455539911)
XLA Ops:
  1.7 3.3 %constant_dynamic-slice_fusion.15 = (bf16[256,1,512]{2,1,0:T(2,128)(2,1)}, bf16[256,1,512]{2,1,0:T(2,128)(2,1)S(1)}) fusion(bf16[256,2,1024]{2,1,0:T(2,128)(2,1)} %param.20, s32[]{:T(128)S(6)} %select_n.151, s32[]{:T(128)S(6)} %add.319), kind=kLoop, calls=%fused_computation.137 | loop fusion | bytes 1048584 | tf_op jit(solution)/shard_map/slice | solution.py:743
  6.1 3.9 %collective-permute-start.2 = (bf16[256,896]{1,0:T(8,128)(2,1)}, bf16[256,896]{1,0:T(8,128)(2,1)}, u32[]{:S(2)}, u32[]{:S(2)}) collective-permute-start(bf16[256,896]{1,0:T(8,128)(2,1)} %concatenate.134.rest_0_), channel_id=1, source_target_pairs={{0,24},{8,16},{16,8},{24,0},{1,25},{9,17},{17,9},{25,1},{2,26},{10... | collective-permute-start | bytes 1376264 | tf_op jit(solution)/shard_map/ppermute | solution.py:646
  10.7 2.2 collective-permute-start.3
  17.1 7.0 %collective-permute-done.3.near = bf16[256,1024]{1,0:T(8,128)(2,1)} collective-permute-done((bf16[256,1024]{1,0:T(8,128)(2,1)S(1)}, bf16[256,1024]{1,0:T(8,128)(2,1)}, u32[]{:S(2)}, u32[]{:S(2)}) %collective-permute-start.3) | collective-permute-done | bytes 524320 | tf_op jit(solution)/shard_map/ppermute | solution.py:638
  25.0 1.7 collective-permute-start.7
  28.4 2.2 collective-permute-done.1.rest_2_
  31.1 1.5 collective-permute-start.11
  32.6 1.5 collective-permute-start.10
  34.6 14.0 %front.1 = (bf16[1024,1024]{1,0:T(8,128)(2,1)}, f32[1024,768]{1,0:T(8,128)}, f32[8,768]{1,0:T(8,128)}, f32[1024,768]{1,0:T(8,128)}, f32[1024,128]{1,0:T(8,128)},...) custom-call(s32[10]{0:T(128)} %stack.79.s_ref, bf16[512,1024]{1,0:T(8,128)(2,1)} %bitcast.92, ...), custom_call_target="tpu_custom_call" | custom-call | tf_op jit(solution)/shard_map/front/pallas_call | solution.py:757
  48.7 4.7 %collective-permute-start.12 = (f32[128,512]{1,0:T(8,128)}, f32[128,512]{1,0:T(8,128)S(1)}, u32[]{:S(2)}, u32[]{:S(2)}) collective-permute-start(f32[128,512]{1,0:T(8,128)} %get-tuple-element.188.hend), channel_id=1, source_target_pairs={{0,4},{2,6},{1,5},{3,7},{8,12},{10,14},{9,13},{11,15},{16,20},{18,... | collective-permute-start | bytes 786440 | tf_op jit(solution)/shard_map/ppermute | solution.py:641
  53.7 6.9 %within.1.yw = f32[1024,512]{1,0:T(8,128)S(1)} custom-call(s32[10]{0:T(128)S(1)} %copy-done.12, f32[1024,768]{1,0:T(8,128)} %get-tuple-element.176.co, f32[1024,128]{1,0:T(8,128)} %get-tuple-element.177.hd), custom_call_target="tpu_custom_call" | custom-call | tf_op jit(solution)/shard_map/within/pallas_call | solution.py:782
  61.9 7.1 %gates.1 = (f32[1024,512]{1,0:T(8,128)S(1)}, f32[1024,512]{1,0:T(8,128)S(1)}, bf16[1024,1024]{1,0:T(8,128)(2,1)}) custom-call(s32[10]{0:T(128)S(1)} %copy-done.12, bf16[1024,1024]{1,0:T(8,128)(2,1)} %get-tuple-element.178.normed.refs_0_, bf16[512,1024]{1,0:T(8,128)(2,1)} %bitcast.94, bf16[256,1024]{1,0:T(8,128)(2,1)} %collective-permute-done.7.near, ...), custom_call_target="tpu_custom_call" | custom-call | tf_op jit(solution)/shard_map/gates/pallas_call | solution.py:793
  69.1 6.5 %output.1 = (f32[1024,512]{1,0:T(8,128)S(1)}, f32[16,1024]{1,0:T(8,128)S(1)}) custom-call(s32[10]{0:T(128)S(1)} %copy-done.12, f32[1024,768]{1,0:T(8,128)} %get-tuple-element.176.co, f32[1024,128]{1,0:T(8,128)} %get-tuple-element.177.hd, f32[1024,512]{1,0:T(8,128)S(1)} %within.1.yw, f32[1024,512]{1,0:T(8,128)S(1)} %get-tuple-element.184.gate, ...), custom_call_target="tpu_custom_call" | custom-call | tf_op jit(solution)/shard_map/output/pallas_call | solution.py:804
  75.6 1.7 collective-permute-start.15
  77.6 2.2 collective-permute-done.15.sums3
  79.8 1.8 collective-permute-done.14.sums2
  83.0 7.8 %turn.1 = (bf16[1024,512]{1,0:T(8,128)(2,1)S(1)}, bf16[1024,512]{1,0:T(8,128)(2,1)S(1)}, f32[1024,512]{1,0:T(8,128)}, f32[8,128,512]{2,1,0:T(8,128)}, f32[128,512]{1,0:T(8,128)S(1)}, /*index=5*/f32[8,512]{1,0:T(8,128)S(1)}) custom-call(s32[10]{0:T(128)S(1)} %copy-done.13, f32[1024,768]{1,0:T(8,128)} %get-tuple-element.176.co, ...), custom_call_target="tpu_custom_call" | custom-call | tf_op jit(solution)/shard_map/turn/pallas_call | solution.py:823
  90.9 6.3 %grad_early.1 = (f32[256,1024]{1,0:T(8,128)S(1)}, f32[256,1024]{1,0:T(8,128)S(1)}, f32[256,1024]{1,0:T(8,128)S(1)}, f32[256,1024]{1,0:T(8,128)S(1)}, f32[16,1024]{1,0:T(8,128)S(1)}, /*index=5*/f32[1,1024]{1,0:T(1,128)S(1)}) custom-call(s32[10]{0:T(128)S(1)} %copy-done.13, bf16[1024,1024]{1,0:T(8,128)(2,1)} %get-tuple-element.178.normed.refs_0_, ...), custom_call_target="tpu_custom_call" | custom-call | tf_op jit(solution)/shard_map/grad_early/pallas_call | solution.py:854
  98.1 1.7 collective-permute-start.19
  101.7 1.5 collective-permute-start.16
  103.2 11.6 %back.1 = (f32[1024,512]{1,0:T(8,128)}, f32[1024,256]{1,0:T(8,128)}) custom-call(s32[10]{0:T(128)} %stack.79.s_ref, f32[1024,768]{1,0:T(8,128)} %get-tuple-element.176.co, f32[1024,128]{1,0:T(8,128)} %get-tuple-element.177.hd, f32[1024,512]{1,0:T(8,128)} %get-tuple-element.202.og, f32[8,128,512]{2,1,0:T(8,128)} %get-tuple-element.186.hloc.hnext, ...), custom_call_target="tpu_custom_call" | custom-call | tf_op jit(solution)/shard_map/back/pallas_call | solution.py:870
  114.8 6.9 %branch.1 = (f32[256,1024]{1,0:T(8,128)}, f32[256,1024]{1,0:T(8,128)}, f32[256,1024]{1,0:T(8,128)}, f32[256,1024]{1,0:T(8,128)}) custom-call(s32[10]{0:T(128)} %stack.79.s_ref, bf16[1024,512]{1,0:T(8,128)(2,1)} %copy-done.5, bf16[256,1024]{1,0:T(8,128)(2,1)} %copy-done.22, bf16[256,1024]{1,0:T(8,128)(2,1)} %copy-done.26, bf16[256,1024]{1,0:T(8,128)(2,1)} %copy-done.25, ...), custom_call_target="tpu_custom_call" | custom-call | tf_op jit(solution)/shard_map/branch/pallas_call | solution.py:881
  121.7 3.5 %collective-permute-done.18 = f16[272,1024]{1,0:T(8,128)(2,1)} collective-permute-done((f16[272,1024]{1,0:T(8,128)(2,1)S(1)}, f16[272,1024]{1,0:T(8,128)(2,1)}, u32[]{:S(2)}, u32[]{:S(2)}) %collective-permute-start.18) | collective-permute-done | bytes 557088 | tf_op jit(solution)/shard_map/ppermute | solution.py:646
  126.0 1.8 multiply_add_fusion
  129.1 2.0 collective-permute-start.22
  131.3 1.5 collective-permute-start.24
  132.8 2.9 %collective-permute-start.23 = (f16[80,1024]{1,0:T(8,128)(2,1)S(1)}, f16[80,1024]{1,0:T(8,128)(2,1)S(1)}, u32[]{:S(2)}, u32[]{:S(2)}) collective-permute-start(f16[80,1024]{1,0:T(8,128)(2,1)S(1)} %get-tuple-element.416), channel_id=1, source_target_pairs={{0,2},{2,0},{4,6},{6,4},{1,3},{3,1},{5,7},{7,5},{8,10},{10,8},{12,... | collective-permute-start | bytes 491528 | tf_op jit(solution)/shard_map/ppermute | solution.py:638
  135.8 7.9 %meet.1 = (f32[1024,512]{1,0:T(8,128)S(1)}, f32[32,512]{1,0:T(8,128)S(1)}, f32[512,256]{1,0:T(8,128)S(1)}, f32[512,256]{1,0:T(8,128)S(1)}, f32[8,512]{1,0:T(8,128)S(1)}) custom-call(s32[10]{0:T(128)S(1)} %copy-done.14, f32[1024,768]{1,0:T(8,128)} %get-tuple-element.176.co, f32[1024,128]{1,0:T(8,128)} %get-tuple-element.177.hd, ...), custom_call_target="tpu_custom_call" | custom-call | tf_op jit(solution)/shard_map/meet/pallas_call | solution.py:911
  145.7 10.0 %join.1 = (bf16[1024,512]{1,0:T(8,128)(2,1)S(1)}, f32[8,512]{1,0:T(8,128)S(1)}, f32[1024,128]{1,0:T(8,128)S(1)}, f32[8,128]{1,0:T(8,128)S(1)}, f32[8,512]{1,0:T(8,128)S(1)}) custom-call(s32[10]{0:T(128)S(1)} %copy-done.14, f32[1024,768]{1,0:T(8,128)} %get-tuple-element.176.co, f32[1024,128]{1,0:T(8,128)} %get-tuple-element.177.hd, ...), custom_call_target="tpu_custom_call" | custom-call | tf_op jit(solution)/shard_map/join/pallas_call | solution.py:930
  159.1 4.7 %grad_signal.1 = (f32[256,512]{1,0:T(8,128)S(1)}, f32[256,512]{1,0:T(8,128)S(1)}, f32[256,512]{1,0:T(8,128)S(1)}, f32[256,512]{1,0:T(8,128)S(1)}, f32[16,512]{1,0:T(8,128)S(1)}, /*index=5*/f32[1,512]{1,0:T(1,128)S(1)}) custom-call(s32[10]{0:T(128)S(1)} %copy-done.14, bf16[1024,1024]{1,0:T(8,128)(2,1)} %get-tuple-element.178.normed.refs_0_, ...), custom_call_target="tpu_custom_call" | custom-call | tf_op jit(solution)/shard_map/grad_signal/pallas_call | solution.py:854
  163.8 3.6 %collective-permute-done.28 = f32[512,128]{1,0:T(8,128)S(1)} collective-permute-done((f32[512,128]{1,0:T(8,128)S(1)}, f32[512,128]{1,0:T(8,128)S(1)}, u32[]{:S(2)}, u32[]{:S(2)}) %collective-permute-start.28) | collective-permute-done | bytes 262176 | tf_op jit(solution)/shard_map/ppermute | solution.py:638
  167.7 1.3 collective-permute-done.29.dbc_other
  169.7 1.6 collective-permute-start.30
  172.2 3.8 %collective-permute-done.30.ahead = f32[8,128]{1,0:T(8,128)S(1)} collective-permute-done((f32[8,128]{1,0:T(8,128)S(1)}, f32[8,128]{1,0:T(8,128)S(1)}, u32[]{:S(2)}, u32[]{:S(2)}) %collective-permute-start.30) | collective-permute-done | bytes 4128 | tf_op jit(solution)/shard_map/ppermute | solution.py:641
  176.4 1.5 collective-permute-start.32
  179.9 9.0 %feature.1 = (f32[256,1024]{1,0:T(8,128)S(1)}, f32[256,1024]{1,0:T(8,128)S(1)}, f32[256,1024]{1,0:T(8,128)S(1)}, f32[256,1024]{1,0:T(8,128)S(1)}, bf16[1024,128]...) custom-call(s32[10]{0:T(128)S(1)} %copy-done.14, bf16[512,1024]{1,0:T(8,128)(2,1)} %bitcast.93, ...), custom_call_target="tpu_custom_call" | custom-call | tf_op jit(solution)/shard_map/feature/pallas_call | solution.py:980
  189.0 3.6 %collective-permute-done.33 = f16[304,512]{1,0:T(8,128)(2,1)} collective-permute-done((f16[304,512]{1,0:T(8,128)(2,1)S(1)}, f16[304,512]{1,0:T(8,128)(2,1)}, u32[]{:S(2)}, u32[]{:S(2)}) %collective-permute-start.33) | collective-permute-done | bytes 311328 | tf_op jit(solution)/shard_map/ppermute | solution.py:646
  192.6 2.4 %collective-permute-done.31 = f32[192,1024]{1,0:T(8,128)S(1)} collective-permute-done((f32[192,1024]{1,0:T(8,128)}, f32[192,1024]{1,0:T(8,128)S(1)}, u32[]{:S(2)}, u32[]{:S(2)}) %collective-permute-start.31) | collective-permute-done | bytes 786464 | tf_op jit(solution)/shard_map/ppermute | solution.py:638
  199.3 3.8 %grad_extra.1 = (f32[256,128]{1,0:T(8,128)S(1)}, f32[256,128]{1,0:T(8,128)S(1)}, f32[256,128]{1,0:T(8,128)S(1)}, f32[256,128]{1,0:T(8,128)S(1)}, f32[16,128]{1,0:T(8,128)S(1)}, /*index=5*/f32[1,128]{1,0:T(1,128)S(1)}) custom-call(s32[10]{0:T(128)S(1)} %copy-done.14, bf16[1024,1024]{1,0:T(8,128)(2,1)} %get-tuple-element.178.normed.refs_0_, ...), custom_call_target="tpu_custom_call" | custom-call | tf_op jit(solution)/shard_map/grad_extra/pallas_call | solution.py:854
  203.4 1.7 collective-permute-start.40
  205.1 1.3 collective-permute-start.39
  207.0 2.2 collective-permute-done.40
  210.8 2.0 collective-permute-done.41
  217.4 3.5 %collective-permute-start.45 = (f16[112,640]{1,0:T(8,128)(2,1)S(1)}, f16[112,640]{1,0:T(8,128)(2,1)S(1)}, u32[]{:S(2)}, u32[]{:S(2)}) collective-permute-start(f16[112,640]{1,0:T(8,128)(2,1)S(1)} %get-tuple-element.295), channel_id=1, source_target_pairs={{0,6},{2,4},{4,2},{6,0},{1,7},{3,5},{5,3},{7,1},{8,14},{10,12},{12... | collective-permute-start | bytes 430088 | tf_op jit(solution)/shard_map/ppermute | solution.py:638
  220.9 2.6 %maximum_select_fusion.1 = bf16[512,1024]{1,0:T(8,128)(2,1)} fusion(bf16[256,1024]{1,0:T(8,128)(2,1)} %collective-permute-done.35, bf16[256,1024]{1,0:T(8,128)(2,1)S(1)} %get-tuple-element.381, pred[]{:T(512)S(6)} %eq.8), kind=kLoop, calls=%fused_computation.14 | loop fusion | flops 4718592 | bytes 2097153 | tf_op jit(solution)/shard_map/jit(_where)/select_n | solution.py:1022
  223.5 1.5 maximum_select_fusion
  225.0 5.5 %collective-permute-done.44 = f16[112,640]{1,0:T(8,128)(2,1)S(1)} collective-permute-done((f16[112,640]{1,0:T(8,128)(2,1)S(1)}, f16[112,640]{1,0:T(8,128)(2,1)S(1)}, u32[]{:S(2)}, u32[]{:S(2)}) %collective-permute-start.44) | collective-permute-done | bytes 143392 | tf_op jit(solution)/shard_map/ppermute | solution.py:638
  231.5 2.6 %finish.1 = (f32[4,1024]{1,0:T(4,128)}, f32[1,1024]{1,0:T(1,128)}, f32[1,1024]{1,0:T(1,128)}, f32[4,256]{1,0:T(4,128)}, f32[1,256]{1,0:T(1,128)}, /*index=5*/f32...) custom-call(s32[10]{0:T(128)} %stack.79.s_ref, f32[16,640]{1,0:T(8,128)} %get-tuple-element.387.first, ...), custom_call_target="tpu_custom_call" | custom-call | tf_op jit(solution)/shard_map/finish/pallas_call | solution.py:1045
  (279 shorter events, 43.7 us)
Async XLA Ops:
  6.1 22.3 %collective-permute-start.2 = (bf16[256,896]{1,0:T(8,128)(2,1)}, bf16[256,896]{1,0:T(8,128)(2,1)}, u32[]{:S(2)}, u32[]{:S(2)}) collective-permute-start(bf16[256,896]{1,0:T(8,128)(2,1)} %concatenate.134.rest_0_), channel_id=1, source_target_pairs={{0,24},{8,16},{16,8},{24,0},{1,25},{9,17},{17,9},{25,1},{2,26},{10... | collective-permute-start | bytes 1376264 | tf_op jit(solution)/shard_map/ppermute | solution.py:646
  10.0 20.7 %collective-permute-start.1 = (bf16[256,896]{1,0:T(8,128)(2,1)}, bf16[256,896]{1,0:T(8,128)(2,1)}, u32[]{:S(2)}, u32[]{:S(2)}) collective-permute-start(bf16[256,896]{1,0:T(8,128)(2,1)} %concatenate.134.rest_0_), channel_id=1, source_target_pairs={{0,16},{8,24},{16,0},{24,8},{1,17},{9,25},{17,1},{25,9},{2,18},{10... | collective-permute-start | bytes 1376264 | tf_op jit(solution)/shard_map/ppermute | solution.py:646
  10.5 20.5 %collective-permute-start = (bf16[256,896]{1,0:T(8,128)(2,1)}, bf16[256,896]{1,0:T(8,128)(2,1)}, u32[]{:S(2)}, u32[]{:S(2)}) collective-permute-start(bf16[256,896]{1,0:T(8,128)(2,1)} %concatenate.134.rest_0_), channel_id=1, source_target_pairs={{0,8},{8,0},{16,24},{24,16},{1,9},{9,1},{17,25},{25,17},{2,10},{10... | collective-permute-start | bytes 1376264 | tf_op jit(solution)/shard_map/ppermute | solution.py:646
  10.7 13.4 %collective-permute-start.3 = (bf16[256,1024]{1,0:T(8,128)(2,1)S(1)}, bf16[256,1024]{1,0:T(8,128)(2,1)}, u32[]{:S(2)}, u32[]{:S(2)}) collective-permute-start(bf16[256,1024]{1,0:T(8,128)(2,1)S(1)} %get-tuple-element.365), channel_id=1, source_target_pairs={{0,2},{2,0},{4,6},{6,4},{1,3},{3,1},{5,7},{7,5},{8,10},{10,8},{12,... | collective-permute-start | bytes 1572872 | tf_op jit(solution)/shard_map/ppermute | solution.py:638
  16.4 0.7 collective-permute-start.5
  17.0 7.9 %collective-permute-start.6 = (bf16[16,1024]{1,0:T(8,128)(2,1)S(1)}, bf16[16,1024]{1,0:T(8,128)(2,1)S(1)}, u32[]{:S(2)}, u32[]{:S(2)}) collective-permute-start(bf16[16,1024]{1,0:T(8,128)(2,1)S(1)} %collective-permute-done.5), channel_id=1, source_target_pairs={{0,1},{1,0},{2,3},{3,2},{4,5},{5,4},{6,7},{7,6},{8,9},{9,8},{10,11... | collective-permute-start | bytes 98312 | tf_op jit(solution)/shard_map/ppermute | solution.py:635
  24.1 10.5 %collective-permute-start.4 = (bf16[256,1024]{1,0:T(8,128)(2,1)}, bf16[256,1024]{1,0:T(8,128)(2,1)}, u32[]{:S(2)}, u32[]{:S(2)}) collective-permute-start(bf16[256,1024]{1,0:T(8,128)(2,1)} %collective-permute-done.3.near), channel_id=1, source_target_pairs={{0,1},{1,0},{2,3},{3,2},{4,5},{5,4},{6,7},{7,6},{8,9},{9,8},{10,11... | collective-permute-start | bytes 1572872 | tf_op jit(solution)/shard_map/ppermute | solution.py:635
  25.0 23.7 %collective-permute-start.7 = (bf16[256,1024]{1,0:T(8,128)(2,1)}, bf16[256,1024]{1,0:T(8,128)(2,1)}, u32[]{:S(2)}, u32[]{:S(2)}) collective-permute-start(bf16[256,1024]{1,0:T(8,128)(2,1)} %constant_dynamic-slice_fusion.12), channel_id=1, source_target_pairs={{0,2},{2,0},{4,6},{6,4},{1,3},{3,1},{5,7},{7,5},{8,10},{10,8},{12,... | collective-permute-start | bytes 1572872 | tf_op jit(solution)/shard_map/ppermute | solution.py:638
  31.1 29.6 %collective-permute-start.11 = (bf16[256,1024]{1,0:T(8,128)(2,1)S(1)}, bf16[256,1024]{1,0:T(8,128)(2,1)S(1)}, u32[]{:S(2)}, u32[]{:S(2)}) collective-permute-start(bf16[256,1024]{1,0:T(8,128)(2,1)S(1)} %pad_maximum_fusion.13.rest_0_.rest_4_), channel_id=1, source_target_pairs={{0,24},{8,16},{16,8},{24,0},{1,25},{9,17},{17,9},{25,1},{2,26},{10... | collective-permute-start | bytes 1572872 | tf_op jit(solution)/shard_map/ppermute | solution.py:646
  32.6 28.1 %collective-permute-start.10 = (bf16[256,1024]{1,0:T(8,128)(2,1)S(1)}, bf16[256,1024]{1,0:T(8,128)(2,1)S(1)}, u32[]{:S(2)}, u32[]{:S(2)}) collective-permute-start(bf16[256,1024]{1,0:T(8,128)(2,1)S(1)} %pad_maximum_fusion.13.rest_0_.rest_4_), channel_id=1, source_target_pairs={{0,16},{8,24},{16,0},{24,8},{1,17},{9,25},{17,1},{25,9},{2,18},{10... | collective-permute-start | bytes 1572872 | tf_op jit(solution)/shard_map/ppermute | solution.py:646
  34.1 26.6 %collective-permute-start.9 = (bf16[256,1024]{1,0:T(8,128)(2,1)S(1)}, bf16[256,1024]{1,0:T(8,128)(2,1)S(1)}, u32[]{:S(2)}, u32[]{:S(2)}) collective-permute-start(bf16[256,1024]{1,0:T(8,128)(2,1)S(1)} %pad_maximum_fusion.13.rest_0_.rest_4_), channel_id=1, source_target_pairs={{0,8},{8,0},{16,24},{24,16},{1,9},{9,1},{17,25},{25,17},{2,10},{10... | collective-permute-start | bytes 1572872 | tf_op jit(solution)/shard_map/ppermute | solution.py:646
  48.6 12.0 %collective-permute-start.8 = (bf16[256,1024]{1,0:T(8,128)(2,1)}, bf16[256,1024]{1,0:T(8,128)(2,1)S(1)}, u32[]{:S(2)}, u32[]{:S(2)}) collective-permute-start(bf16[256,1024]{1,0:T(8,128)(2,1)} %collective-permute-done.7.near), channel_id=1, source_target_pairs={{0,1},{1,0},{2,3},{3,2},{4,5},{5,4},{6,7},{7,6},{8,9},{9,8},{10,11... | collective-permute-start | bytes 1572872 | tf_op jit(solution)/shard_map/ppermute | solution.py:635
  48.7 20.3 %collective-permute-start.12 = (f32[128,512]{1,0:T(8,128)}, f32[128,512]{1,0:T(8,128)S(1)}, u32[]{:S(2)}, u32[]{:S(2)}) collective-permute-start(f32[128,512]{1,0:T(8,128)} %get-tuple-element.188.hend), channel_id=1, source_target_pairs={{0,4},{2,6},{1,5},{3,7},{8,12},{10,14},{9,13},{11,15},{16,20},{18,... | collective-permute-start | bytes 786440 | tf_op jit(solution)/shard_map/ppermute | solution.py:641
  75.6 4.2 %collective-permute-start.15 = (f32[16,1024]{1,0:T(8,128)S(1)}, f32[16,1024]{1,0:T(8,128)S(1)}, u32[]{:S(2)}, u32[]{:S(2)}) collective-permute-start(f32[16,1024]{1,0:T(8,128)S(1)} %get-tuple-element.190.sums), channel_id=1, source_target_pairs={{0,3},{1,2},{2,1},{3,0},{4,7},{5,6},{6,5},{7,4},{8,11},{9,10},{10,... | collective-permute-start | bytes 196616 | tf_op jit(solution)/shard_map/ppermute | solution.py:817
  77.3 4.3 %collective-permute-start.14 = (f32[16,1024]{1,0:T(8,128)S(1)}, f32[16,1024]{1,0:T(8,128)S(1)}, u32[]{:S(2)}, u32[]{:S(2)}) collective-permute-start(f32[16,1024]{1,0:T(8,128)S(1)} %get-tuple-element.190.sums), channel_id=1, source_target_pairs={{0,2},{2,0},{4,6},{6,4},{1,3},{3,1},{5,7},{7,5},{8,10},{10,8},{12,... | collective-permute-start | bytes 196616 | tf_op jit(solution)/shard_map/ppermute | solution.py:638
  77.6 4.0 %collective-permute-start.13 = (f32[16,1024]{1,0:T(8,128)S(1)}, f32[16,1024]{1,0:T(8,128)S(1)}, u32[]{:S(2)}, u32[]{:S(2)}) collective-permute-start(f32[16,1024]{1,0:T(8,128)S(1)} %get-tuple-element.190.sums), channel_id=1, source_target_pairs={{0,1},{1,0},{2,3},{3,2},{4,5},{5,4},{6,7},{7,6},{8,9},{9,8},{10,11... | collective-permute-start | bytes 196616 | tf_op jit(solution)/shard_map/ppermute | solution.py:635
  98.1 23.6 %collective-permute-start.19 = (f16[272,1024]{1,0:T(8,128)(2,1)S(1)}, f16[272,1024]{1,0:T(8,128)(2,1)}, u32[]{:S(2)}, u32[]{:S(2)}) collective-permute-start(f16[272,1024]{1,0:T(8,128)(2,1)S(1)} %get-tuple-element.417), channel_id=1, source_target_pairs={{0,24},{8,16},{16,8},{24,0},{1,25},{9,17},{17,9},{25,1},{2,26},{10... | collective-permute-start | bytes 1671176 | tf_op jit(solution)/shard_map/ppermute | solution.py:646
  99.9 25.3 %collective-permute-start.18 = (f16[272,1024]{1,0:T(8,128)(2,1)S(1)}, f16[272,1024]{1,0:T(8,128)(2,1)}, u32[]{:S(2)}, u32[]{:S(2)}) collective-permute-start(f16[272,1024]{1,0:T(8,128)(2,1)S(1)} %get-tuple-element.418), channel_id=1, source_target_pairs={{0,16},{8,24},{16,0},{24,8},{1,17},{9,25},{17,1},{25,9},{2,18},{10... | collective-permute-start | bytes 1671176 | tf_op jit(solution)/shard_map/ppermute | solution.py:646
  101.1 24.0 %collective-permute-start.17 = (f16[272,1024]{1,0:T(8,128)(2,1)S(1)}, f16[272,1024]{1,0:T(8,128)(2,1)}, u32[]{:S(2)}, u32[]{:S(2)}) collective-permute-start(f16[272,1024]{1,0:T(8,128)(2,1)S(1)} %get-tuple-element.419), channel_id=1, source_target_pairs={{0,8},{8,0},{16,24},{24,16},{1,9},{9,1},{17,25},{25,17},{2,10},{10... | collective-permute-start | bytes 1671176 | tf_op jit(solution)/shard_map/ppermute | solution.py:646
  101.7 20.0 %collective-permute-start.16 = (f32[128,512]{1,0:T(8,128)S(1)}, f32[128,512]{1,0:T(8,128)S(1)}, u32[]{:S(2)}, u32[]{:S(2)}) collective-permute-start(f32[128,512]{1,0:T(8,128)S(1)} %get-tuple-element.191), channel_id=1, source_target_pairs={{4,0},{6,2},{5,1},{7,3},{12,8},{14,10},{13,9},{15,11},{20,16},{22,... | collective-permute-start | bytes 786440 | tf_op jit(solution)/shard_map/ppermute | solution.py:641
  125.2 2.9 %collective-permute-start.21 = (f32[256,1024]{1,0:T(8,128)}, f32[256,1024]{1,0:T(8,128)S(1)}, u32[]{:S(2)}, u32[]{:S(2)}) collective-permute-start(f32[256,1024]{1,0:T(8,128)} %get-tuple-element.216), channel_id=1, source_target_pairs={{0,1},{1,0},{2,3},{3,2},{4,5},{5,4},{6,7},{7,6},{8,9},{9,8},{10,11... | collective-permute-start | bytes 3145736 | tf_op jit(solution)/shard_map/ppermute | solution.py:635
  129.1 15.8 %collective-permute-start.22 = (f32[64,1024]{1,0:T(8,128)S(1)}, f32[64,1024]{1,0:T(8,128)S(1)}, u32[]{:S(2)}, u32[]{:S(2)}) collective-permute-start(f32[64,1024]{1,0:T(8,128)S(1)} %slice_add_fusion.1), channel_id=1, source_target_pairs={{0,2},{2,0},{4,6},{6,4},{1,3},{3,1},{5,7},{7,5},{8,10},{10,8},{12,... | collective-permute-start | bytes 786440 | tf_op jit(solution)/shard_map/ppermute | solution.py:638
  131.2 24.5 %collective-permute-start.25 = (f16[80,1024]{1,0:T(8,128)(2,1)S(1)}, f16[80,1024]{1,0:T(8,128)(2,1)S(1)}, u32[]{:S(2)}, u32[]{:S(2)}) collective-permute-start(f16[80,1024]{1,0:T(8,128)(2,1)S(1)} %get-tuple-element.414), channel_id=1, source_target_pairs={{0,6},{2,4},{4,2},{6,0},{1,7},{3,5},{5,3},{7,1},{8,14},{10,12},{12... | collective-permute-start | bytes 491528 | tf_op jit(solution)/shard_map/ppermute | solution.py:638
  131.3 24.4 %collective-permute-start.24 = (f16[80,1024]{1,0:T(8,128)(2,1)S(1)}, f16[80,1024]{1,0:T(8,128)(2,1)S(1)}, u32[]{:S(2)}, u32[]{:S(2)}) collective-permute-start(f16[80,1024]{1,0:T(8,128)(2,1)S(1)} %get-tuple-element.415), channel_id=1, source_target_pairs={{0,4},{2,6},{4,0},{6,2},{1,5},{3,7},{5,1},{7,3},{8,12},{10,14},{12... | collective-permute-start | bytes 491528 | tf_op jit(solution)/shard_map/ppermute | solution.py:638
  132.8 22.9 %collective-permute-start.23 = (f16[80,1024]{1,0:T(8,128)(2,1)S(1)}, f16[80,1024]{1,0:T(8,128)(2,1)S(1)}, u32[]{:S(2)}, u32[]{:S(2)}) collective-permute-start(f16[80,1024]{1,0:T(8,128)(2,1)S(1)} %get-tuple-element.416), channel_id=1, source_target_pairs={{0,2},{2,0},{4,6},{6,4},{1,3},{3,1},{5,7},{7,5},{8,10},{10,8},{12,... | collective-permute-start | bytes 491528 | tf_op jit(solution)/shard_map/ppermute | solution.py:638
  143.6 13.3 %collective-permute-start.26 = (f32[8,512]{1,0:T(8,128)S(1)}, f32[8,512]{1,0:T(8,128)S(1)}, u32[]{:S(2)}, u32[]{:S(2)}) collective-permute-start(f32[8,512]{1,0:T(8,128)S(1)} %get-tuple-element.235), channel_id=1, source_target_pairs={{4,0},{6,2},{5,1},{7,3},{12,8},{14,10},{13,9},{15,11},{20,16},{22,... | collective-permute-start | bytes 49160 | tf_op jit(solution)/shard_map/ppermute | solution.py:641
  156.9 1.9 collective-permute-start.27
  158.9 8.4 %collective-permute-start.28 = (f32[512,128]{1,0:T(8,128)S(1)}, f32[512,128]{1,0:T(8,128)S(1)}, u32[]{:S(2)}, u32[]{:S(2)}) collective-permute-start(f32[512,128]{1,0:T(8,128)S(1)} %constant_dynamic-slice_fusion.10), channel_id=1, source_target_pairs={{0,2},{2,0},{4,6},{6,4},{1,3},{3,1},{5,7},{7,5},{8,10},{10,8},{12,... | collective-permute-start | bytes 786440 | tf_op jit(solution)/shard_map/ppermute | solution.py:638
  167.4 1.6 collective-permute-start.29
  169.7 6.4 %collective-permute-start.30 = (f32[8,128]{1,0:T(8,128)S(1)}, f32[8,128]{1,0:T(8,128)S(1)}, u32[]{:S(2)}, u32[]{:S(2)}) collective-permute-start(f32[8,128]{1,0:T(8,128)S(1)} %fusion.21), channel_id=1, source_target_pairs={{4,0},{6,2},{5,1},{7,3},{12,8},{14,10},{13,9},{15,11},{20,16},{22,... | collective-permute-start | bytes 12296 | tf_op jit(solution)/shard_map/ppermute | solution.py:641
  176.1 18.9 %collective-permute-start.31 = (f32[192,1024]{1,0:T(8,128)}, f32[192,1024]{1,0:T(8,128)S(1)}, u32[]{:S(2)}, u32[]{:S(2)}) collective-permute-start(f32[192,1024]{1,0:T(8,128)} %slice_add_fusion), channel_id=1, source_target_pairs={{0,2},{2,0},{4,6},{6,4},{1,3},{3,1},{5,7},{7,5},{8,10},{10,8},{12,... | collective-permute-start | bytes 2359304 | tf_op jit(solution)/shard_map/ppermute | solution.py:638
  176.4 12.6 %collective-permute-start.32 = (f16[304,512]{1,0:T(8,128)(2,1)}, f16[304,512]{1,0:T(8,128)(2,1)}, u32[]{:S(2)}, u32[]{:S(2)}) collective-permute-start(f16[304,512]{1,0:T(8,128)(2,1)} %get-tuple-element.264), channel_id=1, source_target_pairs={{0,8},{8,0},{16,24},{24,16},{1,9},{9,1},{17,25},{25,17},{2,10},{10... | collective-permute-start | bytes 933896 | tf_op jit(solution)/shard_map/ppermute | solution.py:646
  177.8 14.7 %collective-permute-start.33 = (f16[304,512]{1,0:T(8,128)(2,1)S(1)}, f16[304,512]{1,0:T(8,128)(2,1)}, u32[]{:S(2)}, u32[]{:S(2)}) collective-permute-start(f16[304,512]{1,0:T(8,128)(2,1)S(1)} %get-tuple-element.265), channel_id=1, source_target_pairs={{0,16},{8,24},{16,0},{24,8},{1,17},{9,25},{17,1},{25,9},{2,18},{10... | collective-permute-start | bytes 933896 | tf_op jit(solution)/shard_map/ppermute | solution.py:646
  178.6 14.0 %collective-permute-start.34 = (f16[304,512]{1,0:T(8,128)(2,1)S(1)}, f16[304,512]{1,0:T(8,128)(2,1)}, u32[]{:S(2)}, u32[]{:S(2)}) collective-permute-start(f16[304,512]{1,0:T(8,128)(2,1)S(1)} %get-tuple-element.266), channel_id=1, source_target_pairs={{0,24},{8,16},{16,8},{24,0},{1,25},{9,17},{17,9},{25,1},{2,26},{10... | collective-permute-start | bytes 933896 | tf_op jit(solution)/shard_map/ppermute | solution.py:646
  195.0 2.7 %collective-permute-start.37 = (f32[256,1024]{1,0:T(8,128)S(1)}, f32[256,1024]{1,0:T(8,128)S(1)}, u32[]{:S(2)}, u32[]{:S(2)}) collective-permute-start(f32[256,1024]{1,0:T(8,128)S(1)} %get-tuple-element.272), channel_id=1, source_target_pairs={{0,1},{1,0},{2,3},{3,2},{4,5},{5,4},{6,7},{7,6},{8,9},{9,8},{10,11... | collective-permute-start | bytes 3145736 | tf_op jit(solution)/shard_map/ppermute | solution.py:635
  195.0 18.8 %collective-permute-start.20 = (f32[256,1024]{1,0:T(8,128)S(1)}, f32[256,1024]{1,0:T(8,128)S(1)}, u32[]{:S(2)}, u32[]{:S(2)}) collective-permute-start(f32[256,1024]{1,0:T(8,128)S(1)} %copy-done.44), channel_id=1, source_target_pairs={{0,1},{1,0},{2,3},{3,2},{4,5},{5,4},{6,7},{7,6},{8,9},{9,8},{10,11... | collective-permute-start | bytes 3145736 | tf_op jit(solution)/shard_map/ppermute | solution.py:635
  198.1 14.7 %collective-permute-start.41 = (f16[272,1024]{1,0:T(8,128)(2,1)S(1)}, f16[272,1024]{1,0:T(8,128)(2,1)S(1)}, u32[]{:S(2)}, u32[]{:S(2)}) collective-permute-start(f16[272,1024]{1,0:T(8,128)(2,1)S(1)} %pad_maximum_fusion.3), channel_id=1, source_target_pairs={{0,2},{2,0},{4,6},{6,4},{1,3},{3,1},{5,7},{7,5},{8,10},{10,8},{12,... | collective-permute-start | bytes 1671176 | tf_op jit(solution)/shard_map/ppermute | solution.py:638
  203.4 5.8 %collective-permute-start.40 = (f16[304,128]{1,0:T(8,128)(2,1)S(1)}, f16[304,128]{1,0:T(8,128)(2,1)S(1)}, u32[]{:S(2)}, u32[]{:S(2)}) collective-permute-start(f16[304,128]{1,0:T(8,128)(2,1)S(1)} %get-tuple-element.420), channel_id=1, source_target_pairs={{0,24},{8,16},{16,8},{24,0},{1,25},{9,17},{17,9},{25,1},{2,26},{10... | collective-permute-start | bytes 233480 | tf_op jit(solution)/shard_map/ppermute | solution.py:646
  205.1 5.0 %collective-permute-start.39 = (f16[304,128]{1,0:T(8,128)(2,1)S(1)}, f16[304,128]{1,0:T(8,128)(2,1)S(1)}, u32[]{:S(2)}, u32[]{:S(2)}) collective-permute-start(f16[304,128]{1,0:T(8,128)(2,1)S(1)} %get-tuple-element.421), channel_id=1, source_target_pairs={{0,16},{8,24},{16,0},{24,8},{1,17},{9,25},{17,1},{25,9},{2,18},{10... | collective-permute-start | bytes 233480 | tf_op jit(solution)/shard_map/ppermute | solution.py:646
  206.4 4.4 %collective-permute-start.38 = (f16[304,128]{1,0:T(8,128)(2,1)S(1)}, f16[304,128]{1,0:T(8,128)(2,1)S(1)}, u32[]{:S(2)}, u32[]{:S(2)}) collective-permute-start(f16[304,128]{1,0:T(8,128)(2,1)S(1)} %get-tuple-element.422), channel_id=1, source_target_pairs={{0,8},{8,0},{16,24},{24,16},{1,9},{9,1},{17,25},{25,17},{2,10},{10... | collective-permute-start | bytes 233480 | tf_op jit(solution)/shard_map/ppermute | solution.py:646
  209.2 4.2 %collective-permute-start.36 = (f32[256,1024]{1,0:T(8,128)S(1)}, f32[256,1024]{1,0:T(8,128)S(1)}, u32[]{:S(2)}, u32[]{:S(2)}) collective-permute-start(f32[256,1024]{1,0:T(8,128)S(1)} %get-tuple-element.269), channel_id=1, source_target_pairs={{0,1},{1,0},{2,3},{3,2},{4,5},{5,4},{6,7},{7,6},{8,9},{9,8},{10,11... | collective-permute-start | bytes 3145736 | tf_op jit(solution)/shard_map/ppermute | solution.py:635
  215.4 8.1 %collective-permute-start.42 = (f32[256,1024]{1,0:T(8,128)S(1)}, f32[256,1024]{1,0:T(8,128)S(1)}, u32[]{:S(2)}, u32[]{:S(2)}) collective-permute-start(f32[256,1024]{1,0:T(8,128)S(1)} %get-tuple-element.380), channel_id=1, source_target_pairs={{0,1},{1,0},{2,3},{3,2},{4,5},{5,4},{6,7},{7,6},{8,9},{9,8},{10,11... | collective-permute-start | bytes 3145736 | tf_op jit(solution)/shard_map/ppermute | solution.py:635
  215.5 5.4 %collective-permute-start.35 = (bf16[256,1024]{1,0:T(8,128)(2,1)S(1)}, bf16[256,1024]{1,0:T(8,128)(2,1)}, u32[]{:S(2)}, u32[]{:S(2)}) collective-permute-start(bf16[256,1024]{1,0:T(8,128)(2,1)S(1)} %get-tuple-element.381), channel_id=1, source_target_pairs={{0,1},{1,0},{2,3},{3,2},{4,5},{5,4},{6,7},{7,6},{8,9},{9,8},{10,11... | collective-permute-start | bytes 1572872 | tf_op jit(solution)/shard_map/ppermute | solution.py:635
  216.5 8.5 %collective-permute-start.43 = (f16[112,640]{1,0:T(8,128)(2,1)S(1)}, f16[112,640]{1,0:T(8,128)(2,1)S(1)}, u32[]{:S(2)}, u32[]{:S(2)}) collective-permute-start(f16[112,640]{1,0:T(8,128)(2,1)S(1)} %get-tuple-element.293), channel_id=1, source_target_pairs={{0,2},{2,0},{4,6},{6,4},{1,3},{3,1},{5,7},{7,5},{8,10},{10,8},{12,... | collective-permute-start | bytes 430088 | tf_op jit(solution)/shard_map/ppermute | solution.py:638
  216.8 13.7 %collective-permute-start.44 = (f16[112,640]{1,0:T(8,128)(2,1)S(1)}, f16[112,640]{1,0:T(8,128)(2,1)S(1)}, u32[]{:S(2)}, u32[]{:S(2)}) collective-permute-start(f16[112,640]{1,0:T(8,128)(2,1)S(1)} %get-tuple-element.294), channel_id=1, source_target_pairs={{0,4},{2,6},{4,0},{6,2},{1,5},{3,7},{5,1},{7,3},{8,12},{10,14},{12... | collective-permute-start | bytes 430088 | tf_op jit(solution)/shard_map/ppermute | solution.py:638
  217.4 13.1 %collective-permute-start.45 = (f16[112,640]{1,0:T(8,128)(2,1)S(1)}, f16[112,640]{1,0:T(8,128)(2,1)S(1)}, u32[]{:S(2)}, u32[]{:S(2)}) collective-permute-start(f16[112,640]{1,0:T(8,128)(2,1)S(1)} %get-tuple-element.295), channel_id=1, source_target_pairs={{0,6},{2,4},{4,2},{6,0},{1,7},{3,5},{5,3},{7,1},{8,14},{10,12},{12... | collective-permute-start | bytes 430088 | tf_op jit(solution)/shard_map/ppermute | solution.py:638
  234.1 2.6 %collective-permute-start.46 = (f32[1024]{0:T(1024)}, f32[1024]{0:T(1024)S(1)}, u32[]{:S(2)}, u32[]{:S(2)}) collective-permute-start(f32[1024]{0:T(1024)} %bitcast.121), channel_id=1, source_target_pairs={{0,1},{1,0},{2,3},{3,2},{4,5},{5,4},{6,7},{7,6},{8,9},{9,8},{10,11... | collective-permute-start | bytes 12296 | tf_op jit(solution)/shard_map/ppermute | solution.py:635
  234.3 3.0 %collective-permute-start.47 = (f32[2,64,64]{2,1,0:T(8,128)S(1)}, f32[2,64,64]{2,1,0:T(8,128)S(1)}, u32[]{:S(2)}, u32[]{:S(2)}) collective-permute-start(f32[2,64,64]{2,1,0:T(8,128)S(1)} %get-tuple-element.403), channel_id=1, source_target_pairs={{0,1},{1,0},{2,3},{3,2},{4,5},{5,4},{6,7},{7,6},{8,9},{9,8},{10,11... | collective-permute-start | bytes 98312 | tf_op jit(solution)/shard_map/ppermute | solution.py:635
  (48 other events, 471.7 us)

commit v8 on v7

--- a/solution.py
+++ b/solution.py
@@ -889,7 +889,7 @@
     )(scalars, gated_later, *ws2)
 
     returned, early_got, branch = lax.optimization_barrier((returned, early_got, branch))
-    front_rows = halfway // 4
+    front_rows = halfway // 16 * 5
     branch_give = swap(branch[3])
     branch_theirs = [branch[1][:front_rows] + branch_give[:front_rows], branch[1][front_rows:] + branch_give[front_rows:]]
     returned, branch_theirs = lax.optimization_barrier((returned, branch_theirs))

time: 240 us -> 238 us (level)
  transfers between devices with their start and end apart: 48 -> 48, of which waited for: 17 -> 17; matrix products, arithmetic and copies ran while one was open for 10% -> 10% of each run, Pallas kernels for 34% -> 35%
where the time goes in v8:
time: 238 us; the launch traced here: 237 us
  Pallas kernels  105 us (44%)
  starting transfers between devices  48.4 us (20%)
  waiting for transfers between devices  42.8 us (18%)
  other arithmetic  22 us (9%)
  local copies, waits for them, and re-layouts  15.9 us (7%)
  between operations  2.56 us (1%)
    ppermute x13, waiting for transfers between devices, across(): return lax.ppermute(value, 'ctx', [(i, i ^ j) for i in range(ctxs)])  21.4 us
    ppermute x15, starting transfers between devices, spread(): return lax.ppermute(value, 'dp', [(i, i ^ j) for i in range(dps)])  18.6 us
    ppermute x13, starting transfers between devices, across(): return lax.ppermute(value, 'ctx', [(i, i ^ j) for i in range(ctxs)])  16.4 us
    pallas_call x3, Pallas kernels, grads(): grid_call(functools.partial(grads_body, parts, [(n, n + 1) for n in range...  14.8 us
    pallas_call x1, Pallas kernels, per_device(): grid_call(functools.partial(front_body, parts, inner, states, quarter), (...  14 us
    ppermute x15, waiting for transfers between devices, spread(): return lax.ppermute(value, 'dp', [(i, i ^ j) for i in range(dps)])  13 us
    pallas_call x1, Pallas kernels, per_device(): grid_call(functools.partial(back_body, inner, states), (count,), [rows_sp...  11.6 us
    pallas_call x1, Pallas kernels, per_device(): grid_call(functools.partial(join_body, inner), (count,), [back(inner), ba...  10 us
  transfers between devices with their start and end apart: 48, of which 17 were waited for; matrix products, arithmetic and copies ran while one was open for 10% of the time, Pallas kernels for 35%

profile of v8, /device:TPU:0, one launch (start us, length us, event | category | flops | bytes accessed | tf_op | source)
XLA Modules:
  0.0 236.9 jit_solution(6955689598423086453)
XLA Ops:
  1.7 3.3 %constant_dynamic-slice_fusion.15 = (bf16[256,1,512]{2,1,0:T(2,128)(2,1)}, bf16[256,1,512]{2,1,0:T(2,128)(2,1)S(1)}) fusion(bf16[256,2,1024]{2,1,0:T(2,128)(2,1)} %param.20, s32[]{:T(128)S(6)} %select_n.151, s32[]{:T(128)S(6)} %add.319), kind=kLoop, calls=%fused_computation.137 | loop fusion | bytes 1048584 | tf_op jit(solution)/shard_map/slice | solution.py:743
  6.1 3.9 %collective-permute-start.2 = (bf16[256,896]{1,0:T(8,128)(2,1)}, bf16[256,896]{1,0:T(8,128)(2,1)}, u32[]{:S(2)}, u32[]{:S(2)}) collective-permute-start(bf16[256,896]{1,0:T(8,128)(2,1)} %concatenate.134.rest_0_), channel_id=1, source_target_pairs={{0,24},{8,16},{16,8},{24,0},{1,25},{9,17},{17,9},{25,1},{2,26},{10... | collective-permute-start | bytes 1376264 | tf_op jit(solution)/shard_map/ppermute | solution.py:646
  10.7 2.2 collective-permute-start.3
  17.1 7.0 %collective-permute-done.3.near = bf16[256,1024]{1,0:T(8,128)(2,1)} collective-permute-done((bf16[256,1024]{1,0:T(8,128)(2,1)S(1)}, bf16[256,1024]{1,0:T(8,128)(2,1)}, u32[]{:S(2)}, u32[]{:S(2)}) %collective-permute-start.3) | collective-permute-done | bytes 524320 | tf_op jit(solution)/shard_map/ppermute | solution.py:638
  25.0 1.7 collective-permute-start.7
  28.4 2.2 collective-permute-done.1.rest_2_
  31.1 1.5 collective-permute-start.11
  32.6 1.5 collective-permute-start.10
  34.6 14.0 %front.1 = (bf16[1024,1024]{1,0:T(8,128)(2,1)}, f32[1024,768]{1,0:T(8,128)}, f32[8,768]{1,0:T(8,128)}, f32[1024,768]{1,0:T(8,128)}, f32[1024,128]{1,0:T(8,128)},...) custom-call(s32[10]{0:T(128)} %stack.79.s_ref, bf16[512,1024]{1,0:T(8,128)(2,1)} %bitcast.92, ...), custom_call_target="tpu_custom_call" | custom-call | tf_op jit(solution)/shard_map/front/pallas_call | solution.py:757
  48.7 4.7 %collective-permute-start.12 = (f32[128,512]{1,0:T(8,128)}, f32[128,512]{1,0:T(8,128)S(1)}, u32[]{:S(2)}, u32[]{:S(2)}) collective-permute-start(f32[128,512]{1,0:T(8,128)} %get-tuple-element.188.hend), channel_id=1, source_target_pairs={{0,4},{2,6},{1,5},{3,7},{8,12},{10,14},{9,13},{11,15},{16,20},{18,... | collective-permute-start | bytes 786440 | tf_op jit(solution)/shard_map/ppermute | solution.py:641
  53.7 6.9 %within.1.yw = f32[1024,512]{1,0:T(8,128)S(1)} custom-call(s32[10]{0:T(128)S(1)} %copy-done.12, f32[1024,768]{1,0:T(8,128)} %get-tuple-element.176.co, f32[1024,128]{1,0:T(8,128)} %get-tuple-element.177.hd), custom_call_target="tpu_custom_call" | custom-call | tf_op jit(solution)/shard_map/within/pallas_call | solution.py:782
  61.9 7.1 %gates.1 = (f32[1024,512]{1,0:T(8,128)S(1)}, f32[1024,512]{1,0:T(8,128)S(1)}, bf16[1024,1024]{1,0:T(8,128)(2,1)}) custom-call(s32[10]{0:T(128)S(1)} %copy-done.12, bf16[1024,1024]{1,0:T(8,128)(2,1)} %get-tuple-element.178.normed.refs_0_, bf16[512,1024]{1,0:T(8,128)(2,1)} %bitcast.94, bf16[256,1024]{1,0:T(8,128)(2,1)} %collective-permute-done.7.near, ...), custom_call_target="tpu_custom_call" | custom-call | tf_op jit(solution)/shard_map/gates/pallas_call | solution.py:793
  69.1 6.5 %output.1 = (f32[1024,512]{1,0:T(8,128)S(1)}, f32[16,1024]{1,0:T(8,128)S(1)}) custom-call(s32[10]{0:T(128)S(1)} %copy-done.12, f32[1024,768]{1,0:T(8,128)} %get-tuple-element.176.co, f32[1024,128]{1,0:T(8,128)} %get-tuple-element.177.hd, f32[1024,512]{1,0:T(8,128)S(1)} %within.1.yw, f32[1024,512]{1,0:T(8,128)S(1)} %get-tuple-element.184.gate, ...), custom_call_target="tpu_custom_call" | custom-call | tf_op jit(solution)/shard_map/output/pallas_call | solution.py:804
  75.6 1.7 collective-permute-start.15
  77.6 2.2 collective-permute-done.15.sums3
  79.8 1.8 collective-permute-done.14.sums2
  83.0 7.8 %turn.1 = (bf16[1024,512]{1,0:T(8,128)(2,1)S(1)}, bf16[1024,512]{1,0:T(8,128)(2,1)S(1)}, f32[1024,512]{1,0:T(8,128)}, f32[8,128,512]{2,1,0:T(8,128)}, f32[128,512]{1,0:T(8,128)S(1)}, /*index=5*/f32[8,512]{1,0:T(8,128)S(1)}) custom-call(s32[10]{0:T(128)S(1)} %copy-done.13, f32[1024,768]{1,0:T(8,128)} %get-tuple-element.176.co, ...), custom_call_target="tpu_custom_call" | custom-call | tf_op jit(solution)/shard_map/turn/pallas_call | solution.py:823
  90.9 6.3 %grad_early.1 = (f32[256,1024]{1,0:T(8,128)S(1)}, f32[256,1024]{1,0:T(8,128)S(1)}, f32[256,1024]{1,0:T(8,128)S(1)}, f32[256,1024]{1,0:T(8,128)S(1)}, f32[16,1024]{1,0:T(8,128)S(1)}, /*index=5*/f32[1,1024]{1,0:T(1,128)S(1)}) custom-call(s32[10]{0:T(128)S(1)} %copy-done.13, bf16[1024,1024]{1,0:T(8,128)(2,1)} %get-tuple-element.178.normed.refs_0_, ...), custom_call_target="tpu_custom_call" | custom-call | tf_op jit(solution)/shard_map/grad_early/pallas_call | solution.py:854
  98.1 1.7 collective-permute-start.19
  99.9 1.3 collective-permute-start.18
  101.7 1.5 collective-permute-start.16
  103.2 11.6 %back.1 = (f32[1024,512]{1,0:T(8,128)}, f32[1024,256]{1,0:T(8,128)}) custom-call(s32[10]{0:T(128)} %stack.79.s_ref, f32[1024,768]{1,0:T(8,128)} %get-tuple-element.176.co, f32[1024,128]{1,0:T(8,128)} %get-tuple-element.177.hd, f32[1024,512]{1,0:T(8,128)} %get-tuple-element.202.og, f32[8,128,512]{2,1,0:T(8,128)} %get-tuple-element.186.hloc.hnext, ...), custom_call_target="tpu_custom_call" | custom-call | tf_op jit(solution)/shard_map/back/pallas_call | solution.py:870
  114.7 6.9 %branch.1 = (f32[256,1024]{1,0:T(8,128)}, f32[256,1024]{1,0:T(8,128)}, f32[256,1024]{1,0:T(8,128)}, f32[256,1024]{1,0:T(8,128)}) custom-call(s32[10]{0:T(128)} %stack.79.s_ref, bf16[1024,512]{1,0:T(8,128)(2,1)} %copy-done.5, bf16[256,1024]{1,0:T(8,128)(2,1)} %copy-done.22, bf16[256,1024]{1,0:T(8,128)(2,1)} %copy-done.26, bf16[256,1024]{1,0:T(8,128)(2,1)} %copy-done.25, ...), custom_call_target="tpu_custom_call" | custom-call | tf_op jit(solution)/shard_map/branch/pallas_call | solution.py:881
  121.7 3.5 %collective-permute-done.18 = f16[272,1024]{1,0:T(8,128)(2,1)} collective-permute-done((f16[272,1024]{1,0:T(8,128)(2,1)S(1)}, f16[272,1024]{1,0:T(8,128)(2,1)}, u32[]{:S(2)}, u32[]{:S(2)}) %collective-permute-start.18) | collective-permute-done | bytes 557088 | tf_op jit(solution)/shard_map/ppermute | solution.py:646
  126.0 1.8 multiply_add_fusion
  129.1 2.0 collective-permute-start.22
  131.3 1.5 collective-permute-start.24
  132.8 2.9 %collective-permute-start.23 = (f16[80,1024]{1,0:T(8,128)(2,1)S(1)}, f16[80,1024]{1,0:T(8,128)(2,1)S(1)}, u32[]{:S(2)}, u32[]{:S(2)}) collective-permute-start(f16[80,1024]{1,0:T(8,128)(2,1)S(1)} %get-tuple-element.416), channel_id=1, source_target_pairs={{0,2},{2,0},{4,6},{6,4},{1,3},{3,1},{5,7},{7,5},{8,10},{10,8},{12,... | collective-permute-start | bytes 491528 | tf_op jit(solution)/shard_map/ppermute | solution.py:638
  135.7 7.9 %meet.1 = (f32[1024,512]{1,0:T(8,128)S(1)}, f32[32,512]{1,0:T(8,128)S(1)}, f32[512,256]{1,0:T(8,128)S(1)}, f32[512,256]{1,0:T(8,128)S(1)}, f32[8,512]{1,0:T(8,128)S(1)}) custom-call(s32[10]{0:T(128)S(1)} %copy-done.14, f32[1024,768]{1,0:T(8,128)} %get-tuple-element.176.co, f32[1024,128]{1,0:T(8,128)} %get-tuple-element.177.hd, ...), custom_call_target="tpu_custom_call" | custom-call | tf_op jit(solution)/shard_map/meet/pallas_call | solution.py:911
  143.6 1.3 collective-permute-start.26
  144.9 10.0 %join.1 = (bf16[1024,512]{1,0:T(8,128)(2,1)S(1)}, f32[8,512]{1,0:T(8,128)S(1)}, f32[1024,128]{1,0:T(8,128)S(1)}, f32[8,128]{1,0:T(8,128)S(1)}, f32[8,512]{1,0:T(8,128)S(1)}) custom-call(s32[10]{0:T(128)S(1)} %copy-done.14, f32[1024,768]{1,0:T(8,128)} %get-tuple-element.176.co, f32[1024,128]{1,0:T(8,128)} %get-tuple-element.177.hd, ...), custom_call_target="tpu_custom_call" | custom-call | tf_op jit(solution)/shard_map/join/pallas_call | solution.py:930
  158.3 4.7 %grad_signal.1 = (f32[256,512]{1,0:T(8,128)S(1)}, f32[256,512]{1,0:T(8,128)S(1)}, f32[256,512]{1,0:T(8,128)S(1)}, f32[256,512]{1,0:T(8,128)S(1)}, f32[16,512]{1,0:T(8,128)S(1)}, /*index=5*/f32[1,512]{1,0:T(1,128)S(1)}) custom-call(s32[10]{0:T(128)S(1)} %copy-done.14, bf16[1024,1024]{1,0:T(8,128)(2,1)} %get-tuple-element.178.normed.refs_0_, ...), custom_call_target="tpu_custom_call" | custom-call | tf_op jit(solution)/shard_map/grad_signal/pallas_call | solution.py:854
  163.0 3.6 %collective-permute-done.28 = f32[512,128]{1,0:T(8,128)S(1)} collective-permute-done((f32[512,128]{1,0:T(8,128)S(1)}, f32[512,128]{1,0:T(8,128)S(1)}, u32[]{:S(2)}, u32[]{:S(2)}) %collective-permute-start.28) | collective-permute-done | bytes 262176 | tf_op jit(solution)/shard_map/ppermute | solution.py:638
  166.9 1.3 collective-permute-done.29.dbc_other
  168.9 1.6 collective-permute-start.30
  171.7 3.7 %collective-permute-done.30.ahead = f32[8,128]{1,0:T(8,128)S(1)} collective-permute-done((f32[8,128]{1,0:T(8,128)S(1)}, f32[8,128]{1,0:T(8,128)S(1)}, u32[]{:S(2)}, u32[]{:S(2)}) %collective-permute-start.30) | collective-permute-done | bytes 4128 | tf_op jit(solution)/shard_map/ppermute | solution.py:641
  175.6 1.5 collective-permute-start.32
  179.2 9.0 %feature.1 = (f32[256,1024]{1,0:T(8,128)S(1)}, f32[256,1024]{1,0:T(8,128)S(1)}, f32[256,1024]{1,0:T(8,128)S(1)}, f32[256,1024]{1,0:T(8,128)S(1)}, bf16[1024,128]...) custom-call(s32[10]{0:T(128)S(1)} %copy-done.14, bf16[512,1024]{1,0:T(8,128)(2,1)} %bitcast.93, ...), custom_call_target="tpu_custom_call" | custom-call | tf_op jit(solution)/shard_map/feature/pallas_call | solution.py:980
  188.3 3.8 %collective-permute-done.33 = f16[304,512]{1,0:T(8,128)(2,1)} collective-permute-done((f16[304,512]{1,0:T(8,128)(2,1)}, f16[304,512]{1,0:T(8,128)(2,1)}, u32[]{:S(2)}, u32[]{:S(2)}) %collective-permute-start.33) | collective-permute-done | bytes 311328 | tf_op jit(solution)/shard_map/ppermute | solution.py:646
  197.9 3.8 %grad_extra.1 = (f32[256,128]{1,0:T(8,128)S(1)}, f32[256,128]{1,0:T(8,128)S(1)}, f32[256,128]{1,0:T(8,128)S(1)}, f32[256,128]{1,0:T(8,128)S(1)}, f32[16,128]{1,0:T(8,128)S(1)}, /*index=5*/f32[1,128]{1,0:T(1,128)S(1)}) custom-call(s32[10]{0:T(128)S(1)} %copy-done.14, bf16[1024,1024]{1,0:T(8,128)(2,1)} %get-tuple-element.178.normed.refs_0_, ...), custom_call_target="tpu_custom_call" | custom-call | tf_op jit(solution)/shard_map/grad_extra/pallas_call | solution.py:854
  201.9 1.5 collective-permute-start.40
  205.5 2.4 %collective-permute-done.40 = f16[304,128]{1,0:T(8,128)(2,1)S(1)} collective-permute-done((f16[304,128]{1,0:T(8,128)(2,1)S(1)}, f16[304,128]{1,0:T(8,128)(2,1)S(1)}, u32[]{:S(2)}, u32[]{:S(2)}) %collective-permute-start.40) | collective-permute-done | bytes 77856 | tf_op jit(solution)/shard_map/ppermute | solution.py:646
  208.7 2.0 collective-permute-done.41
  216.2 2.7 %collective-permute-start.45 = (f16[112,640]{1,0:T(8,128)(2,1)S(1)}, f16[112,640]{1,0:T(8,128)(2,1)S(1)}, u32[]{:S(2)}, u32[]{:S(2)}) collective-permute-start(f16[112,640]{1,0:T(8,128)(2,1)S(1)} %get-tuple-element.295), channel_id=1, source_target_pairs={{0,6},{2,4},{4,2},{6,0},{1,7},{3,5},{5,3},{7,1},{8,14},{10,12},{12... | collective-permute-start | bytes 430088 | tf_op jit(solution)/shard_map/ppermute | solution.py:638
  218.9 2.6 %maximum_select_fusion.1 = bf16[512,1024]{1,0:T(8,128)(2,1)} fusion(bf16[256,1024]{1,0:T(8,128)(2,1)} %collective-permute-done.35, bf16[256,1024]{1,0:T(8,128)(2,1)S(1)} %get-tuple-element.381, pred[]{:T(512)S(6)} %eq.8), kind=kLoop, calls=%fused_computation.14 | loop fusion | flops 4718592 | bytes 2097153 | tf_op jit(solution)/shard_map/jit(_where)/select_n | solution.py:1022
  221.5 1.5 maximum_select_fusion
  223.0 6.2 %collective-permute-done.44 = f16[112,640]{1,0:T(8,128)(2,1)S(1)} collective-permute-done((f16[112,640]{1,0:T(8,128)(2,1)}, f16[112,640]{1,0:T(8,128)(2,1)S(1)}, u32[]{:S(2)}, u32[]{:S(2)}) %collective-permute-start.44) | collective-permute-done | bytes 143392 | tf_op jit(solution)/shard_map/ppermute | solution.py:638
  230.2 2.6 %finish.1 = (f32[4,1024]{1,0:T(4,128)}, f32[1,1024]{1,0:T(1,128)}, f32[1,1024]{1,0:T(1,128)}, f32[4,256]{1,0:T(4,128)}, f32[1,256]{1,0:T(1,128)}, /*index=5*/f32...) custom-call(s32[10]{0:T(128)} %stack.79.s_ref, f32[16,640]{1,0:T(8,128)} %get-tuple-element.387.first, ...), custom_call_target="tpu_custom_call" | custom-call | tf_op jit(solution)/shard_map/finish/pallas_call | solution.py:1045
  (279 shorter events, 43.6 us)
Async XLA Ops:
  6.1 22.3 %collective-permute-start.2 = (bf16[256,896]{1,0:T(8,128)(2,1)}, bf16[256,896]{1,0:T(8,128)(2,1)}, u32[]{:S(2)}, u32[]{:S(2)}) collective-permute-start(bf16[256,896]{1,0:T(8,128)(2,1)} %concatenate.134.rest_0_), channel_id=1, source_target_pairs={{0,24},{8,16},{16,8},{24,0},{1,25},{9,17},{17,9},{25,1},{2,26},{10... | collective-permute-start | bytes 1376264 | tf_op jit(solution)/shard_map/ppermute | solution.py:646
  10.0 20.7 %collective-permute-start.1 = (bf16[256,896]{1,0:T(8,128)(2,1)}, bf16[256,896]{1,0:T(8,128)(2,1)}, u32[]{:S(2)}, u32[]{:S(2)}) collective-permute-start(bf16[256,896]{1,0:T(8,128)(2,1)} %concatenate.134.rest_0_), channel_id=1, source_target_pairs={{0,16},{8,24},{16,0},{24,8},{1,17},{9,25},{17,1},{25,9},{2,18},{10... | collective-permute-start | bytes 1376264 | tf_op jit(solution)/shard_map/ppermute | solution.py:646
  10.5 20.5 %collective-permute-start = (bf16[256,896]{1,0:T(8,128)(2,1)}, bf16[256,896]{1,0:T(8,128)(2,1)}, u32[]{:S(2)}, u32[]{:S(2)}) collective-permute-start(bf16[256,896]{1,0:T(8,128)(2,1)} %concatenate.134.rest_0_), channel_id=1, source_target_pairs={{0,8},{8,0},{16,24},{24,16},{1,9},{9,1},{17,25},{25,17},{2,10},{10... | collective-permute-start | bytes 1376264 | tf_op jit(solution)/shard_map/ppermute | solution.py:646
  10.7 13.4 %collective-permute-start.3 = (bf16[256,1024]{1,0:T(8,128)(2,1)S(1)}, bf16[256,1024]{1,0:T(8,128)(2,1)}, u32[]{:S(2)}, u32[]{:S(2)}) collective-permute-start(bf16[256,1024]{1,0:T(8,128)(2,1)S(1)} %get-tuple-element.365), channel_id=1, source_target_pairs={{0,2},{2,0},{4,6},{6,4},{1,3},{3,1},{5,7},{7,5},{8,10},{10,8},{12,... | collective-permute-start | bytes 1572872 | tf_op jit(solution)/shard_map/ppermute | solution.py:638
  16.4 0.7 collective-permute-start.5
  17.0 7.9 %collective-permute-start.6 = (bf16[16,1024]{1,0:T(8,128)(2,1)S(1)}, bf16[16,1024]{1,0:T(8,128)(2,1)S(1)}, u32[]{:S(2)}, u32[]{:S(2)}) collective-permute-start(bf16[16,1024]{1,0:T(8,128)(2,1)S(1)} %collective-permute-done.5), channel_id=1, source_target_pairs={{0,1},{1,0},{2,3},{3,2},{4,5},{5,4},{6,7},{7,6},{8,9},{9,8},{10,11... | collective-permute-start | bytes 98312 | tf_op jit(solution)/shard_map/ppermute | solution.py:635
  24.1 10.5 %collective-permute-start.4 = (bf16[256,1024]{1,0:T(8,128)(2,1)}, bf16[256,1024]{1,0:T(8,128)(2,1)}, u32[]{:S(2)}, u32[]{:S(2)}) collective-permute-start(bf16[256,1024]{1,0:T(8,128)(2,1)} %collective-permute-done.3.near), channel_id=1, source_target_pairs={{0,1},{1,0},{2,3},{3,2},{4,5},{5,4},{6,7},{7,6},{8,9},{9,8},{10,11... | collective-permute-start | bytes 1572872 | tf_op jit(solution)/shard_map/ppermute | solution.py:635
  25.0 23.7 %collective-permute-start.7 = (bf16[256,1024]{1,0:T(8,128)(2,1)}, bf16[256,1024]{1,0:T(8,128)(2,1)}, u32[]{:S(2)}, u32[]{:S(2)}) collective-permute-start(bf16[256,1024]{1,0:T(8,128)(2,1)} %constant_dynamic-slice_fusion.12), channel_id=1, source_target_pairs={{0,2},{2,0},{4,6},{6,4},{1,3},{3,1},{5,7},{7,5},{8,10},{10,8},{12,... | collective-permute-start | bytes 1572872 | tf_op jit(solution)/shard_map/ppermute | solution.py:638
  31.1 29.6 %collective-permute-start.11 = (bf16[256,1024]{1,0:T(8,128)(2,1)S(1)}, bf16[256,1024]{1,0:T(8,128)(2,1)S(1)}, u32[]{:S(2)}, u32[]{:S(2)}) collective-permute-start(bf16[256,1024]{1,0:T(8,128)(2,1)S(1)} %pad_maximum_fusion.13.rest_0_.rest_4_), channel_id=1, source_target_pairs={{0,24},{8,16},{16,8},{24,0},{1,25},{9,17},{17,9},{25,1},{2,26},{10... | collective-permute-start | bytes 1572872 | tf_op jit(solution)/shard_map/ppermute | solution.py:646
  32.6 28.1 %collective-permute-start.10 = (bf16[256,1024]{1,0:T(8,128)(2,1)S(1)}, bf16[256,1024]{1,0:T(8,128)(2,1)S(1)}, u32[]{:S(2)}, u32[]{:S(2)}) collective-permute-start(bf16[256,1024]{1,0:T(8,128)(2,1)S(1)} %pad_maximum_fusion.13.rest_0_.rest_4_), channel_id=1, source_target_pairs={{0,16},{8,24},{16,0},{24,8},{1,17},{9,25},{17,1},{25,9},{2,18},{10... | collective-permute-start | bytes 1572872 | tf_op jit(solution)/shard_map/ppermute | solution.py:646
  34.1 26.6 %collective-permute-start.9 = (bf16[256,1024]{1,0:T(8,128)(2,1)S(1)}, bf16[256,1024]{1,0:T(8,128)(2,1)S(1)}, u32[]{:S(2)}, u32[]{:S(2)}) collective-permute-start(bf16[256,1024]{1,0:T(8,128)(2,1)S(1)} %pad_maximum_fusion.13.rest_0_.rest_4_), channel_id=1, source_target_pairs={{0,8},{8,0},{16,24},{24,16},{1,9},{9,1},{17,25},{25,17},{2,10},{10... | collective-permute-start | bytes 1572872 | tf_op jit(solution)/shard_map/ppermute | solution.py:646
  48.6 12.0 %collective-permute-start.8 = (bf16[256,1024]{1,0:T(8,128)(2,1)}, bf16[256,1024]{1,0:T(8,128)(2,1)S(1)}, u32[]{:S(2)}, u32[]{:S(2)}) collective-permute-start(bf16[256,1024]{1,0:T(8,128)(2,1)} %collective-permute-done.7.near), channel_id=1, source_target_pairs={{0,1},{1,0},{2,3},{3,2},{4,5},{5,4},{6,7},{7,6},{8,9},{9,8},{10,11... | collective-permute-start | bytes 1572872 | tf_op jit(solution)/shard_map/ppermute | solution.py:635
  48.7 20.3 %collective-permute-start.12 = (f32[128,512]{1,0:T(8,128)}, f32[128,512]{1,0:T(8,128)S(1)}, u32[]{:S(2)}, u32[]{:S(2)}) collective-permute-start(f32[128,512]{1,0:T(8,128)} %get-tuple-element.188.hend), channel_id=1, source_target_pairs={{0,4},{2,6},{1,5},{3,7},{8,12},{10,14},{9,13},{11,15},{16,20},{18,... | collective-permute-start | bytes 786440 | tf_op jit(solution)/shard_map/ppermute | solution.py:641
  75.6 4.2 %collective-permute-start.15 = (f32[16,1024]{1,0:T(8,128)S(1)}, f32[16,1024]{1,0:T(8,128)S(1)}, u32[]{:S(2)}, u32[]{:S(2)}) collective-permute-start(f32[16,1024]{1,0:T(8,128)S(1)} %get-tuple-element.190.sums), channel_id=1, source_target_pairs={{0,3},{1,2},{2,1},{3,0},{4,7},{5,6},{6,5},{7,4},{8,11},{9,10},{10,... | collective-permute-start | bytes 196616 | tf_op jit(solution)/shard_map/ppermute | solution.py:817
  77.3 4.3 %collective-permute-start.14 = (f32[16,1024]{1,0:T(8,128)S(1)}, f32[16,1024]{1,0:T(8,128)S(1)}, u32[]{:S(2)}, u32[]{:S(2)}) collective-permute-start(f32[16,1024]{1,0:T(8,128)S(1)} %get-tuple-element.190.sums), channel_id=1, source_target_pairs={{0,2},{2,0},{4,6},{6,4},{1,3},{3,1},{5,7},{7,5},{8,10},{10,8},{12,... | collective-permute-start | bytes 196616 | tf_op jit(solution)/shard_map/ppermute | solution.py:638
  77.6 4.0 %collective-permute-start.13 = (f32[16,1024]{1,0:T(8,128)S(1)}, f32[16,1024]{1,0:T(8,128)S(1)}, u32[]{:S(2)}, u32[]{:S(2)}) collective-permute-start(f32[16,1024]{1,0:T(8,128)S(1)} %get-tuple-element.190.sums), channel_id=1, source_target_pairs={{0,1},{1,0},{2,3},{3,2},{4,5},{5,4},{6,7},{7,6},{8,9},{9,8},{10,11... | collective-permute-start | bytes 196616 | tf_op jit(solution)/shard_map/ppermute | solution.py:635
  98.1 23.6 %collective-permute-start.19 = (f16[272,1024]{1,0:T(8,128)(2,1)S(1)}, f16[272,1024]{1,0:T(8,128)(2,1)}, u32[]{:S(2)}, u32[]{:S(2)}) collective-permute-start(f16[272,1024]{1,0:T(8,128)(2,1)S(1)} %get-tuple-element.417), channel_id=1, source_target_pairs={{0,24},{8,16},{16,8},{24,0},{1,25},{9,17},{17,9},{25,1},{2,26},{10... | collective-permute-start | bytes 1671176 | tf_op jit(solution)/shard_map/ppermute | solution.py:646
  99.9 25.3 %collective-permute-start.18 = (f16[272,1024]{1,0:T(8,128)(2,1)S(1)}, f16[272,1024]{1,0:T(8,128)(2,1)}, u32[]{:S(2)}, u32[]{:S(2)}) collective-permute-start(f16[272,1024]{1,0:T(8,128)(2,1)S(1)} %get-tuple-element.418), channel_id=1, source_target_pairs={{0,16},{8,24},{16,0},{24,8},{1,17},{9,25},{17,1},{25,9},{2,18},{10... | collective-permute-start | bytes 1671176 | tf_op jit(solution)/shard_map/ppermute | solution.py:646
  101.1 24.0 %collective-permute-start.17 = (f16[272,1024]{1,0:T(8,128)(2,1)S(1)}, f16[272,1024]{1,0:T(8,128)(2,1)}, u32[]{:S(2)}, u32[]{:S(2)}) collective-permute-start(f16[272,1024]{1,0:T(8,128)(2,1)S(1)} %get-tuple-element.419), channel_id=1, source_target_pairs={{0,8},{8,0},{16,24},{24,16},{1,9},{9,1},{17,25},{25,17},{2,10},{10... | collective-permute-start | bytes 1671176 | tf_op jit(solution)/shard_map/ppermute | solution.py:646
  101.7 20.0 %collective-permute-start.16 = (f32[128,512]{1,0:T(8,128)S(1)}, f32[128,512]{1,0:T(8,128)S(1)}, u32[]{:S(2)}, u32[]{:S(2)}) collective-permute-start(f32[128,512]{1,0:T(8,128)S(1)} %get-tuple-element.191), channel_id=1, source_target_pairs={{4,0},{6,2},{5,1},{7,3},{12,8},{14,10},{13,9},{15,11},{20,16},{22,... | collective-permute-start | bytes 786440 | tf_op jit(solution)/shard_map/ppermute | solution.py:641
  125.2 2.9 %collective-permute-start.21 = (f32[256,1024]{1,0:T(8,128)}, f32[256,1024]{1,0:T(8,128)S(1)}, u32[]{:S(2)}, u32[]{:S(2)}) collective-permute-start(f32[256,1024]{1,0:T(8,128)} %get-tuple-element.216), channel_id=1, source_target_pairs={{0,1},{1,0},{2,3},{3,2},{4,5},{5,4},{6,7},{7,6},{8,9},{9,8},{10,11... | collective-permute-start | bytes 3145736 | tf_op jit(solution)/shard_map/ppermute | solution.py:635
  129.1 15.8 %collective-permute-start.22 = (f32[80,1024]{1,0:T(8,128)S(1)}, f32[80,1024]{1,0:T(8,128)S(1)}, u32[]{:S(2)}, u32[]{:S(2)}) collective-permute-start(f32[80,1024]{1,0:T(8,128)S(1)} %slice_add_fusion.1), channel_id=1, source_target_pairs={{0,2},{2,0},{4,6},{6,4},{1,3},{3,1},{5,7},{7,5},{8,10},{10,8},{12,... | collective-permute-start | bytes 983048 | tf_op jit(solution)/shard_map/ppermute | solution.py:638
  131.2 23.8 %collective-permute-start.25 = (f16[80,1024]{1,0:T(8,128)(2,1)S(1)}, f16[80,1024]{1,0:T(8,128)(2,1)S(1)}, u32[]{:S(2)}, u32[]{:S(2)}) collective-permute-start(f16[80,1024]{1,0:T(8,128)(2,1)S(1)} %get-tuple-element.414), channel_id=1, source_target_pairs={{0,6},{2,4},{4,2},{6,0},{1,7},{3,5},{5,3},{7,1},{8,14},{10,12},{12... | collective-permute-start | bytes 491528 | tf_op jit(solution)/shard_map/ppermute | solution.py:638
  131.3 23.7 %collective-permute-start.24 = (f16[80,1024]{1,0:T(8,128)(2,1)S(1)}, f16[80,1024]{1,0:T(8,128)(2,1)S(1)}, u32[]{:S(2)}, u32[]{:S(2)}) collective-permute-start(f16[80,1024]{1,0:T(8,128)(2,1)S(1)} %get-tuple-element.415), channel_id=1, source_target_pairs={{0,4},{2,6},{4,0},{6,2},{1,5},{3,7},{5,1},{7,3},{8,12},{10,14},{12... | collective-permute-start | bytes 491528 | tf_op jit(solution)/shard_map/ppermute | solution.py:638
  132.8 22.2 %collective-permute-start.23 = (f16[80,1024]{1,0:T(8,128)(2,1)S(1)}, f16[80,1024]{1,0:T(8,128)(2,1)S(1)}, u32[]{:S(2)}, u32[]{:S(2)}) collective-permute-start(f16[80,1024]{1,0:T(8,128)(2,1)S(1)} %get-tuple-element.416), channel_id=1, source_target_pairs={{0,2},{2,0},{4,6},{6,4},{1,3},{3,1},{5,7},{7,5},{8,10},{10,8},{12,... | collective-permute-start | bytes 491528 | tf_op jit(solution)/shard_map/ppermute | solution.py:638
  143.6 12.6 %collective-permute-start.26 = (f32[8,512]{1,0:T(8,128)S(1)}, f32[8,512]{1,0:T(8,128)S(1)}, u32[]{:S(2)}, u32[]{:S(2)}) collective-permute-start(f32[8,512]{1,0:T(8,128)S(1)} %get-tuple-element.235), channel_id=1, source_target_pairs={{4,0},{6,2},{5,1},{7,3},{12,8},{14,10},{13,9},{15,11},{20,16},{22,... | collective-permute-start | bytes 49160 | tf_op jit(solution)/shard_map/ppermute | solution.py:641
  156.2 1.9 collective-permute-start.27
  158.2 8.4 %collective-permute-start.28 = (f32[512,128]{1,0:T(8,128)S(1)}, f32[512,128]{1,0:T(8,128)S(1)}, u32[]{:S(2)}, u32[]{:S(2)}) collective-permute-start(f32[512,128]{1,0:T(8,128)S(1)} %constant_dynamic-slice_fusion.10), channel_id=1, source_target_pairs={{0,2},{2,0},{4,6},{6,4},{1,3},{3,1},{5,7},{7,5},{8,10},{10,8},{12,... | collective-permute-start | bytes 786440 | tf_op jit(solution)/shard_map/ppermute | solution.py:638
  166.7 1.6 collective-permute-start.29
  168.9 6.4 %collective-permute-start.30 = (f32[8,128]{1,0:T(8,128)S(1)}, f32[8,128]{1,0:T(8,128)S(1)}, u32[]{:S(2)}, u32[]{:S(2)}) collective-permute-start(f32[8,128]{1,0:T(8,128)S(1)} %fusion.21), channel_id=1, source_target_pairs={{4,0},{6,2},{5,1},{7,3},{12,8},{14,10},{13,9},{15,11},{20,16},{22,... | collective-permute-start | bytes 12296 | tf_op jit(solution)/shard_map/ppermute | solution.py:641
  175.3 17.5 %collective-permute-start.31 = (f32[176,1024]{1,0:T(8,128)}, f32[176,1024]{1,0:T(8,128)S(1)}, u32[]{:S(2)}, u32[]{:S(2)}) collective-permute-start(f32[176,1024]{1,0:T(8,128)} %slice_add_fusion), channel_id=1, source_target_pairs={{0,2},{2,0},{4,6},{6,4},{1,3},{3,1},{5,7},{7,5},{8,10},{10,8},{12,... | collective-permute-start | bytes 2162696 | tf_op jit(solution)/shard_map/ppermute | solution.py:638
  175.6 12.6 %collective-permute-start.32 = (f16[304,512]{1,0:T(8,128)(2,1)}, f16[304,512]{1,0:T(8,128)(2,1)}, u32[]{:S(2)}, u32[]{:S(2)}) collective-permute-start(f16[304,512]{1,0:T(8,128)(2,1)} %get-tuple-element.264), channel_id=1, source_target_pairs={{0,8},{8,0},{16,24},{24,16},{1,9},{9,1},{17,25},{25,17},{2,10},{10... | collective-permute-start | bytes 933896 | tf_op jit(solution)/shard_map/ppermute | solution.py:646
  177.1 15.0 %collective-permute-start.33 = (f16[304,512]{1,0:T(8,128)(2,1)}, f16[304,512]{1,0:T(8,128)(2,1)}, u32[]{:S(2)}, u32[]{:S(2)}) collective-permute-start(f16[304,512]{1,0:T(8,128)(2,1)} %get-tuple-element.265), channel_id=1, source_target_pairs={{0,16},{8,24},{16,0},{24,8},{1,17},{9,25},{17,1},{25,9},{2,18},{10... | collective-permute-start | bytes 933896 | tf_op jit(solution)/shard_map/ppermute | solution.py:646
  177.9 14.2 %collective-permute-start.34 = (f16[304,512]{1,0:T(8,128)(2,1)S(1)}, f16[304,512]{1,0:T(8,128)(2,1)}, u32[]{:S(2)}, u32[]{:S(2)}) collective-permute-start(f16[304,512]{1,0:T(8,128)(2,1)S(1)} %get-tuple-element.266), channel_id=1, source_target_pairs={{0,24},{8,16},{16,8},{24,0},{1,25},{9,17},{17,9},{25,1},{2,26},{10... | collective-permute-start | bytes 933896 | tf_op jit(solution)/shard_map/ppermute | solution.py:646
  192.9 2.7 %collective-permute-start.37 = (f32[256,1024]{1,0:T(8,128)S(1)}, f32[256,1024]{1,0:T(8,128)S(1)}, u32[]{:S(2)}, u32[]{:S(2)}) collective-permute-start(f32[256,1024]{1,0:T(8,128)S(1)} %get-tuple-element.272), channel_id=1, source_target_pairs={{0,1},{1,0},{2,3},{3,2},{4,5},{5,4},{6,7},{7,6},{8,9},{9,8},{10,11... | collective-permute-start | bytes 3145736 | tf_op jit(solution)/shard_map/ppermute | solution.py:635
  192.9 19.8 %collective-permute-start.20 = (f32[256,1024]{1,0:T(8,128)S(1)}, f32[256,1024]{1,0:T(8,128)S(1)}, u32[]{:S(2)}, u32[]{:S(2)}) collective-permute-start(f32[256,1024]{1,0:T(8,128)S(1)} %copy-done.44), channel_id=1, source_target_pairs={{0,1},{1,0},{2,3},{3,2},{4,5},{5,4},{6,7},{7,6},{8,9},{9,8},{10,11... | collective-permute-start | bytes 3145736 | tf_op jit(solution)/shard_map/ppermute | solution.py:635
  196.0 14.7 %collective-permute-start.41 = (f16[272,1024]{1,0:T(8,128)(2,1)S(1)}, f16[272,1024]{1,0:T(8,128)(2,1)S(1)}, u32[]{:S(2)}, u32[]{:S(2)}) collective-permute-start(f16[272,1024]{1,0:T(8,128)(2,1)S(1)} %pad_maximum_fusion.3), channel_id=1, source_target_pairs={{0,2},{2,0},{4,6},{6,4},{1,3},{3,1},{5,7},{7,5},{8,10},{10,8},{12,... | collective-permute-start | bytes 1671176 | tf_op jit(solution)/shard_map/ppermute | solution.py:638
  201.9 6.0 %collective-permute-start.40 = (f16[304,128]{1,0:T(8,128)(2,1)S(1)}, f16[304,128]{1,0:T(8,128)(2,1)S(1)}, u32[]{:S(2)}, u32[]{:S(2)}) collective-permute-start(f16[304,128]{1,0:T(8,128)(2,1)S(1)} %get-tuple-element.420), channel_id=1, source_target_pairs={{0,24},{8,16},{16,8},{24,0},{1,25},{9,17},{17,9},{25,1},{2,26},{10... | collective-permute-start | bytes 233480 | tf_op jit(solution)/shard_map/ppermute | solution.py:646
  203.4 5.2 %collective-permute-start.39 = (f16[304,128]{1,0:T(8,128)(2,1)S(1)}, f16[304,128]{1,0:T(8,128)(2,1)S(1)}, u32[]{:S(2)}, u32[]{:S(2)}) collective-permute-start(f16[304,128]{1,0:T(8,128)(2,1)S(1)} %get-tuple-element.421), channel_id=1, source_target_pairs={{0,16},{8,24},{16,0},{24,8},{1,17},{9,25},{17,1},{25,9},{2,18},{10... | collective-permute-start | bytes 233480 | tf_op jit(solution)/shard_map/ppermute | solution.py:646
  204.3 4.4 %collective-permute-start.38 = (f16[304,128]{1,0:T(8,128)(2,1)S(1)}, f16[304,128]{1,0:T(8,128)(2,1)S(1)}, u32[]{:S(2)}, u32[]{:S(2)}) collective-permute-start(f16[304,128]{1,0:T(8,128)(2,1)S(1)} %get-tuple-element.422), channel_id=1, source_target_pairs={{0,8},{8,0},{16,24},{24,16},{1,9},{9,1},{17,25},{25,17},{2,10},{10... | collective-permute-start | bytes 233480 | tf_op jit(solution)/shard_map/ppermute | solution.py:646
  207.9 4.4 %collective-permute-start.36 = (f32[256,1024]{1,0:T(8,128)S(1)}, f32[256,1024]{1,0:T(8,128)S(1)}, u32[]{:S(2)}, u32[]{:S(2)}) collective-permute-start(f32[256,1024]{1,0:T(8,128)S(1)} %get-tuple-element.269), channel_id=1, source_target_pairs={{0,1},{1,0},{2,3},{3,2},{4,5},{5,4},{6,7},{7,6},{8,9},{9,8},{10,11... | collective-permute-start | bytes 3145736 | tf_op jit(solution)/shard_map/ppermute | solution.py:635
  213.4 8.1 %collective-permute-start.42 = (f32[256,1024]{1,0:T(8,128)S(1)}, f32[256,1024]{1,0:T(8,128)S(1)}, u32[]{:S(2)}, u32[]{:S(2)}) collective-permute-start(f32[256,1024]{1,0:T(8,128)S(1)} %get-tuple-element.380), channel_id=1, source_target_pairs={{0,1},{1,0},{2,3},{3,2},{4,5},{5,4},{6,7},{7,6},{8,9},{9,8},{10,11... | collective-permute-start | bytes 3145736 | tf_op jit(solution)/shard_map/ppermute | solution.py:635
  213.5 5.4 %collective-permute-start.35 = (bf16[256,1024]{1,0:T(8,128)(2,1)S(1)}, bf16[256,1024]{1,0:T(8,128)(2,1)}, u32[]{:S(2)}, u32[]{:S(2)}) collective-permute-start(bf16[256,1024]{1,0:T(8,128)(2,1)S(1)} %get-tuple-element.381), channel_id=1, source_target_pairs={{0,1},{1,0},{2,3},{3,2},{4,5},{5,4},{6,7},{7,6},{8,9},{9,8},{10,11... | collective-permute-start | bytes 1572872 | tf_op jit(solution)/shard_map/ppermute | solution.py:635
  214.5 8.5 %collective-permute-start.43 = (f16[112,640]{1,0:T(8,128)(2,1)}, f16[112,640]{1,0:T(8,128)(2,1)S(1)}, u32[]{:S(2)}, u32[]{:S(2)}) collective-permute-start(f16[112,640]{1,0:T(8,128)(2,1)} %get-tuple-element.293), channel_id=1, source_target_pairs={{0,2},{2,0},{4,6},{6,4},{1,3},{3,1},{5,7},{7,5},{8,10},{10,8},{12,... | collective-permute-start | bytes 430088 | tf_op jit(solution)/shard_map/ppermute | solution.py:638
  215.4 13.7 %collective-permute-start.44 = (f16[112,640]{1,0:T(8,128)(2,1)}, f16[112,640]{1,0:T(8,128)(2,1)S(1)}, u32[]{:S(2)}, u32[]{:S(2)}) collective-permute-start(f16[112,640]{1,0:T(8,128)(2,1)} %get-tuple-element.294), channel_id=1, source_target_pairs={{0,4},{2,6},{4,0},{6,2},{1,5},{3,7},{5,1},{7,3},{8,12},{10,14},{12... | collective-permute-start | bytes 430088 | tf_op jit(solution)/shard_map/ppermute | solution.py:638
  216.2 13.0 %collective-permute-start.45 = (f16[112,640]{1,0:T(8,128)(2,1)S(1)}, f16[112,640]{1,0:T(8,128)(2,1)S(1)}, u32[]{:S(2)}, u32[]{:S(2)}) collective-permute-start(f16[112,640]{1,0:T(8,128)(2,1)S(1)} %get-tuple-element.295), channel_id=1, source_target_pairs={{0,6},{2,4},{4,2},{6,0},{1,7},{3,5},{5,3},{7,1},{8,14},{10,12},{12... | collective-permute-start | bytes 430088 | tf_op jit(solution)/shard_map/ppermute | solution.py:638
  232.8 2.6 %collective-permute-start.46 = (f32[1024]{0:T(1024)}, f32[1024]{0:T(1024)S(1)}, u32[]{:S(2)}, u32[]{:S(2)}) collective-permute-start(f32[1024]{0:T(1024)} %bitcast.121), channel_id=1, source_target_pairs={{0,1},{1,0},{2,3},{3,2},{4,5},{5,4},{6,7},{7,6},{8,9},{9,8},{10,11... | collective-permute-start | bytes 12296 | tf_op jit(solution)/shard_map/ppermute | solution.py:635
  233.0 3.0 %collective-permute-start.47 = (f32[2,64,64]{2,1,0:T(8,128)S(1)}, f32[2,64,64]{2,1,0:T(8,128)S(1)}, u32[]{:S(2)}, u32[]{:S(2)}) collective-permute-start(f32[2,64,64]{2,1,0:T(8,128)S(1)} %get-tuple-element.403), channel_id=1, source_target_pairs={{0,1},{1,0},{2,3},{3,2},{4,5},{5,4},{6,7},{7,6},{8,9},{9,8},{10,11... | collective-permute-start | bytes 98312 | tf_op jit(solution)/shard_map/ppermute | solution.py:635
  (48 other events, 476.2 us)
